TPU v7x, 32 devices: a whole 2x2x4 slice. The times are simulated.
32 devices in a mesh: lat: 4 (over x, core), lon: 8 (over z, y).
Axes of the slice: x: 2, y: 2, z: 4, core: 2. Of those that a mesh axis runs over, the one named last changes fastest.
Arguments:
- control: float32 [256, 512, 128], P('lat', 'lon'), may hold values from -6 to 6
- kappa: float32 [256, 512], P('lat', 'lon'), may hold values from 0.1 to 0.24
- sigma: float32 [256, 512, 128], P('lat', 'lon'), may hold values from 0.5 to 2
- vertical: float32 [128, 128], replicated, may hold values from -0.5 to 0.5
- channel_table: bfloat16 [616, 128], replicated, may hold values from -0.5 to 0.5
- channel_pick: int32 [64], replicated, may hold values from 0 to 615
- r_inverse: float32 [64, 64], replicated, may hold values from -1 to 4, as said below
- innovations: float32 [32768, 64], P(('lat', 'lon')), may hold values from -6 to 6
- error_scale: float32 [32768], P(('lat', 'lon')), may hold values from 0.5 to 2
- obs_owner: int32 [32768, 1], P(('lat', 'lon')), may hold values from 0 to 31; in each aligned block of 1024 rows (0 to 1023, 1024 to 2047, ...) at most 64 rows name the same one
- obs_cell: int32 [32768], P(('lat', 'lon')), may hold values from 0 to 4095
- obs_count: int32 [32], P(('lat', 'lon')), may hold values from 128 to 1024, as said below
Outputs:
- gradient: float32 [256, 512, 128], P('lat', 'lon')
- departures: float32 [32768, 64], P(('lat', 'lon'))
Inputs may be any that keep to these rules, and one draw needn't show every extreme that they name: `obs_owner`: in the rows of one device, at most 64 observations name one owner, a bound that some block reaches of them. `obs_count`: some device holds 1024 valid observations; the valid ones are the first of a device's slots. `r_inverse`: Symmetric.
All inputs are finite; a program needn't handle non-finite values.
Results may differ from a plain program's by a relative error of at most 0.0013.
Values may be sent and summed in bfloat16 or wider, within the bound.
No kernel may reach another device: no remote copies, remote signals or barrier semaphores. Data moves between devices by JAX's collectives and lax.ppermute only.
A program may use at most 64 MiB of HBM per device.

v0:
```python
import jax
import jax.numpy as jnp
from jax import lax
from jax.sharding import PartitionSpec as P

NSTEP = 4


def with_halo(block, sides, width):
    for axis, dim in sides:
        count = lax.axis_size(axis)
        forward = [(i, i + 1) for i in range(count - 1)]
        forward.append((count - 1, 0))
        backward = [(target, source) for source, target in forward]
        low = lax.ppermute(
            lax.slice_in_dim(block, block.shape[dim] - width, None, axis=dim), axis, forward
        )
        high = lax.ppermute(lax.slice_in_dim(block, 0, width, axis=dim), axis, backward)
        block = jnp.concatenate([low, block, high], axis=dim)
    return block


def laplacian(padded):
    return (
        padded[2:, 1:-1]
        + padded[:-2, 1:-1]
        + padded[1:-1, 2:]
        + padded[1:-1, :-2]
        - 4.0 * padded[1:-1, 1:-1]
    )


def crop_margin(field, margin):
    return field[margin : field.shape[0] - margin, margin : field.shape[1] - margin]


def body(
    control,
    kappa,
    sigma,
    vertical,
    channel_table,
    channel_pick,
    r_inverse,
    innovations,
    error_scale,
    obs_owner,
    obs_cell,
    obs_count,
):
    lat_rows, lon_cols, levels = control.shape
    at_north = lax.axis_index("lat") == 0
    at_south = lax.axis_index("lat") == lax.axis_size("lat") - 1

    def clip_poles(padded, width):
        upper_rim = jnp.where(at_north, jnp.zeros_like(padded[:width]), padded[:width])
        lower_rim = jnp.where(at_south, jnp.zeros_like(padded[-width:]), padded[-width:])
        return jnp.concatenate([upper_rim, padded[width:-width], lower_rim], axis=0)

    state = jnp.dot(
        control.reshape(-1, levels),
        vertical,
        precision=lax.Precision.HIGHEST,
        preferred_element_type=jnp.float32,
    ).reshape(lat_rows, lon_cols, levels)

    def rim_wide(field):
        return clip_poles(with_halo(field, (("lat", 0), ("lon", 1)), NSTEP), NSTEP)

    kappa_wide = clip_poles(with_halo(kappa, (("lat", 0), ("lon", 1)), NSTEP), NSTEP)[:, :, None]
    current = rim_wide(state)
    for sweep in range(1, NSTEP + 1):
        current = current[1:-1, 1:-1] + crop_margin(kappa_wide, sweep) * laplacian(current)
    state = current
    profiles = (sigma * state).astype(jnp.bfloat16).reshape(lat_rows * lon_cols, levels)
    table_rows = channel_table.shape[0]
    pick_table = (channel_pick[:, None] == jnp.arange(table_rows, dtype=jnp.int32)[None, :]).astype(
        jnp.bfloat16
    )
    picked = jnp.dot(pick_table, channel_table, preferred_element_type=jnp.float32).astype(
        jnp.bfloat16
    )
    obs_slots = obs_cell.shape[0]
    devices_all = lax.axis_size("lat") * lax.axis_size("lon")
    capacity = max(2, 2 * obs_slots // devices_all)
    total_slots = devices_all * capacity
    owner = obs_owner[:, 0]
    one_hot = (owner[:, None] == jnp.arange(devices_all, dtype=jnp.int32)[None, :]).astype(
        jnp.int32
    )
    position = jnp.sum((jnp.cumsum(one_hot, axis=0) - one_hot) * one_hot, axis=1)
    slot_of = owner * capacity + position
    source = (
        jnp.full((total_slots,), obs_slots, jnp.int32)
        .at[slot_of]
        .set(jnp.arange(obs_slots, dtype=jnp.int32))
    )
    slot_used = source < obs_slots
    source_safe = jnp.minimum(source, obs_slots - 1)
    valid = jnp.arange(obs_slots, dtype=jnp.int32) < obs_count[0]
    weight = jnp.where(valid, 1.0 / (error_scale * error_scale), jnp.float32(0.0))
    send_cells = jnp.where(slot_used, obs_cell[source_safe], 0)
    recv_cells = lax.all_to_all(send_cells, ("lat", "lon"), split_axis=0, concat_axis=0, tiled=True)
    profile_slots = lax.all_to_all(
        profiles[recv_cells], ("lat", "lon"), split_axis=0, concat_axis=0, tiled=True
    )
    evolved = lax.dot_general(
        profile_slots[slot_of], picked, (((1,), (1,)), ((), ())), preferred_element_type=jnp.float32
    )
    departures = (
        jnp.dot(
            evolved - innovations,
            r_inverse,
            precision=lax.Precision.HIGHEST,
            preferred_element_type=jnp.float32,
        )
        * weight[:, None]
    )
    increments = jnp.dot(
        departures.astype(jnp.bfloat16), picked, preferred_element_type=jnp.float32
    )
    send_incr = jnp.where(slot_used[:, None], increments[source_safe], jnp.float32(0.0))
    slot_incr = lax.all_to_all(send_incr, ("lat", "lon"), split_axis=0, concat_axis=0, tiled=True)
    obs_gradient = (
        jnp.zeros((lat_rows * lon_cols, levels), jnp.float32)
        .at[recv_cells]
        .add(slot_incr)
        .reshape(lat_rows, lon_cols, levels)
    )
    adjoint = sigma * obs_gradient
    current = rim_wide(adjoint)
    for sweep in range(1, NSTEP + 1):
        current = current[1:-1, 1:-1] + laplacian(crop_margin(kappa_wide, sweep - 1) * current)
    adjoint = current
    back = lax.dot_general(
        adjoint.reshape(-1, levels),
        vertical,
        (((1,), (1,)), ((), ())),
        precision=lax.Precision.HIGHEST,
        preferred_element_type=jnp.float32,
    )
    gradient = control + back.reshape(lat_rows, lon_cols, levels)
    return (gradient, departures)


def solution(mesh):
    return jax.shard_map(
        body,
        mesh=mesh,
        in_specs=(
            P("lat", "lon", None),
            P("lat", "lon"),
            P("lat", "lon", None),
            P(),
            P(),
            P(),
            P(),
            P(("lat", "lon"), None),
            P(("lat", "lon")),
            P(("lat", "lon"), None),
            P(("lat", "lon")),
            P(("lat", "lon")),
        ),
        out_specs=(P("lat", "lon", None), P(("lat", "lon"), None)),
        check_vma=False,
    )
```

profile of v0, /device:TPU:0, one launch (start us, length us, event | category | flops | bytes accessed | tf_op | source)
XLA Modules:
  0.0 178.6 jit_solution(13804640189942897095)
XLA Ops:
  1.9 1.9 %collective-permute-start.5 = (f32[4,64]{1,0:T(4,128)S(1)}, f32[4,64]{1,0:T(4,128)S(1)}, u32[]{:S(2)}, u32[]{:S(2)}) collective-permute-start(f32[4,64]{1,0:T(4,128)S(1)} %get-tuple-element.31), channel_id=1, source_target_pairs={{8,0},{16,8},{24,16},{0,24},{9,1},{17,9},{25,17},{1,25},{10,2},{18... | collective-permute-start | bytes 3080 | tf_op jit(solution)/shard_map/ppermute | solution.py:18
  4.5 9.0 %reduce-window.6 = s32[32,8,128]{2,1,0:T(8,128)S(1)} reduce-window(s32[32,8,128]{2,1,0:T(8,128)S(1)} %fusion.37, s32[]{:T(128)} %constant.12.clone.1), window={size=1x1x128 pad=0_0x0_0x127_0}, to_apply=%region_0.1 | reduce-window | flops 4161536 | bytes 262148 | tf_op jit(solution)/shard_map/reduce-window
  15.4 4.3 %scatter_custom_fusion = s32[2048]{0:T(1024)S(1)} fusion(s32[1024]{0:T(1024)S(1)} %bitcast.77, s32[1024]{0:T(1024)S(1)} %iota.18, s32[]{:T(128)} %constant.14.clone.1), kind=kCustom, calls=%fused_computation.114 | custom fusion | bytes 8196 | tf_op jit(solution)/shard_map/scatter | solution.py:96
  19.8 8.6 %gather_fusion = s32[2048]{0:T(1024)S(1)} fusion(s32[1024]{0:T(1024)S(1)} %copy-done.1, s32[2048]{0:T(1024)S(1)} %fusion.40), kind=kCustom, calls=%fused_computation | custom fusion | bytes 24576 | tf_op jit(solution)/shard_map/gather | solution.py:102
  29.1 6.7 %all-to-all-start = ((s32[32,64,1]{1,2,0:T(1,128)}), s32[32,64,1]{1,2,0:T(1,128)S(1)}, u32[]{:S(2)}, u32[]{:S(2)}) async-start(s32[32,64,1]{1,2,0:T(1,128)} %bitcast.6), calls=%async_computation | async-start | bytes 32768 | tf_op jit(solution)/shard_map/all_to_all | solution.py:103
  35.7 3.5 %fusion.52 = f32[4096,128]{1,0:T(8,128)S(1)} fusion(f32[4096,128]{1,0:T(8,128)} %bitcast.66, f32[128,128]{1,0:T(8,128)S(1)} %copy-done.7), kind=kOutput, calls=%fused_computation.125 | convolution fusion | flops 805306368 | bytes 4259840 | tf_op jit(solution)/shard_map/dot_general | solution.py:60
  39.3 1.8 collective-permute-start.6
  41.1 3.0 %collective-permute-start.7 = (f32[72,4]{1,0:T(8,128)S(1)}, f32[72,4]{1,0:T(8,128)S(1)}, u32[]{:S(2)}, u32[]{:S(2)}) collective-permute-start(f32[72,4]{1,0:T(8,128)S(1)} %get-tuple-element.29), channel_id=1, source_target_pairs={{1,0},{2,1},{3,2},{4,3},{5,4},{6,5},{7,6},{0,7},{9,8},{10,9},{11,1... | collective-permute-start | bytes 3464 | tf_op jit(solution)/shard_map/ppermute | solution.py:18
  48.7 1.6 collective-permute-done
  50.4 4.7 %collective-permute-start.3 = (f32[72,4,128]{2,1,0:T(4,128)S(1)}, f32[72,4,128]{2,1,0:T(4,128)S(1)}, u32[]{:S(2)}, u32[]{:S(2)}) collective-permute-start(f32[72,4,128]{2,1,0:T(4,128)S(1)} %get-tuple-element.19), channel_id=1, source_target_pairs={{1,0},{2,1},{3,2},{4,3},{5,4},{6,5},{7,6},{0,7},{9,8},{10,9},{11,1... | collective-permute-start | bytes 442376 | tf_op jit(solution)/shard_map/ppermute | solution.py:18
  55.1 3.4 %collective-permute-done.2 = f32[72,4,128]{2,1,0:T(4,128)S(1)} collective-permute-done((f32[72,4,128]{2,1,0:T(4,128)S(1)}, f32[72,4,128]{2,1,0:T(4,128)S(1)}, u32[]{:S(2)}, u32[]{:S(2)}) %collective-permute-start.2) | collective-permute-done | bytes 147488 | tf_op jit(solution)/shard_map/ppermute | solution.py:15
  59.7 1.8 %fusion.4 = f32[70,70,128]{2,1,0:T(8,128)S(1)} fusion(f32[72,72,128]{2,1,0:T(8,128)S(1)} %pad_maximum_fusion.1, f32[70,70]{1,0:T(8,128)S(1)} %slice_bitcast_fusion.2), kind=kLoop, calls=%fused_computation.19 | loop fusion | flops 4390400 | bytes 15072400 | tf_op jit(solution)/shard_map/add | solution.py:73
  61.5 1.8 %fusion.9 = f32[68,68,128]{2,1,0:T(8,128)S(1)} fusion(f32[70,70,128]{2,1,0:T(8,128)S(1)} %fusion.4, f32[68,68]{1,0:T(8,128)S(1)} %slice_bitcast_fusion.1), kind=kLoop, calls=%fused_computation.31 | loop fusion | flops 4143104 | bytes 14223424 | tf_op jit(solution)/shard_map/add | solution.py:73
  63.4 1.8 %fusion.14 = f32[66,66,128]{2,1,0:T(8,128)S(1)} fusion(f32[68,68,128]{2,1,0:T(8,128)S(1)} %fusion.9, f32[66,66]{1,0:T(8,128)S(1)} %slice_bitcast_fusion), kind=kLoop, calls=%fused_computation.43 | loop fusion | flops 3902976 | bytes 13399056 | tf_op jit(solution)/shard_map/add | solution.py:73
  65.2 1.6 fusion.25
  66.8 8.1 %gather_fusion.1 = bf16[2048,128]{1,0:T(8,128)(2,1)} fusion(bf16[4096,128]{1,0:T(8,128)(2,1)S(1)} %bitcast.62, s32[2048]{0:T(1024)S(1)} %broadcast_clamp_fusion), kind=kCustom, calls=%fused_computation.1 | custom fusion | bytes 1056768 | tf_op jit(solution)/shard_map/gather | solution.py:105
  74.8 5.2 %all-to-all-start.1 = ((bf16[32,64,128]{2,1,0:T(8,128)(2,1)}), bf16[32,64,128]{2,1,0:T(8,128)(2,1)S(1)}, u32[]{:S(2)}, u32[]{:S(2)}) async-start(bf16[32,64,128]{2,1,0:T(8,128)(2,1)} %bitcast.18), calls=%async_computation.1 | async-start | bytes 1048576 | tf_op jit(solution)/shard_map/all_to_all | solution.py:104
  81.1 15.4 %all-to-all-done.1 = bf16[32,64,128]{2,1,0:T(8,128)(2,1)S(1)} async-done(((bf16[32,64,128]{2,1,0:T(8,128)(2,1)}), bf16[32,64,128]{2,1,0:T(8,128)(2,1)S(1)}, u32[]{:S(2)}, u32[]{:S(2)}) %all-to-all-start.1) | async-done | bytes 524320 | tf_op jit(solution)/shard_map/all_to_all | solution.py:104
  96.4 3.2 %gather_fusion.2 = bf16[1024,128]{1,0:T(8,128)(2,1)S(1)} fusion(bf16[2048,128]{1,0:T(8,128)(2,1)S(1)} %bitcast.63, s32[1024]{0:T(1024)S(1)} %broadcast_clamp_fusion.1), kind=kCustom, calls=%fused_computation.2 | custom fusion | bytes 528384 | tf_op jit(solution)/shard_map/gather | solution.py:108
  100.6 5.5 %gather_fusion.3 = f32[2048,128]{1,0:T(8,128)S(1)} fusion(f32[1024,128]{1,0:T(8,128)S(1)} %fusion.35, s32[2048]{0:T(1024)S(1)} %fusion.40), kind=kCustom, calls=%fused_computation.3 | custom fusion | bytes 2105344 | tf_op jit(solution)/shard_map/gather | solution.py:122
  106.4 29.7 %all_to_all.33 = f32[32,64,128]{2,1,0:T(8,128)S(1)} all-to-all(f32[32,64,128]{2,1,0:T(8,128)S(1)} %broadcast_select_fusion), channel_id=1, replica_groups=mesh['lat'=4,'lon'=8] {'lat','lon'}, dimensions={0} | all-to-all | bytes 2097152 | tf_op jit(solution)/shard_map/all_to_all | solution.py:123
  136.1 13.3 %scatter_custom_fusion.1 = f32[4096,128]{1,0:T(8,128)S(1)} fusion(s32[2048]{0:T(1024)S(1)} %bitcast.74, f32[2048,128]{1,0:T(8,128)S(1)} %bitcast.67, f32[]{:T(128)} %constant.13.clone.1), kind=kCustom, calls=%fused_computation.72 | custom fusion | flops 262144 | bytes 2097156 | tf_op jit(solution)/shard_map/scatter-add | solution.py:127
  149.4 2.1 %mul.140 = f32[64,64,128]{2,1,0:T(8,128)S(1)} multiply(f32[64,64,128]{2,1,0:T(8,128)} %param.14, f32[64,64,128]{2,1,0:T(8,128)S(1)} %bitcast.64) | non-fusion elementwise | flops 524288 | bytes 6291456 | tf_op jit(solution)/shard_map/mul | solution.py:130
  151.6 1.7 collective-permute-start.9
  153.3 3.9 %collective-permute-done.8 = f32[4,64,128]{2,1,0:T(8,128)S(1)} collective-permute-done((f32[4,64,128]{2,1,0:T(8,128)S(1)}, f32[4,64,128]{2,1,0:T(8,128)S(1)}, u32[]{:S(2)}, u32[]{:S(2)}) %collective-permute-start.8) | collective-permute-done | bytes 131104 | tf_op jit(solution)/shard_map/ppermute | solution.py:15
  158.0 4.1 %collective-permute-start.11 = (f32[72,4,128]{2,1,0:T(4,128)S(1)}, f32[72,4,128]{2,1,0:T(4,128)S(1)}, u32[]{:S(2)}, u32[]{:S(2)}) collective-permute-start(f32[72,4,128]{2,1,0:T(4,128)S(1)} %get-tuple-element.17), channel_id=1, source_target_pairs={{1,0},{2,1},{3,2},{4,3},{5,4},{6,5},{7,6},{0,7},{9,8},{10,9},{11,1... | collective-permute-start | bytes 442376 | tf_op jit(solution)/shard_map/ppermute | solution.py:18
  162.1 3.8 %collective-permute-done.10 = f32[72,4,128]{2,1,0:T(4,128)S(1)} collective-permute-done((f32[72,4,128]{2,1,0:T(4,128)S(1)}, f32[72,4,128]{2,1,0:T(4,128)S(1)}, u32[]{:S(2)}, u32[]{:S(2)}) %collective-permute-start.10) | collective-permute-done | bytes 147488 | tf_op jit(solution)/shard_map/ppermute | solution.py:15
  167.2 1.3 pad_maximum_fusion.3
  168.5 2.1 %broadcast_multiply_fusion.1 = (f32[70,70,128]{2,1,0:T(8,128)S(1)}, f32[70,70,128]{2,1,0:T(8,128)S(1)}) fusion(f32[70,70]{1,0:T(8,128)S(1)} %slice_bitcast_fusion.2, f32[72,72,128]{2,1,0:T(8,128)S(1)} %get-tuple-element.11, f32[72,72,128]{2,1,0:T(8,128)S(1)} %get-tuple-element.10), kind=kLoop, calls=%fused_computation.65 | loop fusion | flops 4390400 | bytes 20090000 | tf_op jit(solution)/shard_map/mul | solution.py:133
  170.6 2.1 %broadcast_multiply_fusion.2 = (f32[68,68,128]{2,1,0:T(8,128)S(1)}, f32[68,68,128]{2,1,0:T(8,128)S(1)}) fusion(f32[68,68]{1,0:T(8,128)S(1)} %slice_bitcast_fusion.1, f32[70,70,128]{2,1,0:T(8,128)S(1)} %get-tuple-element.6, f32[70,70,128]{2,1,0:T(8,128)S(1)} %get-tuple-element.7), kind=kLoop, calls=%fused_computation.66 | loop fusion | flops 4143104 | bytes 18958400 | tf_op jit(solution)/shard_map/mul | solution.py:133
  172.7 1.9 %broadcast_multiply_fusion.3 = (f32[66,66,128]{2,1,0:T(8,128)S(1)}, f32[66,66,128]{2,1,0:T(8,128)S(1)}) fusion(f32[66,66]{1,0:T(8,128)S(1)} %slice_bitcast_fusion, f32[68,68,128]{2,1,0:T(8,128)S(1)} %get-tuple-element.4, f32[68,68,128]{2,1,0:T(8,128)S(1)} %get-tuple-element.5), kind=kLoop, calls=%fused_computation.67 | loop fusion | flops 3902976 | bytes 17859600 | tf_op jit(solution)/shard_map/mul | solution.py:133
  174.7 3.9 %fusion.26 = f32[64,64,128]{2,1,0:T(8,128)} fusion(f32[64,64,128]{2,1,0:T(8,128)S(1)} %copy-done.3, f32[66,66,128]{2,1,0:T(8,128)S(1)} %get-tuple-element.2, f32[66,66,128]{2,1,0:T(8,128)S(1)} %get-tuple-element.3, f32[128,128]{1,0:T(8,128)S(1)} %copy-done.7), kind=kOutput, calls=%fused_computation.63 | convolution fusion | flops 808976384 | bytes 16842752 | tf_op jit(solution)/shard_map/dot_general | solution.py:135
  (85 shorter events, 14.2 us)
Async XLA Ops:
  0.6 80.2 %copy-start = (bf16[616,128]{1,0:T(8,128)(2,1)S(1)}, bf16[616,128]{1,0:T(8,128)(2,1)}, u32[]{:S(2)}) copy-start(bf16[616,128]{1,0:T(8,128)(2,1)} %param.16) | copy-start | bytes 473092
  0.6 19.1 %copy-start.1 = (s32[1024]{0:T(1024)S(1)}, s32[1024]{0:T(1024)}, u32[]{:S(2)}) copy-start(s32[1024]{0:T(1024)} %param.22) | copy-start | bytes 12292
  1.4 37.8 %collective-permute-start.4 = (f32[4,64]{1,0:T(4,128)S(1)}, f32[4,64]{1,0:T(4,128)S(1)}, u32[]{:S(2)}, u32[]{:S(2)}) collective-permute-start(f32[4,64]{1,0:T(4,128)S(1)} %get-tuple-element.30), channel_id=1, source_target_pairs={{0,8},{8,16},{16,24},{24,0},{1,9},{9,17},{17,25},{25,1},{2,10},{10... | collective-permute-start | bytes 3080 | tf_op jit(solution)/shard_map/ppermute | solution.py:15
  1.9 37.4 %collective-permute-start.5 = (f32[4,64]{1,0:T(4,128)S(1)}, f32[4,64]{1,0:T(4,128)S(1)}, u32[]{:S(2)}, u32[]{:S(2)}) collective-permute-start(f32[4,64]{1,0:T(4,128)S(1)} %get-tuple-element.31), channel_id=1, source_target_pairs={{8,0},{16,8},{24,16},{0,24},{9,1},{17,9},{25,17},{1,25},{10,2},{18... | collective-permute-start | bytes 3080 | tf_op jit(solution)/shard_map/ppermute | solution.py:18
  19.7 16.0 %copy-start.7 = (f32[128,128]{1,0:T(8,128)S(1)}, f32[128,128]{1,0:T(8,128)}, u32[]{:S(2)}) copy-start(f32[128,128]{1,0:T(8,128)} %param.15) | copy-start | bytes 196612
  28.4 10.9 %copy-start.5 = (f32[64,64]{1,0:T(8,128)S(1)}, f32[64,64]{1,0:T(8,128)}, u32[]{:S(2)}) copy-start(f32[64,64]{1,0:T(8,128)} %param.13) | copy-start | bytes 49156
  29.1 17.5 %all-to-all-start = ((s32[32,64,1]{1,2,0:T(1,128)}), s32[32,64,1]{1,2,0:T(1,128)S(1)}, u32[]{:S(2)}, u32[]{:S(2)}) async-start(s32[32,64,1]{1,2,0:T(1,128)} %bitcast.6), calls=%async_computation | async-start | bytes 32768 | tf_op jit(solution)/shard_map/all_to_all | solution.py:103
  39.3 6.7 %collective-permute-start.6 = (f32[72,4]{1,0:T(8,128)S(1)}, f32[72,4]{1,0:T(8,128)S(1)}, u32[]{:S(2)}, u32[]{:S(2)}) collective-permute-start(f32[72,4]{1,0:T(8,128)S(1)} %get-tuple-element.28), channel_id=1, source_target_pairs={{0,1},{1,2},{2,3},{3,4},{4,5},{5,6},{6,7},{7,0},{8,9},{9,10},{10,1... | collective-permute-start | bytes 3464 | tf_op jit(solution)/shard_map/ppermute | solution.py:15
  41.1 4.9 %collective-permute-start.7 = (f32[72,4]{1,0:T(8,128)S(1)}, f32[72,4]{1,0:T(8,128)S(1)}, u32[]{:S(2)}, u32[]{:S(2)}) collective-permute-start(f32[72,4]{1,0:T(8,128)S(1)} %get-tuple-element.29), channel_id=1, source_target_pairs={{1,0},{2,1},{3,2},{4,3},{5,4},{6,5},{7,6},{0,7},{9,8},{10,9},{11,1... | collective-permute-start | bytes 3464 | tf_op jit(solution)/shard_map/ppermute | solution.py:18
  44.1 4.6 %collective-permute-start.1 = (f32[4,64,128]{2,1,0:T(8,128)S(1)}, f32[4,64,128]{2,1,0:T(8,128)S(1)}, u32[]{:S(2)}, u32[]{:S(2)}) collective-permute-start(f32[4,64,128]{2,1,0:T(8,128)S(1)} %bitcast.70), channel_id=1, source_target_pairs={{8,0},{16,8},{24,16},{0,24},{9,1},{17,9},{25,17},{1,25},{10,2},{18... | collective-permute-start | bytes 393224 | tf_op jit(solution)/shard_map/ppermute | solution.py:18
  45.1 5.2 %collective-permute-start = (f32[4,64,128]{2,1,0:T(8,128)S(1)}, f32[4,64,128]{2,1,0:T(8,128)S(1)}, u32[]{:S(2)}, u32[]{:S(2)}) collective-permute-start(f32[4,64,128]{2,1,0:T(8,128)S(1)} %bitcast.69), channel_id=1, source_target_pairs={{0,8},{8,16},{16,24},{24,0},{1,9},{9,17},{17,25},{25,1},{2,10},{10... | collective-permute-start | bytes 393224 | tf_op jit(solution)/shard_map/ppermute | solution.py:15
  50.3 8.1 %collective-permute-start.2 = (f32[72,4,128]{2,1,0:T(4,128)S(1)}, f32[72,4,128]{2,1,0:T(4,128)S(1)}, u32[]{:S(2)}, u32[]{:S(2)}) collective-permute-start(f32[72,4,128]{2,1,0:T(4,128)S(1)} %get-tuple-element.18), channel_id=1, source_target_pairs={{0,1},{1,2},{2,3},{3,4},{4,5},{5,6},{6,7},{7,0},{8,9},{9,10},{10,1... | collective-permute-start | bytes 442376 | tf_op jit(solution)/shard_map/ppermute | solution.py:15
  50.4 8.5 %collective-permute-start.3 = (f32[72,4,128]{2,1,0:T(4,128)S(1)}, f32[72,4,128]{2,1,0:T(4,128)S(1)}, u32[]{:S(2)}, u32[]{:S(2)}) collective-permute-start(f32[72,4,128]{2,1,0:T(4,128)S(1)} %get-tuple-element.19), channel_id=1, source_target_pairs={{1,0},{2,1},{3,2},{4,3},{5,4},{6,5},{7,6},{0,7},{9,8},{10,9},{11,1... | collective-permute-start | bytes 442376 | tf_op jit(solution)/shard_map/ppermute | solution.py:18
  63.4 1.8 %copy-start.2 = (f32[64,64,128]{2,1,0:T(8,128)S(1)}, f32[64,64,128]{2,1,0:T(8,128)}, u32[]{:S(2)}) copy-start(f32[64,64,128]{2,1,0:T(8,128)} %param.14) | copy-start | bytes 6291460
  66.8 14.1 %copy-start.9 = (f32[1024]{0:T(1024)S(1)}, f32[1024]{0:T(1024)}, u32[]{:S(2)}) copy-start(f32[1024]{0:T(1024)} %param.20) | copy-start | bytes 12292
  66.8 14.1 %copy-start.10 = (s32[64]{0:T(128)S(1)}, s32[64]{0:T(128)}, u32[]{:S(2)}) copy-start(s32[64]{0:T(128)} %param.17) | copy-start | bytes 772
  74.8 24.8 %copy-start.6 = (f32[1024,64]{0,1:T(8,128)S(1)}, f32[1024,64]{0,1:T(8,128)}, u32[]{:S(2)}) copy-start(f32[1024,64]{0,1:T(8,128)} %param.19) | copy-start | bytes 786436
  74.8 25.0 %copy-start.8 = (f32[64,64]{1,0:T(8,128)S(1)}, f32[64,64]{1,0:T(8,128)}, u32[]{:S(2)}) copy-start(f32[64,64]{1,0:T(8,128)} %param.18) | copy-start | bytes 49156
  74.8 21.6 %all-to-all-start.1 = ((bf16[32,64,128]{2,1,0:T(8,128)(2,1)}), bf16[32,64,128]{2,1,0:T(8,128)(2,1)S(1)}, u32[]{:S(2)}, u32[]{:S(2)}) async-start(bf16[32,64,128]{2,1,0:T(8,128)(2,1)} %bitcast.18), calls=%async_computation.1 | async-start | bytes 1048576 | tf_op jit(solution)/shard_map/all_to_all | solution.py:104
  100.3 5.8 %copy-start.4 = (f32[1024,64]{0,1:T(8,128)}, f32[1024,64]{0,1:T(8,128)S(1)}, u32[]{:S(2)}) copy-start(f32[1024,64]{0,1:T(8,128)S(1)} %convolution_multiply_fusion) | copy-start | bytes 786436
  151.5 5.7 %collective-permute-start.8 = (f32[4,64,128]{2,1,0:T(8,128)S(1)}, f32[4,64,128]{2,1,0:T(8,128)S(1)}, u32[]{:S(2)}, u32[]{:S(2)}) collective-permute-start(f32[4,64,128]{2,1,0:T(8,128)S(1)} %get-tuple-element.20), channel_id=1, source_target_pairs={{0,8},{8,16},{16,24},{24,0},{1,9},{9,17},{17,25},{25,1},{2,10},{10... | collective-permute-start | bytes 393224 | tf_op jit(solution)/shard_map/ppermute | solution.py:15
  151.6 5.7 %collective-permute-start.9 = (f32[4,64,128]{2,1,0:T(8,128)S(1)}, f32[4,64,128]{2,1,0:T(8,128)S(1)}, u32[]{:S(2)}, u32[]{:S(2)}) collective-permute-start(f32[4,64,128]{2,1,0:T(8,128)S(1)} %get-tuple-element.21), channel_id=1, source_target_pairs={{8,0},{16,8},{24,16},{0,24},{9,1},{17,9},{25,17},{1,25},{10,2},{18... | collective-permute-start | bytes 393224 | tf_op jit(solution)/shard_map/ppermute | solution.py:18
  157.3 8.6 %collective-permute-start.10 = (f32[72,4,128]{2,1,0:T(4,128)S(1)}, f32[72,4,128]{2,1,0:T(4,128)S(1)}, u32[]{:S(2)}, u32[]{:S(2)}) collective-permute-start(f32[72,4,128]{2,1,0:T(4,128)S(1)} %get-tuple-element.16), channel_id=1, source_target_pairs={{0,1},{1,2},{2,3},{3,4},{4,5},{5,6},{6,7},{7,0},{8,9},{9,10},{10,1... | collective-permute-start | bytes 442376 | tf_op jit(solution)/shard_map/ppermute | solution.py:15
  158.0 8.6 %collective-permute-start.11 = (f32[72,4,128]{2,1,0:T(4,128)S(1)}, f32[72,4,128]{2,1,0:T(4,128)S(1)}, u32[]{:S(2)}, u32[]{:S(2)}) collective-permute-start(f32[72,4,128]{2,1,0:T(4,128)S(1)} %get-tuple-element.17), channel_id=1, source_target_pairs={{1,0},{2,1},{3,2},{4,3},{5,4},{6,5},{7,6},{0,7},{9,8},{10,9},{11,1... | collective-permute-start | bytes 442376 | tf_op jit(solution)/shard_map/ppermute | solution.py:18
  172.7 1.9 %copy-start.3 = (f32[64,64,128]{2,1,0:T(8,128)S(1)}, f32[64,64,128]{2,1,0:T(8,128)}, u32[]{:S(2)}) copy-start(f32[64,64,128]{2,1,0:T(8,128)} %param.12) | copy-start | bytes 6291460
where the time goes:
time: 179 us
  other arithmetic  43.5 us (24%)
  local copies, waits for them, and re-layouts  32.8 us (18%)
  starting transfers between devices  31.3 us (17%)
  waiting for transfers between devices  30.9 us (17%)
  blocking collectives  29.7 us (17%)
  matrix products  8.44 us (5%)
  between operations  1.82 us (1%)
    all_to_all x1, blocking collectives, body(): lax.all_to_all(send_incr, ('lat', 'lon'), split_axis=0, concat_axis=0, ti...  29.7 us
    ppermute x6, starting transfers between devices, with_halo(): lax.ppermute(lax.slice_in_dim(block, 0, width, axis=dim), axis, backward)  16.4 us
    all_to_all x1, waiting for transfers between devices, body(): lax.all_to_all(profiles[recv_cells], ('lat', 'lon'), split_axis=0, concat...  15.4 us
    ppermute x6, waiting for transfers between devices, with_halo(): lax.ppermute(lax.slice_in_dim(block, block.shape[dim] - width, None, axis...  13.6 us
    scatter-add x1, other arithmetic, body(): obs_gradient = jnp.zeros((lat_rows * lon_cols, levels), jnp.float32).at[r...  13.3 us
    another operation x3, other arithmetic  9.15 us
    gather x1, local copies, waits for them, and re-layouts, body(): send_cells = jnp.where(slot_used, obs_cell[source_safe], 0)  8.58 us
    gather x1, local copies, waits for them, and re-layouts, body(): profiles[recv_cells]  8.06 us
  transfers between devices with their start and end apart: 14, of which 9 were waited for; matrix products, arithmetic and copies ran while one was open for 17% of the time, Pallas kernels for 0%

commit v1 on v0

v1 whole, which is shorter than its diff:
```python
import functools

import jax
import jax.numpy as jnp
from jax import lax
from jax.experimental import pallas as pl
from jax.experimental.pallas import tpu as pltpu
from jax.sharding import PartitionSpec as P

NSTEP = 4
F32 = jnp.float32
BF16 = jnp.bfloat16
I32 = jnp.int32
INNOV_MAX = 6.0
INNOV_STEP = INNOV_MAX / 32767.0
WEIGHT_MAX = 4.0
WEIGHT_STEP = WEIGHT_MAX / 65535.0
VMEM_BYTES = 56 * 1024 * 1024


def split_hi_lo(value):
    high = value.astype(BF16)
    low = (value - high.astype(F32)).astype(BF16)
    return high, low


def iota(shape, dim):
    return lax.broadcasted_iota(I32, shape, dim)


def dot_f32(left, right):
    return jnp.dot(left, right, preferred_element_type=F32)


def dot_nt(left, right):
    return lax.dot_general(left, right, (((1,), (1,)), ((), ())), preferred_element_type=F32)


def dot_tn(left, right):
    return lax.dot_general(left, right, (((0,), (0,)), ((), ())), preferred_element_type=F32)


def params():
    return pltpu.CompilerParams(vmem_limit_bytes=VMEM_BYTES)


def vmem_specs(count):
    return [pl.BlockSpec(memory_space=pltpu.VMEM)] * count


def address_kernel(
    devices_all, quarter, count_ref, owner_ref, cell_ref, scale_ref, innov_ref, out_ref, key_ref,
    rhs_ref, word_ref,
):
    obs = owner_ref.shape[1]
    rows_half = devices_all * quarter
    rows = 2 * rows_half
    owner = owner_ref[...]
    cell = cell_ref[...]
    mine = iota((devices_all, obs), 0) == owner
    mine_f = mine.astype(F32)
    mine_b = mine_f.astype(BF16)
    block = min(256, obs)
    earlier = (iota((block, block), 0) < iota((block, block), 1)).astype(F32).astype(BF16)
    running = jnp.zeros((devices_all, 1), F32)
    parts = []
    for start in range(0, obs, block):
        piece = mine_f[:, start : start + block]
        before = dot_f32(mine_b[:, start : start + block], earlier) + running
        parts.append(jnp.sum(piece * before, axis=0, keepdims=True))
        running = running + jnp.sum(piece, axis=1, keepdims=True)
    position = jnp.concatenate(parts, axis=1).astype(I32)
    group = position // quarter
    key = (
        (group // 2) * rows + (group % 2) * rows_half + owner * quarter + position % quarter
    )
    key_ref[...] = key
    scale = scale_ref[...]
    valid = iota((1, obs), 1) < count_ref[0]
    weight = jnp.where(valid, 1.0 / (scale * scale), 0.0)
    weight = jnp.minimum(jnp.floor(weight * (1.0 / WEIGHT_STEP) + 0.5), 65535.0)
    weight_high = jnp.floor(weight * (1.0 / 256.0))
    weight_low = weight - 256.0 * weight_high
    cell_high = (cell // 64).astype(F32)
    cell_low = (cell % 64).astype(F32)
    left = jnp.concatenate(
        [mine_f * piece for piece in (cell_high, cell_low, weight_high, weight_low)], axis=0
    ).astype(BF16)
    place = (iota((128, obs), 0) == position).astype(F32).astype(BF16)
    table = dot_nt(left, place).astype(I32)
    n = devices_all
    cells = table[:n] * 64 + table[n : 2 * n]
    weights = table[2 * n : 3 * n] * 256 + table[3 * n :]
    out_ref[:, quarter, :] = (cells << 16) | weights

    twice = innov_ref[...]
    level = jnp.floor(jnp.clip(twice, -INNOV_MAX, INNOV_MAX) * (1.0 / INNOV_STEP) + 0.5)
    high = jnp.floor(level * (1.0 / 256.0))
    low = level - 256.0 * high
    left_lane = iota((obs, 128), 1) < 64
    zero = jnp.zeros_like(high)
    for side in range(2):
        keep = left_lane if side == 0 else jnp.logical_not(left_lane)
        rhs_ref[side * obs : (side + 1) * obs, :128] = jnp.where(keep, high, zero).astype(BF16)
        rhs_ref[side * obs : (side + 1) * obs, 128:] = jnp.where(keep, low, zero).astype(BF16)
    chunk = min(256, rows_half)

    def fill(step, carry):
        base = step * chunk
        total = []
        for half in range(2):
            row = iota((chunk, obs), 0) + (base + half * rows_half)
            acc = jnp.zeros((chunk, 256), F32)
            for side in range(2):
                hot = (row + side * rows == key).astype(F32).astype(BF16)
                acc = acc + dot_f32(hot, rhs_ref[side * obs : (side + 1) * obs, :])
            total.append((acc[:, :128] * 256.0 + acc[:, 128:]).astype(I32))
        word_ref[pl.ds(pl.multiple_of(base, chunk), chunk), :] = (total[0] << 16) | (
            total[1] & 0xFFFF
        )
        return carry

    lax.fori_loop(0, rows_half // chunk, fill, 0)
    for device in range(devices_all):
        out_ref[device, :quarter, :] = word_ref[device * quarter : (device + 1) * quarter, :]


def fill_wide(wide_ref, tile, sides, north, south, north_on, south_on):
    rows, cols = tile.shape[0], tile.shape[1]
    wide_ref[NSTEP : NSTEP + rows, :cols, :] = tile
    wide_ref[NSTEP : NSTEP + rows, cols:, :] = sides.astype(F32)
    wide_ref[:NSTEP] = north.astype(F32) * north_on
    wide_ref[NSTEP + rows :] = south.astype(F32) * south_on


def broadcast_kappa(kappa):
    rows, cols = kappa.shape
    spread = jnp.where(
        iota((rows, cols, cols), 1) == iota((rows, cols, cols), 2), kappa[:, None, :], 0.0
    )
    return jnp.broadcast_to(jnp.sum(spread, axis=2, keepdims=True), (rows, cols, 128))


def neighbours(ref, row):
    here = ref[row]
    cols = here.shape[0]
    return (
        ref[row - 1]
        + ref[row + 1]
        + pltpu.roll(here, 1, 0)
        + pltpu.roll(here, cols - 1, 0)
        - 4.0 * here
    ), here


def forward_kernel(
    poles_ref, control_ref, sides_ref, north_ref, south_ref, kappa_ref, sigma_ref, vertical_ref,
    picked_ref, out_ref, first_ref, second_ref, kap_ref, prof_ref, pick_ref,
):
    rows, cols, levels = control_ref.shape
    north_on, south_on = poles_ref[0], poles_ref[1]
    fill_wide(
        first_ref, control_ref[...], sides_ref[0], north_ref[0], south_ref[0], north_on, south_on
    )
    fill_wide(
        kap_ref, broadcast_kappa(kappa_ref[...]), sides_ref[1], north_ref[1], south_ref[1],
        north_on, south_on,
    )
    source, target = first_ref, second_ref
    for sweep in range(1, NSTEP + 1):

        def step(row, carry, source=source, target=target):
            change, here = neighbours(source, row)
            target[row] = here + kap_ref[row] * change
            return carry

        lax.fori_loop(sweep, rows + 2 * NSTEP - sweep, step, 0)
        source, target = target, source
    high, low = split_hi_lo(vertical_ref[...])
    mixing = jnp.concatenate(
        [jnp.concatenate([high, low], axis=1), jnp.concatenate([high, low], axis=1)], axis=0
    )
    quarter = rows // 4
    step_rows = 4
    for part in range(4):

        def mix(step, carry, part=part):
            row = part * quarter + step * step_rows
            block = source[pl.ds(NSTEP + row, step_rows), :cols, :].reshape(step_rows * cols, levels)
            pair = jnp.concatenate(split_hi_lo(block), axis=1)
            both = dot_f32(pair, mixing)
            state = both[:, :levels] + both[:, levels:]
            dev = sigma_ref[pl.ds(row, step_rows)].reshape(step_rows * cols, levels)
            prof_ref[
                pl.ds(pl.multiple_of(step * step_rows * cols, step_rows * cols), step_rows * cols),
                part * levels : (part + 1) * levels,
            ] = (dev * state).astype(BF16)
            return carry

        lax.fori_loop(0, quarter // step_rows, mix, 0)
    fill_picked(pick_ref, picked_ref[...])

    def project(step, carry):
        where = pl.ds(pl.multiple_of(step * 256, 256), 256)
        value = dot_nt(prof_ref[where, :], pick_ref[...])
        high, low = split_hi_lo(value)
        out_ref[where, :] = jnp.concatenate([high, low], axis=1)
        return carry

    lax.fori_loop(0, prof_ref.shape[0] // 256, project, 0)


def fill_picked(pick_ref, picked):
    channels, levels = picked.shape
    pick_ref[...] = jnp.zeros_like(pick_ref)
    for part in range(4):
        pick_ref[
            part * channels : (part + 1) * channels, part * levels : (part + 1) * levels
        ] = picked


def owner_kernel(
    devices_all, quarter, recv_ref, evolved_ref, rinv_ref, picked_ref, sigma_ref, ret_ref, adj_ref,
    word_ref, dep_ref, acc_ref, pick_ref,
):
    rows_half = devices_all * quarter
    rows = 2 * rows_half
    cells_part = evolved_ref.shape[0]
    shift = cells_part.bit_length() - 1
    for device in range(devices_all):
        word_ref[device * quarter : (device + 1) * quarter, :] = recv_ref[device, :quarter, :]
    meta = recv_ref[:, quarter, :]
    cells, weights = meta >> 16, meta & 0xFFFF
    table = jnp.concatenate(
        [
            piece.astype(F32).astype(BF16)
            for piece in (cells >> 6, cells & 63, weights >> 8, weights & 255)
        ],
        axis=1,
    )
    high, low = split_hi_lo(rinv_ref[...])
    zero = jnp.zeros_like(high)
    mixing = jnp.concatenate(
        [jnp.concatenate([high, low], axis=1), jnp.concatenate([high, zero], axis=1)], axis=0
    )
    acc_ref[...] = jnp.zeros_like(acc_ref)
    chunk = min(256, rows_half)
    left_lane = iota((chunk, 128), 1) < 64
    lane_half = iota((chunk, 128), 1) // 64
    per_half = rows_half // chunk

    def work(step, carry):
        half = step // per_half
        base = (step % per_half) * chunk
        row = iota((chunk, devices_all), 0) + base
        spread = (row // quarter == iota((chunk, devices_all), 1)).astype(F32).astype(BF16)
        found = dot_f32(spread, table)
        cell_lane = found[:, :128] * 64.0 + found[:, 128:256]
        weight_lane = (found[:, 256:384] * 256.0 + found[:, 384:]) * WEIGHT_STEP
        lane = iota((chunk, 128), 1)
        r = (iota((chunk, 128), 0) + base) % quarter
        hots, parts, weight, values = [], [], [], []
        for side in range(2):
            pick = lane == (2 * side + half) * quarter + r
            cell = jnp.sum(jnp.where(pick, cell_lane, 0.0), axis=1, keepdims=True).astype(I32)
            weight.append(jnp.sum(jnp.where(pick, weight_lane, 0.0), axis=1, keepdims=True))
            part = cell >> shift
            inside = cell & (cells_part - 1)
            hot = (iota((chunk, cells_part), 1) == inside).astype(F32).astype(BF16)
            got = dot_f32(hot, evolved_ref[...])
            got = got[:, :256] + got[:, 256:]
            lanes = jnp.where(part >= 2, got[:, 128:], got[:, :128])
            swapped = pltpu.roll(lanes, 64, 1)
            odd = (part & 1) == 1
            values.append(
                jnp.where(odd, swapped, lanes) if side == 0 else jnp.where(odd, lanes, swapped)
            )
            hots.append(hot)
            parts.append(part)
        evolved = jnp.where(left_lane, values[0], values[1])
        words = word_ref[pl.ds(pl.multiple_of(base, chunk), chunk), :]
        words = jnp.where(half == 0, words, words << 16) >> 16
        gap = evolved - words.astype(F32) * INNOV_STEP
        both = dot_f32(jnp.concatenate(split_hi_lo(gap), axis=1), mixing)
        dep = (both[:, :128] + both[:, 128:]) * jnp.where(left_lane, weight[0], weight[1])
        dep_ref[pl.ds(pl.multiple_of(step * chunk, chunk), chunk), :] = dep
        rounded = dep.astype(BF16).astype(F32)
        swapped = pltpu.roll(rounded, 64, 1)
        for side in range(2):
            twice = (
                jnp.where(left_lane, rounded, swapped)
                if side == 0
                else jnp.where(left_lane, swapped, rounded)
            )
            wide = jnp.concatenate(
                [
                    jnp.where(parts[side] == lane_half, twice, 0.0).astype(BF16),
                    jnp.where(parts[side] == lane_half + 2, twice, 0.0).astype(BF16),
                ],
                axis=1,
            )
            acc_ref[...] += dot_tn(hots[side], wide)
        return carry

    lax.fori_loop(0, rows // chunk, work, 0)
    for half in range(2):
        for device in range(devices_all):
            at = half * rows_half + device * quarter
            ret_ref[device, half * quarter : (half + 1) * quarter, :] = dep_ref[
                at : at + quarter, :
            ]
    fill_picked(pick_ref, picked_ref[...])
    lat_rows, cols, levels = sigma_ref.shape
    quarter_rows = lat_rows // 4
    step_rows = 4

    def spread_out(step, carry):
        where = pl.ds(pl.multiple_of(step * step_rows * cols, step_rows * cols), step_rows * cols)
        high, low = split_hi_lo(acc_ref[where, :])
        both = dot_f32(high, pick_ref[...]) + dot_f32(low, pick_ref[...])
        for part in range(4):
            at = pl.ds(part * quarter_rows + step * step_rows, step_rows)
            adj_ref[at] = sigma_ref[at] * both[:, part * levels : (part + 1) * levels].reshape(
                step_rows, cols, levels
            )
        return carry

    lax.fori_loop(0, quarter_rows // step_rows, spread_out, 0)


def backward_kernel(
    poles_ref, adj_ref, sides_ref, north_ref, south_ref, kappa_ref, ksides_ref, knorth_ref,
    ksouth_ref, vertical_ref, control_ref, out_ref, first_ref, second_ref, kap_ref,
):
    rows, cols, levels = control_ref.shape
    north_on, south_on = poles_ref[0], poles_ref[1]
    fill_wide(first_ref, adj_ref[...], sides_ref[...], north_ref[...], south_ref[...], north_on, south_on)
    fill_wide(
        kap_ref, broadcast_kappa(kappa_ref[...]), ksides_ref[1], knorth_ref[1], ksouth_ref[1],
        north_on, south_on,
    )

    def scale(row, carry):
        second_ref[row] = first_ref[row] * kap_ref[row]
        return carry

    wide_rows = rows + 2 * NSTEP
    lax.fori_loop(0, wide_rows, scale, 0)
    for sweep in range(1, NSTEP + 1):

        def step(row, carry):
            change, _ = neighbours(second_ref, row)
            first_ref[row] = first_ref[row] + change
            return carry

        lax.fori_loop(sweep, wide_rows - sweep, step, 0)
        if sweep < NSTEP:
            lax.fori_loop(sweep, wide_rows - sweep, scale, 0)
    high, low = split_hi_lo(vertical_ref[...])
    mixing = jnp.concatenate(
        [jnp.concatenate([high, high], axis=1), jnp.concatenate([low, low], axis=1)], axis=0
    )
    step_rows = 4

    def mix(step, carry):
        row = step * step_rows
        block = first_ref[pl.ds(NSTEP + row, step_rows), :cols, :].reshape(step_rows * cols, levels)
        pair = jnp.concatenate(split_hi_lo(block), axis=1)
        both = dot_nt(pair, mixing)
        back = (both[:, :levels] + both[:, levels:]).reshape(step_rows, cols, levels)
        at = pl.ds(row, step_rows)
        out_ref[at] = control_ref[at] + back
        return carry

    lax.fori_loop(0, rows // step_rows, mix, 0)


def return_kernel(devices_all, quarter, recv_ref, key_ref, out_ref, pair_ref):
    rows_half = devices_all * quarter
    rows = 2 * rows_half
    obs = out_ref.shape[0]
    for half in range(2):
        for device in range(devices_all):
            at = half * rows_half + device * quarter
            high, low = split_hi_lo(recv_ref[device, half * quarter : (half + 1) * quarter, :])
            pair_ref[at : at + quarter, :128] = high
            pair_ref[at : at + quarter, 128:] = low
    chunk = min(256, obs)
    for start in range(0, obs, chunk):
        key_rows = jnp.broadcast_to(key_ref[:, start : start + chunk], (128, chunk))
        key = jnp.transpose(key_rows.astype(F32))
        side = key >= rows
        row = jnp.where(side, key - rows, key)[:, :1].astype(I32)
        hot = (iota((chunk, rows), 1) == row).astype(F32).astype(BF16)
        both = dot_f32(hot, pair_ref[...])
        both = both[:, :128] + both[:, 128:]
        out_ref[start : start + chunk, :] = jnp.where(side, pltpu.roll(both, 64, 1), both)[:, :64]


def shifts(axis):
    count = lax.axis_size(axis)
    forward = [(i, (i + 1) % count) for i in range(count)]
    return forward, [(target, source) for source, target in forward]


def exchange_sides(left, right):
    forward, backward = shifts("lon")
    east = lax.ppermute(left, "lon", backward)
    west = lax.ppermute(right, "lon", forward)
    return jnp.concatenate([east, west], axis=-2)


def exchange_rims(top, bottom):
    forward, backward = shifts("lat")
    south = lax.ppermute(top, "lat", backward)
    north = lax.ppermute(bottom, "lat", forward)
    return north, south


def body(
    control,
    kappa,
    sigma,
    vertical,
    channel_table,
    channel_pick,
    r_inverse,
    innovations,
    error_scale,
    obs_owner,
    obs_cell,
    obs_count,
):
    lat_rows, lon_cols, levels = control.shape
    lat_at, lat_count = lax.axis_index("lat"), lax.axis_size("lat")
    poles = jnp.stack([lat_at > 0, lat_at < lat_count - 1]).astype(F32)
    obs_slots = obs_cell.shape[0]
    channels = innovations.shape[1]
    devices_all = lat_count * lax.axis_size("lon")
    capacity = max(4, 2 * obs_slots // devices_all)
    quarter = capacity // 4
    rows_half = devices_all * quarter
    wide = (lat_rows + 2 * NSTEP, lon_cols + 2 * NSTEP, levels)

    payload, key = pl.pallas_call(
        functools.partial(address_kernel, devices_all, quarter),
        out_shape=(
            jax.ShapeDtypeStruct((devices_all, quarter + 1, 128), I32),
            jax.ShapeDtypeStruct((1, obs_slots), I32),
        ),
        in_specs=[pl.BlockSpec(memory_space=pltpu.SMEM)] + vmem_specs(4),
        out_specs=tuple(vmem_specs(2)),
        scratch_shapes=[
            pltpu.VMEM((2 * obs_slots, 256), BF16),
            pltpu.VMEM((rows_half, 128), I32),
        ],
        compiler_params=params(),
        name="address",
    )(
        obs_count,
        obs_owner.reshape(1, obs_slots),
        obs_cell.reshape(1, obs_slots),
        error_scale.reshape(1, obs_slots),
        jnp.concatenate([innovations, innovations], axis=1),
    )
    received = lax.all_to_all(payload, ("lat", "lon"), split_axis=0, concat_axis=0, tiled=True)

    both = jnp.stack(
        [control, jnp.broadcast_to(kappa[:, :, None], control.shape)]
    )
    sides = exchange_sides(both[:, :, :NSTEP].astype(BF16), both[:, :, -NSTEP:].astype(BF16))
    top = jnp.concatenate([both[:, :NSTEP].astype(BF16), sides[:, :NSTEP]], axis=2)
    bottom = jnp.concatenate([both[:, -NSTEP:].astype(BF16), sides[:, -NSTEP:]], axis=2)
    north, south = exchange_rims(top, bottom)

    table_rows = channel_table.shape[0]
    pick_table = (channel_pick[:, None] == jnp.arange(table_rows, dtype=I32)[None, :]).astype(BF16)
    picked = jnp.dot(pick_table, channel_table, preferred_element_type=F32).astype(BF16)

    columns = lat_rows * lon_cols
    evolved = pl.pallas_call(
        forward_kernel,
        out_shape=jax.ShapeDtypeStruct((columns // 4, 8 * channels), BF16),
        in_specs=[pl.BlockSpec(memory_space=pltpu.SMEM)] + vmem_specs(8),
        out_specs=vmem_specs(1)[0],
        scratch_shapes=[pltpu.VMEM(wide, F32)] * 3
        + [
            pltpu.VMEM((columns // 4, 4 * levels), BF16),
            pltpu.VMEM((4 * channels, 4 * levels), BF16),
        ],
        compiler_params=params(),
        name="forward",
    )(poles, control, sides, north, south, kappa, sigma, vertical, picked)

    rinv_pair = jnp.kron(jnp.eye(2, dtype=F32), r_inverse)
    returned, adjoint = pl.pallas_call(
        functools.partial(owner_kernel, devices_all, quarter),
        out_shape=(
            jax.ShapeDtypeStruct((devices_all, 2 * quarter, 128), F32),
            jax.ShapeDtypeStruct(control.shape, F32),
        ),
        in_specs=vmem_specs(5),
        out_specs=tuple(vmem_specs(2)),
        scratch_shapes=[
            pltpu.VMEM((rows_half, 128), I32),
            pltpu.VMEM((2 * rows_half, 128), F32),
            pltpu.VMEM((columns // 4, 4 * channels), F32),
            pltpu.VMEM((4 * channels, 4 * levels), BF16),
        ],
        compiler_params=params(),
        name="owner",
    )(received, evolved, rinv_pair, picked, sigma)
    home = lax.all_to_all(returned, ("lat", "lon"), split_axis=0, concat_axis=0, tiled=True)

    asides = exchange_sides(adjoint[:, :NSTEP].astype(BF16), adjoint[:, -NSTEP:].astype(BF16))
    atop = jnp.concatenate([adjoint[:NSTEP].astype(BF16), asides[:NSTEP]], axis=1)
    abottom = jnp.concatenate([adjoint[-NSTEP:].astype(BF16), asides[-NSTEP:]], axis=1)
    anorth, asouth = exchange_rims(atop, abottom)
    gradient = pl.pallas_call(
        backward_kernel,
        out_shape=jax.ShapeDtypeStruct(control.shape, F32),
        in_specs=[pl.BlockSpec(memory_space=pltpu.SMEM)] + vmem_specs(10),
        out_specs=vmem_specs(1)[0],
        scratch_shapes=[pltpu.VMEM(wide, F32)] * 3,
        compiler_params=params(),
        name="backward",
    )(poles, adjoint, asides, anorth, asouth, kappa, sides, north, south, vertical, control)

    departures = pl.pallas_call(
        functools.partial(return_kernel, devices_all, quarter),
        out_shape=jax.ShapeDtypeStruct(innovations.shape, F32),
        in_specs=vmem_specs(2),
        out_specs=vmem_specs(1)[0],
        scratch_shapes=[pltpu.VMEM((2 * rows_half, 256), BF16)],
        compiler_params=params(),
        name="give_back",
    )(home, key)
    return (gradient, departures)


def solution(mesh):
    return jax.shard_map(
        body,
        mesh=mesh,
        in_specs=(
            P("lat", "lon", None),
            P("lat", "lon"),
            P("lat", "lon", None),
            P(),
            P(),
            P(),
            P(),
            P(("lat", "lon"), None),
            P(("lat", "lon")),
            P(("lat", "lon"), None),
            P(("lat", "lon")),
            P(("lat", "lon")),
        ),
        out_specs=(P("lat", "lon", None), P(("lat", "lon"), None)),
        check_vma=False,
    )
```

time: 179 us -> 109 us (0.61)
  Pallas kernels: 0 us -> 48 us
  other arithmetic: 43.5 us -> 7.71 us
  blocking collectives: 29.7 us -> 0 us
  local copies, waits for them, and re-layouts: 32.8 us -> 7.93 us
  waiting for transfers between devices: 30.9 us -> 18.3 us
  starting transfers between devices: 31.3 us -> 23.3 us
  matrix products: 8.44 us -> 0.82 us
    pallas_call x0 -> x5, Pallas kernels: none -> 48 us  [the longest x1 15.4 us: body(): pl.pallas_call(backward_kernel, out_shape=jax.ShapeDtypeStruct(control.sh...]
    all_to_all x1 -> x0, blocking collectives: 29.7 us -> none  [body(): lax.all_to_all(send_incr, ('lat', 'lon'), split_axis=0, concat_axis=0, ti...]
    gather x4 -> x0, local copies, waits for them, and re-layouts: 25.3 us -> none  [the longest x1 8.58 us: body(): send_cells = jnp.where(slot_used, obs_cell[source_safe], 0)]
    all_to_all x2, waiting for transfers between devices: 15.4 us -> 0.01 us  [the longest x1 0.01 us: body(): lax.all_to_all(payload, ('lat', 'lon'), split_axis=0, concat_axis=0, tile...]
    scatter-add x1 -> x0, other arithmetic: 13.3 us -> none  [body(): obs_gradient = jnp.zeros((lat_rows * lon_cols, levels), jnp.float32).at[r...]
    mul x4 -> x1, other arithmetic: 8.17 us -> 0.1 us  [body(): rinv_pair = jnp.kron(jnp.eye(2, dtype=F32), r_inverse)]
    dot_general x6 -> x1, matrix products: 8.44 us -> 0.82 us  [body(): jnp.dot(pick_table, channel_table, preferred_element_type=F32).astype(BF16)]
    another operation x3 -> x2, other arithmetic: 9.15 us -> 1.81 us
  transfers between devices with their start and end apart: 14 -> 10, of which waited for: 9 -> 6; matrix products, arithmetic and copies ran while one was open for 17% -> 8% of each run, Pallas kernels for 0% -> 27%
where the time goes in v1:
time: 109 us; the launch traced here: 108 us
  Pallas kernels  48 us (44%)
  starting transfers between devices  23.3 us (21%)
  waiting for transfers between devices  18.3 us (17%)
  local copies, waits for them, and re-layouts  7.93 us (7%)
  other arithmetic  7.71 us (7%)
  between operations  1.53 us (1%)
    pallas_call x1, Pallas kernels, body(): pl.pallas_call(backward_kernel, out_shape=jax.ShapeDtypeStruct(control.sh...  15.4 us
    pallas_call x1, Pallas kernels, body(): pl.pallas_call(forward_kernel, out_shape=jax.ShapeDtypeStruct((columns //...  13.9 us
    pallas_call x1, Pallas kernels, body(): pl.pallas_call(functools.partial(owner_kernel, devices_all, quarter), out...  11.6 us
    ppermute x2, waiting for transfers between devices, exchange_sides(): west = lax.ppermute(right, 'lon', forward)  9.51 us
    ppermute x2, starting transfers between devices, exchange_sides(): east = lax.ppermute(left, 'lon', backward)  9.09 us
    all_to_all x1, starting transfers between devices, body(): lax.all_to_all(payload, ('lat', 'lon'), split_axis=0, concat_axis=0, tile...  7.42 us
    ppermute x2, waiting for transfers between devices, exchange_sides(): east = lax.ppermute(left, 'lon', backward)  7.33 us
    unnamed x22, local copies, waits for them, and re-layouts  6.5 us
  transfers between devices with their start and end apart: 10, of which 6 were waited for; matrix products, arithmetic and copies ran while one was open for 8% of the time, Pallas kernels for 27%

profile of v1, /device:TPU:0, one launch (start us, length us, event | category | flops | bytes accessed | tf_op | source)
XLA Modules:
  0.0 107.6 jit_solution(341184183513669441)
XLA Ops:
  1.4 1.3 %copy.14 = f32[1024,64]{1,0:T(8,128)S(1)} copy(f32[1024,64]{0,1:T(8,128)} %param.19) | data formatting | bytes 524288 | tf_op args[7]
  2.7 1.0 pad_maximum_fusion.innov_ref
  3.7 4.2 %address.1 = (s32[32,17,128]{2,1,0:T(8,128)}, s32[1,1024]{1,0:T(1,128)}) custom-call(s32[1]{0:T(128)S(6)} %copy.17.count_ref, s32[1,1024]{1,0:T(1,128)} %bitcast.9, s32[1,1024]{1,0:T(1,128)} %bitcast.10, f32[1,1024]{1,0:T(1,128)} %bitcast.11, f32[1024,128]{1,0:T(8,128)} %pad_maximum_fusion.innov_ref), custom_call_target="tpu_custom_call" | custom-call | tf_op jit(solution)/shard_map/address/pallas_call | solution.py:445
  7.9 7.4 %all-to-all-start = ((s32[32,17,128]{2,1,0:T(8,128)}), s32[32,17,128]{2,1,0:T(8,128)}, u32[]{:S(2)}, u32[]{:S(2)}) async-start(s32[32,17,128]{2,1,0:T(8,128)} %get-tuple-element.6), calls=%async_computation | async-start | bytes 786432 | tf_op jit(solution)/shard_map/all_to_all | solution.py:466
  15.3 0.6 stack_broadcast_in_dim.2
  16.0 0.8 maximum_convert_fusion.2
  16.8 4.5 %collective-permute-start = (bf16[2,64,4,128]{3,2,1,0:T(4,128)(2,1)}, bf16[2,64,4,128]{3,2,1,0:T(4,128)(2,1)}, u32[]{:S(2)}, u32[]{:S(2)}) collective-permute-start(bf16[2,64,4,128]{3,2,1,0:T(4,128)(2,1)} %get-tuple-element.14), channel_id=1, source_target_pairs={{1,0},{2,1},{3,2},{4,3},{5,4},{6,5},{7,6},{0,7},{9,8},{10,9},{11,1... | collective-permute-start | bytes 393224 | tf_op jit(solution)/shard_map/ppermute | solution.py:408
  21.3 0.8 convolution_convert_fusion.picked_ref
  22.2 3.2 %collective-permute-done = bf16[2,64,4,128]{3,2,1,0:T(4,128)(2,1)} collective-permute-done((bf16[2,64,4,128]{3,2,1,0:T(4,128)(2,1)}, bf16[2,64,4,128]{3,2,1,0:T(4,128)(2,1)}, u32[]{:S(2)}, u32[]{:S(2)}) %collective-permute-start) | collective-permute-done | bytes 131104 | tf_op jit(solution)/shard_map/ppermute | solution.py:408
  25.5 4.6 %collective-permute-done.1 = bf16[2,64,4,128]{3,2,1,0:T(4,128)(2,1)} collective-permute-done((bf16[2,64,4,128]{3,2,1,0:T(4,128)(2,1)}, bf16[2,64,4,128]{3,2,1,0:T(4,128)(2,1)}, u32[]{:S(2)}, u32[]{:S(2)}) %collective-permute-start.1) | collective-permute-done | bytes 131104 | tf_op jit(solution)/shard_map/ppermute | solution.py:409
  30.1 0.8 fusion.3
  31.0 1.8 %collective-permute-start.3 = (bf16[2,4,72,128]{3,2,1,0:T(8,128)(2,1)S(1)}, bf16[2,4,72,128]{3,2,1,0:T(8,128)(2,1)S(1)}, u32[]{:S(2)}, u32[]{:S(2)}) collective-permute-start(bf16[2,4,72,128]{3,2,1,0:T(8,128)(2,1)S(1)} %pad_maximum_fusion.5), channel_id=1, source_target_pairs={{8,0},{16,8},{24,16},{0,24},{9,1},{17,9},{25,17},{1,25},{10,2},{18... | collective-permute-start | bytes 442376 | tf_op jit(solution)/shard_map/ppermute | solution.py:415
  32.7 0.6 add_convert_fusion.poles_ref
  33.4 0.8 mul.27.rinv_ref
  34.1 1.8 %pad_maximum_fusion.1.sides_ref.ksides_ref = bf16[2,64,8,128]{3,2,1,0:T(8,128)(2,1)} fusion(bf16[2,64,4,128]{3,2,1,0:T(4,128)(2,1)} %collective-permute-done.1, bf16[2,64,4,128]{3,2,1,0:T(4,128)(2,1)} %collective-permute-done), kind=kLoop, calls=%fused_computation.4 | loop fusion | flops 524288 | bytes 524288 | tf_op jit(solution)/shard_map/concatenate | solution.py:410
  36.6 0.6 copy-done.4
  37.3 13.9 %forward.1.evolved_ref = bf16[1024,512]{1,0:T(8,128)(2,1)} custom-call(f32[2]{0:T(128)} %add_convert_fusion.poles_ref, f32[64,64,128]{2,1,0:T(8,128)} %control_ref.3, bf16[2,64,8,128]{3,2,1,0:T(8,128)(2,1)} %pad_maximum_fusion.1.sides_ref.ksides_ref, bf16[2,4,72,128]{3,2,1,0:T(8,128)(2,1)} %copy-done.3, bf16[2,4,72,128]{3,2,1,0:T(8,128)(2,1)} %copy-done.4, ...), custom_call_target="tpu_custom_call" | custom-call | tf_op jit(solution)/shard_map/forward/pallas_call | solution.py:481
  51.2 11.6 %owner.1 = (f32[32,32,128]{2,1,0:T(8,128)}, f32[64,64,128]{2,1,0:T(8,128)}) custom-call(s32[32,17,128]{2,1,0:T(8,128)} %all-to-all-done.recv_ref, bf16[1024,512]{1,0:T(8,128)(2,1)} %forward.1.evolved_ref, f32[128,128]{1,0:T(8,128)} %mul.27.rinv_ref, bf16[64,128]{1,0:T(8,128)(2,1)} %convolution_convert_fusion.picked_ref, f32[64,64,128]{2,1,0:T(8,128)} %sigma_ref.3), custom_call_target="tpu_custom_call" | custom-call | tf_op jit(solution)/shard_map/owner/pallas_call | solution.py:496
  62.8 3.2 %all-to-all-start.1 = ((f32[32,32,128]{2,1,0:T(8,128)}), f32[32,32,128]{2,1,0:T(8,128)S(1)}, u32[]{:S(2)}, u32[]{:S(2)}) async-start(f32[32,32,128]{2,1,0:T(8,128)} %get-tuple-element.8), calls=%async_computation.1 | async-start | bytes 1048576 | tf_op jit(solution)/shard_map/all_to_all | solution.py:513
  66.0 1.8 %convert.13 = bf16[64,64,128]{2,1,0:T(8,128)(2,1)S(1)} convert(f32[64,64,128]{2,1,0:T(8,128)} %get-tuple-element.7.adj_ref) | non-fusion elementwise | flops 524288 | bytes 3145728 | tf_op jit(solution)/shard_map/convert.3
  67.9 4.6 %collective-permute-start.4 = (bf16[64,4,128]{2,1,0:T(4,128)(2,1)S(1)}, bf16[64,4,128]{2,1,0:T(4,128)(2,1)S(1)}, u32[]{:S(2)}, u32[]{:S(2)}) collective-permute-start(bf16[64,4,128]{2,1,0:T(4,128)(2,1)S(1)} %get-tuple-element.18), channel_id=1, source_target_pairs={{1,0},{2,1},{3,2},{4,3},{5,4},{6,5},{7,6},{0,7},{9,8},{10,9},{11,1... | collective-permute-start | bytes 196616 | tf_op jit(solution)/shard_map/ppermute | solution.py:408
  72.5 4.1 %collective-permute-done.4 = bf16[64,4,128]{2,1,0:T(4,128)(2,1)S(1)} collective-permute-done((bf16[64,4,128]{2,1,0:T(4,128)(2,1)S(1)}, bf16[64,4,128]{2,1,0:T(4,128)(2,1)S(1)}, u32[]{:S(2)}, u32[]{:S(2)}) %collective-permute-start.4) | collective-permute-done | bytes 65568 | tf_op jit(solution)/shard_map/ppermute | solution.py:408
  76.6 4.9 %collective-permute-done.5 = bf16[64,4,128]{2,1,0:T(4,128)(2,1)S(1)} collective-permute-done((bf16[64,4,128]{2,1,0:T(4,128)(2,1)S(1)}, bf16[64,4,128]{2,1,0:T(4,128)(2,1)S(1)}, u32[]{:S(2)}, u32[]{:S(2)}) %collective-permute-start.5) | collective-permute-done | bytes 65568 | tf_op jit(solution)/shard_map/ppermute | solution.py:409
  81.6 1.7 %collective-permute-start.7 = (bf16[4,72,128]{2,1,0:T(8,128)(2,1)S(1)}, bf16[4,72,128]{2,1,0:T(8,128)(2,1)S(1)}, u32[]{:S(2)}, u32[]{:S(2)}) collective-permute-start(bf16[4,72,128]{2,1,0:T(8,128)(2,1)S(1)} %pad_maximum_fusion.7), channel_id=1, source_target_pairs={{8,0},{16,8},{24,16},{0,24},{9,1},{17,9},{25,17},{1,25},{10,2},{18... | collective-permute-start | bytes 221192 | tf_op jit(solution)/shard_map/ppermute | solution.py:415
  83.4 0.7 pad_maximum_fusion.3.sides_ref
  84.1 1.3 %collective-permute-done.6.north_ref = bf16[4,72,128]{2,1,0:T(8,128)(2,1)S(1)} collective-permute-done((bf16[4,72,128]{2,1,0:T(8,128)(2,1)S(1)}, bf16[4,72,128]{2,1,0:T(8,128)(2,1)S(1)}, u32[]{:S(2)}, u32[]{:S(2)}) %collective-permute-start.6) | collective-permute-done | bytes 73760 | tf_op jit(solution)/shard_map/ppermute | solution.py:416
  85.4 0.6 copy-done.6
  86.0 0.6 copy-done.7
  86.6 15.4 %backward.1 = f32[64,64,128]{2,1,0:T(8,128)} custom-call(f32[2]{0:T(128)} %add_convert_fusion.poles_ref, f32[64,64,128]{2,1,0:T(8,128)} %get-tuple-element.7.adj_ref, bf16[64,8,128]{2,1,0:T(8,128)(2,1)} %pad_maximum_fusion.3.sides_ref, bf16[4,72,128]{2,1,0:T(8,128)(2,1)} %copy-done.6, bf16[4,72,128]{2,1,0:T(8,128)(2,1)} %copy-done.7, f32[64,64]{1,0:T(8,128)} %kappa_ref.3, ...), custom_call_target="tpu_custom_call" | custom-call | tf_op jit(solution)/shard_map/backward/pallas_call | solution.py:519
  102.1 0.8 copy-done.2
  102.9 2.8 %give_back.1 = f32[1024,64]{1,0:T(8,128)} custom-call(f32[32,32,128]{2,1,0:T(8,128)} %copy-done.2, s32[1,1024]{1,0:T(1,128)} %get-tuple-element.9.key_ref), custom_call_target="tpu_custom_call" | custom-call | tf_op jit(solution)/shard_map/give_back/pallas_call | solution.py:529
  105.6 1.9 %copy.16 = f32[1024,64]{0,1:T(8,128)} copy(f32[1024,64]{1,0:T(8,128)} %give_back.1) | data formatting | bytes 524288
  (35 shorter events, 1.1 us)
Async XLA Ops:
  0.6 20.6 %copy-start = (bf16[616,128]{1,0:T(8,128)(2,1)S(1)}, bf16[616,128]{1,0:T(8,128)(2,1)}, u32[]{:S(2)}) copy-start(bf16[616,128]{1,0:T(8,128)(2,1)} %param.16) | copy-start | bytes 473092
  0.6 14.7 %copy-start.5 = (f32[64,64]{1,0:T(8,128)S(1)}, f32[64,64]{1,0:T(8,128)}, u32[]{:S(2)}) copy-start(f32[64,64]{1,0:T(8,128)} %kappa_ref.3) | copy-start | bytes 49156
  1.3 14.6 %copy-start.1 = (f32[64,64,128]{2,1,0:T(8,128)S(1)}, f32[64,64,128]{2,1,0:T(8,128)}, u32[]{:S(2)}) copy-start(f32[64,64,128]{2,1,0:T(8,128)} %control_ref.3) | copy-start | bytes 6291460
  7.9 43.3 %all-to-all-start = ((s32[32,17,128]{2,1,0:T(8,128)}), s32[32,17,128]{2,1,0:T(8,128)}, u32[]{:S(2)}, u32[]{:S(2)}) async-start(s32[32,17,128]{2,1,0:T(8,128)} %get-tuple-element.6), calls=%async_computation | async-start | bytes 786432 | tf_op jit(solution)/shard_map/all_to_all | solution.py:466
  15.3 5.9 %copy-start.9 = (s32[64]{0:T(128)S(1)}, s32[64]{0:T(128)}, u32[]{:S(2)}) copy-start(s32[64]{0:T(128)} %param.17) | copy-start | bytes 772
  15.3 6.8 %copy-start.8 = (f32[64,64]{1,0:T(8,128)S(1)}, f32[64,64]{1,0:T(8,128)}, u32[]{:S(2)}) copy-start(f32[64,64]{1,0:T(8,128)} %param.18) | copy-start | bytes 49156
  16.8 8.7 %collective-permute-start = (bf16[2,64,4,128]{3,2,1,0:T(4,128)(2,1)}, bf16[2,64,4,128]{3,2,1,0:T(4,128)(2,1)}, u32[]{:S(2)}, u32[]{:S(2)}) collective-permute-start(bf16[2,64,4,128]{3,2,1,0:T(4,128)(2,1)} %get-tuple-element.14), channel_id=1, source_target_pairs={{1,0},{2,1},{3,2},{4,3},{5,4},{6,5},{7,6},{0,7},{9,8},{10,9},{11,1... | collective-permute-start | bytes 393224 | tf_op jit(solution)/shard_map/ppermute | solution.py:408
  21.2 8.8 %collective-permute-start.1 = (bf16[2,64,4,128]{3,2,1,0:T(4,128)(2,1)}, bf16[2,64,4,128]{3,2,1,0:T(4,128)(2,1)}, u32[]{:S(2)}, u32[]{:S(2)}) collective-permute-start(bf16[2,64,4,128]{3,2,1,0:T(4,128)(2,1)} %get-tuple-element.15), channel_id=1, source_target_pairs={{0,1},{1,2},{2,3},{3,4},{4,5},{5,6},{6,7},{7,0},{8,9},{9,10},{10,1... | collective-permute-start | bytes 393224 | tf_op jit(solution)/shard_map/ppermute | solution.py:409
  30.9 5.1 %collective-permute-start.2 = (bf16[2,4,72,128]{3,2,1,0:T(8,128)(2,1)S(1)}, bf16[2,4,72,128]{3,2,1,0:T(8,128)(2,1)S(1)}, u32[]{:S(2)}, u32[]{:S(2)}) collective-permute-start(bf16[2,4,72,128]{3,2,1,0:T(8,128)(2,1)S(1)} %pad_maximum_fusion.4), channel_id=1, source_target_pairs={{0,8},{8,16},{16,24},{24,0},{1,9},{9,17},{17,25},{25,1},{2,10},{10... | collective-permute-start | bytes 442376 | tf_op jit(solution)/shard_map/ppermute | solution.py:416
  31.0 5.1 %collective-permute-start.3 = (bf16[2,4,72,128]{3,2,1,0:T(8,128)(2,1)S(1)}, bf16[2,4,72,128]{3,2,1,0:T(8,128)(2,1)S(1)}, u32[]{:S(2)}, u32[]{:S(2)}) collective-permute-start(bf16[2,4,72,128]{3,2,1,0:T(8,128)(2,1)S(1)} %pad_maximum_fusion.5), channel_id=1, source_target_pairs={{8,0},{16,8},{24,16},{0,24},{9,1},{17,9},{25,17},{1,25},{10,2},{18... | collective-permute-start | bytes 442376 | tf_op jit(solution)/shard_map/ppermute | solution.py:415
  36.0 0.7 copy-start.3
  36.6 0.6 copy-start.4
  62.8 39.2 %all-to-all-start.1 = ((f32[32,32,128]{2,1,0:T(8,128)}), f32[32,32,128]{2,1,0:T(8,128)S(1)}, u32[]{:S(2)}, u32[]{:S(2)}) async-start(f32[32,32,128]{2,1,0:T(8,128)} %get-tuple-element.8), calls=%async_computation.1 | async-start | bytes 1048576 | tf_op jit(solution)/shard_map/all_to_all | solution.py:513
  67.9 8.7 %collective-permute-start.4 = (bf16[64,4,128]{2,1,0:T(4,128)(2,1)S(1)}, bf16[64,4,128]{2,1,0:T(4,128)(2,1)S(1)}, u32[]{:S(2)}, u32[]{:S(2)}) collective-permute-start(bf16[64,4,128]{2,1,0:T(4,128)(2,1)S(1)} %get-tuple-element.18), channel_id=1, source_target_pairs={{1,0},{2,1},{3,2},{4,3},{5,4},{6,5},{7,6},{0,7},{9,8},{10,9},{11,1... | collective-permute-start | bytes 196616 | tf_op jit(solution)/shard_map/ppermute | solution.py:408
  72.5 9.0 %collective-permute-start.5 = (bf16[64,4,128]{2,1,0:T(4,128)(2,1)S(1)}, bf16[64,4,128]{2,1,0:T(4,128)(2,1)S(1)}, u32[]{:S(2)}, u32[]{:S(2)}) collective-permute-start(bf16[64,4,128]{2,1,0:T(4,128)(2,1)S(1)} %get-tuple-element.19), channel_id=1, source_target_pairs={{0,1},{1,2},{2,3},{3,4},{4,5},{5,6},{6,7},{7,0},{8,9},{9,10},{10,1... | collective-permute-start | bytes 196616 | tf_op jit(solution)/shard_map/ppermute | solution.py:409
  81.6 3.8 %collective-permute-start.6 = (bf16[4,72,128]{2,1,0:T(8,128)(2,1)S(1)}, bf16[4,72,128]{2,1,0:T(8,128)(2,1)S(1)}, u32[]{:S(2)}, u32[]{:S(2)}) collective-permute-start(bf16[4,72,128]{2,1,0:T(8,128)(2,1)S(1)} %pad_maximum_fusion.6), channel_id=1, source_target_pairs={{0,8},{8,16},{16,24},{24,0},{1,9},{9,17},{17,25},{25,1},{2,10},{10... | collective-permute-start | bytes 221192 | tf_op jit(solution)/shard_map/ppermute | solution.py:416
  81.6 3.8 %collective-permute-start.7 = (bf16[4,72,128]{2,1,0:T(8,128)(2,1)S(1)}, bf16[4,72,128]{2,1,0:T(8,128)(2,1)S(1)}, u32[]{:S(2)}, u32[]{:S(2)}) collective-permute-start(bf16[4,72,128]{2,1,0:T(8,128)(2,1)S(1)} %pad_maximum_fusion.7), channel_id=1, source_target_pairs={{8,0},{16,8},{24,16},{0,24},{9,1},{17,9},{25,17},{1,25},{10,2},{18... | collective-permute-start | bytes 221192 | tf_op jit(solution)/shard_map/ppermute | solution.py:415
  85.4 0.6 copy-start.6
  86.0 0.6 copy-start.7
  102.0 0.8 copy-start.2

commit v2 on v1

v2 whole, which is shorter than its diff:
```python
import functools

import jax
import jax.numpy as jnp
from jax import lax
from jax.experimental import pallas as pl
from jax.experimental.pallas import tpu as pltpu
from jax.sharding import PartitionSpec as P

NSTEP = 4
F32 = jnp.float32
BF16 = jnp.bfloat16
I32 = jnp.int32
INNOV_MAX = 6.0
INNOV_STEP = INNOV_MAX / 32767.0
WEIGHT_MAX = 4.0
WEIGHT_STEP = WEIGHT_MAX / 65535.0
VMEM_BYTES = 56 * 1024 * 1024


def split_hi_lo(value):
    high = value.astype(BF16)
    low = (value - high.astype(F32)).astype(BF16)
    return high, low


def iota(shape, dim):
    return lax.broadcasted_iota(I32, shape, dim)


def dot_f32(left, right):
    return jnp.dot(left, right, preferred_element_type=F32)


def dot_nt(left, right):
    return lax.dot_general(left, right, (((1,), (1,)), ((), ())), preferred_element_type=F32)


def dot_tn(left, right):
    return lax.dot_general(left, right, (((0,), (0,)), ((), ())), preferred_element_type=F32)


def params():
    return pltpu.CompilerParams(vmem_limit_bytes=VMEM_BYTES)


def vmem_specs(count):
    return [pl.BlockSpec(memory_space=pltpu.VMEM)] * count


def address_kernel(
    devices_all, quarter, count_ref, owner_ref, cell_ref, scale_ref, innov_ref, out_ref, key_ref,
    word_ref,
):
    obs = owner_ref.shape[1]
    rows_half = devices_all * quarter
    rows = 2 * rows_half
    owner = owner_ref[...]
    cell = cell_ref[...]
    mine = iota((devices_all, obs), 0) == owner
    mine_f = mine.astype(F32)
    mine_b = mine_f.astype(BF16)
    block = min(256, obs)
    earlier = (iota((block, block), 0) < iota((block, block), 1)).astype(F32).astype(BF16)
    running = jnp.zeros((devices_all, 1), F32)
    parts = []
    for start in range(0, obs, block):
        piece = mine_f[:, start : start + block]
        before = dot_f32(mine_b[:, start : start + block], earlier) + running
        parts.append(jnp.sum(piece * before, axis=0, keepdims=True))
        running = running + jnp.sum(piece, axis=1, keepdims=True)
    position = jnp.concatenate(parts, axis=1).astype(I32)
    group = position // quarter
    key = (
        (group // 2) * rows + (group % 2) * rows_half + owner * quarter + position % quarter
    )
    key_ref[...] = key
    scale = scale_ref[...]
    valid = iota((1, obs), 1) < count_ref[0]
    weight = jnp.where(valid, 1.0 / (scale * scale), 0.0)
    weight = jnp.minimum(jnp.floor(weight * (1.0 / WEIGHT_STEP) + 0.5), 65535.0)
    weight_high = jnp.floor(weight * (1.0 / 256.0))
    weight_low = weight - 256.0 * weight_high
    cell_high = (cell // 64).astype(F32)
    cell_low = (cell % 64).astype(F32)
    left = jnp.concatenate(
        [mine_f * piece for piece in (cell_high, cell_low, weight_high, weight_low)], axis=0
    ).astype(BF16)
    place = (iota((128, obs), 0) == position).astype(F32).astype(BF16)
    table = dot_nt(left, place).astype(I32)
    n = devices_all
    cells = table[:n] * 64 + table[n : 2 * n]
    weights = table[2 * n : 3 * n] * 256 + table[3 * n :]
    out_ref[:, quarter, :] = (cells << 16) | weights

    level = jnp.floor(
        jnp.clip(innov_ref[...], -INNOV_MAX, INNOV_MAX) * (1.0 / INNOV_STEP) + 0.5
    )
    high = jnp.floor(level * (1.0 / 256.0))
    low = (level - 256.0 * high).astype(BF16)
    high = high.astype(BF16)
    bytes_of = [jnp.concatenate([high, low], axis=0), jnp.concatenate([low, high], axis=0)]
    chunk = min(256, rows_half)
    left_lane = iota((chunk, 128), 1) < 64
    for base in range(0, rows_half, chunk):
        total = []
        for half in range(2):
            row = iota((chunk, obs), 0) + (base + half * rows_half)
            found = []
            for side in range(2):
                hot = (row + side * rows == key).astype(F32).astype(BF16)
                got = dot_nt(hot, bytes_of[side])
                found.append(got * 256.0 + pltpu.roll(got, 64, 1))
            total.append(jnp.where(left_lane, found[0], found[1]).astype(I32))
        word_ref[base : base + chunk, :] = (total[0] << 16) | (total[1] & 0xFFFF)
    for device in range(devices_all):
        out_ref[device, :quarter, :] = word_ref[device * quarter : (device + 1) * quarter, :]


def put_row_block(wide_ref, at, count, tile, east, west):
    cols = tile.shape[1]
    wide_ref[at : at + count, :cols, :] = tile
    wide_ref[at : at + count, cols : cols + NSTEP, :] = east.astype(F32)
    wide_ref[at : at + count, cols + NSTEP :, :] = west.astype(F32)


def spread_kappa(kappa):
    rows, cols = kappa.shape
    high, low = split_hi_lo(kappa)
    pair = jnp.concatenate([high.astype(F32), low.astype(F32)], axis=1)
    hot = iota((rows, cols, 2 * cols), 1) == iota((rows, cols, 2 * cols), 2) % cols
    spread = jnp.where(hot, pair[:, None, :], 0.0).astype(BF16)
    ones = jnp.ones((2 * cols, 128), BF16)
    return dot_f32(spread.reshape(rows * cols, 2 * cols), ones).reshape(rows, cols, 128)


def sweep_rows(source, target, kap_ref, low, high, block=8):
    cols = source.shape[1]

    def update(first, count):
        rows = [source[first + i] for i in range(-1, count + 1)]
        for i in range(count):
            here = rows[i + 1]
            change = (
                (rows[i] + rows[i + 2])
                + (pltpu.roll(here, 1, 0) + pltpu.roll(here, cols - 1, 0))
                - 4.0 * here
            )
            target[first + i] = here + kap_ref[first + i] * change

    whole = (high - low) // block

    def step(index, carry):
        update(low + index * block, block)
        return carry

    lax.fori_loop(0, whole, step, 0)
    if low + whole * block < high:
        update(low + whole * block, high - low - whole * block)


def sweeps(first_ref, second_ref, kap_ref, rows, block=8):
    source, target = first_ref, second_ref
    for sweep in range(1, NSTEP + 1):
        sweep_rows(source, target, kap_ref, sweep, rows - sweep, block)
        source, target = target, source
    return source


def fill_picked(pick_ref, picked):
    channels, levels = picked.shape
    pick_ref[...] = jnp.zeros_like(pick_ref)
    for part in range(4):
        pick_ref[
            part * channels : (part + 1) * channels, part * levels : (part + 1) * levels
        ] = picked


def forward_mixing(vertical):
    high, low = split_hi_lo(vertical)
    pair = jnp.concatenate([high, low], axis=1)
    return jnp.concatenate([pair, pair], axis=0)


def project_rows(rows, dev, mixing, pick):
    count, cols, levels = rows.shape
    pair = jnp.concatenate(split_hi_lo(rows.reshape(count * cols, levels)), axis=1)
    both = dot_f32(pair, mixing)
    state = both[:, :levels] + both[:, levels:]
    prof = (dev.reshape(count * cols, levels) * state).astype(BF16)
    prof = prof.reshape(count // 4, 4, cols, levels)
    wide = jnp.concatenate(
        [prof[:, part].reshape(count // 4 * cols, levels) for part in range(4)], axis=1
    )
    return jnp.concatenate(split_hi_lo(dot_f32(wide, pick)), axis=1)


def forward_kernel(
    control_ref, east_ref, west_ref, kappa_ref, sigma_ref, vertical_ref, table_ref, choice_ref,
    out_ref, pick_ref, first_ref, second_ref, kap_ref,
):
    rows, cols, levels = control_ref.shape
    put_row_block(first_ref, 0, rows, control_ref[...], east_ref[0], west_ref[0])
    put_row_block(kap_ref, 0, rows, spread_kappa(kappa_ref[...]), east_ref[1], west_ref[1])
    done = sweeps(first_ref, second_ref, kap_ref, rows)
    channels = choice_ref.shape[1]
    table_rows = table_ref.shape[0]
    hot = (iota((table_rows, channels), 0) == choice_ref[...]).astype(F32).astype(BF16)
    fill_picked(pick_ref, dot_tn(hot, table_ref[...]).astype(BF16))
    mixing = forward_mixing(vertical_ref[...])
    pick = jnp.transpose(pick_ref[...].astype(F32)).astype(BF16)
    count = 8
    out_ref[:cols, :] = jnp.zeros((cols, out_ref.shape[1]), BF16)
    out_ref[rows // 4 * cols - cols :, :] = jnp.zeros((cols, out_ref.shape[1]), BF16)

    def step(index, carry):
        row = NSTEP + index * count
        at = pl.multiple_of(cols + index * (count // 4 * cols), cols)
        out_ref[pl.ds(at, count // 4 * cols), :] = project_rows(
            done[pl.ds(row, count), :cols, :], sigma_ref[pl.ds(row, count)], mixing, pick
        )
        return carry

    lax.fori_loop(0, (rows - 2 * NSTEP) // count, step, 0)


def pole_flags():
    at = lax.axis_index("lat")
    last = lax.axis_size("lat") - 1
    return jnp.where(at > 0, 1.0, 0.0), jnp.where(at < last, 1.0, 0.0)


def put_rims(wide_ref, tile_of, east_of, west_of, north, south, flags, rows):
    span = 2 * NSTEP
    wide_ref[:NSTEP] = north.astype(F32) * flags[0]
    put_row_block(wide_ref, NSTEP, span, tile_of(0, span), east_of(0, span), west_of(0, span))
    put_row_block(
        wide_ref, 3 * NSTEP, span, tile_of(rows - span, rows), east_of(rows - span, rows),
        west_of(rows - span, rows),
    )
    wide_ref[5 * NSTEP :] = south.astype(F32) * flags[1]


def put_rim_kappa(kap_ref, kappa_ref, east_ref, west_ref, north_ref, south_ref, flags):
    rows = kappa_ref.shape[0]
    span = 2 * NSTEP
    spread = spread_kappa(
        jnp.concatenate([kappa_ref[:span, :], kappa_ref[rows - span :, :]], axis=0)
    )
    put_rims(
        kap_ref,
        lambda low, high: spread[:span] if low == 0 else spread[span:],
        lambda low, high: east_ref[1, low:high],
        lambda low, high: west_ref[1, low:high],
        north_ref[1],
        south_ref[1],
        flags,
        rows,
    )


def owner_kernel(
    devices_all, quarter, recv_ref, evolved_ref, rinv_ref, pick_ref, sigma_ref, control_ref,
    east_ref, west_ref, north_ref, south_ref, kappa_ref, vertical_ref,
    ret_ref, adj_ref, left_ref, right_ref, top_ref, bottom_ref,
    word_ref, dep_ref, acc_ref, first_ref, second_ref, kap_ref, table_ref, pair_ref,
):
    lat_rows, cols, levels = sigma_ref.shape
    flags = pole_flags()
    put_rim_kappa(kap_ref, kappa_ref, east_ref, west_ref, north_ref, south_ref, flags)
    put_rims(
        first_ref,
        lambda low, high: control_ref[low:high],
        lambda low, high: east_ref[0, low:high],
        lambda low, high: west_ref[0, low:high],
        north_ref[0],
        south_ref[0],
        flags,
        lat_rows,
    )
    done = sweeps(first_ref, second_ref, kap_ref, 6 * NSTEP)
    pick = jnp.transpose(pick_ref[...].astype(F32)).astype(BF16)
    ends = project_rows(
        jnp.concatenate(
            [done[NSTEP : 2 * NSTEP, :cols, :], done[4 * NSTEP : 5 * NSTEP, :cols, :]], axis=0
        ),
        jnp.concatenate([sigma_ref[:NSTEP], sigma_ref[lat_rows - NSTEP :]], axis=0),
        forward_mixing(vertical_ref[...]),
        pick,
    )
    cells_part = evolved_ref.shape[0]
    table_ref[...] = evolved_ref[...]
    table_ref[:cols, :] = ends[:cols]
    table_ref[cells_part - cols :, :] = ends[cols:]

    rows_half = devices_all * quarter
    rows = 2 * rows_half
    for device in range(devices_all):
        word_ref[device * quarter : (device + 1) * quarter, :] = recv_ref[device, :quarter, :]
    meta = recv_ref[:, quarter, :]
    cells, weights = meta >> 16, meta & 0xFFFF
    facts = jnp.concatenate(
        [
            piece.astype(F32).astype(BF16)
            for piece in (cells >> 6, cells & 63, weights >> 8, weights & 255)
        ],
        axis=1,
    )
    channels = rinv_ref.shape[0]
    pair_ref[...] = jnp.zeros_like(pair_ref)
    pair_ref[:channels, :channels] = rinv_ref[...]
    pair_ref[channels:, channels:] = rinv_ref[...]
    high, low = split_hi_lo(pair_ref[...])
    zero = jnp.zeros_like(high)
    mixing = jnp.concatenate(
        [jnp.concatenate([high, low], axis=1), jnp.concatenate([high, zero], axis=1)], axis=0
    )
    acc_ref[...] = jnp.zeros_like(acc_ref)
    chunk = min(512, rows_half)
    left_lane = iota((chunk, 128), 1) < 64
    lane_half = iota((chunk, 128), 1) // 64
    per_half = rows_half // chunk
    for step in range(rows // chunk):
        half = step // per_half
        base = (step % per_half) * chunk
        row = iota((chunk, devices_all), 0) + base
        spread = (row // quarter == iota((chunk, devices_all), 1)).astype(F32).astype(BF16)
        found = dot_f32(spread, facts)
        lat_lane = found[:, :128]
        lon_lane = found[:, 128:256]
        weight_lane = (found[:, 256:384] * 256.0 + found[:, 384:]) * WEIGHT_STEP
        lane = iota((chunk, 128), 1)
        r = (iota((chunk, 128), 0) + base) % quarter
        hots, parts, weight, values = [], [], [], []
        for side in range(2):
            take = lane == (2 * side + half) * quarter + r
            lat = jnp.sum(jnp.where(take, lat_lane, 0.0), axis=1, keepdims=True).astype(I32)
            lon = jnp.sum(jnp.where(take, lon_lane, 0.0), axis=1, keepdims=True).astype(I32)
            weight.append(jnp.sum(jnp.where(take, weight_lane, 0.0), axis=1, keepdims=True))
            part = lat & 3
            inside = (lat >> 2) * cols + lon
            hot = (iota((chunk, cells_part), 1) == inside).astype(F32).astype(BF16)
            got = dot_f32(hot, table_ref[...])
            got = got[:, :256] + got[:, 256:]
            lanes = jnp.where(part >= 2, got[:, 128:], got[:, :128])
            swapped = pltpu.roll(lanes, 64, 1)
            odd = (part & 1) == 1
            values.append(
                jnp.where(odd, swapped, lanes) if side == 0 else jnp.where(odd, lanes, swapped)
            )
            hots.append(hot)
            parts.append(part)
        evolved = jnp.where(left_lane, values[0], values[1])
        words = word_ref[base : base + chunk, :]
        words = (words if half == 0 else words << 16) >> 16
        gap = evolved - words.astype(F32) * INNOV_STEP
        both = dot_f32(jnp.concatenate(split_hi_lo(gap), axis=1), mixing)
        dep = (both[:, :128] + both[:, 128:]) * jnp.where(left_lane, weight[0], weight[1])
        dep_ref[step * chunk : (step + 1) * chunk, :] = dep
        rounded = dep.astype(BF16).astype(F32)
        swapped = pltpu.roll(rounded, 64, 1)
        for side in range(2):
            twice = (
                jnp.where(left_lane, rounded, swapped)
                if side == 0
                else jnp.where(left_lane, swapped, rounded)
            )
            wide = jnp.concatenate(
                [
                    jnp.where(parts[side] == lane_half, twice, 0.0).astype(BF16),
                    jnp.where(parts[side] == lane_half + 2, twice, 0.0).astype(BF16),
                ],
                axis=1,
            )
            acc_ref[...] += dot_tn(hots[side], wide)
    for half in range(2):
        for device in range(devices_all):
            at = half * rows_half + device * quarter
            ret_ref[device, half * quarter : (half + 1) * quarter, :] = dep_ref[
                at : at + quarter, :
            ]
    groups = 4
    count = groups * 4

    def spread_out(step, carry):
        high, low = split_hi_lo(
            acc_ref[pl.ds(pl.multiple_of(step * groups * cols, cols), groups * cols), :]
        )
        both = dot_f32(high, pick_ref[...]) + dot_f32(low, pick_ref[...])
        for group in range(groups):
            for part in range(4):
                at = step * count + group * 4 + part
                value = sigma_ref[at] * both[
                    group * cols : (group + 1) * cols, part * levels : (part + 1) * levels
                ]
                adj_ref[at] = value
                left_ref[at] = value[:NSTEP].astype(BF16)
                right_ref[at] = value[cols - NSTEP :].astype(BF16)
        return carry

    lax.fori_loop(0, lat_rows // count, spread_out, 0)
    top_ref[...] = adj_ref[:NSTEP].astype(BF16)
    bottom_ref[...] = adj_ref[lat_rows - NSTEP :].astype(BF16)


def backward_mixing(vertical):
    high, low = split_hi_lo(vertical)
    return jnp.concatenate(
        [jnp.concatenate([high, high], axis=1), jnp.concatenate([low, low], axis=1)], axis=0
    )


def finish_rows(scaled, kap, mixing):
    count, cols, levels = scaled.shape
    adjoint = (scaled / kap).reshape(count * cols, levels)
    both = dot_nt(jnp.concatenate(split_hi_lo(adjoint), axis=1), mixing)
    return (both[:, :levels] + both[:, levels:]).reshape(count, cols, levels)


def inner_kernel(
    adj_ref, east_ref, west_ref, kappa_ref, keast_ref, kwest_ref, vertical_ref, control_ref,
    out_ref, first_ref, second_ref, kap_ref,
):
    rows, cols, levels = control_ref.shape
    put_row_block(kap_ref, 0, rows, spread_kappa(kappa_ref[...]), keast_ref[1], kwest_ref[1])
    put_row_block(first_ref, 0, rows, adj_ref[...], east_ref[...], west_ref[...])
    first_ref[:rows] = first_ref[:rows] * kap_ref[:rows]
    done = sweeps(first_ref, second_ref, kap_ref, rows)
    mixing = backward_mixing(vertical_ref[...])
    count = 8

    def step(index, carry):
        at = pl.ds(NSTEP + index * count, count)
        out_ref[at] = control_ref[at] + finish_rows(
            done[at, :cols, :], kap_ref[at, :cols, :], mixing
        )
        return carry

    lax.fori_loop(0, (rows - 2 * NSTEP) // count, step, 0)


def rim_kernel(
    adj_ref, east_ref, west_ref, north_ref, south_ref, kappa_ref, keast_ref, kwest_ref,
    knorth_ref, ksouth_ref, vertical_ref, control_ref, inner_ref, out_ref,
    first_ref, second_ref, kap_ref, edge_ref, sem_ref,
):
    del inner_ref
    span = 2 * NSTEP
    lat_rows, cols = kappa_ref.shape
    levels = vertical_ref.shape[0]
    flags = pole_flags()
    put_rim_kappa(kap_ref, kappa_ref, keast_ref, kwest_ref, knorth_ref, ksouth_ref, flags)
    put_rims(
        first_ref,
        lambda low, high: adj_ref[0] if low == 0 else adj_ref[1],
        lambda low, high: east_ref[low:high],
        lambda low, high: west_ref[low:high],
        north_ref[...],
        south_ref[...],
        flags,
        lat_rows,
    )
    first_ref[...] = first_ref[...] * kap_ref[...]
    done = sweeps(first_ref, second_ref, kap_ref, 6 * NSTEP)
    mixing = backward_mixing(vertical_ref[...])
    for end in range(2):
        at = pl.ds((1 + 3 * end) * NSTEP, NSTEP)
        back = finish_rows(done[at, :cols, :], kap_ref[at, :cols, :], mixing)
        edge_ref[end] = control_ref[end] + back
    copies = []
    for end in range(2):
        copy = pltpu.make_async_copy(
            edge_ref.at[end], out_ref.at[pl.ds(end * (lat_rows - NSTEP), NSTEP)], sem_ref.at[end]
        )
        copy.start()
        copies.append(copy)
    for copy in copies:
        copy.wait()


def return_kernel(devices_all, quarter, recv_ref, key_ref, out_ref, pair_ref):
    rows_half = devices_all * quarter
    rows = 2 * rows_half
    channels, obs = out_ref.shape
    for half in range(2):
        for device in range(devices_all):
            at = half * rows_half + device * quarter
            high, low = split_hi_lo(recv_ref[device, half * quarter : (half + 1) * quarter, :])
            pair_ref[at : at + quarter, :128] = high
            pair_ref[at : at + quarter, 128:] = low
    chunk = min(512, obs)
    for start in range(0, obs, chunk):
        key = key_ref[:, start : start + chunk]
        side = key >= rows
        row = jnp.where(side, key - rows, key)
        hot = (iota((rows, chunk), 0) == row).astype(F32).astype(BF16)
        both = dot_tn(pair_ref[...], hot)
        both = both[:128] + both[128:]
        out_ref[:, start : start + chunk] = jnp.where(side, both[channels:], both[:channels])


def shifts(axis):
    count = lax.axis_size(axis)
    forward = [(i, (i + 1) % count) for i in range(count)]
    return forward, [(target, source) for source, target in forward]


def exchange_sides(left, right):
    forward, backward = shifts("lon")
    return lax.ppermute(left, "lon", backward), lax.ppermute(right, "lon", forward)


def exchange_rims(top, bottom):
    forward, backward = shifts("lat")
    return lax.ppermute(bottom, "lat", forward), lax.ppermute(top, "lat", backward)


def estimate(flops, bytes_accessed):
    return pl.CostEstimate(flops=flops, bytes_accessed=bytes_accessed, transcendentals=0)


def body(
    control,
    kappa,
    sigma,
    vertical,
    channel_table,
    channel_pick,
    r_inverse,
    innovations,
    error_scale,
    obs_owner,
    obs_cell,
    obs_count,
):
    lat_rows, lon_cols, levels = control.shape
    obs_slots = obs_cell.shape[0]
    channels = innovations.shape[1]
    devices_all = lax.axis_size("lat") * lax.axis_size("lon")
    capacity = max(4, 2 * obs_slots // devices_all)
    quarter = capacity // 4
    rows_half = devices_all * quarter
    columns = lat_rows * lon_cols
    wide = (lat_rows + 1, lon_cols + 2 * NSTEP, levels)
    rim = (6 * NSTEP, lon_cols + 2 * NSTEP, levels)
    span = 2 * NSTEP
    smem = pl.BlockSpec(memory_space=pltpu.SMEM)
    anywhere = pl.BlockSpec(memory_space=pl.ANY)

    def side_of(low, high):
        edge = kappa[:, low:high, None]
        return jnp.stack(
            [
                control[:, low:high].astype(BF16),
                jnp.broadcast_to(edge.astype(BF16), (lat_rows, high - low, levels)),
            ]
        )

    east, west = exchange_sides(side_of(0, NSTEP), side_of(lon_cols - NSTEP, lon_cols))

    payload, key = pl.pallas_call(
        functools.partial(address_kernel, devices_all, quarter),
        out_shape=(
            jax.ShapeDtypeStruct((devices_all, quarter + 1, 128), I32),
            jax.ShapeDtypeStruct((1, obs_slots), I32),
        ),
        in_specs=[smem] + vmem_specs(4),
        out_specs=tuple(vmem_specs(2)),
        scratch_shapes=[pltpu.VMEM((rows_half, 128), I32)],
        compiler_params=params(),
        cost_estimate=estimate(2_000_000_000, 8_000_000),
        name="address",
    )(
        obs_count,
        obs_owner.reshape(1, obs_slots),
        obs_cell.reshape(1, obs_slots),
        error_scale.reshape(1, obs_slots),
        innovations.T,
    )
    received = lax.all_to_all(payload, ("lat", "lon"), split_axis=0, concat_axis=0, tiled=True)

    def rim_of(low, high):
        tile = jnp.stack(
            [
                control[low:high].astype(BF16),
                jnp.broadcast_to(
                    kappa[low:high, :, None].astype(BF16), (high - low, lon_cols, levels)
                ),
            ]
        )
        return jnp.concatenate([tile, east[:, low:high], west[:, low:high]], axis=2)

    north, south = exchange_rims(rim_of(0, NSTEP), rim_of(lat_rows - NSTEP, lat_rows))

    evolved, picked = pl.pallas_call(
        forward_kernel,
        out_shape=(
            jax.ShapeDtypeStruct((columns // 4, 8 * channels), BF16),
            jax.ShapeDtypeStruct((4 * channels, 4 * levels), BF16),
        ),
        in_specs=vmem_specs(8),
        out_specs=tuple(vmem_specs(2)),
        scratch_shapes=[pltpu.VMEM(wide, F32)] * 3,
        compiler_params=params(),
        cost_estimate=estimate(4_000_000_000, 16_000_000),
        name="forward",
    )(
        control, east, west, kappa, sigma, vertical, channel_table,
        channel_pick.reshape(1, channels),
    )

    returned, adjoint, left, right, top, bottom = pl.pallas_call(
        functools.partial(owner_kernel, devices_all, quarter),
        out_shape=(
            jax.ShapeDtypeStruct((devices_all, 2 * quarter, 128), F32),
            jax.ShapeDtypeStruct(control.shape, F32),
            jax.ShapeDtypeStruct((lat_rows, NSTEP, levels), BF16),
            jax.ShapeDtypeStruct((lat_rows, NSTEP, levels), BF16),
            jax.ShapeDtypeStruct((NSTEP, lon_cols, levels), BF16),
            jax.ShapeDtypeStruct((NSTEP, lon_cols, levels), BF16),
        ),
        in_specs=vmem_specs(12),
        out_specs=tuple(vmem_specs(6)),
        scratch_shapes=[
            pltpu.VMEM((rows_half, 128), I32),
            pltpu.VMEM((2 * rows_half, 128), F32),
            pltpu.VMEM((columns // 4, 4 * channels), F32),
            pltpu.VMEM(rim, F32),
            pltpu.VMEM(rim, F32),
            pltpu.VMEM(rim, F32),
            pltpu.VMEM((columns // 4, 8 * channels), BF16),
            pltpu.VMEM((2 * channels, 2 * channels), F32),
        ],
        compiler_params=params(),
        cost_estimate=estimate(4_000_000_000, 16_000_000),
        name="owner",
    )(
        received, evolved, r_inverse, picked, sigma, control, east, west, north, south, kappa,
        vertical,
    )
    home = lax.all_to_all(returned, ("lat", "lon"), split_axis=0, concat_axis=0, tiled=True)

    aeast, awest = exchange_sides(left, right)
    anorth, asouth = exchange_rims(
        jnp.concatenate([top, aeast[:NSTEP], awest[:NSTEP]], axis=1),
        jnp.concatenate([bottom, aeast[-NSTEP:], awest[-NSTEP:]], axis=1),
    )
    inner = pl.pallas_call(
        inner_kernel,
        out_shape=jax.ShapeDtypeStruct(control.shape, F32),
        in_specs=vmem_specs(8),
        out_specs=vmem_specs(1)[0],
        scratch_shapes=[pltpu.VMEM(wide, F32)] * 3,
        compiler_params=params(),
        cost_estimate=estimate(4_000_000_000, 16_000_000),
        name="inner",
    )(adjoint, aeast, awest, kappa, east, west, vertical, control)

    def ends(field, width):
        return jnp.stack([field[:width], field[lat_rows - width :]])

    gradient = pl.pallas_call(
        rim_kernel,
        out_shape=jax.ShapeDtypeStruct(control.shape, F32),
        in_specs=vmem_specs(12) + [anywhere],
        out_specs=anywhere,
        scratch_shapes=[pltpu.VMEM(rim, F32)] * 3
        + [
            pltpu.VMEM((2, NSTEP, lon_cols, levels), F32),
            pltpu.SemaphoreType.DMA((2,)),
        ],
        input_output_aliases={12: 0},
        compiler_params=params(),
        cost_estimate=estimate(1_000_000_000, 2_000_000),
        name="rims",
    )(
        ends(adjoint, span), aeast, awest, anorth, asouth, kappa, east, west, north, south,
        vertical, ends(control, NSTEP), inner,
    )

    departures = pl.pallas_call(
        functools.partial(return_kernel, devices_all, quarter),
        out_shape=jax.ShapeDtypeStruct((channels, obs_slots), F32),
        in_specs=vmem_specs(2),
        out_specs=vmem_specs(1)[0],
        scratch_shapes=[pltpu.VMEM((2 * rows_half, 256), BF16)],
        compiler_params=params(),
        cost_estimate=estimate(500_000_000, 2_000_000),
        name="give_back",
    )(home, key)
    return (gradient, departures.T)


def solution(mesh):
    return jax.shard_map(
        body,
        mesh=mesh,
        in_specs=(
            P("lat", "lon", None),
            P("lat", "lon"),
            P("lat", "lon", None),
            P(),
            P(),
            P(),
            P(),
            P(("lat", "lon"), None),
            P(("lat", "lon")),
            P(("lat", "lon"), None),
            P(("lat", "lon")),
            P(("lat", "lon")),
        ),
        out_specs=(P("lat", "lon", None), P(("lat", "lon"), None)),
        check_vma=False,
    )
```

time: 109 us -> 92.5 us (0.85)
  other arithmetic: 7.71 us -> 1.99 us
  Pallas kernels: 48 us -> 43.2 us
  local copies, waits for them, and re-layouts: 7.93 us -> 4.59 us
    pallas_call x2 -> x3, Pallas kernels: 29.3 us -> 24.1 us  [the longest x1 10.6 us: body(): pl.pallas_call(forward_kernel, out_shape=(jax.ShapeDtypeStruct((columns /...]
    concatenate x9 -> x4, other arithmetic: 4.36 us -> 0.06 us  [the longest x2 0.04 us: rim_of(): return jnp.concatenate([tile, east[:, low:high], west[:, low:high]], axis=2)]
    unnamed x22 -> x28, local copies, waits for them, and re-layouts: 6.5 us -> 2.87 us
    pallas_call x1, Pallas kernels: 11.6 us -> 13 us  [body(): pl.pallas_call(functools.partial(owner_kernel, devices_all, quarter), out...]
  transfers between devices with their start and end apart: 10 -> 10, of which waited for: 6 -> 4; matrix products, arithmetic and copies ran while one was open for 8% -> 4% of each run, Pallas kernels for 27% -> 26%
where the time goes in v2:
time: 92.5 us; the launch traced here: 92.1 us
  Pallas kernels  43.2 us (47%)
  starting transfers between devices  23.2 us (25%)
  waiting for transfers between devices  17.4 us (19%)
  local copies, waits for them, and re-layouts  4.59 us (5%)
  other arithmetic  1.99 us (2%)
  between operations  1.58 us (2%)
    pallas_call x1, Pallas kernels, body(): pl.pallas_call(functools.partial(owner_kernel, devices_all, quarter), out...  13 us
    pallas_call x1, Pallas kernels, body(): pl.pallas_call(forward_kernel, out_shape=(jax.ShapeDtypeStruct((columns /...  10.6 us
    ppermute x2, waiting for transfers between devices, exchange_sides(): lax.ppermute(right, 'lon', forward)  9.69 us
    pallas_call x1, Pallas kernels, body(): pl.pallas_call(inner_kernel, out_shape=jax.ShapeDtypeStruct(control.shape...  9.58 us
    ppermute x2, starting transfers between devices, exchange_sides(): lax.ppermute(left, 'lon', backward)  9.21 us
    ppermute x2, waiting for transfers between devices, exchange_sides(): lax.ppermute(left, 'lon', backward)  7.73 us
    all_to_all x1, starting transfers between devices, body(): lax.all_to_all(payload, ('lat', 'lon'), split_axis=0, concat_axis=0, tile...  7.3 us
    pallas_call x1, Pallas kernels, body(): pl.pallas_call(rim_kernel, out_shape=jax.ShapeDtypeStruct(control.shape,...  3.94 us
  transfers between devices with their start and end apart: 10, of which 4 were waited for; matrix products, arithmetic and copies ran while one was open for 4% of the time, Pallas kernels for 26%

profile of v2, /device:TPU:0, one launch (start us, length us, event | category | flops | bytes accessed | tf_op | source)
XLA Modules:
  0.0 92.1 jit_solution(2625989180119738583)
XLA Ops:
  1.3 3.5 %address.1 = (s32[32,17,128]{2,1,0:T(8,128)}, s32[1,1024]{1,0:T(1,128)}) custom-call(s32[1]{0:T(128)S(6)} %copy.16.count_ref, s32[1,1024]{1,0:T(1,128)} %bitcast.23, s32[1,1024]{1,0:T(1,128)} %bitcast.24, f32[1,1024]{1,0:T(1,128)} %bitcast.25, f32[64,1024]{1,0:T(8,128)} %bitcast.22), custom_call_target="tpu_custom_call" | custom-call | flops 2000000000 | bytes 8000000 | tf_op jit(solution)/shard_map/address/pallas_call | solution.py:561
  4.8 7.3 %all-to-all-start = ((s32[32,17,128]{2,1,0:T(8,128)}), s32[32,17,128]{2,1,0:T(8,128)S(1)}, u32[]{:S(2)}, u32[]{:S(2)}) async-start(s32[32,17,128]{2,1,0:T(8,128)} %get-tuple-element.12), calls=%async_computation | async-start | bytes 786432 | tf_op jit(solution)/shard_map/all_to_all | solution.py:580
  12.2 0.1 fusion.7
  12.3 0.2 convert.10
  12.5 0.1 stack_broadcast_in_dim.8
  12.7 0.1 pad_maximum_fusion.4
  12.8 4.6 %collective-permute-start = (bf16[2,64,4,128]{3,2,1,0:T(4,128)(2,1)S(1)}, bf16[2,64,4,128]{3,2,1,0:T(4,128)(2,1)S(1)}, u32[]{:S(2)}, u32[]{:S(2)}) collective-permute-start(bf16[2,64,4,128]{3,2,1,0:T(4,128)(2,1)S(1)} %pad_maximum_fusion.4), channel_id=1, source_target_pairs={{1,0},{2,1},{3,2},{4,3},{5,4},{6,5},{7,6},{0,7},{9,8},{10,9},{11,1... | collective-permute-start | bytes 393224 | tf_op jit(solution)/shard_map/ppermute | solution.py:510
  17.4 0.1 stack_broadcast_in_dim.9
  17.5 0.1 pad_maximum_fusion.5
  17.7 0.7 pad_maximum_fusion.1.control_ref
  18.5 3.6 %collective-permute-done.east_ref.keast_ref = bf16[2,64,4,128]{3,2,1,0:T(4,128)(2,1)S(1)} collective-permute-done((bf16[2,64,4,128]{3,2,1,0:T(4,128)(2,1)S(1)}, bf16[2,64,4,128]{3,2,1,0:T(4,128)(2,1)S(1)}, u32[]{:S(2)}, u32[]{:S(2)}) %collective-permute-start) | collective-permute-done | bytes 131104 | tf_op jit(solution)/shard_map/ppermute | solution.py:510
  22.0 4.9 %collective-permute-done.1.west_ref.kwest_ref = bf16[2,64,4,128]{3,2,1,0:T(4,128)(2,1)S(1)} collective-permute-done((bf16[2,64,4,128]{3,2,1,0:T(4,128)(2,1)S(1)}, bf16[2,64,4,128]{3,2,1,0:T(4,128)(2,1)S(1)}, u32[]{:S(2)}, u32[]{:S(2)}) %collective-permute-start.1) | collective-permute-done | bytes 131104 | tf_op jit(solution)/shard_map/ppermute | solution.py:510
  26.9 0.1 stack_broadcast_in_dim.10
  27.1 0.1 stack_broadcast_in_dim.11
  27.3 1.8 %collective-permute-start.3 = (bf16[2,4,72,128]{3,2,1,0:T(8,128)(2,1)S(1)}, bf16[2,4,72,128]{3,2,1,0:T(8,128)(2,1)S(1)}, u32[]{:S(2)}, u32[]{:S(2)}) collective-permute-start(bf16[2,4,72,128]{3,2,1,0:T(8,128)(2,1)S(1)} %pad_maximum_fusion.3), channel_id=1, source_target_pairs={{8,0},{16,8},{24,16},{0,24},{9,1},{17,9},{25,17},{1,25},{10,2},{18... | collective-permute-start | bytes 442376 | tf_op jit(solution)/shard_map/ppermute | solution.py:515
  29.1 10.6 %forward.1 = (bf16[1024,512]{1,0:T(8,128)(2,1)}, bf16[256,512]{1,0:T(8,128)(2,1)}) custom-call(f32[64,64,128]{2,1,0:T(8,128)} %control_ref.5, bf16[2,64,4,128]{3,2,1,0:T(4,128)(2,1)} %copy-done.3, bf16[2,64,4,128]{3,2,1,0:T(4,128)(2,1)} %copy-done.4, f32[64,64]{1,0:T(8,128)} %kappa_ref.7, f32[64,64,128]{2,1,0:T(8,128)} %sigma_ref.3, ...), custom_call_target="tpu_custom_call" | custom-call | flops 4000000000 | bytes 16000000 | tf_op jit(solution)/shard_map/forward/pallas_call | solution.py:595
  39.7 0.6 copy-done.5
  40.4 0.1 copy-done.2
  40.5 13.0 %owner.1 = (f32[32,32,128]{2,1,0:T(8,128)}, f32[64,64,128]{2,1,0:T(8,128)}, bf16[64,4,128]{2,1,0:T(4,128)(2,1)}, bf16[64,4,128]{2,1,0:T(4,128)(2,1)}, bf16[4,64,...) custom-call(s32[32,17,128]{2,1,0:T(8,128)} %copy-done.2, bf16[1024,512]{1,0:T(8,128)(2,1)} %get-tuple-element.13.evolved_ref, ...), custom_call_target="tpu_custom_call" | custom-call | flops 4000000000 | bytes 16000000 | tf_op jit(solution)/shard_map/owner/pallas_call | solution.py:612
  53.5 3.0 %all-to-all-start.1 = ((f32[32,32,128]{2,1,0:T(8,128)}), f32[32,32,128]{2,1,0:T(8,128)S(1)}, u32[]{:S(2)}, u32[]{:S(2)}) async-start(f32[32,32,128]{2,1,0:T(8,128)} %get-tuple-element.20), calls=%async_computation.1 | async-start | bytes 1048576 | tf_op jit(solution)/shard_map/all_to_all | solution.py:641
  56.5 4.6 %collective-permute-start.4 = (bf16[64,4,128]{2,1,0:T(4,128)(2,1)}, bf16[64,4,128]{2,1,0:T(4,128)(2,1)S(1)}, u32[]{:S(2)}, u32[]{:S(2)}) collective-permute-start(bf16[64,4,128]{2,1,0:T(4,128)(2,1)} %get-tuple-element.16), channel_id=1, source_target_pairs={{1,0},{2,1},{3,2},{4,3},{5,4},{6,5},{7,6},{0,7},{9,8},{10,9},{11,1... | collective-permute-start | bytes 196616 | tf_op jit(solution)/shard_map/ppermute | solution.py:510
  61.1 1.1 %slice_bitcast_fusion.1 = (f32[1,8,64,128]{3,2,1,0:T(8,128)S(1)}, f32[1,8,64,128]{3,2,1,0:T(8,128)S(1)}) fusion(f32[64,64,128]{2,1,0:T(8,128)} %get-tuple-element.15.adj_ref), kind=kLoop, calls=%fused_computation.3 | loop fusion | bytes 1048576 | tf_op jit(solution)/shard_map/stack | solution.py:660
  62.2 0.8 pad_maximum_fusion.adj_ref
  63.0 4.2 %collective-permute-done.4.east_ref = bf16[64,4,128]{2,1,0:T(4,128)(2,1)S(1)} collective-permute-done((bf16[64,4,128]{2,1,0:T(4,128)(2,1)}, bf16[64,4,128]{2,1,0:T(4,128)(2,1)S(1)}, u32[]{:S(2)}, u32[]{:S(2)}) %collective-permute-start.4) | collective-permute-done | bytes 65568 | tf_op jit(solution)/shard_map/ppermute | solution.py:510
  67.2 4.8 %collective-permute-done.5.west_ref = bf16[64,4,128]{2,1,0:T(4,128)(2,1)S(1)} collective-permute-done((bf16[64,4,128]{2,1,0:T(4,128)(2,1)}, bf16[64,4,128]{2,1,0:T(4,128)(2,1)S(1)}, u32[]{:S(2)}, u32[]{:S(2)}) %collective-permute-start.5) | collective-permute-done | bytes 65568 | tf_op jit(solution)/shard_map/ppermute | solution.py:510
  72.1 1.8 %collective-permute-start.7 = (bf16[4,72,128]{2,1,0:T(8,128)(2,1)S(1)}, bf16[4,72,128]{2,1,0:T(8,128)(2,1)S(1)}, u32[]{:S(2)}, u32[]{:S(2)}) collective-permute-start(bf16[4,72,128]{2,1,0:T(8,128)(2,1)S(1)} %pad_maximum_fusion.7), channel_id=1, source_target_pairs={{8,0},{16,8},{24,16},{0,24},{9,1},{17,9},{25,17},{1,25},{10,2},{18... | collective-permute-start | bytes 221192 | tf_op jit(solution)/shard_map/ppermute | solution.py:515
  73.9 9.6 %inner.1.inner_ref = f32[64,64,128]{2,1,0:T(8,128)} custom-call(f32[64,64,128]{2,1,0:T(8,128)} %get-tuple-element.15.adj_ref, bf16[64,4,128]{2,1,0:T(4,128)(2,1)} %copy-done.8, bf16[64,4,128]{2,1,0:T(4,128)(2,1)} %copy-done.9, f32[64,64]{1,0:T(8,128)} %kappa_ref.7, bf16[2,64,4,128]{3,2,1,0:T(4,128)(2,1)} %copy-done.3, bf16[2,64,4,128]{3,2,1,0:T(4,128)(2,1)} %copy-done.4, ...), custom_call_target="tpu_custom_call" | custom-call | flops 4000000000 | bytes 16000000 | tf_op jit(solution)/shard_map/inner/pallas_call | solution.py:648
  83.5 0.6 copy-done.10
  84.1 0.6 copy-done.11
  84.7 3.9 %rims.1 = f32[64,64,128]{2,1,0:T(8,128)} custom-call(f32[2,8,64,128]{3,2,1,0:T(8,128)} %pad_maximum_fusion.adj_ref, bf16[64,4,128]{2,1,0:T(4,128)(2,1)} %copy-done.8, bf16[64,4,128]{2,1,0:T(4,128)(2,1)} %copy-done.9, bf16[4,72,128]{2,1,0:T(8,128)(2,1)} %copy-done.10, bf16[4,72,128]{2,1,0:T(8,128)(2,1)} %copy-done.11, ...), custom_call_target="tpu_custom_call", output_to_operand_aliasing={{}: (12, {})} | custom-call | flops 1000000000 | bytes 2000000 | tf_op jit(solution)/shard_map/rims/pallas_call | solution.py:662
  88.7 0.8 copy-done.1
  89.5 2.6 %give_back.1 = f32[64,1024]{1,0:T(8,128)} custom-call(f32[32,32,128]{2,1,0:T(8,128)} %copy-done.1, s32[1,1024]{1,0:T(1,128)} %get-tuple-element.21.key_ref), custom_call_target="tpu_custom_call" | custom-call | flops 500000000 | bytes 2000000 | tf_op jit(solution)/shard_map/give_back/pallas_call | solution.py:681
  (46 shorter events, 0.5 us)
Async XLA Ops:
  1.3 10.9 %copy-start.7 = (f32[64,64]{1,0:T(8,128)S(1)}, f32[64,64]{1,0:T(8,128)}, u32[]{:S(2)}) copy-start(f32[64,64]{1,0:T(8,128)} %kappa_ref.7) | copy-start | bytes 49156
  1.3 11.0 %copy-start = (f32[64,64,128]{2,1,0:T(8,128)S(1)}, f32[64,64,128]{2,1,0:T(8,128)}, u32[]{:S(2)}) copy-start(f32[64,64,128]{2,1,0:T(8,128)} %control_ref.5) | copy-start | bytes 6291460
  4.8 34.8 %all-to-all-start = ((s32[32,17,128]{2,1,0:T(8,128)}), s32[32,17,128]{2,1,0:T(8,128)S(1)}, u32[]{:S(2)}, u32[]{:S(2)}) async-start(s32[32,17,128]{2,1,0:T(8,128)} %get-tuple-element.12), calls=%async_computation | async-start | bytes 786432 | tf_op jit(solution)/shard_map/all_to_all | solution.py:580
  12.8 9.3 %collective-permute-start = (bf16[2,64,4,128]{3,2,1,0:T(4,128)(2,1)S(1)}, bf16[2,64,4,128]{3,2,1,0:T(4,128)(2,1)S(1)}, u32[]{:S(2)}, u32[]{:S(2)}) collective-permute-start(bf16[2,64,4,128]{3,2,1,0:T(4,128)(2,1)S(1)} %pad_maximum_fusion.4), channel_id=1, source_target_pairs={{1,0},{2,1},{3,2},{4,3},{5,4},{6,5},{7,6},{0,7},{9,8},{10,9},{11,1... | collective-permute-start | bytes 393224 | tf_op jit(solution)/shard_map/ppermute | solution.py:510
  17.6 9.3 %collective-permute-start.1 = (bf16[2,64,4,128]{3,2,1,0:T(4,128)(2,1)S(1)}, bf16[2,64,4,128]{3,2,1,0:T(4,128)(2,1)S(1)}, u32[]{:S(2)}, u32[]{:S(2)}) collective-permute-start(bf16[2,64,4,128]{3,2,1,0:T(4,128)(2,1)S(1)} %pad_maximum_fusion.5), channel_id=1, source_target_pairs={{0,1},{1,2},{2,3},{3,4},{4,5},{5,6},{6,7},{7,0},{8,9},{9,10},{10,1... | collective-permute-start | bytes 393224 | tf_op jit(solution)/shard_map/ppermute | solution.py:510
  22.0 7.0 %copy-start.3 = (bf16[2,64,4,128]{3,2,1,0:T(4,128)(2,1)}, bf16[2,64,4,128]{3,2,1,0:T(4,128)(2,1)S(1)}, u32[]{:S(2)}) copy-start(bf16[2,64,4,128]{3,2,1,0:T(4,128)(2,1)S(1)} %collective-permute-done.east_ref.keast_ref) | copy-start | bytes 393220
  26.9 2.1 %copy-start.4 = (bf16[2,64,4,128]{3,2,1,0:T(4,128)(2,1)}, bf16[2,64,4,128]{3,2,1,0:T(4,128)(2,1)S(1)}, u32[]{:S(2)}) copy-start(bf16[2,64,4,128]{3,2,1,0:T(4,128)(2,1)S(1)} %collective-permute-done.1.west_ref.kwest_ref) | copy-start | bytes 393220
  27.1 12.6 %collective-permute-start.2 = (bf16[2,4,72,128]{3,2,1,0:T(8,128)(2,1)S(1)}, bf16[2,4,72,128]{3,2,1,0:T(8,128)(2,1)S(1)}, u32[]{:S(2)}, u32[]{:S(2)}) collective-permute-start(bf16[2,4,72,128]{3,2,1,0:T(8,128)(2,1)S(1)} %pad_maximum_fusion.2), channel_id=1, source_target_pairs={{0,8},{8,16},{16,24},{24,0},{1,9},{9,17},{17,25},{25,1},{2,10},{10... | collective-permute-start | bytes 442376 | tf_op jit(solution)/shard_map/ppermute | solution.py:515
  27.3 12.4 %collective-permute-start.3 = (bf16[2,4,72,128]{3,2,1,0:T(8,128)(2,1)S(1)}, bf16[2,4,72,128]{3,2,1,0:T(8,128)(2,1)S(1)}, u32[]{:S(2)}, u32[]{:S(2)}) collective-permute-start(bf16[2,4,72,128]{3,2,1,0:T(8,128)(2,1)S(1)} %pad_maximum_fusion.3), channel_id=1, source_target_pairs={{8,0},{16,8},{24,16},{0,24},{9,1},{17,9},{25,17},{1,25},{10,2},{18... | collective-permute-start | bytes 442376 | tf_op jit(solution)/shard_map/ppermute | solution.py:515
  39.7 0.7 copy-start.5
  39.7 0.7 copy-start.6
  39.7 0.8 copy-start.2
  53.5 18.5 %copy-start.13 = (bf16[4,64,128]{2,1,0:T(8,128)(2,1)S(1)}, bf16[4,64,128]{2,1,0:T(8,128)(2,1)}, u32[]{:S(2)}) copy-start(bf16[4,64,128]{2,1,0:T(8,128)(2,1)} %get-tuple-element.18) | copy-start | bytes 196612
  53.5 18.6 %copy-start.12 = (bf16[4,64,128]{2,1,0:T(8,128)(2,1)S(1)}, bf16[4,64,128]{2,1,0:T(8,128)(2,1)}, u32[]{:S(2)}) copy-start(bf16[4,64,128]{2,1,0:T(8,128)(2,1)} %get-tuple-element.19) | copy-start | bytes 196612
  53.5 35.2 %all-to-all-start.1 = ((f32[32,32,128]{2,1,0:T(8,128)}), f32[32,32,128]{2,1,0:T(8,128)S(1)}, u32[]{:S(2)}, u32[]{:S(2)}) async-start(f32[32,32,128]{2,1,0:T(8,128)} %get-tuple-element.20), calls=%async_computation.1 | async-start | bytes 1048576 | tf_op jit(solution)/shard_map/all_to_all | solution.py:641
  56.5 10.7 %collective-permute-start.4 = (bf16[64,4,128]{2,1,0:T(4,128)(2,1)}, bf16[64,4,128]{2,1,0:T(4,128)(2,1)S(1)}, u32[]{:S(2)}, u32[]{:S(2)}) collective-permute-start(bf16[64,4,128]{2,1,0:T(4,128)(2,1)} %get-tuple-element.16), channel_id=1, source_target_pairs={{1,0},{2,1},{3,2},{4,3},{5,4},{6,5},{7,6},{0,7},{9,8},{10,9},{11,1... | collective-permute-start | bytes 196616 | tf_op jit(solution)/shard_map/ppermute | solution.py:510
  61.1 10.9 %collective-permute-start.5 = (bf16[64,4,128]{2,1,0:T(4,128)(2,1)}, bf16[64,4,128]{2,1,0:T(4,128)(2,1)S(1)}, u32[]{:S(2)}, u32[]{:S(2)}) collective-permute-start(bf16[64,4,128]{2,1,0:T(4,128)(2,1)} %get-tuple-element.17), channel_id=1, source_target_pairs={{0,1},{1,2},{2,3},{3,4},{4,5},{5,6},{6,7},{7,0},{8,9},{9,10},{10,1... | collective-permute-start | bytes 196616 | tf_op jit(solution)/shard_map/ppermute | solution.py:510
  67.2 6.7 %copy-start.8 = (bf16[64,4,128]{2,1,0:T(4,128)(2,1)}, bf16[64,4,128]{2,1,0:T(4,128)(2,1)S(1)}, u32[]{:S(2)}) copy-start(bf16[64,4,128]{2,1,0:T(4,128)(2,1)S(1)} %collective-permute-done.4.east_ref) | copy-start | bytes 196612
  72.0 1.9 %copy-start.9 = (bf16[64,4,128]{2,1,0:T(4,128)(2,1)}, bf16[64,4,128]{2,1,0:T(4,128)(2,1)S(1)}, u32[]{:S(2)}) copy-start(bf16[64,4,128]{2,1,0:T(4,128)(2,1)S(1)} %collective-permute-done.5.west_ref) | copy-start | bytes 196612
  72.0 11.5 %collective-permute-start.6 = (bf16[4,72,128]{2,1,0:T(8,128)(2,1)S(1)}, bf16[4,72,128]{2,1,0:T(8,128)(2,1)S(1)}, u32[]{:S(2)}, u32[]{:S(2)}) collective-permute-start(bf16[4,72,128]{2,1,0:T(8,128)(2,1)S(1)} %pad_maximum_fusion.6), channel_id=1, source_target_pairs={{0,8},{8,16},{16,24},{24,0},{1,9},{9,17},{17,25},{25,1},{2,10},{10... | collective-permute-start | bytes 221192 | tf_op jit(solution)/shard_map/ppermute | solution.py:515
  72.1 11.4 %collective-permute-start.7 = (bf16[4,72,128]{2,1,0:T(8,128)(2,1)S(1)}, bf16[4,72,128]{2,1,0:T(8,128)(2,1)S(1)}, u32[]{:S(2)}, u32[]{:S(2)}) collective-permute-start(bf16[4,72,128]{2,1,0:T(8,128)(2,1)S(1)} %pad_maximum_fusion.7), channel_id=1, source_target_pairs={{8,0},{16,8},{24,16},{0,24},{9,1},{17,9},{25,17},{1,25},{10,2},{18... | collective-permute-start | bytes 221192 | tf_op jit(solution)/shard_map/ppermute | solution.py:515
  83.5 0.6 copy-start.10
  84.1 0.6 copy-start.11
  88.7 0.8 copy-start.1

commit v3 on v2

--- a/solution.py
+++ b/solution.py
@@ -15,7 +15,6 @@
 INNOV_STEP = INNOV_MAX / 32767.0
 WEIGHT_MAX = 4.0
 WEIGHT_STEP = WEIGHT_MAX / 65535.0
-VMEM_BYTES = 56 * 1024 * 1024
 
 
 def split_hi_lo(value):
@@ -40,8 +39,25 @@
     return lax.dot_general(left, right, (((0,), (0,)), ((), ())), preferred_element_type=F32)
 
 
-def params():
-    return pltpu.CompilerParams(vmem_limit_bytes=VMEM_BYTES)
+def params(mebibytes):
+    return pltpu.CompilerParams(vmem_limit_bytes=mebibytes * 1024 * 1024)
+
+
+HBM_SPEC = pl.BlockSpec(memory_space=pltpu.HBM)
+
+
+def start_copies(pairs, sem_ref, first=0):
+    copies = []
+    for index, (source, target) in enumerate(pairs):
+        copy = pltpu.make_async_copy(source, target, sem_ref.at[first + index])
+        copy.start()
+        copies.append(copy)
+    return copies
+
+
+def wait_copies(copies):
+    for copy in copies:
+        copy.wait()
 
 
 def vmem_specs(count):
@@ -120,6 +136,10 @@
 def put_row_block(wide_ref, at, count, tile, east, west):
     cols = tile.shape[1]
     wide_ref[at : at + count, :cols, :] = tile
+    put_sides(wide_ref, at, count, cols, east, west)
+
+
+def put_sides(wide_ref, at, count, cols, east, west):
     wide_ref[at : at + count, cols : cols + NSTEP, :] = east.astype(F32)
     wide_ref[at : at + count, cols + NSTEP :, :] = west.astype(F32)
 
@@ -196,32 +216,36 @@
 
 
 def forward_kernel(
-    control_ref, east_ref, west_ref, kappa_ref, sigma_ref, vertical_ref, table_ref, choice_ref,
-    out_ref, pick_ref, first_ref, second_ref, kap_ref,
+    control_hbm, sigma_hbm, east_ref, west_ref, kappa_ref, vertical_ref, table_ref, choice_ref,
+    out_hbm, pick_hbm, first_ref, second_ref, kap_ref, out_ref, pick_ref, sigma_ref, sem_ref,
 ):
-    rows, cols, levels = control_ref.shape
-    put_row_block(first_ref, 0, rows, control_ref[...], east_ref[0], west_ref[0])
-    put_row_block(kap_ref, 0, rows, spread_kappa(kappa_ref[...]), east_ref[1], west_ref[1])
+    rows, cols, levels = control_hbm.shape
+    tile_in = start_copies(
+        [(control_hbm, first_ref.at[pl.ds(0, rows), pl.ds(0, cols)])], sem_ref
+    )
+    sigma_in = start_copies([(sigma_hbm, sigma_ref)], sem_ref, 1)
+    put_sides(first_ref, 0, rows, cols, east_ref[0], west_ref[0])
+    kap_ref[:rows, :cols, :] = spread_kappa(kappa_ref[...])
+    put_sides(kap_ref, 0, rows, cols, east_ref[1], west_ref[1])
+    wait_copies(tile_in)
     done = sweeps(first_ref, second_ref, kap_ref, rows)
+    wait_copies(sigma_in)
     channels = choice_ref.shape[1]
     table_rows = table_ref.shape[0]
     hot = (iota((table_rows, channels), 0) == choice_ref[...]).astype(F32).astype(BF16)
     fill_picked(pick_ref, dot_tn(hot, table_ref[...]).astype(BF16))
     mixing = forward_mixing(vertical_ref[...])
     pick = jnp.transpose(pick_ref[...].astype(F32)).astype(BF16)
+    copies = start_copies([(pick_ref, pick_hbm)], sem_ref)
     count = 8
-    out_ref[:cols, :] = jnp.zeros((cols, out_ref.shape[1]), BF16)
-    out_ref[rows // 4 * cols - cols :, :] = jnp.zeros((cols, out_ref.shape[1]), BF16)
-
-    def step(index, carry):
+    for index in range((rows - 2 * NSTEP) // count):
         row = NSTEP + index * count
-        at = pl.multiple_of(cols + index * (count // 4 * cols), cols)
-        out_ref[pl.ds(at, count // 4 * cols), :] = project_rows(
-            done[pl.ds(row, count), :cols, :], sigma_ref[pl.ds(row, count)], mixing, pick
+        where = pl.ds(row // 4 * cols, count // 4 * cols)
+        out_ref[where, :] = project_rows(
+            done[row : row + count, :cols, :], sigma_ref[row : row + count], mixing, pick
         )
-        return carry
-
-    lax.fori_loop(0, (rows - 2 * NSTEP) // count, step, 0)
+        copies += start_copies([(out_ref.at[where], out_hbm.at[where])], sem_ref, index + 1)
+    wait_copies(copies)
 
 
 def pole_flags():
@@ -260,17 +284,34 @@
 
 
 def owner_kernel(
-    devices_all, quarter, recv_ref, evolved_ref, rinv_ref, pick_ref, sigma_ref, control_ref,
+    devices_all, quarter, recv_hbm, evolved_hbm, pick_hbm, sigma_hbm, control_hbm, rinv_ref,
     east_ref, west_ref, north_ref, south_ref, kappa_ref, vertical_ref,
-    ret_ref, adj_ref, left_ref, right_ref, top_ref, bottom_ref,
+    ret_ref, adj_hbm, left_hbm, right_hbm, top_hbm, bottom_hbm,
     word_ref, dep_ref, acc_ref, first_ref, second_ref, kap_ref, table_ref, pair_ref,
+    recv_ref, pick_ref, sigma_ref, ends_ref, adj_ref, left_ref, right_ref, top_ref, bottom_ref,
+    sem_ref,
 ):
-    lat_rows, cols, levels = sigma_ref.shape
+    lat_rows, cols, levels = sigma_hbm.shape
+    cells_part = evolved_hbm.shape[0]
     flags = pole_flags()
+    span = 2 * NSTEP
+    inside = pl.ds(cols, cells_part - 2 * cols)
+    control_in = start_copies(
+        [
+            (control_hbm.at[pl.ds(0, span)], ends_ref.at[0]),
+            (control_hbm.at[pl.ds(lat_rows - span, span)], ends_ref.at[1]),
+        ],
+        sem_ref,
+    )
+    sigma_in = start_copies([(sigma_hbm, sigma_ref), (pick_hbm, pick_ref)], sem_ref, 2)
+    others_in = start_copies(
+        [(recv_hbm, recv_ref), (evolved_hbm.at[inside], table_ref.at[inside])], sem_ref, 4
+    )
     put_rim_kappa(kap_ref, kappa_ref, east_ref, west_ref, north_ref, south_ref, flags)
+    wait_copies(control_in)
     put_rims(
         first_ref,
-        lambda low, high: control_ref[low:high],
+        lambda low, high: ends_ref[0] if low == 0 else ends_ref[1],
         lambda low, high: east_ref[0, low:high],
         lambda low, high: west_ref[0, low:high],
         north_ref[0],
@@ -279,6 +320,7 @@
         lat_rows,
     )
     done = sweeps(first_ref, second_ref, kap_ref, 6 * NSTEP)
+    wait_copies(sigma_in)
     pick = jnp.transpose(pick_ref[...].astype(F32)).astype(BF16)
     ends = project_rows(
         jnp.concatenate(
@@ -288,11 +330,10 @@
         forward_mixing(vertical_ref[...]),
         pick,
     )
-    cells_part = evolved_ref.shape[0]
-    table_ref[...] = evolved_ref[...]
     table_ref[:cols, :] = ends[:cols]
     table_ref[cells_part - cols :, :] = ends[cols:]
 
+    wait_copies(others_in)
     rows_half = devices_all * quarter
     rows = 2 * rows_half
     for device in range(devices_all):
@@ -356,7 +397,7 @@
         gap = evolved - words.astype(F32) * INNOV_STEP
         both = dot_f32(jnp.concatenate(split_hi_lo(gap), axis=1), mixing)
         dep = (both[:, :128] + both[:, 128:]) * jnp.where(left_lane, weight[0], weight[1])
-        dep_ref[step * chunk : (step + 1) * chunk, :] = dep
+        dep_ref[step * chunk : (step + 1) * chunk, :] = evolved
         rounded = dep.astype(BF16).astype(F32)
         swapped = pltpu.roll(rounded, 64, 1)
         for side in range(2):
@@ -381,11 +422,9 @@
             ]
     groups = 4
     count = groups * 4
-
-    def spread_out(step, carry):
-        high, low = split_hi_lo(
-            acc_ref[pl.ds(pl.multiple_of(step * groups * cols, cols), groups * cols), :]
-        )
+    copies = []
+    for step in range(lat_rows // count):
+        high, low = split_hi_lo(acc_ref[step * groups * cols : (step + 1) * groups * cols, :])
         both = dot_f32(high, pick_ref[...]) + dot_f32(low, pick_ref[...])
         for group in range(groups):
             for part in range(4):
@@ -396,11 +435,23 @@
                 adj_ref[at] = value
                 left_ref[at] = value[:NSTEP].astype(BF16)
                 right_ref[at] = value[cols - NSTEP :].astype(BF16)
-        return carry
-
-    lax.fori_loop(0, lat_rows // count, spread_out, 0)
-    top_ref[...] = adj_ref[:NSTEP].astype(BF16)
-    bottom_ref[...] = adj_ref[lat_rows - NSTEP :].astype(BF16)
+                if at < NSTEP:
+                    top_ref[at] = value.astype(BF16)
+                if at >= lat_rows - NSTEP:
+                    bottom_ref[at - (lat_rows - NSTEP)] = value.astype(BF16)
+        where = pl.ds(step * count, count)
+        copies += start_copies([(adj_ref.at[where], adj_hbm.at[where])], sem_ref, step)
+    copies += start_copies(
+        [
+            (left_ref, left_hbm),
+            (right_ref, right_hbm),
+            (top_ref, top_hbm),
+            (bottom_ref, bottom_hbm),
+        ],
+        sem_ref,
+        lat_rows // count,
+    )
+    wait_copies(copies)
 
 
 def backward_mixing(vertical):
@@ -419,7 +470,7 @@
 
 def inner_kernel(
     adj_ref, east_ref, west_ref, kappa_ref, keast_ref, kwest_ref, vertical_ref, control_ref,
-    out_ref, first_ref, second_ref, kap_ref,
+    out_hbm, first_ref, second_ref, kap_ref, out_ref, sem_ref,
 ):
     rows, cols, levels = control_ref.shape
     put_row_block(kap_ref, 0, rows, spread_kappa(kappa_ref[...]), keast_ref[1], kwest_ref[1])
@@ -428,15 +479,15 @@
     done = sweeps(first_ref, second_ref, kap_ref, rows)
     mixing = backward_mixing(vertical_ref[...])
     count = 8
-
-    def step(index, carry):
-        at = pl.ds(NSTEP + index * count, count)
+    copies = []
+    for index in range((rows - 2 * NSTEP) // count):
+        row = NSTEP + index * count
+        at = pl.ds(row, count)
         out_ref[at] = control_ref[at] + finish_rows(
-            done[at, :cols, :], kap_ref[at, :cols, :], mixing
+            done[row : row + count, :cols, :], kap_ref[row : row + count, :cols, :], mixing
         )
-        return carry
-
-    lax.fori_loop(0, (rows - 2 * NSTEP) // count, step, 0)
+        copies += start_copies([(out_ref.at[at], out_hbm.at[at])], sem_ref, index)
+    wait_copies(copies)
 
 
 def rim_kernel(
@@ -478,7 +529,10 @@
         copy.wait()
 
 
-def return_kernel(devices_all, quarter, recv_ref, key_ref, out_ref, pair_ref):
+def return_kernel(
+    devices_all, quarter, count_ref, recv_ref, key_ref, innov_ref, scale_ref, rinv_ref, out_ref,
+    pair_ref,
+):
     rows_half = devices_all * quarter
     rows = 2 * rows_half
     channels, obs = out_ref.shape
@@ -488,6 +542,9 @@
             high, low = split_hi_lo(recv_ref[device, half * quarter : (half + 1) * quarter, :])
             pair_ref[at : at + quarter, :128] = high
             pair_ref[at : at + quarter, 128:] = low
+    scale = scale_ref[...]
+    valid = iota((1, obs), 1) < count_ref[0]
+    weight = jnp.where(valid, 1.0 / (scale * scale), 0.0)
     chunk = min(512, obs)
     for start in range(0, obs, chunk):
         key = key_ref[:, start : start + chunk]
@@ -496,7 +553,13 @@
         hot = (iota((rows, chunk), 0) == row).astype(F32).astype(BF16)
         both = dot_tn(pair_ref[...], hot)
         both = both[:128] + both[128:]
-        out_ref[:, start : start + chunk] = jnp.where(side, both[channels:], both[:channels])
+        evolved = jnp.where(side, both[channels:], both[:channels])
+        gap = evolved - innov_ref[:, start : start + chunk]
+        mixed = lax.dot_general(
+            rinv_ref[...], gap, (((0,), (0,)), ((), ())), precision=lax.Precision.HIGHEST,
+            preferred_element_type=F32,
+        )
+        out_ref[:, start : start + chunk] = mixed * weight[:, start : start + chunk]
 
 
 def shifts(axis):
@@ -556,7 +619,9 @@
             ]
         )
 
-    east, west = exchange_sides(side_of(0, NSTEP), side_of(lon_cols - NSTEP, lon_cols))
+    near, far = side_of(0, NSTEP), side_of(lon_cols - NSTEP, lon_cols)
+    near, far, obs_cell = lax.optimization_barrier((near, far, obs_cell))
+    east, west = exchange_sides(near, far)
 
     payload, key = pl.pallas_call(
         functools.partial(address_kernel, devices_all, quarter),
@@ -567,7 +632,7 @@
         in_specs=[smem] + vmem_specs(4),
         out_specs=tuple(vmem_specs(2)),
         scratch_shapes=[pltpu.VMEM((rows_half, 128), I32)],
-        compiler_params=params(),
+        compiler_params=params(10),
         cost_estimate=estimate(2_000_000_000, 8_000_000),
         name="address",
     )(
@@ -598,14 +663,20 @@
             jax.ShapeDtypeStruct((columns // 4, 8 * channels), BF16),
             jax.ShapeDtypeStruct((4 * channels, 4 * levels), BF16),
         ),
-        in_specs=vmem_specs(8),
-        out_specs=tuple(vmem_specs(2)),
-        scratch_shapes=[pltpu.VMEM(wide, F32)] * 3,
-        compiler_params=params(),
+        in_specs=[HBM_SPEC] * 2 + vmem_specs(6),
+        out_specs=(HBM_SPEC, HBM_SPEC),
+        scratch_shapes=[pltpu.VMEM(wide, F32)] * 3
+        + [
+            pltpu.VMEM((columns // 4, 8 * channels), BF16),
+            pltpu.VMEM((4 * channels, 4 * levels), BF16),
+            pltpu.VMEM(control.shape, F32),
+            pltpu.SemaphoreType.DMA((lat_rows // 8 + 2,)),
+        ],
+        compiler_params=params(58),
         cost_estimate=estimate(4_000_000_000, 16_000_000),
         name="forward",
     )(
-        control, east, west, kappa, sigma, vertical, channel_table,
+        control, sigma, east, west, kappa, vertical, channel_table,
         channel_pick.reshape(1, channels),
     )
 
@@ -619,8 +690,8 @@
             jax.ShapeDtypeStruct((NSTEP, lon_cols, levels), BF16),
             jax.ShapeDtypeStruct((NSTEP, lon_cols, levels), BF16),
         ),
-        in_specs=vmem_specs(12),
-        out_specs=tuple(vmem_specs(6)),
+        in_specs=[HBM_SPEC] * 5 + vmem_specs(7),
+        out_specs=tuple(vmem_specs(1) + [HBM_SPEC] * 5),
         scratch_shapes=[
             pltpu.VMEM((rows_half, 128), I32),
             pltpu.VMEM((2 * rows_half, 128), F32),
@@ -630,15 +701,28 @@
             pltpu.VMEM(rim, F32),
             pltpu.VMEM((columns // 4, 8 * channels), BF16),
             pltpu.VMEM((2 * channels, 2 * channels), F32),
+            pltpu.VMEM((devices_all, quarter + 1, 128), I32),
+            pltpu.VMEM((4 * channels, 4 * levels), BF16),
+            pltpu.VMEM(control.shape, F32),
+            pltpu.VMEM((2, span, lon_cols, levels), F32),
+            pltpu.VMEM(control.shape, F32),
+            pltpu.VMEM((lat_rows, NSTEP, levels), BF16),
+            pltpu.VMEM((lat_rows, NSTEP, levels), BF16),
+            pltpu.VMEM((NSTEP, lon_cols, levels), BF16),
+            pltpu.VMEM((NSTEP, lon_cols, levels), BF16),
+            pltpu.SemaphoreType.DMA((lat_rows // 16 + 4,)),
         ],
-        compiler_params=params(),
+        compiler_params=params(58),
         cost_estimate=estimate(4_000_000_000, 16_000_000),
         name="owner",
     )(
-        received, evolved, r_inverse, picked, sigma, control, east, west, north, south, kappa,
+        received, evolved, picked, sigma, control, r_inverse, east, west, north, south, kappa,
         vertical,
     )
-    home = lax.all_to_all(returned, ("lat", "lon"), split_axis=0, concat_axis=0, tiled=True)
+    left, right, returned = lax.optimization_barrier((left, right, returned))
+    home = lax.all_to_all(
+        returned.astype(jnp.float16), ("lat", "lon"), split_axis=0, concat_axis=0, tiled=True
+    )
 
     aeast, awest = exchange_sides(left, right)
     anorth, asouth = exchange_rims(
@@ -649,9 +733,10 @@
         inner_kernel,
         out_shape=jax.ShapeDtypeStruct(control.shape, F32),
         in_specs=vmem_specs(8),
-        out_specs=vmem_specs(1)[0],
-        scratch_shapes=[pltpu.VMEM(wide, F32)] * 3,
-        compiler_params=params(),
+        out_specs=HBM_SPEC,
+        scratch_shapes=[pltpu.VMEM(wide, F32)] * 3
+        + [pltpu.VMEM(control.shape, F32), pltpu.SemaphoreType.DMA((lat_rows // 8,))],
+        compiler_params=params(20),
         cost_estimate=estimate(4_000_000_000, 16_000_000),
         name="inner",
     )(adjoint, aeast, awest, kappa, east, west, vertical, control)
@@ -670,7 +755,7 @@
             pltpu.SemaphoreType.DMA((2,)),
         ],
         input_output_aliases={12: 0},
-        compiler_params=params(),
+        compiler_params=params(12),
         cost_estimate=estimate(1_000_000_000, 2_000_000),
         name="rims",
     )(
@@ -681,13 +766,16 @@
     departures = pl.pallas_call(
         functools.partial(return_kernel, devices_all, quarter),
         out_shape=jax.ShapeDtypeStruct((channels, obs_slots), F32),
-        in_specs=vmem_specs(2),
+        in_specs=[smem] + vmem_specs(5),
         out_specs=vmem_specs(1)[0],
         scratch_shapes=[pltpu.VMEM((2 * rows_half, 256), BF16)],
-        compiler_params=params(),
+        compiler_params=params(10),
         cost_estimate=estimate(500_000_000, 2_000_000),
         name="give_back",
-    )(home, key)
+    )(
+        obs_count, home.astype(F32), key, innovations.T, error_scale.reshape(1, obs_slots),
+        r_inverse,
+    )
     return (gradient, departures.T)
 
 

time: 92.5 us -> 73.5 us (0.79)
  waiting for transfers between devices: 17.4 us -> 0.3 us
  Pallas kernels: 43.2 us -> 33.5 us
  starting transfers between devices: 23.2 us -> 26.6 us
  other arithmetic: 1.99 us -> 4.72 us
  local copies, waits for them, and re-layouts: 4.59 us -> 6.08 us
    ppermute x2, waiting for transfers between devices: 9.69 us -> 0.01 us  [exchange_sides(): lax.ppermute(right, 'lon', forward)]
    ppermute x2, waiting for transfers between devices: 7.73 us -> 0.01 us  [exchange_sides(): lax.ppermute(left, 'lon', backward)]
    pallas_call x1, Pallas kernels: 9.58 us -> 5.81 us  [body(): pl.pallas_call(inner_kernel, out_shape=jax.ShapeDtypeStruct(control.shape...]
    all_to_all x1, starting transfers between devices: 2.99 us -> 6 us  [body(): lax.all_to_all(returned.astype(jnp.float16), ('lat', 'lon'), split_axis=0...]
    another operation x2, other arithmetic: 0.19 us -> 2.57 us
    convert_element_type x0 -> x2, other arithmetic: none -> 1.84 us  [the longest x1 1.79 us: body(): returned.astype(jnp.float16)]
    pallas_call x1, Pallas kernels: 10.6 us -> 8.82 us  [body(): pl.pallas_call(forward_kernel, out_shape=(jax.ShapeDtypeStruct((columns /...]
    pallas_call x1, Pallas kernels: 3.94 us -> 2.43 us  [body(): pl.pallas_call(rim_kernel, out_shape=jax.ShapeDtypeStruct(control.shape,...]
  transfers between devices with their start and end apart: 10 -> 10, of which waited for: 4 -> 1; matrix products, arithmetic and copies ran while one was open for 4% -> 7% of each run, Pallas kernels for 26% -> 27%
where the time goes in v3:
time: 73.5 us; the launch traced here: 72.9 us
  Pallas kernels  33.5 us (46%)
  starting transfers between devices  26.6 us (36%)
  local copies, waits for them, and re-layouts  6.08 us (8%)
  other arithmetic  4.72 us (6%)
  between operations  1.77 us (2%)
    pallas_call x1, Pallas kernels, body(): pl.pallas_call(functools.partial(owner_kernel, devices_all, quarter), out...  12 us
    ppermute x2, starting transfers between devices, exchange_sides(): lax.ppermute(left, 'lon', backward)  10.4 us
    pallas_call x1, Pallas kernels, body(): pl.pallas_call(forward_kernel, out_shape=(jax.ShapeDtypeStruct((columns /...  8.82 us
    all_to_all x1, starting transfers between devices, body(): lax.all_to_all(payload, ('lat', 'lon'), split_axis=0, concat_axis=0, tile...  6.01 us
    all_to_all x1, starting transfers between devices, body(): lax.all_to_all(returned.astype(jnp.float16), ('lat', 'lon'), split_axis=0...  6 us
    pallas_call x1, Pallas kernels, body(): pl.pallas_call(inner_kernel, out_shape=jax.ShapeDtypeStruct(control.shape...  5.81 us
    ppermute x2, starting transfers between devices, exchange_rims(): lax.ppermute(top, 'lat', backward)  3.49 us
    another operation x2, other arithmetic  2.57 us
  transfers between devices with their start and end apart: 10, of which 1 were waited for; matrix products, arithmetic and copies ran while one was open for 7% of the time, Pallas kernels for 27%

profile of v3, /device:TPU:0, one launch (start us, length us, event | category | flops | bytes accessed | tf_op | source)
XLA Modules:
  0.0 72.9 jit_solution(3786026451623821766)
XLA Ops:
  0.6 0.8 %convert.11 = bf16[64,64]{1,0:T(8,128)(2,1)S(1)} convert(f32[64,64]{1,0:T(8,128)} %kappa_ref.7) | non-fusion elementwise | flops 4096 | bytes 24576 | tf_op jit(solution)/shard_map/convert.4
  1.4 0.1 fusion.7
  1.5 1.8 %convert.10 = bf16[64,64,128]{2,1,0:T(8,128)(2,1)S(1)} convert(f32[64,64,128]{2,1,0:T(8,128)} %control_ref.1) | non-fusion elementwise | flops 524288 | bytes 3145728 | tf_op jit(solution)/shard_map/convert.5
  3.3 0.1 slice_bitcast_fusion.4
  3.4 0.1 stack_broadcast_in_dim.9
  3.5 0.1 stack_broadcast_in_dim.8
  3.6 0.2 pad_maximum_fusion.4
  3.8 6.1 %collective-permute-start = (bf16[2,64,4,128]{3,2,1,0:T(4,128)(2,1)S(1)}, bf16[2,64,4,128]{3,2,1,0:T(4,128)(2,1)S(1)}, u32[]{:S(2)}, u32[]{:S(2)}) collective-permute-start(bf16[2,64,4,128]{3,2,1,0:T(4,128)(2,1)S(1)} %get-tuple-element.20), channel_id=1, source_target_pairs={{1,0},{2,1},{3,2},{4,3},{5,4},{6,5},{7,6},{0,7},{9,8},{10,9},{11,1... | collective-permute-start | bytes 393224 | tf_op jit(solution)/shard_map/ppermute | solution.py:573
  10.6 2.4 %address.1 = (s32[32,17,128]{2,1,0:T(8,128)}, s32[1,1024]{1,0:T(1,128)S(1)}) custom-call(s32[1]{0:T(128)S(6)} %copy.16.count_ref, s32[1,1024]{1,0:T(1,128)S(1)} %bitcast.24, s32[1,1024]{1,0:T(1,128)S(1)} %bitcast.25, f32[1,1024]{1,0:T(1,128)S(1)} %bitcast.26, f32[64,1024]{1,0:T(8,128)S(1)} %bitcast.22), custom_call_target="tpu_custom_call" | custom-call | flops 2000000000 | bytes 8000000 | tf_op jit(solution)/shard_map/address/pallas_call | solution.py:626
  13.0 6.0 %all-to-all-start = ((s32[32,17,128]{2,1,0:T(8,128)}), s32[32,17,128]{2,1,0:T(8,128)S(1)}, u32[]{:S(2)}, u32[]{:S(2)}) async-start(s32[32,17,128]{2,1,0:T(8,128)} %get-tuple-element.19), calls=%async_computation | async-start | bytes 786432 | tf_op jit(solution)/shard_map/all_to_all | solution.py:645
  19.0 1.0 %fusion.1 = (bf16[1,4,64,128]{3,2,1,0:T(8,128)(2,1)S(1)}, bf16[1,4,64,128]{3,2,1,0:T(8,128)(2,1)S(1)}) fusion(f32[64,64,128]{2,1,0:T(8,128)} %control_ref.1), kind=kLoop, calls=%fused_computation.15 | loop fusion | bytes 262144 | tf_op jit(solution)/shard_map/stack | solution.py:648
  20.0 1.0 %slice_bitcast_fusion.2 = (f32[1,4,64,128]{3,2,1,0:T(8,128)S(1)}, f32[1,4,64,128]{3,2,1,0:T(8,128)S(1)}) fusion(f32[64,64,128]{2,1,0:T(8,128)} %control_ref.1), kind=kLoop, calls=%fused_computation.8 | loop fusion | bytes 524288 | tf_op jit(solution)/shard_map/stack | solution.py:745
  21.1 0.1 stack_broadcast_in_dim.10
  21.2 0.3 collective-permute-start.2
  21.5 0.1 stack_broadcast_in_dim.11
  21.7 1.7 %collective-permute-start.3 = (bf16[2,4,72,128]{3,2,1,0:T(8,128)(2,1)S(1)}, bf16[2,4,72,128]{3,2,1,0:T(8,128)(2,1)S(1)}, u32[]{:S(2)}, u32[]{:S(2)}) collective-permute-start(bf16[2,4,72,128]{3,2,1,0:T(8,128)(2,1)S(1)} %pad_maximum_fusion.3), channel_id=1, source_target_pairs={{8,0},{16,8},{24,16},{0,24},{9,1},{17,9},{25,17},{1,25},{10,2},{18... | collective-permute-start | bytes 442376 | tf_op jit(solution)/shard_map/ppermute | solution.py:578
  23.4 8.8 %forward.1 = (bf16[1024,512]{1,0:T(8,128)(2,1)}, bf16[256,512]{1,0:T(8,128)(2,1)}) custom-call(f32[64,64,128]{2,1,0:T(8,128)} %control_ref.1, f32[64,64,128]{2,1,0:T(8,128)} %sigma_hbm.3, bf16[2,64,4,128]{3,2,1,0:T(4,128)(2,1)} %copy-done.1, bf16[2,64,4,128]{3,2,1,0:T(4,128)(2,1)} %copy-done.3, f32[64,64]{1,0:T(8,128)} %kappa_ref.7, ...), custom_call_target="tpu_custom_call" | custom-call | flops 4000000000 | bytes 16000000 | tf_op jit(solution)/shard_map/forward/pallas_call | solution.py:660
  32.3 0.3 all-to-all-done.recv_hbm
  32.6 0.4 copy-done.5
  33.0 0.3 copy-done.17
  33.3 12.0 %owner.1 = (f32[32,32,128]{2,1,0:T(8,128)}, f32[64,64,128]{2,1,0:T(8,128)}, bf16[64,4,128]{2,1,0:T(4,128)(2,1)}, bf16[64,4,128]{2,1,0:T(4,128)(2,1)}, bf16[4,64,...) custom-call(s32[32,17,128]{2,1,0:T(8,128)} %copy-done.17, bf16[1024,512]{1,0:T(8,128)(2,1)} %get-tuple-element.22.evolved_hbm, ...), custom_call_target="tpu_custom_call" | custom-call | flops 4000000000 | bytes 16000000 | tf_op jit(solution)/shard_map/owner/pallas_call | solution.py:683
  45.4 4.4 %collective-permute-start.4 = (bf16[64,4,128]{2,1,0:T(4,128)(2,1)}, bf16[64,4,128]{2,1,0:T(4,128)(2,1)S(1)}, u32[]{:S(2)}, u32[]{:S(2)}) collective-permute-start(bf16[64,4,128]{2,1,0:T(4,128)(2,1)} %get-tuple-element.28), channel_id=1, source_target_pairs={{1,0},{2,1},{3,2},{4,3},{5,4},{6,5},{7,6},{0,7},{9,8},{10,9},{11,1... | collective-permute-start | bytes 196616 | tf_op jit(solution)/shard_map/ppermute | solution.py:573
  49.8 1.8 %convert_element_type.24 = f16[32,32,128]{2,1,0:T(8,128)(2,1)} convert(f32[32,32,128]{2,1,0:T(8,128)} %get-tuple-element.32) | non-fusion elementwise | flops 131072 | bytes 786432 | tf_op jit(solution)/shard_map/convert_element_type | solution.py:724
  51.6 6.0 %all-to-all-start.1 = ((f16[32,32,128]{2,1,0:T(8,128)(2,1)}), f16[32,32,128]{2,1,0:T(8,128)(2,1)S(1)}, u32[]{:S(2)}, u32[]{:S(2)}) async-start(f16[32,32,128]{2,1,0:T(8,128)(2,1)} %convert_element_type.24), calls=%async_computation.1 | async-start | bytes 524288 | tf_op jit(solution)/shard_map/all_to_all | solution.py:723
  57.6 1.1 %slice_bitcast_fusion.1 = (f32[1,8,64,128]{3,2,1,0:T(8,128)S(1)}, f32[1,8,64,128]{3,2,1,0:T(8,128)S(1)}) fusion(f32[64,64,128]{2,1,0:T(8,128)} %get-tuple-element.24.adj_ref), kind=kLoop, calls=%fused_computation.3 | loop fusion | bytes 1048576 | tf_op jit(solution)/shard_map/stack | solution.py:745
  58.8 0.3 collective-permute-start.6
  59.1 1.8 %collective-permute-start.7 = (bf16[4,72,128]{2,1,0:T(8,128)(2,1)S(1)}, bf16[4,72,128]{2,1,0:T(8,128)(2,1)S(1)}, u32[]{:S(2)}, u32[]{:S(2)}) collective-permute-start(bf16[4,72,128]{2,1,0:T(8,128)(2,1)S(1)} %pad_maximum_fusion.7), channel_id=1, source_target_pairs={{8,0},{16,8},{24,16},{0,24},{9,1},{17,9},{25,17},{1,25},{10,2},{18... | collective-permute-start | bytes 221192 | tf_op jit(solution)/shard_map/ppermute | solution.py:578
  60.9 1.6 %copy-done.10 = f32[64,64,128]{2,1,0:T(8,128)S(1)} copy-done((f32[64,64,128]{2,1,0:T(8,128)S(1)}, f32[64,64,128]{2,1,0:T(8,128)}, u32[]{:S(2)}) %copy-start.10) | copy-done | bytes 2097176
  62.5 5.8 %inner.1.inner_ref = f32[64,64,128]{2,1,0:T(8,128)} custom-call(f32[64,64,128]{2,1,0:T(8,128)S(1)} %copy-done.10, bf16[64,4,128]{2,1,0:T(4,128)(2,1)S(1)} %collective-permute-done.4.east_ref, bf16[64,4,128]{2,1,0:T(4,128)(2,1)S(1)} %collective-permute-done.5.west_ref, f32[64,64]{1,0:T(8,128)S(1)} %copy-done.9, bf16[2,64,4,128]{3,2,1,0:T(4,128)(2,1)S(1)} %copy-done.2, ...), custom_call_target="tpu_custom_call" | custom-call | flops 4000000000 | bytes 16000000 | tf_op jit(solution)/shard_map/inner/pallas_call | solution.py:732
  68.4 2.4 %rims.1 = f32[64,64,128]{2,1,0:T(8,128)} custom-call(f32[2,8,64,128]{3,2,1,0:T(8,128)S(1)} %pad_maximum_fusion.adj_ref, bf16[64,4,128]{2,1,0:T(4,128)(2,1)S(1)} %collective-permute-done.4.east_ref, bf16[64,4,128]{2,1,0:T(4,128)(2,1)S(1)} %collective-permute-done.5.west_ref, ...), custom_call_target="tpu_custom_call", output_to_operand_aliasing={{}: (12, {})} | custom-call | flops 1000000000 | bytes 2000000 | tf_op jit(solution)/shard_map/rims/pallas_call | solution.py:747
  70.8 0.1 convert_element_type.25.recv_ref
  70.9 2.0 %give_back.1 = f32[64,1024]{1,0:T(8,128)} custom-call(s32[1]{0:T(128)S(6)} %copy.16.count_ref, f32[32,32,128]{2,1,0:T(8,128)S(1)} %convert_element_type.25.recv_ref, s32[1,1024]{1,0:T(1,128)S(1)} %get-tuple-element.33.key_ref, f32[64,1024]{1,0:T(8,128)S(1)} %bitcast.23, f32[1,1024]{1,0:T(1,128)S(1)} %bitcast.27, f32[64,64]{1,0:T(8,128)S(1)} %copy-done.13), custom_call_target="tpu_custom_call" | custom-call | flops 500000000 | bytes 2000000 | tf_op jit(solution)/shard_map/give_back/pallas_call | solution.py:766
  (59 shorter events, 0.3 us)
Async XLA Ops:
  1.4 9.2 %copy-start.12 = (f32[1024,64]{0,1:T(8,128)S(1)}, f32[1024,64]{0,1:T(8,128)}, u32[]{:S(2)}) copy-start(f32[1024,64]{0,1:T(8,128)} %param.19) | copy-start | bytes 786436
  1.4 9.2 %copy-start.14 = (s32[1024,1]{0,1:T(1,128)S(1)}, s32[1024,1]{0,1:T(1,128)}, u32[]{:S(2)}) copy-start(s32[1024,1]{0,1:T(1,128)} %param.21) | copy-start | bytes 12292
  1.4 9.2 %copy-start.15 = (s32[1024]{0:T(1024)S(1)}, s32[1024]{0:T(1024)}, u32[]{:S(2)}) copy-start(s32[1024]{0:T(1024)} %param.22) | copy-start | bytes 12292
  1.4 9.2 %copy-start.16 = (f32[1024]{0:T(1024)S(1)}, f32[1024]{0:T(1024)}, u32[]{:S(2)}) copy-start(f32[1024]{0:T(1024)} %param.20) | copy-start | bytes 12292
  3.8 17.2 %collective-permute-start = (bf16[2,64,4,128]{3,2,1,0:T(4,128)(2,1)S(1)}, bf16[2,64,4,128]{3,2,1,0:T(4,128)(2,1)S(1)}, u32[]{:S(2)}, u32[]{:S(2)}) collective-permute-start(bf16[2,64,4,128]{3,2,1,0:T(4,128)(2,1)S(1)} %get-tuple-element.20), channel_id=1, source_target_pairs={{1,0},{2,1},{3,2},{4,3},{5,4},{6,5},{7,6},{0,7},{9,8},{10,9},{11,1... | collective-permute-start | bytes 393224 | tf_op jit(solution)/shard_map/ppermute | solution.py:573
  9.9 11.2 %collective-permute-start.1 = (bf16[2,64,4,128]{3,2,1,0:T(4,128)(2,1)S(1)}, bf16[2,64,4,128]{3,2,1,0:T(4,128)(2,1)S(1)}, u32[]{:S(2)}, u32[]{:S(2)}) collective-permute-start(bf16[2,64,4,128]{3,2,1,0:T(4,128)(2,1)S(1)} %get-tuple-element.21), channel_id=1, source_target_pairs={{0,1},{1,2},{2,3},{3,4},{4,5},{5,6},{6,7},{7,0},{8,9},{9,10},{10,1... | collective-permute-start | bytes 393224 | tf_op jit(solution)/shard_map/ppermute | solution.py:573
  13.0 19.6 %all-to-all-start = ((s32[32,17,128]{2,1,0:T(8,128)}), s32[32,17,128]{2,1,0:T(8,128)S(1)}, u32[]{:S(2)}, u32[]{:S(2)}) async-start(s32[32,17,128]{2,1,0:T(8,128)} %get-tuple-element.19), calls=%async_computation | async-start | bytes 786432 | tf_op jit(solution)/shard_map/all_to_all | solution.py:645
  21.0 2.4 %copy-start.1 = (bf16[2,64,4,128]{3,2,1,0:T(4,128)(2,1)}, bf16[2,64,4,128]{3,2,1,0:T(4,128)(2,1)S(1)}, u32[]{:S(2)}) copy-start(bf16[2,64,4,128]{3,2,1,0:T(4,128)(2,1)S(1)} %collective-permute-done.east_ref.keast_ref) | copy-start | bytes 393220
  21.1 2.3 %copy-start.3 = (bf16[2,64,4,128]{3,2,1,0:T(4,128)(2,1)}, bf16[2,64,4,128]{3,2,1,0:T(4,128)(2,1)S(1)}, u32[]{:S(2)}) copy-start(bf16[2,64,4,128]{3,2,1,0:T(4,128)(2,1)S(1)} %collective-permute-done.1.west_ref.kwest_ref) | copy-start | bytes 393220
  21.2 11.0 %collective-permute-start.2 = (bf16[2,4,72,128]{3,2,1,0:T(8,128)(2,1)S(1)}, bf16[2,4,72,128]{3,2,1,0:T(8,128)(2,1)S(1)}, u32[]{:S(2)}, u32[]{:S(2)}) collective-permute-start(bf16[2,4,72,128]{3,2,1,0:T(8,128)(2,1)S(1)} %pad_maximum_fusion.2), channel_id=1, source_target_pairs={{0,8},{8,16},{16,24},{24,0},{1,9},{9,17},{17,25},{25,1},{2,10},{10... | collective-permute-start | bytes 442376 | tf_op jit(solution)/shard_map/ppermute | solution.py:578
  21.7 10.6 %collective-permute-start.3 = (bf16[2,4,72,128]{3,2,1,0:T(8,128)(2,1)S(1)}, bf16[2,4,72,128]{3,2,1,0:T(8,128)(2,1)S(1)}, u32[]{:S(2)}, u32[]{:S(2)}) collective-permute-start(bf16[2,4,72,128]{3,2,1,0:T(8,128)(2,1)S(1)} %pad_maximum_fusion.3), channel_id=1, source_target_pairs={{8,0},{16,8},{24,16},{0,24},{9,1},{17,9},{25,17},{1,25},{10,2},{18... | collective-permute-start | bytes 442376 | tf_op jit(solution)/shard_map/ppermute | solution.py:578
  32.2 0.7 copy-start.5
  32.3 0.7 copy-start.7
  32.6 0.7 %copy-start.17 = (s32[32,17,128]{2,1,0:T(8,128)}, s32[32,17,128]{2,1,0:T(8,128)S(1)}, u32[]{:S(2)}) copy-start(s32[32,17,128]{2,1,0:T(8,128)S(1)} %all-to-all-done.recv_hbm) | copy-start | bytes 835588
  45.3 13.4 %copy-start.19 = (bf16[4,64,128]{2,1,0:T(8,128)(2,1)S(1)}, bf16[4,64,128]{2,1,0:T(8,128)(2,1)}, u32[]{:S(2)}) copy-start(bf16[4,64,128]{2,1,0:T(8,128)(2,1)} %get-tuple-element.30) | copy-start | bytes 196612
  45.3 13.8 %copy-start.18 = (bf16[4,64,128]{2,1,0:T(8,128)(2,1)S(1)}, bf16[4,64,128]{2,1,0:T(8,128)(2,1)}, u32[]{:S(2)}) copy-start(bf16[4,64,128]{2,1,0:T(8,128)(2,1)} %get-tuple-element.31) | copy-start | bytes 196612
  45.3 15.6 %copy-start = (f32[64,64,128]{2,1,0:T(8,128)S(1)}, f32[64,64,128]{2,1,0:T(8,128)}, u32[]{:S(2)}) copy-start(f32[64,64,128]{2,1,0:T(8,128)} %control_ref.1) | copy-start | bytes 6291460
  45.3 15.5 %copy-start.2 = (bf16[2,64,4,128]{3,2,1,0:T(4,128)(2,1)S(1)}, bf16[2,64,4,128]{3,2,1,0:T(4,128)(2,1)}, u32[]{:S(2)}) copy-start(bf16[2,64,4,128]{3,2,1,0:T(4,128)(2,1)} %copy-done.1) | copy-start | bytes 393220
  45.4 15.5 %copy-start.4 = (bf16[2,64,4,128]{3,2,1,0:T(4,128)(2,1)S(1)}, bf16[2,64,4,128]{3,2,1,0:T(4,128)(2,1)}, u32[]{:S(2)}) copy-start(bf16[2,64,4,128]{3,2,1,0:T(4,128)(2,1)} %copy-done.3) | copy-start | bytes 393220
  45.4 15.5 %copy-start.9 = (f32[64,64]{1,0:T(8,128)S(1)}, f32[64,64]{1,0:T(8,128)}, u32[]{:S(2)}) copy-start(f32[64,64]{1,0:T(8,128)} %kappa_ref.7) | copy-start | bytes 49156
  45.4 15.5 %copy-start.11 = (f32[128,128]{1,0:T(8,128)S(1)}, f32[128,128]{1,0:T(8,128)}, u32[]{:S(2)}) copy-start(f32[128,128]{1,0:T(8,128)} %vertical_ref.7) | copy-start | bytes 196612
  45.4 13.3 %collective-permute-start.4 = (bf16[64,4,128]{2,1,0:T(4,128)(2,1)}, bf16[64,4,128]{2,1,0:T(4,128)(2,1)S(1)}, u32[]{:S(2)}, u32[]{:S(2)}) collective-permute-start(bf16[64,4,128]{2,1,0:T(4,128)(2,1)} %get-tuple-element.28), channel_id=1, source_target_pairs={{1,0},{2,1},{3,2},{4,3},{5,4},{6,5},{7,6},{0,7},{9,8},{10,9},{11,1... | collective-permute-start | bytes 196616 | tf_op jit(solution)/shard_map/ppermute | solution.py:573
  49.8 8.9 %collective-permute-start.5 = (bf16[64,4,128]{2,1,0:T(4,128)(2,1)}, bf16[64,4,128]{2,1,0:T(4,128)(2,1)S(1)}, u32[]{:S(2)}, u32[]{:S(2)}) collective-permute-start(bf16[64,4,128]{2,1,0:T(4,128)(2,1)} %get-tuple-element.29), channel_id=1, source_target_pairs={{0,1},{1,2},{2,3},{3,4},{4,5},{5,6},{6,7},{7,0},{8,9},{9,10},{10,1... | collective-permute-start | bytes 196616 | tf_op jit(solution)/shard_map/ppermute | solution.py:573
  51.6 19.2 %all-to-all-start.1 = ((f16[32,32,128]{2,1,0:T(8,128)(2,1)}), f16[32,32,128]{2,1,0:T(8,128)(2,1)S(1)}, u32[]{:S(2)}, u32[]{:S(2)}) async-start(f16[32,32,128]{2,1,0:T(8,128)(2,1)} %convert_element_type.24), calls=%async_computation.1 | async-start | bytes 524288 | tf_op jit(solution)/shard_map/all_to_all | solution.py:723
  58.8 9.6 %collective-permute-start.6 = (bf16[4,72,128]{2,1,0:T(8,128)(2,1)S(1)}, bf16[4,72,128]{2,1,0:T(8,128)(2,1)S(1)}, u32[]{:S(2)}, u32[]{:S(2)}) collective-permute-start(bf16[4,72,128]{2,1,0:T(8,128)(2,1)S(1)} %pad_maximum_fusion.6), channel_id=1, source_target_pairs={{0,8},{8,16},{16,24},{24,0},{1,9},{9,17},{17,25},{25,1},{2,10},{10... | collective-permute-start | bytes 221192 | tf_op jit(solution)/shard_map/ppermute | solution.py:578
  59.1 9.3 %copy-start.6 = (bf16[2,4,72,128]{3,2,1,0:T(8,128)(2,1)S(1)}, bf16[2,4,72,128]{3,2,1,0:T(8,128)(2,1)}, u32[]{:S(2)}) copy-start(bf16[2,4,72,128]{3,2,1,0:T(8,128)(2,1)} %copy-done.5) | copy-start | bytes 442372
  59.1 9.3 %copy-start.8 = (bf16[2,4,72,128]{3,2,1,0:T(8,128)(2,1)S(1)}, bf16[2,4,72,128]{3,2,1,0:T(8,128)(2,1)}, u32[]{:S(2)}) copy-start(bf16[2,4,72,128]{3,2,1,0:T(8,128)(2,1)} %copy-done.7) | copy-start | bytes 442372
  59.1 9.2 %collective-permute-start.7 = (bf16[4,72,128]{2,1,0:T(8,128)(2,1)S(1)}, bf16[4,72,128]{2,1,0:T(8,128)(2,1)S(1)}, u32[]{:S(2)}, u32[]{:S(2)}) collective-permute-start(bf16[4,72,128]{2,1,0:T(8,128)(2,1)S(1)} %pad_maximum_fusion.7), channel_id=1, source_target_pairs={{8,0},{16,8},{24,16},{0,24},{9,1},{17,9},{25,17},{1,25},{10,2},{18... | collective-permute-start | bytes 221192 | tf_op jit(solution)/shard_map/ppermute | solution.py:578
  60.9 1.6 %copy-start.10 = (f32[64,64,128]{2,1,0:T(8,128)S(1)}, f32[64,64,128]{2,1,0:T(8,128)}, u32[]{:S(2)}) copy-start(f32[64,64,128]{2,1,0:T(8,128)} %get-tuple-element.24.adj_ref) | copy-start | bytes 6291460
  68.3 2.6 %copy-start.13 = (f32[64,64]{1,0:T(8,128)S(1)}, f32[64,64]{1,0:T(8,128)}, u32[]{:S(2)}) copy-start(f32[64,64]{1,0:T(8,128)} %rinv_ref.3) | copy-start | bytes 49156

commit v4 on v3

--- a/solution.py
+++ b/solution.py
@@ -15,12 +15,28 @@
 INNOV_STEP = INNOV_MAX / 32767.0
 WEIGHT_MAX = 4.0
 WEIGHT_STEP = WEIGHT_MAX / 65535.0
+CODE_FLOOR = -15.0
+CODE_STEPS = 1056.0
 
 
 def split_hi_lo(value):
     high = value.astype(BF16)
     low = (value - high.astype(F32)).astype(BF16)
     return high, low
+
+
+def encode(value):
+    size = jnp.maximum(jnp.abs(value), 2.0**CODE_FLOOR)
+    level = (jnp.log2(size) - CODE_FLOOR) * CODE_STEPS + 0.5
+    code = jnp.minimum(level, 32767.0).astype(I32)
+    return jnp.where(value < 0.0, code + 32768, code)
+
+
+def decode(code):
+    level = code & 32767
+    size = jnp.exp2(level.astype(F32) * (1.0 / CODE_STEPS) + CODE_FLOOR)
+    size = jnp.where(level == 0, 0.0, size)
+    return jnp.where(code >= 32768, -size, size)
 
 
 def iota(shape, dim):
@@ -65,9 +81,17 @@
 
 
 def address_kernel(
-    devices_all, quarter, count_ref, owner_ref, cell_ref, scale_ref, innov_ref, out_ref, key_ref,
-    word_ref,
+    devices_all, quarter, count_ref, owner_ref, cell_ref, scale_ref, innov_ref, kappa_ref,
+    control_hbm, out_ref, key_ref, top_ref, bottom_ref, word_ref, ends_ref, sem_ref,
 ):
+    grid_rows = control_hbm.shape[0]
+    ends_in = start_copies(
+        [
+            (control_hbm.at[pl.ds(0, NSTEP)], ends_ref.at[0]),
+            (control_hbm.at[pl.ds(grid_rows - NSTEP, NSTEP)], ends_ref.at[1]),
+        ],
+        sem_ref,
+    )
     obs = owner_ref.shape[1]
     rows_half = devices_all * quarter
     rows = 2 * rows_half
@@ -107,7 +131,7 @@
     n = devices_all
     cells = table[:n] * 64 + table[n : 2 * n]
     weights = table[2 * n : 3 * n] * 256 + table[3 * n :]
-    out_ref[:, quarter, :] = (cells << 16) | weights
+    meta = (cells << 16) | weights
 
     level = jnp.floor(
         jnp.clip(innov_ref[...], -INNOV_MAX, INNOV_MAX) * (1.0 / INNOV_STEP) + 0.5
@@ -130,13 +154,14 @@
             total.append(jnp.where(left_lane, found[0], found[1]).astype(I32))
         word_ref[base : base + chunk, :] = (total[0] << 16) | (total[1] & 0xFFFF)
     for device in range(devices_all):
-        out_ref[device, :quarter, :] = word_ref[device * quarter : (device + 1) * quarter, :]
-
-
-def put_row_block(wide_ref, at, count, tile, east, west):
-    cols = tile.shape[1]
-    wide_ref[at : at + count, :cols, :] = tile
-    put_sides(wide_ref, at, count, cols, east, west)
+        at = device * (quarter + 1)
+        out_ref[at : at + quarter, :] = word_ref[device * quarter : (device + 1) * quarter, :]
+        out_ref[at + quarter : at + quarter + 1, :] = meta[device : device + 1]
+    top_ref[1] = spread_kappa(kappa_ref[:NSTEP, :]).astype(BF16)
+    bottom_ref[1] = spread_kappa(kappa_ref[grid_rows - NSTEP :, :]).astype(BF16)
+    wait_copies(ends_in)
+    top_ref[0] = ends_ref[0].astype(BF16)
+    bottom_ref[0] = ends_ref[1].astype(BF16)
 
 
 def put_sides(wide_ref, at, count, cols, east, west):
@@ -144,14 +169,33 @@
     wide_ref[at : at + count, cols + NSTEP :, :] = west.astype(F32)
 
 
-def spread_kappa(kappa):
+def spread_kappa(kappa, low=0, high=None):
     rows, cols = kappa.shape
-    high, low = split_hi_lo(kappa)
-    pair = jnp.concatenate([high.astype(F32), low.astype(F32)], axis=1)
-    hot = iota((rows, cols, 2 * cols), 1) == iota((rows, cols, 2 * cols), 2) % cols
+    count = (cols if high is None else high) - low
+    top, rest = split_hi_lo(kappa)
+    pair = jnp.concatenate([top.astype(F32), rest.astype(F32)], axis=1)
+    shape = (rows, count, 2 * cols)
+    hot = iota(shape, 1) + low == iota(shape, 2) % cols
     spread = jnp.where(hot, pair[:, None, :], 0.0).astype(BF16)
     ones = jnp.ones((2 * cols, 128), BF16)
-    return dot_f32(spread.reshape(rows * cols, 2 * cols), ones).reshape(rows, cols, 128)
+    return dot_f32(spread.reshape(rows * count, 2 * cols), ones).reshape(rows, count, 128)
+
+
+def pack_kernel(control_hbm, kappa_ref, near_ref, far_ref, left_ref, right_ref, sem_ref):
+    cols = control_hbm.shape[1]
+    copies = start_copies(
+        [
+            (control_hbm.at[:, pl.ds(0, 8)], left_ref),
+            (control_hbm.at[:, pl.ds(cols - 8, 8)], right_ref),
+        ],
+        sem_ref,
+    )
+    kappa = kappa_ref[...]
+    near_ref[1] = spread_kappa(kappa, 0, 8)[:, :NSTEP].astype(BF16)
+    far_ref[1] = spread_kappa(kappa, cols - 8, cols)[:, 8 - NSTEP :].astype(BF16)
+    wait_copies(copies)
+    near_ref[0] = left_ref[:, :NSTEP].astype(BF16)
+    far_ref[0] = right_ref[:, 8 - NSTEP :].astype(BF16)
 
 
 def sweep_rows(source, target, kap_ref, low, high, block=8):
@@ -202,17 +246,16 @@
     return jnp.concatenate([pair, pair], axis=0)
 
 
-def project_rows(rows, dev, mixing, pick):
+def project_rows(rows, dev, mixing):
     count, cols, levels = rows.shape
     pair = jnp.concatenate(split_hi_lo(rows.reshape(count * cols, levels)), axis=1)
     both = dot_f32(pair, mixing)
     state = both[:, :levels] + both[:, levels:]
     prof = (dev.reshape(count * cols, levels) * state).astype(BF16)
     prof = prof.reshape(count // 4, 4, cols, levels)
-    wide = jnp.concatenate(
+    return jnp.concatenate(
         [prof[:, part].reshape(count // 4 * cols, levels) for part in range(4)], axis=1
     )
-    return jnp.concatenate(split_hi_lo(dot_f32(wide, pick)), axis=1)
 
 
 def forward_kernel(
@@ -235,14 +278,13 @@
     hot = (iota((table_rows, channels), 0) == choice_ref[...]).astype(F32).astype(BF16)
     fill_picked(pick_ref, dot_tn(hot, table_ref[...]).astype(BF16))
     mixing = forward_mixing(vertical_ref[...])
-    pick = jnp.transpose(pick_ref[...].astype(F32)).astype(BF16)
     copies = start_copies([(pick_ref, pick_hbm)], sem_ref)
     count = 8
     for index in range((rows - 2 * NSTEP) // count):
         row = NSTEP + index * count
         where = pl.ds(row // 4 * cols, count // 4 * cols)
         out_ref[where, :] = project_rows(
-            done[row : row + count, :cols, :], sigma_ref[row : row + count], mixing, pick
+            done[row : row + count, :cols, :], sigma_ref[row : row + count], mixing
         )
         copies += start_copies([(out_ref.at[where], out_hbm.at[where])], sem_ref, index + 1)
     wait_copies(copies)
@@ -254,41 +296,49 @@
     return jnp.where(at > 0, 1.0, 0.0), jnp.where(at < last, 1.0, 0.0)
 
 
-def put_rims(wide_ref, tile_of, east_of, west_of, north, south, flags, rows):
+def put_rims(wide_ref, east_of, west_of, north, south, flags, rows, cols):
     span = 2 * NSTEP
     wide_ref[:NSTEP] = north.astype(F32) * flags[0]
-    put_row_block(wide_ref, NSTEP, span, tile_of(0, span), east_of(0, span), west_of(0, span))
-    put_row_block(
-        wide_ref, 3 * NSTEP, span, tile_of(rows - span, rows), east_of(rows - span, rows),
-        west_of(rows - span, rows),
-    )
-    wide_ref[5 * NSTEP :] = south.astype(F32) * flags[1]
+    put_sides(wide_ref, NSTEP, span, cols, east_of(0, span), west_of(0, span))
+    put_sides(
+        wide_ref, NSTEP + span, span, cols, east_of(rows - span, rows), west_of(rows - span, rows)
+    )
+    wide_ref[NSTEP + 2 * span :] = south.astype(F32) * flags[1]
+
+
+def rim_tiles(hbm, wide_ref):
+    span = 2 * NSTEP
+    rows, cols, _ = hbm.shape
+    return [
+        (hbm.at[pl.ds(0, span)], wide_ref.at[pl.ds(NSTEP, span), pl.ds(0, cols)]),
+        (hbm.at[pl.ds(rows - span, span)], wide_ref.at[pl.ds(NSTEP + span, span), pl.ds(0, cols)]),
+    ]
 
 
 def put_rim_kappa(kap_ref, kappa_ref, east_ref, west_ref, north_ref, south_ref, flags):
-    rows = kappa_ref.shape[0]
+    rows, cols = kappa_ref.shape
     span = 2 * NSTEP
-    spread = spread_kappa(
+    kap_ref[NSTEP : NSTEP + 2 * span, :cols, :] = spread_kappa(
         jnp.concatenate([kappa_ref[:span, :], kappa_ref[rows - span :, :]], axis=0)
     )
     put_rims(
         kap_ref,
-        lambda low, high: spread[:span] if low == 0 else spread[span:],
         lambda low, high: east_ref[1, low:high],
         lambda low, high: west_ref[1, low:high],
         north_ref[1],
         south_ref[1],
         flags,
         rows,
+        cols,
     )
 
 
 def owner_kernel(
     devices_all, quarter, recv_hbm, evolved_hbm, pick_hbm, sigma_hbm, control_hbm, rinv_ref,
     east_ref, west_ref, north_ref, south_ref, kappa_ref, vertical_ref,
-    ret_ref, adj_hbm, left_hbm, right_hbm, top_hbm, bottom_hbm,
+    ret_hbm, adj_hbm, left_hbm, right_hbm, top_hbm, bottom_hbm,
     word_ref, dep_ref, acc_ref, first_ref, second_ref, kap_ref, table_ref, pair_ref,
-    recv_ref, pick_ref, sigma_ref, ends_ref, adj_ref, left_ref, right_ref, top_ref, bottom_ref,
+    recv_ref, ret_ref, pick_ref, sigma_ref, adj_ref, left_ref, right_ref, top_ref, bottom_ref,
     sem_ref,
 ):
     lat_rows, cols, levels = sigma_hbm.shape
@@ -296,39 +346,38 @@
     flags = pole_flags()
     span = 2 * NSTEP
     inside = pl.ds(cols, cells_part - 2 * cols)
-    control_in = start_copies(
-        [
-            (control_hbm.at[pl.ds(0, span)], ends_ref.at[0]),
-            (control_hbm.at[pl.ds(lat_rows - span, span)], ends_ref.at[1]),
-        ],
+    control_in = start_copies(rim_tiles(control_hbm, first_ref), sem_ref)
+    ends_at = (pl.ds(0, NSTEP), pl.ds(lat_rows - NSTEP, NSTEP))
+    ends_in = start_copies(
+        [(sigma_hbm.at[at], sigma_ref.at[at]) for at in ends_at] + [(pick_hbm, pick_ref)],
         sem_ref,
-    )
-    sigma_in = start_copies([(sigma_hbm, sigma_ref), (pick_hbm, pick_ref)], sem_ref, 2)
+        2,
+    )
     others_in = start_copies(
-        [(recv_hbm, recv_ref), (evolved_hbm.at[inside], table_ref.at[inside])], sem_ref, 4
-    )
+        [(recv_hbm, recv_ref), (evolved_hbm.at[inside], table_ref.at[inside])], sem_ref, 5
+    )
+    rest = pl.ds(NSTEP, lat_rows - 2 * NSTEP)
+    sigma_in = start_copies([(sigma_hbm.at[rest], sigma_ref.at[rest])], sem_ref, 7)
     put_rim_kappa(kap_ref, kappa_ref, east_ref, west_ref, north_ref, south_ref, flags)
-    wait_copies(control_in)
     put_rims(
         first_ref,
-        lambda low, high: ends_ref[0] if low == 0 else ends_ref[1],
         lambda low, high: east_ref[0, low:high],
         lambda low, high: west_ref[0, low:high],
         north_ref[0],
         south_ref[0],
         flags,
         lat_rows,
-    )
+        cols,
+    )
+    wait_copies(control_in)
     done = sweeps(first_ref, second_ref, kap_ref, 6 * NSTEP)
-    wait_copies(sigma_in)
-    pick = jnp.transpose(pick_ref[...].astype(F32)).astype(BF16)
+    wait_copies(ends_in)
     ends = project_rows(
         jnp.concatenate(
             [done[NSTEP : 2 * NSTEP, :cols, :], done[4 * NSTEP : 5 * NSTEP, :cols, :]], axis=0
         ),
         jnp.concatenate([sigma_ref[:NSTEP], sigma_ref[lat_rows - NSTEP :]], axis=0),
         forward_mixing(vertical_ref[...]),
-        pick,
     )
     table_ref[:cols, :] = ends[:cols]
     table_ref[cells_part - cols :, :] = ends[cols:]
@@ -336,9 +385,12 @@
     wait_copies(others_in)
     rows_half = devices_all * quarter
     rows = 2 * rows_half
+    metas = []
     for device in range(devices_all):
-        word_ref[device * quarter : (device + 1) * quarter, :] = recv_ref[device, :quarter, :]
-    meta = recv_ref[:, quarter, :]
+        at = device * (quarter + 1)
+        word_ref[device * quarter : (device + 1) * quarter, :] = recv_ref[at : at + quarter, :]
+        metas.append(recv_ref[at + quarter : at + quarter + 1, :])
+    meta = jnp.concatenate(metas, axis=0)
     cells, weights = meta >> 16, meta & 0xFFFF
     facts = jnp.concatenate(
         [
@@ -356,6 +408,9 @@
     mixing = jnp.concatenate(
         [jnp.concatenate([high, low], axis=1), jnp.concatenate([high, zero], axis=1)], axis=0
     )
+    pick_pair = jnp.transpose(
+        pick_ref[: 2 * channels, : 2 * levels].astype(F32)
+    ).astype(BF16)
     acc_ref[...] = jnp.zeros_like(acc_ref)
     chunk = min(512, rows_half)
     left_lane = iota((chunk, 128), 1) < 64
@@ -382,22 +437,20 @@
             inside = (lat >> 2) * cols + lon
             hot = (iota((chunk, cells_part), 1) == inside).astype(F32).astype(BF16)
             got = dot_f32(hot, table_ref[...])
-            got = got[:, :256] + got[:, 256:]
-            lanes = jnp.where(part >= 2, got[:, 128:], got[:, :128])
-            swapped = pltpu.roll(lanes, 64, 1)
-            odd = (part & 1) == 1
-            values.append(
-                jnp.where(odd, swapped, lanes) if side == 0 else jnp.where(odd, lanes, swapped)
+            low_parts = jnp.where(part == 0, got[:, :levels], got[:, levels : 2 * levels])
+            high_parts = jnp.where(
+                part == 2, got[:, 2 * levels : 3 * levels], got[:, 3 * levels :]
             )
+            values.append(jnp.where(part < 2, low_parts, high_parts).astype(BF16))
             hots.append(hot)
             parts.append(part)
-        evolved = jnp.where(left_lane, values[0], values[1])
+        evolved = dot_f32(jnp.concatenate(values, axis=1), pick_pair)
         words = word_ref[base : base + chunk, :]
         words = (words if half == 0 else words << 16) >> 16
         gap = evolved - words.astype(F32) * INNOV_STEP
         both = dot_f32(jnp.concatenate(split_hi_lo(gap), axis=1), mixing)
         dep = (both[:, :128] + both[:, 128:]) * jnp.where(left_lane, weight[0], weight[1])
-        dep_ref[step * chunk : (step + 1) * chunk, :] = evolved
+        dep_ref[step * chunk : (step + 1) * chunk, :] = encode(evolved)
         rounded = dep.astype(BF16).astype(F32)
         swapped = pltpu.roll(rounded, 64, 1)
         for side in range(2):
@@ -414,15 +467,11 @@
                 axis=1,
             )
             acc_ref[...] += dot_tn(hots[side], wide)
-    for half in range(2):
-        for device in range(devices_all):
-            at = half * rows_half + device * quarter
-            ret_ref[device, half * quarter : (half + 1) * quarter, :] = dep_ref[
-                at : at + quarter, :
-            ]
+    ret_ref[...] = (dep_ref[:rows_half, :] << 16) | dep_ref[rows_half:, :]
+    copies = start_copies([(ret_ref, ret_hbm)], sem_ref)
+    wait_copies(sigma_in)
     groups = 4
     count = groups * 4
-    copies = []
     for step in range(lat_rows // count):
         high, low = split_hi_lo(acc_ref[step * groups * cols : (step + 1) * groups * cols, :])
         both = dot_f32(high, pick_ref[...]) + dot_f32(low, pick_ref[...])
@@ -440,7 +489,7 @@
                 if at >= lat_rows - NSTEP:
                     bottom_ref[at - (lat_rows - NSTEP)] = value.astype(BF16)
         where = pl.ds(step * count, count)
-        copies += start_copies([(adj_ref.at[where], adj_hbm.at[where])], sem_ref, step)
+        copies += start_copies([(adj_ref.at[where], adj_hbm.at[where])], sem_ref, step + 1)
     copies += start_copies(
         [
             (left_ref, left_hbm),
@@ -449,7 +498,7 @@
             (bottom_ref, bottom_hbm),
         ],
         sem_ref,
-        lat_rows // count,
+        lat_rows // count + 1,
     )
     wait_copies(copies)
 
@@ -469,15 +518,20 @@
 
 
 def inner_kernel(
-    adj_ref, east_ref, west_ref, kappa_ref, keast_ref, kwest_ref, vertical_ref, control_ref,
-    out_hbm, first_ref, second_ref, kap_ref, out_ref, sem_ref,
+    adj_hbm, control_hbm, east_ref, west_ref, kappa_ref, keast_ref, kwest_ref, vertical_ref,
+    out_hbm, first_ref, second_ref, kap_ref, out_ref, control_ref, sem_ref,
 ):
-    rows, cols, levels = control_ref.shape
-    put_row_block(kap_ref, 0, rows, spread_kappa(kappa_ref[...]), keast_ref[1], kwest_ref[1])
-    put_row_block(first_ref, 0, rows, adj_ref[...], east_ref[...], west_ref[...])
+    rows, cols, levels = control_hbm.shape
+    tile_in = start_copies([(adj_hbm, first_ref.at[pl.ds(0, rows), pl.ds(0, cols)])], sem_ref)
+    control_in = start_copies([(control_hbm, control_ref)], sem_ref, 1)
+    kap_ref[:rows, :cols, :] = spread_kappa(kappa_ref[...])
+    put_sides(kap_ref, 0, rows, cols, keast_ref[1], kwest_ref[1])
+    put_sides(first_ref, 0, rows, cols, east_ref[...], west_ref[...])
+    wait_copies(tile_in)
     first_ref[:rows] = first_ref[:rows] * kap_ref[:rows]
     done = sweeps(first_ref, second_ref, kap_ref, rows)
     mixing = backward_mixing(vertical_ref[...])
+    wait_copies(control_in)
     count = 8
     copies = []
     for index in range((rows - 2 * NSTEP) // count):
@@ -491,42 +545,49 @@
 
 
 def rim_kernel(
-    adj_ref, east_ref, west_ref, north_ref, south_ref, kappa_ref, keast_ref, kwest_ref,
-    knorth_ref, ksouth_ref, vertical_ref, control_ref, inner_ref, out_ref,
-    first_ref, second_ref, kap_ref, edge_ref, sem_ref,
+    adj_hbm, control_hbm, east_ref, west_ref, north_ref, south_ref, kappa_ref, keast_ref,
+    kwest_ref, knorth_ref, ksouth_ref, vertical_ref, inner_ref, out_ref,
+    first_ref, second_ref, kap_ref, edge_ref, control_ref, sem_ref,
 ):
     del inner_ref
-    span = 2 * NSTEP
     lat_rows, cols = kappa_ref.shape
-    levels = vertical_ref.shape[0]
     flags = pole_flags()
+    tile_in = start_copies(rim_tiles(adj_hbm, first_ref), sem_ref)
+    starts = (0, lat_rows - NSTEP)
+    control_in = start_copies(
+        [(control_hbm.at[pl.ds(at, NSTEP)], control_ref.at[i]) for i, at in enumerate(starts)],
+        sem_ref,
+        2,
+    )
     put_rim_kappa(kap_ref, kappa_ref, keast_ref, kwest_ref, knorth_ref, ksouth_ref, flags)
     put_rims(
         first_ref,
-        lambda low, high: adj_ref[0] if low == 0 else adj_ref[1],
         lambda low, high: east_ref[low:high],
         lambda low, high: west_ref[low:high],
         north_ref[...],
         south_ref[...],
         flags,
         lat_rows,
-    )
+        cols,
+    )
+    wait_copies(tile_in)
     first_ref[...] = first_ref[...] * kap_ref[...]
     done = sweeps(first_ref, second_ref, kap_ref, 6 * NSTEP)
     mixing = backward_mixing(vertical_ref[...])
+    wait_copies(control_in)
+    copies = []
     for end in range(2):
         at = pl.ds((1 + 3 * end) * NSTEP, NSTEP)
         back = finish_rows(done[at, :cols, :], kap_ref[at, :cols, :], mixing)
         edge_ref[end] = control_ref[end] + back
-    copies = []
-    for end in range(2):
-        copy = pltpu.make_async_copy(
-            edge_ref.at[end], out_ref.at[pl.ds(end * (lat_rows - NSTEP), NSTEP)], sem_ref.at[end]
+        copies += start_copies(
+            [(edge_ref.at[end], out_ref.at[pl.ds(starts[end], NSTEP)])], sem_ref, 4 + end
         )
-        copy.start()
-        copies.append(copy)
-    for copy in copies:
-        copy.wait()
+    wait_copies(copies)
+
+
+def pass_kernel(array_hbm, first_hbm, second_hbm, out_hbm):
+    del array_hbm, first_hbm, second_hbm, out_hbm
 
 
 def return_kernel(
@@ -536,12 +597,12 @@
     rows_half = devices_all * quarter
     rows = 2 * rows_half
     channels, obs = out_ref.shape
+    words = recv_ref[...]
     for half in range(2):
-        for device in range(devices_all):
-            at = half * rows_half + device * quarter
-            high, low = split_hi_lo(recv_ref[device, half * quarter : (half + 1) * quarter, :])
-            pair_ref[at : at + quarter, :128] = high
-            pair_ref[at : at + quarter, 128:] = low
+        code = (words >> 16) & 0xFFFF if half == 0 else words & 0xFFFF
+        high, low = split_hi_lo(decode(code))
+        pair_ref[half * rows_half : (half + 1) * rows_half, :128] = high
+        pair_ref[half * rows_half : (half + 1) * rows_half, 128:] = low
     scale = scale_ref[...]
     valid = iota((1, obs), 1) < count_ref[0]
     weight = jnp.where(valid, 1.0 / (scale * scale), 0.0)
@@ -606,32 +667,40 @@
     columns = lat_rows * lon_cols
     wide = (lat_rows + 1, lon_cols + 2 * NSTEP, levels)
     rim = (6 * NSTEP, lon_cols + 2 * NSTEP, levels)
-    span = 2 * NSTEP
     smem = pl.BlockSpec(memory_space=pltpu.SMEM)
     anywhere = pl.BlockSpec(memory_space=pl.ANY)
 
-    def side_of(low, high):
-        edge = kappa[:, low:high, None]
-        return jnp.stack(
-            [
-                control[:, low:high].astype(BF16),
-                jnp.broadcast_to(edge.astype(BF16), (lat_rows, high - low, levels)),
-            ]
-        )
-
-    near, far = side_of(0, NSTEP), side_of(lon_cols - NSTEP, lon_cols)
+    near, far = pl.pallas_call(
+        pack_kernel,
+        out_shape=(jax.ShapeDtypeStruct((2, lat_rows, NSTEP, levels), BF16),) * 2,
+        in_specs=[HBM_SPEC] + vmem_specs(1),
+        out_specs=tuple(vmem_specs(2)),
+        scratch_shapes=[
+            pltpu.VMEM((lat_rows, 8, levels), F32),
+            pltpu.VMEM((lat_rows, 8, levels), F32),
+            pltpu.SemaphoreType.DMA((2,)),
+        ],
+        compiler_params=params(58),
+        name="pack",
+    )(control, kappa)
     near, far, obs_cell = lax.optimization_barrier((near, far, obs_cell))
     east, west = exchange_sides(near, far)
 
-    payload, key = pl.pallas_call(
+    payload, key, top, bottom = pl.pallas_call(
         functools.partial(address_kernel, devices_all, quarter),
         out_shape=(
-            jax.ShapeDtypeStruct((devices_all, quarter + 1, 128), I32),
+            jax.ShapeDtypeStruct((devices_all * (quarter + 1), 128), I32),
             jax.ShapeDtypeStruct((1, obs_slots), I32),
+            jax.ShapeDtypeStruct((2, NSTEP, lon_cols, levels), BF16),
+            jax.ShapeDtypeStruct((2, NSTEP, lon_cols, levels), BF16),
         ),
-        in_specs=[smem] + vmem_specs(4),
-        out_specs=tuple(vmem_specs(2)),
-        scratch_shapes=[pltpu.VMEM((rows_half, 128), I32)],
+        in_specs=[smem] + vmem_specs(5) + [HBM_SPEC],
+        out_specs=tuple(vmem_specs(4)),
+        scratch_shapes=[
+            pltpu.VMEM((rows_half, 128), I32),
+            pltpu.VMEM((2, NSTEP, lon_cols, levels), F32),
+            pltpu.SemaphoreType.DMA((2,)),
+        ],
         compiler_params=params(10),
         cost_estimate=estimate(2_000_000_000, 8_000_000),
         name="address",
@@ -641,21 +710,23 @@
         obs_cell.reshape(1, obs_slots),
         error_scale.reshape(1, obs_slots),
         innovations.T,
-    )
-    received = lax.all_to_all(payload, ("lat", "lon"), split_axis=0, concat_axis=0, tiled=True)
-
-    def rim_of(low, high):
-        tile = jnp.stack(
-            [
-                control[low:high].astype(BF16),
-                jnp.broadcast_to(
-                    kappa[low:high, :, None].astype(BF16), (high - low, lon_cols, levels)
-                ),
-            ]
-        )
+        kappa,
+        control,
+    )
+    received = lax.all_to_all(
+        payload.reshape(devices_all, 1, (quarter + 1) * 128),
+        ("lat", "lon"),
+        split_axis=0,
+        concat_axis=0,
+        tiled=True,
+    ).reshape(payload.shape)
+
+    def with_sides(tile, low, high):
         return jnp.concatenate([tile, east[:, low:high], west[:, low:high]], axis=2)
 
-    north, south = exchange_rims(rim_of(0, NSTEP), rim_of(lat_rows - NSTEP, lat_rows))
+    north, south = exchange_rims(
+        with_sides(top, 0, NSTEP), with_sides(bottom, lat_rows - NSTEP, lat_rows)
+    )
 
     evolved, picked = pl.pallas_call(
         forward_kernel,
@@ -680,10 +751,10 @@
         channel_pick.reshape(1, channels),
     )
 
-    returned, adjoint, left, right, top, bottom = pl.pallas_call(
+    returned, adjoint, left, right, atop, abottom = pl.pallas_call(
         functools.partial(owner_kernel, devices_all, quarter),
         out_shape=(
-            jax.ShapeDtypeStruct((devices_all, 2 * quarter, 128), F32),
+            jax.ShapeDtypeStruct((rows_half, 128), I32),
             jax.ShapeDtypeStruct(control.shape, F32),
             jax.ShapeDtypeStruct((lat_rows, NSTEP, levels), BF16),
             jax.ShapeDtypeStruct((lat_rows, NSTEP, levels), BF16),
@@ -691,26 +762,26 @@
             jax.ShapeDtypeStruct((NSTEP, lon_cols, levels), BF16),
         ),
         in_specs=[HBM_SPEC] * 5 + vmem_specs(7),
-        out_specs=tuple(vmem_specs(1) + [HBM_SPEC] * 5),
+        out_specs=(HBM_SPEC,) * 6,
         scratch_shapes=[
             pltpu.VMEM((rows_half, 128), I32),
-            pltpu.VMEM((2 * rows_half, 128), F32),
+            pltpu.VMEM((2 * rows_half, 128), I32),
             pltpu.VMEM((columns // 4, 4 * channels), F32),
             pltpu.VMEM(rim, F32),
             pltpu.VMEM(rim, F32),
             pltpu.VMEM(rim, F32),
             pltpu.VMEM((columns // 4, 8 * channels), BF16),
             pltpu.VMEM((2 * channels, 2 * channels), F32),
-            pltpu.VMEM((devices_all, quarter + 1, 128), I32),
+            pltpu.VMEM((devices_all * (quarter + 1), 128), I32),
+            pltpu.VMEM((rows_half, 128), I32),
             pltpu.VMEM((4 * channels, 4 * levels), BF16),
             pltpu.VMEM(control.shape, F32),
-            pltpu.VMEM((2, span, lon_cols, levels), F32),
             pltpu.VMEM(control.shape, F32),
             pltpu.VMEM((lat_rows, NSTEP, levels), BF16),
             pltpu.VMEM((lat_rows, NSTEP, levels), BF16),
             pltpu.VMEM((NSTEP, lon_cols, levels), BF16),
             pltpu.VMEM((NSTEP, lon_cols, levels), BF16),
-            pltpu.SemaphoreType.DMA((lat_rows // 16 + 4,)),
+            pltpu.SemaphoreType.DMA((max(8, lat_rows // 16 + 5),)),
         ],
         compiler_params=params(58),
         cost_estimate=estimate(4_000_000_000, 16_000_000),
@@ -719,48 +790,59 @@
         received, evolved, picked, sigma, control, r_inverse, east, west, north, south, kappa,
         vertical,
     )
-    left, right, returned = lax.optimization_barrier((left, right, returned))
+    returned = pl.pallas_call(
+        pass_kernel,
+        out_shape=jax.ShapeDtypeStruct(returned.shape, I32),
+        in_specs=[anywhere] * 3,
+        out_specs=anywhere,
+        input_output_aliases={0: 0},
+        cost_estimate=estimate(1_000_000, 1_000_000),
+        name="pass",
+    )(returned, left, right)
     home = lax.all_to_all(
-        returned.astype(jnp.float16), ("lat", "lon"), split_axis=0, concat_axis=0, tiled=True
-    )
+        returned.reshape(devices_all, quarter, 128),
+        ("lat", "lon"),
+        split_axis=0,
+        concat_axis=0,
+        tiled=True,
+    ).reshape(returned.shape)
 
     aeast, awest = exchange_sides(left, right)
     anorth, asouth = exchange_rims(
-        jnp.concatenate([top, aeast[:NSTEP], awest[:NSTEP]], axis=1),
-        jnp.concatenate([bottom, aeast[-NSTEP:], awest[-NSTEP:]], axis=1),
+        jnp.concatenate([atop, aeast[:NSTEP], awest[:NSTEP]], axis=1),
+        jnp.concatenate([abottom, aeast[-NSTEP:], awest[-NSTEP:]], axis=1),
     )
     inner = pl.pallas_call(
         inner_kernel,
         out_shape=jax.ShapeDtypeStruct(control.shape, F32),
-        in_specs=vmem_specs(8),
+        in_specs=[HBM_SPEC] * 2 + vmem_specs(6),
         out_specs=HBM_SPEC,
         scratch_shapes=[pltpu.VMEM(wide, F32)] * 3
-        + [pltpu.VMEM(control.shape, F32), pltpu.SemaphoreType.DMA((lat_rows // 8,))],
+        + [pltpu.VMEM(control.shape, F32)] * 2
+        + [pltpu.SemaphoreType.DMA((lat_rows // 8,))],
         compiler_params=params(20),
         cost_estimate=estimate(4_000_000_000, 16_000_000),
         name="inner",
-    )(adjoint, aeast, awest, kappa, east, west, vertical, control)
-
-    def ends(field, width):
-        return jnp.stack([field[:width], field[lat_rows - width :]])
+    )(adjoint, control, aeast, awest, kappa, east, west, vertical)
 
     gradient = pl.pallas_call(
         rim_kernel,
         out_shape=jax.ShapeDtypeStruct(control.shape, F32),
-        in_specs=vmem_specs(12) + [anywhere],
+        in_specs=[HBM_SPEC] * 2 + vmem_specs(10) + [anywhere],
         out_specs=anywhere,
         scratch_shapes=[pltpu.VMEM(rim, F32)] * 3
         + [
             pltpu.VMEM((2, NSTEP, lon_cols, levels), F32),
-            pltpu.SemaphoreType.DMA((2,)),
+            pltpu.VMEM((2, NSTEP, lon_cols, levels), F32),
+            pltpu.SemaphoreType.DMA((6,)),
         ],
         input_output_aliases={12: 0},
         compiler_params=params(12),
         cost_estimate=estimate(1_000_000_000, 2_000_000),
         name="rims",
     )(
-        ends(adjoint, span), aeast, awest, anorth, asouth, kappa, east, west, north, south,
-        vertical, ends(control, NSTEP), inner,
+        adjoint, control, aeast, awest, anorth, asouth, kappa, east, west, north, south, vertical,
+        inner,
     )
 
     departures = pl.pallas_call(
@@ -773,7 +855,7 @@
         cost_estimate=estimate(500_000_000, 2_000_000),
         name="give_back",
     )(
-        obs_count, home.astype(F32), key, innovations.T, error_scale.reshape(1, obs_slots),
+        obs_count, home, key, innovations.T, error_scale.reshape(1, obs_slots),
         r_inverse,
     )
     return (gradient, departures.T)

time: 73.5 us -> 70.5 us (0.959)
  other arithmetic: 4.72 us -> 1.74 us
  waiting for transfers between devices: 0.3 us -> 3.12 us
  local copies, waits for them, and re-layouts: 6.08 us -> 3.34 us
  Pallas kernels: 33.5 us -> 35.9 us
  starting transfers between devices: 26.6 us -> 24.3 us
    another operation x8 -> x0, local copies, waits for them, and re-layouts: 3.55 us -> none  [the longest x2 2.06 us: ends(): return jnp.stack([field[:width], field[lat_rows - width:]])]
    another operation x5 -> x0, other arithmetic: 2.81 us -> none
    pallas_call x0 -> x2, Pallas kernels: none -> 2.69 us  [the longest x1 2.69 us: body(): pl.pallas_call(pack_kernel, out_shape=(jax.ShapeDtypeStruct((2, lat_rows,...]
    convert_element_type x2 -> x0, other arithmetic: 1.84 us -> none  [the longest x1 1.79 us: body(): returned.astype(jnp.float16)]
    concatenate x4, other arithmetic: 0.06 us -> 1.74 us  [the longest x1 0.86 us: body(): jnp.concatenate([atop, aeast[:NSTEP], awest[:NSTEP]], axis=1)]
    ppermute x2, waiting for transfers between devices: 0.01 us -> 1.55 us  [exchange_sides(): lax.ppermute(right, 'lon', forward)]
    ppermute x2, starting transfers between devices: 10.4 us -> 9.09 us  [exchange_sides(): lax.ppermute(left, 'lon', backward)]
    all_to_all x2, waiting for transfers between devices: 0.28 us -> 1.56 us  [the longest x1 1.55 us: body(): lax.all_to_all(payload.reshape(devices_all, 1, (quarter + 1) * 128), ('la...]
  transfers between devices with their start and end apart: 10 -> 10, of which waited for: 1 -> 2; matrix products, arithmetic and copies ran while one was open for 7% -> 3% of each run, Pallas kernels for 27% -> 28%
where the time goes in v4:
time: 70.5 us; the launch traced here: 70.1 us
  Pallas kernels  35.9 us (51%)
  starting transfers between devices  24.3 us (34%)
  local copies, waits for them, and re-layouts  3.34 us (5%)
  waiting for transfers between devices  3.12 us (4%)
  other arithmetic  1.74 us (2%)
  between operations  1.69 us (2%)
    pallas_call x1, Pallas kernels, body(): pl.pallas_call(functools.partial(owner_kernel, devices_all, quarter), out...  11.2 us
    ppermute x2, starting transfers between devices, exchange_sides(): lax.ppermute(left, 'lon', backward)  9.09 us
    pallas_call x1, Pallas kernels, body(): pl.pallas_call(forward_kernel, out_shape=(jax.ShapeDtypeStruct((columns /...  7.71 us
    pallas_call x1, Pallas kernels, body(): pl.pallas_call(inner_kernel, out_shape=jax.ShapeDtypeStruct(control.shape...  6.43 us
    all_to_all x1, starting transfers between devices, body(): lax.all_to_all(payload.reshape(devices_all, 1, (quarter + 1) * 128), ('la...  6.02 us
    all_to_all x1, starting transfers between devices, body(): lax.all_to_all(returned.reshape(devices_all, quarter, 128), ('lat', 'lon'...  5.67 us
    ppermute x2, starting transfers between devices, exchange_rims(): lax.ppermute(top, 'lat', backward)  3.35 us
    unnamed x42, local copies, waits for them, and re-layouts  3.31 us
  transfers between devices with their start and end apart: 10, of which 2 were waited for; matrix products, arithmetic and copies ran while one was open for 3% of the time, Pallas kernels for 28%

profile of v4, /device:TPU:0, one launch (start us, length us, event | category | flops | bytes accessed | tf_op | source)
XLA Modules:
  0.0 70.1 jit_solution(8388062284812812945)
XLA Ops:
  0.6 0.0 copy-start.11
  0.6 0.0 copy-start
  0.7 2.7 %pack.1 = (bf16[2,64,4,128]{3,2,1,0:T(4,128)(2,1)}, bf16[2,64,4,128]{3,2,1,0:T(4,128)(2,1)}) custom-call(f32[64,64,128]{2,1,0:T(8,128)} %control_hbm.11, f32[64,64]{1,0:T(8,128)} %kappa_ref.11), custom_call_target="tpu_custom_call" | custom-call | tf_op jit(solution)/shard_map/pack/pallas_call | solution.py:673
  3.4 6.1 %collective-permute-start = (bf16[2,64,4,128]{3,2,1,0:T(4,128)(2,1)}, bf16[2,64,4,128]{3,2,1,0:T(4,128)(2,1)S(1)}, u32[]{:S(2)}, u32[]{:S(2)}) collective-permute-start(bf16[2,64,4,128]{3,2,1,0:T(4,128)(2,1)} %get-tuple-element.23), channel_id=1, source_target_pairs={{1,0},{2,1},{3,2},{4,3},{5,4},{6,5},{7,6},{0,7},{9,8},{10,9},{11,1... | collective-permute-start | bytes 393224 | tf_op jit(solution)/shard_map/ppermute | solution.py:634
  9.4 0.0 collective-permute-start.1
  10.1 0.0 copy-start.14
  10.2 0.9 %copy-done.14 = f32[1024,64]{0,1:T(8,128)S(1)} copy-done((f32[1024,64]{0,1:T(8,128)S(1)}, f32[1024,64]{0,1:T(8,128)}, u32[]{:S(2)}) %copy-start.14) | copy-done | bytes 262168
  11.1 2.8 %address.1 = (s32[544,128]{1,0:T(8,128)}, s32[1,1024]{1,0:T(1,128)S(1)}, bf16[2,4,64,128]{3,2,1,0:T(8,128)(2,1)S(1)}, bf16[2,4,64,128]{3,2,1,0:T(8,128)(2,1)S(1)}) custom-call(s32[1]{0:T(128)S(6)} %copy.19.count_ref, s32[1,1024]{1,0:T(1,128)S(1)} %bitcast.13, s32[1,1024]{1,0:T(1,128)S(1)} %bitcast.14, f32[1,1024]{1,0:T(1,128)S(1)} %bitcast.15, ...), custom_call_target="tpu_custom_call" | custom-call | flops 2000000000 | bytes 8000000 | tf_op jit(solution)/shard_map/address/pallas_call | solution.py:689
  13.9 6.0 %all-to-all-start = ((s32[32,1,2176]{2,1,0:T(1,128)}), s32[32,1,2176]{2,1,0:T(1,128)S(1)}, u32[]{:S(2)}, u32[]{:S(2)}) async-start(s32[32,1,2176]{2,1,0:T(1,128)} %bitcast.4), calls=%async_computation | async-start | bytes 557056 | tf_op jit(solution)/shard_map/all_to_all | solution.py:716
  19.9 0.0 collective-permute-done.east_ref.keast_ref
  19.9 0.0 collective-permute-done.1.west_ref.kwest_ref
  20.0 1.6 %collective-permute-start.3 = (bf16[2,4,72,128]{3,2,1,0:T(8,128)(2,1)S(1)}, bf16[2,4,72,128]{3,2,1,0:T(8,128)(2,1)S(1)}, u32[]{:S(2)}, u32[]{:S(2)}) collective-permute-start(bf16[2,4,72,128]{3,2,1,0:T(8,128)(2,1)S(1)} %pad_maximum_fusion.1), channel_id=1, source_target_pairs={{8,0},{16,8},{24,16},{0,24},{9,1},{17,9},{25,17},{1,25},{10,2},{18... | collective-permute-start | bytes 442376 | tf_op jit(solution)/shard_map/ppermute | solution.py:639
  21.6 0.1 collective-permute-start.2
  21.7 7.7 %forward.1 = (bf16[1024,512]{1,0:T(8,128)(2,1)}, bf16[256,512]{1,0:T(8,128)(2,1)}) custom-call(f32[64,64,128]{2,1,0:T(8,128)} %control_hbm.11, f32[64,64,128]{2,1,0:T(8,128)} %sigma_hbm.3, bf16[2,64,4,128]{3,2,1,0:T(4,128)(2,1)} %copy-done.3, bf16[2,64,4,128]{3,2,1,0:T(4,128)(2,1)} %copy-done.5, f32[64,64]{1,0:T(8,128)} %kappa_ref.11, ...), custom_call_target="tpu_custom_call" | custom-call | flops 4000000000 | bytes 16000000 | tf_op jit(solution)/shard_map/forward/pallas_call | solution.py:731
  29.4 1.6 %all-to-all-done = s32[32,1,2176]{2,1,0:T(1,128)S(1)} async-done(((s32[32,1,2176]{2,1,0:T(1,128)}), s32[32,1,2176]{2,1,0:T(1,128)S(1)}, u32[]{:S(2)}, u32[]{:S(2)}) %all-to-all-start) | async-done | bytes 278560 | tf_op jit(solution)/shard_map/all_to_all | solution.py:716
  31.0 0.7 copy-done.20
  31.7 0.0 copy-start.13
  31.7 11.2 %owner.1 = (s32[512,128]{1,0:T(8,128)}, f32[64,64,128]{2,1,0:T(8,128)}, bf16[64,4,128]{2,1,0:T(4,128)(2,1)}, bf16[64,4,128]{2,1,0:T(4,128)(2,1)}, bf16[4,64,128]...) custom-call(s32[544,128]{1,0:T(8,128)} %bitcast.18, bf16[1024,512]{1,0:T(8,128)(2,1)} %get-tuple-element.25.evolved_hbm, ...), custom_call_target="tpu_custom_call" | custom-call | flops 4000000000 | bytes 16000000 | tf_op jit(solution)/shard_map/owner/pallas_call | solution.py:754
  42.9 3.0 %collective-permute-start.4 = (bf16[64,4,128]{2,1,0:T(4,128)(2,1)}, bf16[64,4,128]{2,1,0:T(4,128)(2,1)S(1)}, u32[]{:S(2)}, u32[]{:S(2)}) collective-permute-start(bf16[64,4,128]{2,1,0:T(4,128)(2,1)} %get-tuple-element.30.first_hbm), channel_id=1, source_target_pairs={{1,0},{2,1},{3,2},{4,3},{5,4},{6,5},{7,6},{0,7},{9,8},{10,9},{11,1... | collective-permute-start | bytes 196616 | tf_op jit(solution)/shard_map/ppermute | solution.py:634
  45.9 5.7 %all-to-all-start.1 = ((s32[32,16,128]{2,1,0:T(8,128)}), s32[32,16,128]{2,1,0:T(8,128)S(1)}, u32[]{:S(2)}, u32[]{:S(2)}) async-start(s32[32,16,128]{2,1,0:T(8,128)} %bitcast.17), calls=%async_computation.1 | async-start | bytes 524288 | tf_op jit(solution)/shard_map/all_to_all | solution.py:802
  51.6 1.5 %collective-permute-done.5.west_ref = bf16[64,4,128]{2,1,0:T(4,128)(2,1)S(1)} collective-permute-done((bf16[64,4,128]{2,1,0:T(4,128)(2,1)}, bf16[64,4,128]{2,1,0:T(4,128)(2,1)S(1)}, u32[]{:S(2)}, u32[]{:S(2)}) %collective-permute-start.5) | collective-permute-done | bytes 65568 | tf_op jit(solution)/shard_map/ppermute | solution.py:634
  53.2 0.9 %pad_maximum_fusion.2 = bf16[4,72,128]{2,1,0:T(8,128)(2,1)S(1)} fusion(bf16[4,4,128]{2,1,0:T(4,128)(2,1)S(1)} %get-tuple-element.43, bf16[4,4,128]{2,1,0:T(4,128)(2,1)S(1)} %get-tuple-element.41, bf16[4,64,128]{2,1,0:T(8,128)(2,1)} %get-tuple-element.32), kind=kLoop, calls=%fused_computation.2 | loop fusion | flops 221184 | bytes 147456 | tf_op jit(solution)/shard_map/concatenate | solution.py:813
  54.0 0.1 collective-permute-start.6
  54.1 0.9 %pad_maximum_fusion.3 = bf16[4,72,128]{2,1,0:T(8,128)(2,1)S(1)} fusion(bf16[4,4,128]{2,1,0:T(4,128)(2,1)S(1)} %get-tuple-element.42, bf16[4,4,128]{2,1,0:T(4,128)(2,1)S(1)} %get-tuple-element.40, bf16[4,64,128]{2,1,0:T(8,128)(2,1)} %get-tuple-element.33), kind=kLoop, calls=%fused_computation.3 | loop fusion | flops 221184 | bytes 147456 | tf_op jit(solution)/shard_map/concatenate | solution.py:812
  55.0 1.8 %collective-permute-start.7 = (bf16[4,72,128]{2,1,0:T(8,128)(2,1)S(1)}, bf16[4,72,128]{2,1,0:T(8,128)(2,1)S(1)}, u32[]{:S(2)}, u32[]{:S(2)}) collective-permute-start(bf16[4,72,128]{2,1,0:T(8,128)(2,1)S(1)} %pad_maximum_fusion.3), channel_id=1, source_target_pairs={{8,0},{16,8},{24,16},{0,24},{9,1},{17,9},{25,17},{1,25},{10,2},{18... | collective-permute-start | bytes 221192 | tf_op jit(solution)/shard_map/ppermute | solution.py:639
  56.8 0.0 copy-start.2
  56.8 1.6 %copy-done.2 = f32[64,64,128]{2,1,0:T(8,128)S(1)} copy-done((f32[64,64,128]{2,1,0:T(8,128)S(1)}, f32[64,64,128]{2,1,0:T(8,128)}, u32[]{:S(2)}) %copy-start.2) | copy-done | bytes 2097176
  58.4 6.4 %inner.1.inner_ref = f32[64,64,128]{2,1,0:T(8,128)} custom-call(f32[64,64,128]{2,1,0:T(8,128)S(1)} %copy-done.2, f32[64,64,128]{2,1,0:T(8,128)S(1)} %copy-done.1, bf16[64,4,128]{2,1,0:T(4,128)(2,1)S(1)} %collective-permute-done.4.east_ref, bf16[64,4,128]{2,1,0:T(4,128)(2,1)S(1)} %collective-permute-done.5.west_ref, f32[64,64]{1,0:T(8,128)S(1)} %copy-done.12, ...), custom_call_target="tpu_custom_call" | custom-call | flops 4000000000 | bytes 16000000 | tf_op jit(solution)/shard_map/inner/pallas_call | solution.py:815
  64.8 0.0 copy-start.15
  64.8 0.0 copy-start.16
  64.9 2.9 %rims.1 = f32[64,64,128]{2,1,0:T(8,128)} custom-call(f32[64,64,128]{2,1,0:T(8,128)S(1)} %copy-done.2, f32[64,64,128]{2,1,0:T(8,128)S(1)} %copy-done.1, bf16[64,4,128]{2,1,0:T(4,128)(2,1)S(1)} %collective-permute-done.4.east_ref, bf16[64,4,128]{2,1,0:T(4,128)(2,1)S(1)} %collective-permute-done.5.west_ref, ...), custom_call_target="tpu_custom_call", output_to_operand_aliasing={{}: (12, {})} | custom-call | flops 1000000000 | bytes 2000000 | tf_op jit(solution)/shard_map/rims/pallas_call | solution.py:828
  67.8 2.3 %give_back.1 = f32[64,1024]{1,0:T(8,128)} custom-call(s32[1]{0:T(128)S(6)} %copy.19.count_ref, s32[512,128]{1,0:T(8,128)S(1)} %bitcast.10, s32[1,1024]{1,0:T(1,128)S(1)} %get-tuple-element.35.key_ref, f32[64,1024]{1,0:T(8,128)S(1)} %bitcast.12, f32[1,1024]{1,0:T(1,128)S(1)} %bitcast.16, f32[64,64]{1,0:T(8,128)S(1)} %copy-done.16), custom_call_target="tpu_custom_call" | custom-call | flops 500000000 | bytes 2000000 | tf_op jit(solution)/shard_map/give_back/pallas_call | solution.py:848
  (46 shorter events, 0.1 us)
Async XLA Ops:
  0.6 9.5 %copy-start.11 = (f32[64,64]{1,0:T(8,128)S(1)}, f32[64,64]{1,0:T(8,128)}, u32[]{:S(2)}) copy-start(f32[64,64]{1,0:T(8,128)} %kappa_ref.11) | copy-start | bytes 49156
  0.6 9.5 %copy-start = (f32[64,64,128]{2,1,0:T(8,128)S(1)}, f32[64,64,128]{2,1,0:T(8,128)}, u32[]{:S(2)}) copy-start(f32[64,64,128]{2,1,0:T(8,128)} %control_hbm.11) | copy-start | bytes 6291460
  0.7 9.5 %copy-start.18 = (s32[1024]{0:T(1024)S(1)}, s32[1024]{0:T(1024)}, u32[]{:S(2)}) copy-start(s32[1024]{0:T(1024)} %param.22) | copy-start | bytes 12292
  0.7 9.5 %copy-start.17 = (s32[1024,1]{0,1:T(1,128)S(1)}, s32[1024,1]{0,1:T(1,128)}, u32[]{:S(2)}) copy-start(s32[1024,1]{0,1:T(1,128)} %param.21) | copy-start | bytes 12292
  0.7 9.5 %copy-start.19 = (f32[1024]{0:T(1024)S(1)}, f32[1024]{0:T(1024)}, u32[]{:S(2)}) copy-start(f32[1024]{0:T(1024)} %param.20) | copy-start | bytes 12292
  3.4 16.5 %collective-permute-start = (bf16[2,64,4,128]{3,2,1,0:T(4,128)(2,1)}, bf16[2,64,4,128]{3,2,1,0:T(4,128)(2,1)S(1)}, u32[]{:S(2)}, u32[]{:S(2)}) collective-permute-start(bf16[2,64,4,128]{3,2,1,0:T(4,128)(2,1)} %get-tuple-element.23), channel_id=1, source_target_pairs={{1,0},{2,1},{3,2},{4,3},{5,4},{6,5},{7,6},{0,7},{9,8},{10,9},{11,1... | collective-permute-start | bytes 393224 | tf_op jit(solution)/shard_map/ppermute | solution.py:634
  9.4 10.5 %collective-permute-start.1 = (bf16[2,64,4,128]{3,2,1,0:T(4,128)(2,1)}, bf16[2,64,4,128]{3,2,1,0:T(4,128)(2,1)S(1)}, u32[]{:S(2)}, u32[]{:S(2)}) collective-permute-start(bf16[2,64,4,128]{3,2,1,0:T(4,128)(2,1)} %get-tuple-element.24), channel_id=1, source_target_pairs={{0,1},{1,2},{2,3},{3,4},{4,5},{5,6},{6,7},{7,0},{8,9},{9,10},{10,1... | collective-permute-start | bytes 393224 | tf_op jit(solution)/shard_map/ppermute | solution.py:634
  10.1 1.0 %copy-start.14 = (f32[1024,64]{0,1:T(8,128)S(1)}, f32[1024,64]{0,1:T(8,128)}, u32[]{:S(2)}) copy-start(f32[1024,64]{0,1:T(8,128)} %param.19) | copy-start | bytes 786436
  13.9 17.1 %all-to-all-start = ((s32[32,1,2176]{2,1,0:T(1,128)}), s32[32,1,2176]{2,1,0:T(1,128)S(1)}, u32[]{:S(2)}, u32[]{:S(2)}) async-start(s32[32,1,2176]{2,1,0:T(1,128)} %bitcast.4), calls=%async_computation | async-start | bytes 557056 | tf_op jit(solution)/shard_map/all_to_all | solution.py:716
  19.9 1.7 %copy-start.3 = (bf16[2,64,4,128]{3,2,1,0:T(4,128)(2,1)}, bf16[2,64,4,128]{3,2,1,0:T(4,128)(2,1)S(1)}, u32[]{:S(2)}) copy-start(bf16[2,64,4,128]{3,2,1,0:T(4,128)(2,1)S(1)} %collective-permute-done.east_ref.keast_ref) | copy-start | bytes 393220
  19.9 1.7 %copy-start.5 = (bf16[2,64,4,128]{3,2,1,0:T(4,128)(2,1)}, bf16[2,64,4,128]{3,2,1,0:T(4,128)(2,1)S(1)}, u32[]{:S(2)}) copy-start(bf16[2,64,4,128]{3,2,1,0:T(4,128)(2,1)S(1)} %collective-permute-done.1.west_ref.kwest_ref) | copy-start | bytes 393220
  20.0 9.4 %collective-permute-start.3 = (bf16[2,4,72,128]{3,2,1,0:T(8,128)(2,1)S(1)}, bf16[2,4,72,128]{3,2,1,0:T(8,128)(2,1)S(1)}, u32[]{:S(2)}, u32[]{:S(2)}) collective-permute-start(bf16[2,4,72,128]{3,2,1,0:T(8,128)(2,1)S(1)} %pad_maximum_fusion.1), channel_id=1, source_target_pairs={{8,0},{16,8},{24,16},{0,24},{9,1},{17,9},{25,17},{1,25},{10,2},{18... | collective-permute-start | bytes 442376 | tf_op jit(solution)/shard_map/ppermute | solution.py:639
  21.6 7.8 %collective-permute-start.2 = (bf16[2,4,72,128]{3,2,1,0:T(8,128)(2,1)S(1)}, bf16[2,4,72,128]{3,2,1,0:T(8,128)(2,1)S(1)}, u32[]{:S(2)}, u32[]{:S(2)}) collective-permute-start(bf16[2,4,72,128]{3,2,1,0:T(8,128)(2,1)S(1)} %pad_maximum_fusion), channel_id=1, source_target_pairs={{0,8},{8,16},{16,24},{24,0},{1,9},{9,17},{17,25},{25,1},{2,10},{10... | collective-permute-start | bytes 442376 | tf_op jit(solution)/shard_map/ppermute | solution.py:639
  29.4 1.6 %copy-start.7 = (bf16[2,4,72,128]{3,2,1,0:T(8,128)(2,1)}, bf16[2,4,72,128]{3,2,1,0:T(8,128)(2,1)S(1)}, u32[]{:S(2)}) copy-start(bf16[2,4,72,128]{3,2,1,0:T(8,128)(2,1)S(1)} %collective-permute-done.3.south_ref.ksouth_ref) | copy-start | bytes 442372
  29.4 1.6 %copy-start.9 = (bf16[2,4,72,128]{3,2,1,0:T(8,128)(2,1)}, bf16[2,4,72,128]{3,2,1,0:T(8,128)(2,1)S(1)}, u32[]{:S(2)}) copy-start(bf16[2,4,72,128]{3,2,1,0:T(8,128)(2,1)S(1)} %collective-permute-done.2.north_ref.knorth_ref) | copy-start | bytes 442372
  31.0 0.7 %copy-start.20 = (s32[32,1,2176]{2,1,0:T(1,128)}, s32[32,1,2176]{2,1,0:T(1,128)S(1)}, u32[]{:S(2)}) copy-start(s32[32,1,2176]{2,1,0:T(1,128)S(1)} %all-to-all-done) | copy-start | bytes 835588
  31.7 25.1 %copy-start.1 = (f32[64,64,128]{2,1,0:T(8,128)S(1)}, f32[64,64,128]{2,1,0:T(8,128)}, u32[]{:S(2)}) copy-start(f32[64,64,128]{2,1,0:T(8,128)} %control_hbm.11) | copy-start | bytes 6291460
  31.7 25.1 %copy-start.4 = (bf16[2,64,4,128]{3,2,1,0:T(4,128)(2,1)S(1)}, bf16[2,64,4,128]{3,2,1,0:T(4,128)(2,1)}, u32[]{:S(2)}) copy-start(bf16[2,64,4,128]{3,2,1,0:T(4,128)(2,1)} %copy-done.3) | copy-start | bytes 393220
  31.7 25.1 %copy-start.6 = (bf16[2,64,4,128]{3,2,1,0:T(4,128)(2,1)S(1)}, bf16[2,64,4,128]{3,2,1,0:T(4,128)(2,1)}, u32[]{:S(2)}) copy-start(bf16[2,64,4,128]{3,2,1,0:T(4,128)(2,1)} %copy-done.5) | copy-start | bytes 393220
  31.7 25.1 %copy-start.12 = (f32[64,64]{1,0:T(8,128)S(1)}, f32[64,64]{1,0:T(8,128)}, u32[]{:S(2)}) copy-start(f32[64,64]{1,0:T(8,128)} %kappa_ref.11) | copy-start | bytes 49156
  31.7 25.1 %copy-start.13 = (f32[128,128]{1,0:T(8,128)S(1)}, f32[128,128]{1,0:T(8,128)}, u32[]{:S(2)}) copy-start(f32[128,128]{1,0:T(8,128)} %vertical_ref.7) | copy-start | bytes 196612
  42.9 8.7 %collective-permute-start.4 = (bf16[64,4,128]{2,1,0:T(4,128)(2,1)}, bf16[64,4,128]{2,1,0:T(4,128)(2,1)S(1)}, u32[]{:S(2)}, u32[]{:S(2)}) collective-permute-start(bf16[64,4,128]{2,1,0:T(4,128)(2,1)} %get-tuple-element.30.first_hbm), channel_id=1, source_target_pairs={{1,0},{2,1},{3,2},{4,3},{5,4},{6,5},{7,6},{0,7},{9,8},{10,9},{11,1... | collective-permute-start | bytes 196616 | tf_op jit(solution)/shard_map/ppermute | solution.py:634
  45.9 7.3 %collective-permute-start.5 = (bf16[64,4,128]{2,1,0:T(4,128)(2,1)}, bf16[64,4,128]{2,1,0:T(4,128)(2,1)S(1)}, u32[]{:S(2)}, u32[]{:S(2)}) collective-permute-start(bf16[64,4,128]{2,1,0:T(4,128)(2,1)} %get-tuple-element.31.second_hbm), channel_id=1, source_target_pairs={{0,1},{1,2},{2,3},{3,4},{4,5},{5,6},{6,7},{7,0},{8,9},{9,10},{10,1... | collective-permute-start | bytes 196616 | tf_op jit(solution)/shard_map/ppermute | solution.py:634
  45.9 21.8 %all-to-all-start.1 = ((s32[32,16,128]{2,1,0:T(8,128)}), s32[32,16,128]{2,1,0:T(8,128)S(1)}, u32[]{:S(2)}, u32[]{:S(2)}) async-start(s32[32,16,128]{2,1,0:T(8,128)} %bitcast.17), calls=%async_computation.1 | async-start | bytes 524288 | tf_op jit(solution)/shard_map/all_to_all | solution.py:802
  54.0 10.8 %collective-permute-start.6 = (bf16[4,72,128]{2,1,0:T(8,128)(2,1)S(1)}, bf16[4,72,128]{2,1,0:T(8,128)(2,1)S(1)}, u32[]{:S(2)}, u32[]{:S(2)}) collective-permute-start(bf16[4,72,128]{2,1,0:T(8,128)(2,1)S(1)} %pad_maximum_fusion.2), channel_id=1, source_target_pairs={{0,8},{8,16},{16,24},{24,0},{1,9},{9,17},{17,25},{25,1},{2,10},{10... | collective-permute-start | bytes 221192 | tf_op jit(solution)/shard_map/ppermute | solution.py:639
  55.0 9.9 %collective-permute-start.7 = (bf16[4,72,128]{2,1,0:T(8,128)(2,1)S(1)}, bf16[4,72,128]{2,1,0:T(8,128)(2,1)S(1)}, u32[]{:S(2)}, u32[]{:S(2)}) collective-permute-start(bf16[4,72,128]{2,1,0:T(8,128)(2,1)S(1)} %pad_maximum_fusion.3), channel_id=1, source_target_pairs={{8,0},{16,8},{24,16},{0,24},{9,1},{17,9},{25,17},{1,25},{10,2},{18... | collective-permute-start | bytes 221192 | tf_op jit(solution)/shard_map/ppermute | solution.py:639
  56.8 1.6 %copy-start.2 = (f32[64,64,128]{2,1,0:T(8,128)S(1)}, f32[64,64,128]{2,1,0:T(8,128)}, u32[]{:S(2)}) copy-start(f32[64,64,128]{2,1,0:T(8,128)} %get-tuple-element.29.adj_hbm) | copy-start | bytes 6291460
  58.4 6.5 %copy-start.8 = (bf16[2,4,72,128]{3,2,1,0:T(8,128)(2,1)S(1)}, bf16[2,4,72,128]{3,2,1,0:T(8,128)(2,1)}, u32[]{:S(2)}) copy-start(bf16[2,4,72,128]{3,2,1,0:T(8,128)(2,1)} %copy-done.7) | copy-start | bytes 442372
  58.4 6.5 %copy-start.10 = (bf16[2,4,72,128]{3,2,1,0:T(8,128)(2,1)S(1)}, bf16[2,4,72,128]{3,2,1,0:T(8,128)(2,1)}, u32[]{:S(2)}) copy-start(bf16[2,4,72,128]{3,2,1,0:T(8,128)(2,1)} %copy-done.9) | copy-start | bytes 442372
  64.8 2.9 %copy-start.15 = (f32[1024,64]{0,1:T(8,128)S(1)}, f32[1024,64]{0,1:T(8,128)}, u32[]{:S(2)}) copy-start(f32[1024,64]{0,1:T(8,128)} %param.19) | copy-start | bytes 786436
  64.8 2.9 %copy-start.16 = (f32[64,64]{1,0:T(8,128)S(1)}, f32[64,64]{1,0:T(8,128)}, u32[]{:S(2)}) copy-start(f32[64,64]{1,0:T(8,128)} %rinv_ref.3) | copy-start | bytes 49156

commit v5 on v4

--- a/solution.py
+++ b/solution.py
@@ -60,6 +60,10 @@
 
 
 HBM_SPEC = pl.BlockSpec(memory_space=pltpu.HBM)
+
+
+def in_hbm(array):
+    return pltpu.with_memory_space_constraint(array, pltpu.HBM)
 
 
 def start_copies(pairs, sem_ref, first=0):
@@ -181,8 +185,11 @@
     return dot_f32(spread.reshape(rows * count, 2 * cols), ones).reshape(rows, count, 128)
 
 
-def pack_kernel(control_hbm, kappa_ref, near_ref, far_ref, left_ref, right_ref, sem_ref):
+def pack_kernel(
+    control_hbm, kappa_hbm, near_ref, far_ref, left_ref, right_ref, kappa_ref, sem_ref
+):
     cols = control_hbm.shape[1]
+    kappa_in = start_copies([(kappa_hbm, kappa_ref)], sem_ref, 2)
     copies = start_copies(
         [
             (control_hbm.at[:, pl.ds(0, 8)], left_ref),
@@ -190,6 +197,7 @@
         ],
         sem_ref,
     )
+    wait_copies(kappa_in)
     kappa = kappa_ref[...]
     near_ref[1] = spread_kappa(kappa, 0, 8)[:, :NSTEP].astype(BF16)
     far_ref[1] = spread_kappa(kappa, cols - 8, cols)[:, 8 - NSTEP :].astype(BF16)
@@ -260,25 +268,24 @@
 
 def forward_kernel(
     control_hbm, sigma_hbm, east_ref, west_ref, kappa_ref, vertical_ref, table_ref, choice_ref,
-    out_hbm, pick_hbm, first_ref, second_ref, kap_ref, out_ref, pick_ref, sigma_ref, sem_ref,
+    out_ref, pick_ref, first_ref, second_ref, kap_ref, sigma_ref, sem_ref,
 ):
     rows, cols, levels = control_hbm.shape
     tile_in = start_copies(
         [(control_hbm, first_ref.at[pl.ds(0, rows), pl.ds(0, cols)])], sem_ref
     )
-    sigma_in = start_copies([(sigma_hbm, sigma_ref)], sem_ref, 1)
     put_sides(first_ref, 0, rows, cols, east_ref[0], west_ref[0])
     kap_ref[:rows, :cols, :] = spread_kappa(kappa_ref[...])
     put_sides(kap_ref, 0, rows, cols, east_ref[1], west_ref[1])
     wait_copies(tile_in)
+    sigma_in = start_copies([(sigma_hbm, sigma_ref)], sem_ref, 1)
     done = sweeps(first_ref, second_ref, kap_ref, rows)
-    wait_copies(sigma_in)
     channels = choice_ref.shape[1]
     table_rows = table_ref.shape[0]
     hot = (iota((table_rows, channels), 0) == choice_ref[...]).astype(F32).astype(BF16)
     fill_picked(pick_ref, dot_tn(hot, table_ref[...]).astype(BF16))
     mixing = forward_mixing(vertical_ref[...])
-    copies = start_copies([(pick_ref, pick_hbm)], sem_ref)
+    wait_copies(sigma_in)
     count = 8
     for index in range((rows - 2 * NSTEP) // count):
         row = NSTEP + index * count
@@ -286,8 +293,6 @@
         out_ref[where, :] = project_rows(
             done[row : row + count, :cols, :], sigma_ref[row : row + count], mixing
         )
-        copies += start_copies([(out_ref.at[where], out_hbm.at[where])], sem_ref, index + 1)
-    wait_copies(copies)
 
 
 def pole_flags():
@@ -334,30 +339,22 @@
 
 
 def owner_kernel(
-    devices_all, quarter, recv_hbm, evolved_hbm, pick_hbm, sigma_hbm, control_hbm, rinv_ref,
+    devices_all, quarter, recv_hbm, sigma_hbm, control_hbm, inner_ref, pick_ref, rinv_ref,
     east_ref, west_ref, north_ref, south_ref, kappa_ref, vertical_ref,
     ret_hbm, adj_hbm, left_hbm, right_hbm, top_hbm, bottom_hbm,
     word_ref, dep_ref, acc_ref, first_ref, second_ref, kap_ref, table_ref, pair_ref,
-    recv_ref, ret_ref, pick_ref, sigma_ref, adj_ref, left_ref, right_ref, top_ref, bottom_ref,
+    recv_ref, ret_ref, sigma_ref, adj_ref, left_ref, right_ref, top_ref, bottom_ref,
     sem_ref,
 ):
     lat_rows, cols, levels = sigma_hbm.shape
-    cells_part = evolved_hbm.shape[0]
+    cells_part = inner_ref.shape[0]
     flags = pole_flags()
     span = 2 * NSTEP
-    inside = pl.ds(cols, cells_part - 2 * cols)
     control_in = start_copies(rim_tiles(control_hbm, first_ref), sem_ref)
-    ends_at = (pl.ds(0, NSTEP), pl.ds(lat_rows - NSTEP, NSTEP))
-    ends_in = start_copies(
-        [(sigma_hbm.at[at], sigma_ref.at[at]) for at in ends_at] + [(pick_hbm, pick_ref)],
-        sem_ref,
-        2,
-    )
-    others_in = start_copies(
-        [(recv_hbm, recv_ref), (evolved_hbm.at[inside], table_ref.at[inside])], sem_ref, 5
-    )
-    rest = pl.ds(NSTEP, lat_rows - 2 * NSTEP)
-    sigma_in = start_copies([(sigma_hbm.at[rest], sigma_ref.at[rest])], sem_ref, 7)
+    others_in = start_copies([(recv_hbm, recv_ref)], sem_ref, 2)
+    sigma_in = start_copies([(sigma_hbm, sigma_ref)], sem_ref, 3)
+    inside = slice(cols, cells_part - cols)
+    table_ref[inside, :] = inner_ref[inside, :]
     put_rim_kappa(kap_ref, kappa_ref, east_ref, west_ref, north_ref, south_ref, flags)
     put_rims(
         first_ref,
@@ -371,7 +368,7 @@
     )
     wait_copies(control_in)
     done = sweeps(first_ref, second_ref, kap_ref, 6 * NSTEP)
-    wait_copies(ends_in)
+    wait_copies(sigma_in)
     ends = project_rows(
         jnp.concatenate(
             [done[NSTEP : 2 * NSTEP, :cols, :], done[4 * NSTEP : 5 * NSTEP, :cols, :]], axis=0
@@ -469,7 +466,6 @@
             acc_ref[...] += dot_tn(hots[side], wide)
     ret_ref[...] = (dep_ref[:rows_half, :] << 16) | dep_ref[rows_half:, :]
     copies = start_copies([(ret_ref, ret_hbm)], sem_ref)
-    wait_copies(sigma_in)
     groups = 4
     count = groups * 4
     for step in range(lat_rows // count):
@@ -519,19 +515,26 @@
 
 def inner_kernel(
     adj_hbm, control_hbm, east_ref, west_ref, kappa_ref, keast_ref, kwest_ref, vertical_ref,
-    out_hbm, first_ref, second_ref, kap_ref, out_ref, control_ref, sem_ref,
+    out_hbm, rim_ref, rim_kap_ref, rim_control_ref, first_ref, second_ref, kap_ref, out_ref,
+    control_ref, sem_ref,
 ):
     rows, cols, levels = control_hbm.shape
     tile_in = start_copies([(adj_hbm, first_ref.at[pl.ds(0, rows), pl.ds(0, cols)])], sem_ref)
-    control_in = start_copies([(control_hbm, control_ref)], sem_ref, 1)
     kap_ref[:rows, :cols, :] = spread_kappa(kappa_ref[...])
     put_sides(kap_ref, 0, rows, cols, keast_ref[1], kwest_ref[1])
     put_sides(first_ref, 0, rows, cols, east_ref[...], west_ref[...])
     wait_copies(tile_in)
+    control_in = start_copies([(control_hbm, control_ref)], sem_ref, 1)
     first_ref[:rows] = first_ref[:rows] * kap_ref[:rows]
+    span = 2 * NSTEP
+    for end, low in enumerate((0, rows - span)):
+        rim_ref[end * span : (end + 1) * span] = first_ref[low : low + span]
+        rim_kap_ref[end * span : (end + 1) * span] = kap_ref[low : low + span]
     done = sweeps(first_ref, second_ref, kap_ref, rows)
     mixing = backward_mixing(vertical_ref[...])
     wait_copies(control_in)
+    rim_control_ref[0] = control_ref[:NSTEP]
+    rim_control_ref[1] = control_ref[rows - NSTEP :]
     count = 8
     copies = []
     for index in range((rows - 2 * NSTEP) // count):
@@ -545,43 +548,29 @@
 
 
 def rim_kernel(
-    adj_hbm, control_hbm, east_ref, west_ref, north_ref, south_ref, kappa_ref, keast_ref,
-    kwest_ref, knorth_ref, ksouth_ref, vertical_ref, inner_ref, out_ref,
-    first_ref, second_ref, kap_ref, edge_ref, control_ref, sem_ref,
+    rim_ref, rim_kap_ref, control_ref, north_ref, south_ref, knorth_ref, ksouth_ref, vertical_ref,
+    inner_ref, out_ref, first_ref, second_ref, kap_ref, edge_ref, sem_ref,
 ):
     del inner_ref
-    lat_rows, cols = kappa_ref.shape
-    flags = pole_flags()
-    tile_in = start_copies(rim_tiles(adj_hbm, first_ref), sem_ref)
-    starts = (0, lat_rows - NSTEP)
-    control_in = start_copies(
-        [(control_hbm.at[pl.ds(at, NSTEP)], control_ref.at[i]) for i, at in enumerate(starts)],
-        sem_ref,
-        2,
-    )
-    put_rim_kappa(kap_ref, kappa_ref, keast_ref, kwest_ref, knorth_ref, ksouth_ref, flags)
-    put_rims(
-        first_ref,
-        lambda low, high: east_ref[low:high],
-        lambda low, high: west_ref[low:high],
-        north_ref[...],
-        south_ref[...],
-        flags,
-        lat_rows,
-        cols,
-    )
-    wait_copies(tile_in)
-    first_ref[...] = first_ref[...] * kap_ref[...]
+    lat_rows = out_ref.shape[0]
+    cols = out_ref.shape[1]
+    north_on, south_on = pole_flags()
+    tiles = slice(NSTEP, 5 * NSTEP)
+    kap_ref[:NSTEP] = knorth_ref[1].astype(F32) * north_on
+    kap_ref[tiles] = rim_kap_ref[...]
+    kap_ref[5 * NSTEP :] = ksouth_ref[1].astype(F32) * south_on
+    first_ref[:NSTEP] = north_ref[...].astype(F32) * kap_ref[:NSTEP]
+    first_ref[tiles] = rim_ref[...]
+    first_ref[5 * NSTEP :] = south_ref[...].astype(F32) * kap_ref[5 * NSTEP :]
     done = sweeps(first_ref, second_ref, kap_ref, 6 * NSTEP)
     mixing = backward_mixing(vertical_ref[...])
-    wait_copies(control_in)
     copies = []
     for end in range(2):
         at = pl.ds((1 + 3 * end) * NSTEP, NSTEP)
         back = finish_rows(done[at, :cols, :], kap_ref[at, :cols, :], mixing)
         edge_ref[end] = control_ref[end] + back
         copies += start_copies(
-            [(edge_ref.at[end], out_ref.at[pl.ds(starts[end], NSTEP)])], sem_ref, 4 + end
+            [(edge_ref.at[end], out_ref.at[pl.ds(end * (lat_rows - NSTEP), NSTEP)])], sem_ref, end
         )
     wait_copies(copies)
 
@@ -670,19 +659,21 @@
     smem = pl.BlockSpec(memory_space=pltpu.SMEM)
     anywhere = pl.BlockSpec(memory_space=pl.ANY)
 
+    control, sigma = in_hbm(control), in_hbm(sigma)
     near, far = pl.pallas_call(
         pack_kernel,
         out_shape=(jax.ShapeDtypeStruct((2, lat_rows, NSTEP, levels), BF16),) * 2,
-        in_specs=[HBM_SPEC] + vmem_specs(1),
+        in_specs=[HBM_SPEC] * 2,
         out_specs=tuple(vmem_specs(2)),
         scratch_shapes=[
             pltpu.VMEM((lat_rows, 8, levels), F32),
             pltpu.VMEM((lat_rows, 8, levels), F32),
-            pltpu.SemaphoreType.DMA((2,)),
+            pltpu.VMEM(kappa.shape, F32),
+            pltpu.SemaphoreType.DMA((3,)),
         ],
-        compiler_params=params(58),
+        compiler_params=params(6),
         name="pack",
-    )(control, kappa)
+    )(control, in_hbm(kappa))
     near, far, obs_cell = lax.optimization_barrier((near, far, obs_cell))
     east, west = exchange_sides(near, far)
 
@@ -731,19 +722,14 @@
     evolved, picked = pl.pallas_call(
         forward_kernel,
         out_shape=(
-            jax.ShapeDtypeStruct((columns // 4, 8 * channels), BF16),
-            jax.ShapeDtypeStruct((4 * channels, 4 * levels), BF16),
+            pltpu.VMEM((columns // 4, 8 * channels), BF16),
+            pltpu.VMEM((4 * channels, 4 * levels), BF16),
         ),
         in_specs=[HBM_SPEC] * 2 + vmem_specs(6),
-        out_specs=(HBM_SPEC, HBM_SPEC),
+        out_specs=tuple(vmem_specs(2)),
         scratch_shapes=[pltpu.VMEM(wide, F32)] * 3
-        + [
-            pltpu.VMEM((columns // 4, 8 * channels), BF16),
-            pltpu.VMEM((4 * channels, 4 * levels), BF16),
-            pltpu.VMEM(control.shape, F32),
-            pltpu.SemaphoreType.DMA((lat_rows // 8 + 2,)),
-        ],
-        compiler_params=params(58),
+        + [pltpu.VMEM(control.shape, F32), pltpu.SemaphoreType.DMA((2,))],
+        compiler_params=params(24),
         cost_estimate=estimate(4_000_000_000, 16_000_000),
         name="forward",
     )(
@@ -754,14 +740,14 @@
     returned, adjoint, left, right, atop, abottom = pl.pallas_call(
         functools.partial(owner_kernel, devices_all, quarter),
         out_shape=(
-            jax.ShapeDtypeStruct((rows_half, 128), I32),
-            jax.ShapeDtypeStruct(control.shape, F32),
-            jax.ShapeDtypeStruct((lat_rows, NSTEP, levels), BF16),
-            jax.ShapeDtypeStruct((lat_rows, NSTEP, levels), BF16),
+            pltpu.HBM((rows_half, 128), I32),
+            pltpu.HBM(control.shape, F32),
+            pltpu.HBM((lat_rows, NSTEP, levels), BF16),
+            pltpu.HBM((lat_rows, NSTEP, levels), BF16),
             jax.ShapeDtypeStruct((NSTEP, lon_cols, levels), BF16),
             jax.ShapeDtypeStruct((NSTEP, lon_cols, levels), BF16),
         ),
-        in_specs=[HBM_SPEC] * 5 + vmem_specs(7),
+        in_specs=[HBM_SPEC] * 3 + vmem_specs(9),
         out_specs=(HBM_SPEC,) * 6,
         scratch_shapes=[
             pltpu.VMEM((rows_half, 128), I32),
@@ -774,7 +760,6 @@
             pltpu.VMEM((2 * channels, 2 * channels), F32),
             pltpu.VMEM((devices_all * (quarter + 1), 128), I32),
             pltpu.VMEM((rows_half, 128), I32),
-            pltpu.VMEM((4 * channels, 4 * levels), BF16),
             pltpu.VMEM(control.shape, F32),
             pltpu.VMEM(control.shape, F32),
             pltpu.VMEM((lat_rows, NSTEP, levels), BF16),
@@ -783,22 +768,22 @@
             pltpu.VMEM((NSTEP, lon_cols, levels), BF16),
             pltpu.SemaphoreType.DMA((max(8, lat_rows // 16 + 5),)),
         ],
-        compiler_params=params(58),
+        compiler_params=params(28),
         cost_estimate=estimate(4_000_000_000, 16_000_000),
         name="owner",
     )(
-        received, evolved, picked, sigma, control, r_inverse, east, west, north, south, kappa,
+        received, sigma, control, evolved, picked, r_inverse, east, west, north, south, kappa,
         vertical,
     )
     returned = pl.pallas_call(
         pass_kernel,
-        out_shape=jax.ShapeDtypeStruct(returned.shape, I32),
-        in_specs=[anywhere] * 3,
-        out_specs=anywhere,
+        out_shape=pltpu.HBM(returned.shape, I32),
+        in_specs=[HBM_SPEC] * 3,
+        out_specs=HBM_SPEC,
         input_output_aliases={0: 0},
         cost_estimate=estimate(1_000_000, 1_000_000),
         name="pass",
-    )(returned, left, right)
+    )(in_hbm(returned), in_hbm(left), in_hbm(right))
     home = lax.all_to_all(
         returned.reshape(devices_all, quarter, 128),
         ("lat", "lon"),
@@ -812,37 +797,41 @@
         jnp.concatenate([atop, aeast[:NSTEP], awest[:NSTEP]], axis=1),
         jnp.concatenate([abottom, aeast[-NSTEP:], awest[-NSTEP:]], axis=1),
     )
-    inner = pl.pallas_call(
+    rim_tile = (4 * NSTEP, lon_cols + 2 * NSTEP, levels)
+    inner, rim_scaled, rim_kappa, rim_control = pl.pallas_call(
         inner_kernel,
-        out_shape=jax.ShapeDtypeStruct(control.shape, F32),
+        out_shape=(
+            pltpu.HBM(control.shape, F32),
+            pltpu.VMEM(rim_tile, F32),
+            pltpu.VMEM(rim_tile, F32),
+            pltpu.VMEM((2, NSTEP, lon_cols, levels), F32),
+        ),
         in_specs=[HBM_SPEC] * 2 + vmem_specs(6),
-        out_specs=HBM_SPEC,
+        out_specs=(HBM_SPEC,) + tuple(vmem_specs(3)),
         scratch_shapes=[pltpu.VMEM(wide, F32)] * 3
         + [pltpu.VMEM(control.shape, F32)] * 2
         + [pltpu.SemaphoreType.DMA((lat_rows // 8,))],
-        compiler_params=params(20),
+        compiler_params=params(24),
         cost_estimate=estimate(4_000_000_000, 16_000_000),
         name="inner",
-    )(adjoint, control, aeast, awest, kappa, east, west, vertical)
+    )(in_hbm(adjoint), control, aeast, awest, kappa, east, west, vertical)
 
     gradient = pl.pallas_call(
         rim_kernel,
         out_shape=jax.ShapeDtypeStruct(control.shape, F32),
-        in_specs=[HBM_SPEC] * 2 + vmem_specs(10) + [anywhere],
+        in_specs=vmem_specs(8) + [anywhere],
         out_specs=anywhere,
         scratch_shapes=[pltpu.VMEM(rim, F32)] * 3
         + [
             pltpu.VMEM((2, NSTEP, lon_cols, levels), F32),
-            pltpu.VMEM((2, NSTEP, lon_cols, levels), F32),
-            pltpu.SemaphoreType.DMA((6,)),
+            pltpu.SemaphoreType.DMA((2,)),
         ],
-        input_output_aliases={12: 0},
+        input_output_aliases={8: 0},
         compiler_params=params(12),
         cost_estimate=estimate(1_000_000_000, 2_000_000),
         name="rims",
     )(
-        adjoint, control, aeast, awest, anorth, asouth, kappa, east, west, north, south, vertical,
-        inner,
+        rim_scaled, rim_kappa, rim_control, anorth, asouth, north, south, vertical, inner,
     )
 
     departures = pl.pallas_call(

time: 70.5 us -> 61.1 us (0.87)
  Pallas kernels: 35.9 us -> 31.1 us
  local copies, waits for them, and re-layouts: 3.34 us -> 0.08 us
  waiting for transfers between devices: 3.12 us -> 4.91 us
  other arithmetic: 1.74 us -> 0.06 us
  starting transfers between devices: 24.3 us -> 23 us
    unnamed x42 -> x18, local copies, waits for them, and re-layouts: 3.31 us -> 0.05 us
    pallas_call x1, Pallas kernels: 11.2 us -> 9.55 us  [body(): pl.pallas_call(functools.partial(owner_kernel, devices_all, quarter), out...]
    pallas_call x1, Pallas kernels: 2.69 us -> 1.17 us  [body(): pl.pallas_call(pack_kernel, out_shape=(jax.ShapeDtypeStruct((2, lat_rows,...]
    all_to_all x1, waiting for transfers between devices: 1.55 us -> 2.49 us  [body(): lax.all_to_all(payload.reshape(devices_all, 1, (quarter + 1) * 128), ('la...]
    concatenate x1, other arithmetic: 0.86 us -> 0.01 us  [body(): jnp.concatenate([atop, aeast[:NSTEP], awest[:NSTEP]], axis=1)]
    concatenate x1, other arithmetic: 0.85 us -> 0.01 us  [body(): jnp.concatenate([abottom, aeast[-NSTEP:], awest[-NSTEP:]], axis=1)]
    ppermute x2, starting transfers between devices: 9.09 us -> 8.29 us  [exchange_sides(): lax.ppermute(left, 'lon', backward)]
    pallas_call x1, Pallas kernels: 2.86 us -> 2.15 us  [body(): pl.pallas_call(rim_kernel, out_shape=jax.ShapeDtypeStruct(control.shape,...]
  transfers between devices with their start and end apart: 10 -> 10, of which waited for: 2 -> 3; matrix products, arithmetic and copies ran while one was open for 3% -> 0% of each run, Pallas kernels for 28% -> 30%
where the time goes in v5:
time: 61.1 us; the launch traced here: 60.8 us
  Pallas kernels  31.1 us (51%)
  starting transfers between devices  23 us (38%)
  waiting for transfers between devices  4.91 us (8%)
  between operations  1.6 us (3%)
    pallas_call x1, Pallas kernels, body(): pl.pallas_call(functools.partial(owner_kernel, devices_all, quarter), out...  9.55 us
    ppermute x2, starting transfers between devices, exchange_sides(): lax.ppermute(left, 'lon', backward)  8.29 us
    pallas_call x1, Pallas kernels, body(): pl.pallas_call(inner_kernel, out_shape=(pltpu.HBM(control.shape, F32), pl...  7.22 us
    pallas_call x1, Pallas kernels, body(): pl.pallas_call(forward_kernel, out_shape=(pltpu.VMEM((columns // 4, 8 * c...  6.27 us
    all_to_all x1, starting transfers between devices, body(): lax.all_to_all(payload.reshape(devices_all, 1, (quarter + 1) * 128), ('la...  6.02 us
    all_to_all x1, starting transfers between devices, body(): lax.all_to_all(returned.reshape(devices_all, quarter, 128), ('lat', 'lon'...  5.26 us
    ppermute x2, starting transfers between devices, exchange_rims(): lax.ppermute(top, 'lat', backward)  3.35 us
    all_to_all x1, waiting for transfers between devices, body(): lax.all_to_all(payload.reshape(devices_all, 1, (quarter + 1) * 128), ('la...  2.49 us
  transfers between devices with their start and end apart: 10, of which 3 were waited for; matrix products, arithmetic and copies ran while one was open for 0% of the time, Pallas kernels for 30%

profile of v5, /device:TPU:0, one launch (start us, length us, event | category | flops | bytes accessed | tf_op | source)
XLA Modules:
  0.0 60.8 jit_solution(1140581731202220485)
XLA Ops:
  0.6 0.0 copy-start.1
  0.7 1.2 %pack.1 = (bf16[2,64,4,128]{3,2,1,0:T(4,128)(2,1)S(1)}, bf16[2,64,4,128]{3,2,1,0:T(4,128)(2,1)S(1)}) custom-call(f32[64,64,128]{2,1,0:T(8,128)} %control_hbm.9, f32[64,64]{1,0:T(8,128)} %kappa_ref.7), custom_call_target="tpu_custom_call" | custom-call | tf_op jit(solution)/shard_map/pack/pallas_call | solution.py:663
  1.9 6.1 %collective-permute-start = (bf16[2,64,4,128]{3,2,1,0:T(4,128)(2,1)S(1)}, bf16[2,64,4,128]{3,2,1,0:T(4,128)(2,1)S(1)}, u32[]{:S(2)}, u32[]{:S(2)}) collective-permute-start(bf16[2,64,4,128]{3,2,1,0:T(4,128)(2,1)S(1)} %get-tuple-element.27), channel_id=1, source_target_pairs={{1,0},{2,1},{3,2},{4,3},{5,4},{6,5},{7,6},{0,7},{9,8},{10,9},{11,1... | collective-permute-start | bytes 393224 | tf_op jit(solution)/shard_map/ppermute | solution.py:623
  7.9 0.0 collective-permute-start.1
  8.6 0.0 copy-start
  8.6 0.0 copy-start.3
  8.6 0.0 copy-start.8
  8.7 2.4 %address.1 = (s32[544,128]{1,0:T(8,128)}, s32[1,1024]{1,0:T(1,128)S(1)}, bf16[2,4,64,128]{3,2,1,0:T(8,128)(2,1)S(1)}, bf16[2,4,64,128]{3,2,1,0:T(8,128)(2,1)S(1)}) custom-call(s32[1]{0:T(128)S(6)} %copy.19.count_ref, s32[1,1024]{1,0:T(1,128)S(1)} %bitcast.14, s32[1,1024]{1,0:T(1,128)S(1)} %bitcast.15, f32[1,1024]{1,0:T(1,128)S(1)} %bitcast.16, ...), custom_call_target="tpu_custom_call" | custom-call | flops 2000000000 | bytes 8000000 | tf_op jit(solution)/shard_map/address/pallas_call | solution.py:680
  11.1 6.0 %all-to-all-start = ((s32[32,1,2176]{2,1,0:T(1,128)}), s32[32,1,2176]{2,1,0:T(1,128)S(1)}, u32[]{:S(2)}, u32[]{:S(2)}) async-start(s32[32,1,2176]{2,1,0:T(1,128)} %bitcast.4), calls=%async_computation | async-start | bytes 557056 | tf_op jit(solution)/shard_map/all_to_all | solution.py:707
  17.1 0.0 collective-permute-done.east_ref.keast_ref
  17.2 0.0 collective-permute-done.1.west_ref.kwest_ref
  17.2 1.6 %collective-permute-start.3 = (bf16[2,4,72,128]{3,2,1,0:T(8,128)(2,1)S(1)}, bf16[2,4,72,128]{3,2,1,0:T(8,128)(2,1)S(1)}, u32[]{:S(2)}, u32[]{:S(2)}) collective-permute-start(bf16[2,4,72,128]{3,2,1,0:T(8,128)(2,1)S(1)} %pad_maximum_fusion.1), channel_id=1, source_target_pairs={{8,0},{16,8},{24,16},{0,24},{9,1},{17,9},{25,17},{1,25},{10,2},{18... | collective-permute-start | bytes 442376 | tf_op jit(solution)/shard_map/ppermute | solution.py:628
  18.8 0.1 collective-permute-start.2
  18.9 0.0 copy-start.4
  18.9 6.3 %forward.1 = (bf16[1024,512]{1,0:T(8,128)(2,1)S(1)}, bf16[256,512]{1,0:T(8,128)(2,1)S(1)}) custom-call(f32[64,64,128]{2,1,0:T(8,128)} %control_hbm.9, f32[64,64,128]{2,1,0:T(8,128)} %sigma_hbm.3, bf16[2,64,4,128]{3,2,1,0:T(4,128)(2,1)S(1)} %collective-permute-done.east_ref.keast_ref, bf16[2,64,4,128]{3,2,1,0:T(4,128)(2,1)S(1)} %collective-permute-done.1.west_ref.kwest_ref, ...), custom_call_target="tpu_custom_call" | custom-call | flops 4000000000 | bytes 16000000 | tf_op jit(solution)/shard_map/forward/pallas_call | solution.py:722
  25.2 0.0 collective-permute-done.3.south_ref.ksouth_ref
  25.2 0.5 collective-permute-done.2.north_ref.knorth_ref
  25.7 2.5 %all-to-all-done = s32[32,1,2176]{2,1,0:T(1,128)S(1)} async-done(((s32[32,1,2176]{2,1,0:T(1,128)}), s32[32,1,2176]{2,1,0:T(1,128)S(1)}, u32[]{:S(2)}, u32[]{:S(2)}) %all-to-all-start) | async-done | bytes 278560 | tf_op jit(solution)/shard_map/all_to_all | solution.py:707
  28.2 9.5 %owner.1 = (s32[512,128]{1,0:T(8,128)}, f32[64,64,128]{2,1,0:T(8,128)}, bf16[64,4,128]{2,1,0:T(4,128)(2,1)}, bf16[64,4,128]{2,1,0:T(4,128)(2,1)}, bf16[4,64,128]...) custom-call(s32[544,128]{1,0:T(8,128)S(1)} %bitcast.10, f32[64,64,128]{2,1,0:T(8,128)} %sigma_hbm.3, ...), custom_call_target="tpu_custom_call" | custom-call | flops 4000000000 | bytes 16000000 | tf_op jit(solution)/shard_map/owner/pallas_call | solution.py:740
  37.8 2.2 %collective-permute-start.4 = (bf16[64,4,128]{2,1,0:T(4,128)(2,1)}, bf16[64,4,128]{2,1,0:T(4,128)(2,1)S(1)}, u32[]{:S(2)}, u32[]{:S(2)}) collective-permute-start(bf16[64,4,128]{2,1,0:T(4,128)(2,1)} %get-tuple-element.34.first_hbm), channel_id=1, source_target_pairs={{1,0},{2,1},{3,2},{4,3},{5,4},{6,5},{7,6},{0,7},{9,8},{10,9},{11,1... | collective-permute-start | bytes 196616 | tf_op jit(solution)/shard_map/ppermute | solution.py:623
  40.0 0.0 collective-permute-start.5
  40.0 5.3 %all-to-all-start.1 = ((s32[32,16,128]{2,1,0:T(8,128)}), s32[32,16,128]{2,1,0:T(8,128)S(1)}, u32[]{:S(2)}, u32[]{:S(2)}) async-start(s32[32,16,128]{2,1,0:T(8,128)} %bitcast.19), calls=%async_computation.1 | async-start | bytes 524288 | tf_op jit(solution)/shard_map/all_to_all | solution.py:787
  45.3 0.0 collective-permute-done.4.east_ref
  45.3 1.9 %collective-permute-done.5.west_ref = bf16[64,4,128]{2,1,0:T(4,128)(2,1)S(1)} collective-permute-done((bf16[64,4,128]{2,1,0:T(4,128)(2,1)}, bf16[64,4,128]{2,1,0:T(4,128)(2,1)S(1)}, u32[]{:S(2)}, u32[]{:S(2)}) %collective-permute-start.5) | collective-permute-done | bytes 65568 | tf_op jit(solution)/shard_map/ppermute | solution.py:623
  47.2 0.1 collective-permute-start.6
  47.3 1.8 %collective-permute-start.7 = (bf16[4,72,128]{2,1,0:T(8,128)(2,1)S(1)}, bf16[4,72,128]{2,1,0:T(8,128)(2,1)S(1)}, u32[]{:S(2)}, u32[]{:S(2)}) collective-permute-start(bf16[4,72,128]{2,1,0:T(8,128)(2,1)S(1)} %pad_maximum_fusion.3), channel_id=1, source_target_pairs={{8,0},{16,8},{24,16},{0,24},{9,1},{17,9},{25,17},{1,25},{10,2},{18... | collective-permute-start | bytes 221192 | tf_op jit(solution)/shard_map/ppermute | solution.py:628
  49.1 7.2 %inner.1 = (f32[64,64,128]{2,1,0:T(8,128)}, f32[16,72,128]{2,1,0:T(8,128)S(1)}, f32[16,72,128]{2,1,0:T(8,128)S(1)}, f32[2,4,64,128]{3,2,1,0:T(8,128)S(1)}) custom-call(f32[64,64,128]{2,1,0:T(8,128)} %get-tuple-element.33.adj_hbm, f32[64,64,128]{2,1,0:T(8,128)} %control_hbm.9, bf16[64,4,128]{2,1,0:T(4,128)(2,1)S(1)} %collective-permute-done.4.east_ref, ...), custom_call_target="tpu_custom_call" | custom-call | flops 4000000000 | bytes 16000000 | tf_op jit(solution)/shard_map/inner/pallas_call | solution.py:801
  56.3 0.0 collective-permute-done.6.north_ref
  56.3 0.0 collective-permute-done.7.south_ref
  56.3 2.2 %rims.1 = f32[64,64,128]{2,1,0:T(8,128)} custom-call(f32[16,72,128]{2,1,0:T(8,128)S(1)} %get-tuple-element.36.rim_ref, f32[16,72,128]{2,1,0:T(8,128)S(1)} %get-tuple-element.37.rim_kap_ref, f32[2,4,64,128]{3,2,1,0:T(8,128)S(1)} %get-tuple-element.38.control_ref, ...), custom_call_target="tpu_custom_call", output_to_operand_aliasing={{}: (8, {})} | custom-call | flops 1000000000 | bytes 2000000 | tf_op jit(solution)/shard_map/rims/pallas_call | solution.py:819
  58.5 0.0 all-to-all-done.1
  58.5 2.3 %give_back.1 = f32[64,1024]{1,0:T(8,128)} custom-call(s32[1]{0:T(128)S(6)} %copy.19.count_ref, s32[512,128]{1,0:T(8,128)S(1)} %bitcast.11, s32[1,1024]{1,0:T(1,128)S(1)} %get-tuple-element.43.key_ref, f32[64,1024]{1,0:T(8,128)S(1)} %bitcast.13, f32[1,1024]{1,0:T(1,128)S(1)} %bitcast.17, f32[64,64]{1,0:T(8,128)S(1)} %copy-done.4), custom_call_target="tpu_custom_call" | custom-call | flops 500000000 | bytes 2000000 | tf_op jit(solution)/shard_map/give_back/pallas_call | solution.py:837
  (22 shorter events, 0.1 us)
Async XLA Ops:
  0.6 7.9 %copy-start.1 = (f32[64,64]{1,0:T(8,128)S(1)}, f32[64,64]{1,0:T(8,128)}, u32[]{:S(2)}) copy-start(f32[64,64]{1,0:T(8,128)} %kappa_ref.7) | copy-start | bytes 49156
  0.6 7.9 %copy-start.6 = (s32[1024]{0:T(1024)S(1)}, s32[1024]{0:T(1024)}, u32[]{:S(2)}) copy-start(s32[1024]{0:T(1024)} %param.22) | copy-start | bytes 12292
  0.7 7.9 %copy-start.5 = (s32[1024,1]{0,1:T(1,128)S(1)}, s32[1024,1]{0,1:T(1,128)}, u32[]{:S(2)}) copy-start(s32[1024,1]{0,1:T(1,128)} %param.21) | copy-start | bytes 12292
  0.7 7.9 %copy-start.7 = (f32[1024]{0:T(1024)S(1)}, f32[1024]{0:T(1024)}, u32[]{:S(2)}) copy-start(f32[1024]{0:T(1024)} %param.20) | copy-start | bytes 12292
  0.7 7.9 %copy-start.2 = (f32[1024,64]{0,1:T(8,128)S(1)}, f32[1024,64]{0,1:T(8,128)}, u32[]{:S(2)}) copy-start(f32[1024,64]{0,1:T(8,128)} %param.19) | copy-start | bytes 786436
  1.9 15.3 %collective-permute-start = (bf16[2,64,4,128]{3,2,1,0:T(4,128)(2,1)S(1)}, bf16[2,64,4,128]{3,2,1,0:T(4,128)(2,1)S(1)}, u32[]{:S(2)}, u32[]{:S(2)}) collective-permute-start(bf16[2,64,4,128]{3,2,1,0:T(4,128)(2,1)S(1)} %get-tuple-element.27), channel_id=1, source_target_pairs={{1,0},{2,1},{3,2},{4,3},{5,4},{6,5},{7,6},{0,7},{9,8},{10,9},{11,1... | collective-permute-start | bytes 393224 | tf_op jit(solution)/shard_map/ppermute | solution.py:623
  7.9 9.3 %collective-permute-start.1 = (bf16[2,64,4,128]{3,2,1,0:T(4,128)(2,1)S(1)}, bf16[2,64,4,128]{3,2,1,0:T(4,128)(2,1)S(1)}, u32[]{:S(2)}, u32[]{:S(2)}) collective-permute-start(bf16[2,64,4,128]{3,2,1,0:T(4,128)(2,1)S(1)} %get-tuple-element.28), channel_id=1, source_target_pairs={{0,1},{1,2},{2,3},{3,4},{4,5},{5,6},{6,7},{7,0},{8,9},{9,10},{10,1... | collective-permute-start | bytes 393224 | tf_op jit(solution)/shard_map/ppermute | solution.py:623
  8.6 10.3 %copy-start = (f32[128,128]{1,0:T(8,128)S(1)}, f32[128,128]{1,0:T(8,128)}, u32[]{:S(2)}) copy-start(f32[128,128]{1,0:T(8,128)} %vertical_ref.7) | copy-start | bytes 196612
  8.6 10.3 %copy-start.3 = (bf16[616,128]{1,0:T(8,128)(2,1)S(1)}, bf16[616,128]{1,0:T(8,128)(2,1)}, u32[]{:S(2)}) copy-start(bf16[616,128]{1,0:T(8,128)(2,1)} %table_ref.1) | copy-start | bytes 473092
  8.6 10.3 %copy-start.8 = (s32[64]{0:T(128)S(1)}, s32[64]{0:T(128)}, u32[]{:S(2)}) copy-start(s32[64]{0:T(128)} %param.17) | copy-start | bytes 772
  11.1 17.1 %all-to-all-start = ((s32[32,1,2176]{2,1,0:T(1,128)}), s32[32,1,2176]{2,1,0:T(1,128)S(1)}, u32[]{:S(2)}, u32[]{:S(2)}) async-start(s32[32,1,2176]{2,1,0:T(1,128)} %bitcast.4), calls=%async_computation | async-start | bytes 557056 | tf_op jit(solution)/shard_map/all_to_all | solution.py:707
  17.2 8.0 %collective-permute-start.3 = (bf16[2,4,72,128]{3,2,1,0:T(8,128)(2,1)S(1)}, bf16[2,4,72,128]{3,2,1,0:T(8,128)(2,1)S(1)}, u32[]{:S(2)}, u32[]{:S(2)}) collective-permute-start(bf16[2,4,72,128]{3,2,1,0:T(8,128)(2,1)S(1)} %pad_maximum_fusion.1), channel_id=1, source_target_pairs={{8,0},{16,8},{24,16},{0,24},{9,1},{17,9},{25,17},{1,25},{10,2},{18... | collective-permute-start | bytes 442376 | tf_op jit(solution)/shard_map/ppermute | solution.py:628
  18.8 6.9 %collective-permute-start.2 = (bf16[2,4,72,128]{3,2,1,0:T(8,128)(2,1)S(1)}, bf16[2,4,72,128]{3,2,1,0:T(8,128)(2,1)S(1)}, u32[]{:S(2)}, u32[]{:S(2)}) collective-permute-start(bf16[2,4,72,128]{3,2,1,0:T(8,128)(2,1)S(1)} %pad_maximum_fusion), channel_id=1, source_target_pairs={{0,8},{8,16},{16,24},{24,0},{1,9},{9,17},{17,25},{25,1},{2,10},{10... | collective-permute-start | bytes 442376 | tf_op jit(solution)/shard_map/ppermute | solution.py:628
  18.9 9.3 %copy-start.4 = (f32[64,64]{1,0:T(8,128)S(1)}, f32[64,64]{1,0:T(8,128)}, u32[]{:S(2)}) copy-start(f32[64,64]{1,0:T(8,128)} %rinv_ref.3) | copy-start | bytes 49156
  37.8 7.5 %collective-permute-start.4 = (bf16[64,4,128]{2,1,0:T(4,128)(2,1)}, bf16[64,4,128]{2,1,0:T(4,128)(2,1)S(1)}, u32[]{:S(2)}, u32[]{:S(2)}) collective-permute-start(bf16[64,4,128]{2,1,0:T(4,128)(2,1)} %get-tuple-element.34.first_hbm), channel_id=1, source_target_pairs={{1,0},{2,1},{3,2},{4,3},{5,4},{6,5},{7,6},{0,7},{9,8},{10,9},{11,1... | collective-permute-start | bytes 196616 | tf_op jit(solution)/shard_map/ppermute | solution.py:623
  40.0 7.2 %collective-permute-start.5 = (bf16[64,4,128]{2,1,0:T(4,128)(2,1)}, bf16[64,4,128]{2,1,0:T(4,128)(2,1)S(1)}, u32[]{:S(2)}, u32[]{:S(2)}) collective-permute-start(bf16[64,4,128]{2,1,0:T(4,128)(2,1)} %get-tuple-element.35.second_hbm), channel_id=1, source_target_pairs={{0,1},{1,2},{2,3},{3,4},{4,5},{5,6},{6,7},{7,0},{8,9},{9,10},{10,1... | collective-permute-start | bytes 196616 | tf_op jit(solution)/shard_map/ppermute | solution.py:623
  40.0 18.5 %all-to-all-start.1 = ((s32[32,16,128]{2,1,0:T(8,128)}), s32[32,16,128]{2,1,0:T(8,128)S(1)}, u32[]{:S(2)}, u32[]{:S(2)}) async-start(s32[32,16,128]{2,1,0:T(8,128)} %bitcast.19), calls=%async_computation.1 | async-start | bytes 524288 | tf_op jit(solution)/shard_map/all_to_all | solution.py:787
  47.2 9.1 %collective-permute-start.6 = (bf16[4,72,128]{2,1,0:T(8,128)(2,1)S(1)}, bf16[4,72,128]{2,1,0:T(8,128)(2,1)S(1)}, u32[]{:S(2)}, u32[]{:S(2)}) collective-permute-start(bf16[4,72,128]{2,1,0:T(8,128)(2,1)S(1)} %pad_maximum_fusion.2), channel_id=1, source_target_pairs={{0,8},{8,16},{16,24},{24,0},{1,9},{9,17},{17,25},{25,1},{2,10},{10... | collective-permute-start | bytes 221192 | tf_op jit(solution)/shard_map/ppermute | solution.py:628
  47.3 9.0 %collective-permute-start.7 = (bf16[4,72,128]{2,1,0:T(8,128)(2,1)S(1)}, bf16[4,72,128]{2,1,0:T(8,128)(2,1)S(1)}, u32[]{:S(2)}, u32[]{:S(2)}) collective-permute-start(bf16[4,72,128]{2,1,0:T(8,128)(2,1)S(1)} %pad_maximum_fusion.3), channel_id=1, source_target_pairs={{8,0},{16,8},{24,16},{0,24},{9,1},{17,9},{25,17},{1,25},{10,2},{18... | collective-permute-start | bytes 221192 | tf_op jit(solution)/shard_map/ppermute | solution.py:628

commit v6 on v5

--- a/solution.py
+++ b/solution.py
@@ -268,7 +268,8 @@
 
 def forward_kernel(
     control_hbm, sigma_hbm, east_ref, west_ref, kappa_ref, vertical_ref, table_ref, choice_ref,
-    out_ref, pick_ref, first_ref, second_ref, kap_ref, sigma_ref, sem_ref,
+    out_ref, pick_ref, rim_ref, rim_kap_ref, rim_sigma_ref, first_ref, second_ref, kap_ref,
+    sigma_ref, sem_ref,
 ):
     rows, cols, levels = control_hbm.shape
     tile_in = start_copies(
@@ -279,6 +280,8 @@
     put_sides(kap_ref, 0, rows, cols, east_ref[1], west_ref[1])
     wait_copies(tile_in)
     sigma_in = start_copies([(sigma_hbm, sigma_ref)], sem_ref, 1)
+    keep_rims(rim_ref, first_ref, rows)
+    keep_rims(rim_kap_ref, kap_ref, rows)
     done = sweeps(first_ref, second_ref, kap_ref, rows)
     channels = choice_ref.shape[1]
     table_rows = table_ref.shape[0]
@@ -286,6 +289,8 @@
     fill_picked(pick_ref, dot_tn(hot, table_ref[...]).astype(BF16))
     mixing = forward_mixing(vertical_ref[...])
     wait_copies(sigma_in)
+    rim_sigma_ref[0] = sigma_ref[:NSTEP]
+    rim_sigma_ref[1] = sigma_ref[rows - NSTEP :]
     count = 8
     for index in range((rows - 2 * NSTEP) // count):
         row = NSTEP + index * count
@@ -295,90 +300,59 @@
         )
 
 
+def keep_rims(rim_ref, wide_ref, rows):
+    span = 2 * NSTEP
+    for end, low in enumerate((0, rows - span)):
+        rim_ref[end * span : (end + 1) * span] = wide_ref[low : low + span]
+
+
 def pole_flags():
     at = lax.axis_index("lat")
     last = lax.axis_size("lat") - 1
     return jnp.where(at > 0, 1.0, 0.0), jnp.where(at < last, 1.0, 0.0)
 
 
-def put_rims(wide_ref, east_of, west_of, north, south, flags, rows, cols):
-    span = 2 * NSTEP
-    wide_ref[:NSTEP] = north.astype(F32) * flags[0]
-    put_sides(wide_ref, NSTEP, span, cols, east_of(0, span), west_of(0, span))
-    put_sides(
-        wide_ref, NSTEP + span, span, cols, east_of(rows - span, rows), west_of(rows - span, rows)
-    )
-    wide_ref[NSTEP + 2 * span :] = south.astype(F32) * flags[1]
-
-
-def rim_tiles(hbm, wide_ref):
-    span = 2 * NSTEP
-    rows, cols, _ = hbm.shape
-    return [
-        (hbm.at[pl.ds(0, span)], wide_ref.at[pl.ds(NSTEP, span), pl.ds(0, cols)]),
-        (hbm.at[pl.ds(rows - span, span)], wide_ref.at[pl.ds(NSTEP + span, span), pl.ds(0, cols)]),
-    ]
-
-
-def put_rim_kappa(kap_ref, kappa_ref, east_ref, west_ref, north_ref, south_ref, flags):
-    rows, cols = kappa_ref.shape
-    span = 2 * NSTEP
-    kap_ref[NSTEP : NSTEP + 2 * span, :cols, :] = spread_kappa(
-        jnp.concatenate([kappa_ref[:span, :], kappa_ref[rows - span :, :]], axis=0)
-    )
+def put_rims(wide_ref, rim_ref, north, south):
+    wide_ref[:NSTEP] = north
+    wide_ref[NSTEP : 5 * NSTEP] = rim_ref[...]
+    wide_ref[5 * NSTEP :] = south
+
+
+def ends_kernel(
+    rim_ref, rim_kap_ref, sigma_ref, north_ref, south_ref, vertical_ref, out_ref,
+    first_ref, second_ref, kap_ref,
+):
+    cols = sigma_ref.shape[2]
+    north_on, south_on = pole_flags()
     put_rims(
-        kap_ref,
-        lambda low, high: east_ref[1, low:high],
-        lambda low, high: west_ref[1, low:high],
-        north_ref[1],
-        south_ref[1],
-        flags,
-        rows,
-        cols,
-    )
+        kap_ref, rim_kap_ref, north_ref[1].astype(F32) * north_on,
+        south_ref[1].astype(F32) * south_on,
+    )
+    put_rims(
+        first_ref, rim_ref, north_ref[0].astype(F32) * north_on,
+        south_ref[0].astype(F32) * south_on,
+    )
+    done = sweeps(first_ref, second_ref, kap_ref, 6 * NSTEP)
+    mixing = forward_mixing(vertical_ref[...])
+    for end in range(2):
+        at = slice((1 + 3 * end) * NSTEP, (2 + 3 * end) * NSTEP)
+        out_ref[end] = project_rows(done[at, :cols, :], sigma_ref[end], mixing)
 
 
 def owner_kernel(
-    devices_all, quarter, recv_hbm, sigma_hbm, control_hbm, inner_ref, pick_ref, rinv_ref,
-    east_ref, west_ref, north_ref, south_ref, kappa_ref, vertical_ref,
+    devices_all, quarter, recv_hbm, sigma_hbm, inner_ref, ends_ref, pick_ref, rinv_ref,
     ret_hbm, adj_hbm, left_hbm, right_hbm, top_hbm, bottom_hbm,
-    word_ref, dep_ref, acc_ref, first_ref, second_ref, kap_ref, table_ref, pair_ref,
+    word_ref, dep_ref, acc_ref, table_ref, pair_ref,
     recv_ref, ret_ref, sigma_ref, adj_ref, left_ref, right_ref, top_ref, bottom_ref,
     sem_ref,
 ):
     lat_rows, cols, levels = sigma_hbm.shape
     cells_part = inner_ref.shape[0]
-    flags = pole_flags()
-    span = 2 * NSTEP
-    control_in = start_copies(rim_tiles(control_hbm, first_ref), sem_ref)
-    others_in = start_copies([(recv_hbm, recv_ref)], sem_ref, 2)
-    sigma_in = start_copies([(sigma_hbm, sigma_ref)], sem_ref, 3)
-    inside = slice(cols, cells_part - cols)
-    table_ref[inside, :] = inner_ref[inside, :]
-    put_rim_kappa(kap_ref, kappa_ref, east_ref, west_ref, north_ref, south_ref, flags)
-    put_rims(
-        first_ref,
-        lambda low, high: east_ref[0, low:high],
-        lambda low, high: west_ref[0, low:high],
-        north_ref[0],
-        south_ref[0],
-        flags,
-        lat_rows,
-        cols,
-    )
-    wait_copies(control_in)
-    done = sweeps(first_ref, second_ref, kap_ref, 6 * NSTEP)
-    wait_copies(sigma_in)
-    ends = project_rows(
-        jnp.concatenate(
-            [done[NSTEP : 2 * NSTEP, :cols, :], done[4 * NSTEP : 5 * NSTEP, :cols, :]], axis=0
-        ),
-        jnp.concatenate([sigma_ref[:NSTEP], sigma_ref[lat_rows - NSTEP :]], axis=0),
-        forward_mixing(vertical_ref[...]),
-    )
-    table_ref[:cols, :] = ends[:cols]
-    table_ref[cells_part - cols :, :] = ends[cols:]
-
+    others_in = start_copies([(recv_hbm, recv_ref)], sem_ref)
+    sigma_in = start_copies([(sigma_hbm, sigma_ref)], sem_ref, 1)
+    table_ref[:cols, :] = ends_ref[0]
+    table_ref[cols : cells_part - cols, :] = inner_ref[cols : cells_part - cols, :]
+    table_ref[cells_part - cols :, :] = ends_ref[1]
     wait_copies(others_in)
     rows_half = devices_all * quarter
     rows = 2 * rows_half
@@ -466,6 +440,7 @@
             acc_ref[...] += dot_tn(hots[side], wide)
     ret_ref[...] = (dep_ref[:rows_half, :] << 16) | dep_ref[rows_half:, :]
     copies = start_copies([(ret_ref, ret_hbm)], sem_ref)
+    wait_copies(sigma_in)
     groups = 4
     count = groups * 4
     for step in range(lat_rows // count):
@@ -526,10 +501,8 @@
     wait_copies(tile_in)
     control_in = start_copies([(control_hbm, control_ref)], sem_ref, 1)
     first_ref[:rows] = first_ref[:rows] * kap_ref[:rows]
-    span = 2 * NSTEP
-    for end, low in enumerate((0, rows - span)):
-        rim_ref[end * span : (end + 1) * span] = first_ref[low : low + span]
-        rim_kap_ref[end * span : (end + 1) * span] = kap_ref[low : low + span]
+    keep_rims(rim_ref, first_ref, rows)
+    keep_rims(rim_kap_ref, kap_ref, rows)
     done = sweeps(first_ref, second_ref, kap_ref, rows)
     mixing = backward_mixing(vertical_ref[...])
     wait_copies(control_in)
@@ -555,13 +528,14 @@
     lat_rows = out_ref.shape[0]
     cols = out_ref.shape[1]
     north_on, south_on = pole_flags()
-    tiles = slice(NSTEP, 5 * NSTEP)
-    kap_ref[:NSTEP] = knorth_ref[1].astype(F32) * north_on
-    kap_ref[tiles] = rim_kap_ref[...]
-    kap_ref[5 * NSTEP :] = ksouth_ref[1].astype(F32) * south_on
-    first_ref[:NSTEP] = north_ref[...].astype(F32) * kap_ref[:NSTEP]
-    first_ref[tiles] = rim_ref[...]
-    first_ref[5 * NSTEP :] = south_ref[...].astype(F32) * kap_ref[5 * NSTEP :]
+    put_rims(
+        kap_ref, rim_kap_ref, knorth_ref[1].astype(F32) * north_on,
+        ksouth_ref[1].astype(F32) * south_on,
+    )
+    put_rims(
+        first_ref, rim_ref, north_ref[...].astype(F32) * kap_ref[:NSTEP],
+        south_ref[...].astype(F32) * kap_ref[5 * NSTEP :],
+    )
     done = sweeps(first_ref, second_ref, kap_ref, 6 * NSTEP)
     mixing = backward_mixing(vertical_ref[...])
     copies = []
@@ -655,6 +629,7 @@
     rows_half = devices_all * quarter
     columns = lat_rows * lon_cols
     wide = (lat_rows + 1, lon_cols + 2 * NSTEP, levels)
+    rim_tile = (4 * NSTEP, lon_cols + 2 * NSTEP, levels)
     rim = (6 * NSTEP, lon_cols + 2 * NSTEP, levels)
     smem = pl.BlockSpec(memory_space=pltpu.SMEM)
     anywhere = pl.BlockSpec(memory_space=pl.ANY)
@@ -719,14 +694,17 @@
         with_sides(top, 0, NSTEP), with_sides(bottom, lat_rows - NSTEP, lat_rows)
     )
 
-    evolved, picked = pl.pallas_call(
+    evolved, picked, rim_state, rim_kappa, rim_sigma = pl.pallas_call(
         forward_kernel,
         out_shape=(
             pltpu.VMEM((columns // 4, 8 * channels), BF16),
             pltpu.VMEM((4 * channels, 4 * levels), BF16),
+            pltpu.VMEM(rim_tile, F32),
+            pltpu.VMEM(rim_tile, F32),
+            pltpu.VMEM((2, NSTEP, lon_cols, levels), F32),
         ),
         in_specs=[HBM_SPEC] * 2 + vmem_specs(6),
-        out_specs=tuple(vmem_specs(2)),
+        out_specs=tuple(vmem_specs(5)),
         scratch_shapes=[pltpu.VMEM(wide, F32)] * 3
         + [pltpu.VMEM(control.shape, F32), pltpu.SemaphoreType.DMA((2,))],
         compiler_params=params(24),
@@ -736,6 +714,17 @@
         control, sigma, east, west, kappa, vertical, channel_table,
         channel_pick.reshape(1, channels),
     )
+
+    ends = pl.pallas_call(
+        ends_kernel,
+        out_shape=pltpu.VMEM((2, lon_cols, 8 * channels), BF16),
+        in_specs=vmem_specs(6),
+        out_specs=vmem_specs(1)[0],
+        scratch_shapes=[pltpu.VMEM(rim, F32)] * 3,
+        compiler_params=params(12),
+        cost_estimate=estimate(1_000_000_000, 2_000_000),
+        name="ends",
+    )(rim_state, rim_kappa, rim_sigma, north, south, vertical)
 
     returned, adjoint, left, right, atop, abottom = pl.pallas_call(
         functools.partial(owner_kernel, devices_all, quarter),
@@ -747,15 +736,12 @@
             jax.ShapeDtypeStruct((NSTEP, lon_cols, levels), BF16),
             jax.ShapeDtypeStruct((NSTEP, lon_cols, levels), BF16),
         ),
-        in_specs=[HBM_SPEC] * 3 + vmem_specs(9),
+        in_specs=[HBM_SPEC] * 2 + vmem_specs(4),
         out_specs=(HBM_SPEC,) * 6,
         scratch_shapes=[
             pltpu.VMEM((rows_half, 128), I32),
             pltpu.VMEM((2 * rows_half, 128), I32),
             pltpu.VMEM((columns // 4, 4 * channels), F32),
-            pltpu.VMEM(rim, F32),
-            pltpu.VMEM(rim, F32),
-            pltpu.VMEM(rim, F32),
             pltpu.VMEM((columns // 4, 8 * channels), BF16),
             pltpu.VMEM((2 * channels, 2 * channels), F32),
             pltpu.VMEM((devices_all * (quarter + 1), 128), I32),
@@ -771,10 +757,7 @@
         compiler_params=params(28),
         cost_estimate=estimate(4_000_000_000, 16_000_000),
         name="owner",
-    )(
-        received, sigma, control, evolved, picked, r_inverse, east, west, north, south, kappa,
-        vertical,
-    )
+    )(received, sigma, evolved, ends, picked, r_inverse)
     returned = pl.pallas_call(
         pass_kernel,
         out_shape=pltpu.HBM(returned.shape, I32),
@@ -797,7 +780,6 @@
         jnp.concatenate([atop, aeast[:NSTEP], awest[:NSTEP]], axis=1),
         jnp.concatenate([abottom, aeast[-NSTEP:], awest[-NSTEP:]], axis=1),
     )
-    rim_tile = (4 * NSTEP, lon_cols + 2 * NSTEP, levels)
     inner, rim_scaled, rim_kappa, rim_control = pl.pallas_call(
         inner_kernel,
         out_shape=(

time: 61.1 us -> 60.6 us (level)
  starting transfers between devices: 23 us -> 24.5 us
  waiting for transfers between devices: 4.91 us -> 3.44 us
    pallas_call x1, Pallas kernels: 9.55 us -> 7.61 us  [body(): pl.pallas_call(functools.partial(owner_kernel, devices_all, quarter), out...]
    ppermute x2, starting transfers between devices: 8.29 us -> 9.71 us  [exchange_sides(): lax.ppermute(left, 'lon', backward)]
    all_to_all x1, waiting for transfers between devices: 2.49 us -> 1.1 us  [body(): lax.all_to_all(payload.reshape(devices_all, 1, (quarter + 1) * 128), ('la...]
    pallas_call x0 -> x1, Pallas kernels: none -> 1.38 us  [body(): pl.pallas_call(ends_kernel, out_shape=pltpu.VMEM((2, lon_cols, 8 * channe...]
  transfers between devices with their start and end apart: 10 -> 10, of which waited for: 3 -> 3; matrix products, arithmetic and copies ran while one was open for 0% -> 0% of each run, Pallas kernels for 30% -> 32%
where the time goes in v6:
time: 60.6 us; the launch traced here: 60.3 us
  Pallas kernels  30.6 us (50%)
  starting transfers between devices  24.5 us (40%)
  waiting for transfers between devices  3.44 us (6%)
  between operations  1.61 us (3%)
    ppermute x2, starting transfers between devices, exchange_sides(): lax.ppermute(left, 'lon', backward)  9.71 us
    pallas_call x1, Pallas kernels, body(): pl.pallas_call(functools.partial(owner_kernel, devices_all, quarter), out...  7.61 us
    pallas_call x1, Pallas kernels, body(): pl.pallas_call(inner_kernel, out_shape=(pltpu.HBM(control.shape, F32), pl...  7.22 us
    pallas_call x1, Pallas kernels, body(): pl.pallas_call(forward_kernel, out_shape=(pltpu.VMEM((columns // 4, 8 * c...  6.35 us
    all_to_all x1, starting transfers between devices, body(): lax.all_to_all(payload.reshape(devices_all, 1, (quarter + 1) * 128), ('la...  6.02 us
    all_to_all x1, starting transfers between devices, body(): lax.all_to_all(returned.reshape(devices_all, quarter, 128), ('lat', 'lon'...  5.26 us
    ppermute x2, starting transfers between devices, exchange_rims(): lax.ppermute(top, 'lat', backward)  3.35 us
    pallas_call x1, Pallas kernels, body(): pl.pallas_call(functools.partial(address_kernel, devices_all, quarter), o...  2.45 us
  transfers between devices with their start and end apart: 10, of which 3 were waited for; matrix products, arithmetic and copies ran while one was open for 0% of the time, Pallas kernels for 32%

profile of v6, /device:TPU:0, one launch (start us, length us, event | category | flops | bytes accessed | tf_op | source)
XLA Modules:
  0.0 60.3 jit_solution(7337910597716887180)
XLA Ops:
  0.7 1.2 %pack.1 = (bf16[2,64,4,128]{3,2,1,0:T(4,128)(2,1)S(1)}, bf16[2,64,4,128]{3,2,1,0:T(4,128)(2,1)S(1)}) custom-call(f32[64,64,128]{2,1,0:T(8,128)} %control_hbm.7, f32[64,64]{1,0:T(8,128)} %kappa_ref.5), custom_call_target="tpu_custom_call" | custom-call | tf_op jit(solution)/shard_map/pack/pallas_call | solution.py:638
  1.9 6.1 %collective-permute-start = (bf16[2,64,4,128]{3,2,1,0:T(4,128)(2,1)S(1)}, bf16[2,64,4,128]{3,2,1,0:T(4,128)(2,1)S(1)}, u32[]{:S(2)}, u32[]{:S(2)}) collective-permute-start(bf16[2,64,4,128]{3,2,1,0:T(4,128)(2,1)S(1)} %get-tuple-element.30), channel_id=1, source_target_pairs={{1,0},{2,1},{3,2},{4,3},{5,4},{6,5},{7,6},{0,7},{9,8},{10,9},{11,1... | collective-permute-start | bytes 393224 | tf_op jit(solution)/shard_map/ppermute | solution.py:597
  7.9 0.0 collective-permute-start.1
  8.6 0.0 copy-start
  8.6 0.0 copy-start.3
  8.6 0.0 copy-start.8
  8.7 2.4 %address.1 = (s32[544,128]{1,0:T(8,128)}, s32[1,1024]{1,0:T(1,128)S(1)}, bf16[2,4,64,128]{3,2,1,0:T(8,128)(2,1)S(1)}, bf16[2,4,64,128]{3,2,1,0:T(8,128)(2,1)S(1)}) custom-call(s32[1]{0:T(128)S(6)} %copy.19.count_ref, s32[1,1024]{1,0:T(1,128)S(1)} %bitcast.14, s32[1,1024]{1,0:T(1,128)S(1)} %bitcast.15, f32[1,1024]{1,0:T(1,128)S(1)} %bitcast.16, ...), custom_call_target="tpu_custom_call" | custom-call | flops 2000000000 | bytes 8000000 | tf_op jit(solution)/shard_map/address/pallas_call | solution.py:655
  11.1 6.0 %all-to-all-start = ((s32[32,1,2176]{2,1,0:T(1,128)}), s32[32,1,2176]{2,1,0:T(1,128)S(1)}, u32[]{:S(2)}, u32[]{:S(2)}) async-start(s32[32,1,2176]{2,1,0:T(1,128)} %bitcast.4), calls=%async_computation | async-start | bytes 557056 | tf_op jit(solution)/shard_map/all_to_all | solution.py:682
  17.1 0.0 collective-permute-done.east_ref.keast_ref
  17.2 0.0 collective-permute-done.1.west_ref.kwest_ref
  17.2 1.6 %collective-permute-start.3 = (bf16[2,4,72,128]{3,2,1,0:T(8,128)(2,1)S(1)}, bf16[2,4,72,128]{3,2,1,0:T(8,128)(2,1)S(1)}, u32[]{:S(2)}, u32[]{:S(2)}) collective-permute-start(bf16[2,4,72,128]{3,2,1,0:T(8,128)(2,1)S(1)} %pad_maximum_fusion.1), channel_id=1, source_target_pairs={{8,0},{16,8},{24,16},{0,24},{9,1},{17,9},{25,17},{1,25},{10,2},{18... | collective-permute-start | bytes 442376 | tf_op jit(solution)/shard_map/ppermute | solution.py:602
  18.8 0.1 collective-permute-start.2
  18.9 6.3 %forward.1 = (bf16[1024,512]{1,0:T(8,128)(2,1)S(1)}, bf16[256,512]{1,0:T(8,128)(2,1)S(1)}, f32[16,72,128]{2,1,0:T(8,128)S(1)}, f32[16,72,128]{2,1,0:T(8,128)S(1)}, f32[2,4,64,128]{3,2,1,0:T(8,128)S(1)}) custom-call(f32[64,64,128]{2,1,0:T(8,128)} %control_hbm.7, f32[64,64,128]{2,1,0:T(8,128)} %sigma_hbm.3, ...), custom_call_target="tpu_custom_call" | custom-call | flops 4000000000 | bytes 16000000 | tf_op jit(solution)/shard_map/forward/pallas_call | solution.py:697
  25.3 0.0 copy-start.4
  25.3 0.0 collective-permute-done.3.south_ref.ksouth_ref
  25.3 0.4 collective-permute-done.2.north_ref.knorth_ref
  25.7 1.4 %ends.1.ends_ref = bf16[2,64,512]{2,1,0:T(8,128)(2,1)S(1)} custom-call(f32[16,72,128]{2,1,0:T(8,128)S(1)} %get-tuple-element.33.rim_ref, f32[16,72,128]{2,1,0:T(8,128)S(1)} %get-tuple-element.34.rim_kap_ref, f32[2,4,64,128]{3,2,1,0:T(8,128)S(1)} %get-tuple-element.35.sigma_ref, bf16[2,4,72,128]{3,2,1,0:T(8,128)(2,1)S(1)} %collective-permute-done.2.north_ref.knorth_ref, ...), custom_call_target="tpu_custom_call" | custom-call | flops 1000000000 | bytes 2000000 | tf_op jit(solution)/shard_map/ends/pallas_call | solution.py:718
  27.1 1.1 %all-to-all-done = s32[32,1,2176]{2,1,0:T(1,128)S(1)} async-done(((s32[32,1,2176]{2,1,0:T(1,128)}), s32[32,1,2176]{2,1,0:T(1,128)S(1)}, u32[]{:S(2)}, u32[]{:S(2)}) %all-to-all-start) | async-done | bytes 278560 | tf_op jit(solution)/shard_map/all_to_all | solution.py:682
  28.2 7.6 %owner.1 = (s32[512,128]{1,0:T(8,128)}, f32[64,64,128]{2,1,0:T(8,128)}, bf16[64,4,128]{2,1,0:T(4,128)(2,1)}, bf16[64,4,128]{2,1,0:T(4,128)(2,1)}, bf16[4,64,128]...) custom-call(s32[544,128]{1,0:T(8,128)S(1)} %bitcast.10, f32[64,64,128]{2,1,0:T(8,128)} %sigma_hbm.3, ...), custom_call_target="tpu_custom_call" | custom-call | flops 4000000000 | bytes 16000000 | tf_op jit(solution)/shard_map/owner/pallas_call | solution.py:729
  35.8 3.7 %collective-permute-start.4 = (bf16[64,4,128]{2,1,0:T(4,128)(2,1)}, bf16[64,4,128]{2,1,0:T(4,128)(2,1)S(1)}, u32[]{:S(2)}, u32[]{:S(2)}) collective-permute-start(bf16[64,4,128]{2,1,0:T(4,128)(2,1)} %get-tuple-element.40.first_hbm), channel_id=1, source_target_pairs={{1,0},{2,1},{3,2},{4,3},{5,4},{6,5},{7,6},{0,7},{9,8},{10,9},{11,1... | collective-permute-start | bytes 196616 | tf_op jit(solution)/shard_map/ppermute | solution.py:597
  39.5 0.0 collective-permute-start.5
  39.5 5.3 %all-to-all-start.1 = ((s32[32,16,128]{2,1,0:T(8,128)}), s32[32,16,128]{2,1,0:T(8,128)S(1)}, u32[]{:S(2)}, u32[]{:S(2)}) async-start(s32[32,16,128]{2,1,0:T(8,128)} %bitcast.19), calls=%async_computation.1 | async-start | bytes 524288 | tf_op jit(solution)/shard_map/all_to_all | solution.py:770
  44.8 0.0 collective-permute-done.4.east_ref
  44.8 1.9 %collective-permute-done.5.west_ref = bf16[64,4,128]{2,1,0:T(4,128)(2,1)S(1)} collective-permute-done((bf16[64,4,128]{2,1,0:T(4,128)(2,1)}, bf16[64,4,128]{2,1,0:T(4,128)(2,1)S(1)}, u32[]{:S(2)}, u32[]{:S(2)}) %collective-permute-start.5) | collective-permute-done | bytes 65568 | tf_op jit(solution)/shard_map/ppermute | solution.py:597
  46.7 0.1 collective-permute-start.6
  46.8 1.8 %collective-permute-start.7 = (bf16[4,72,128]{2,1,0:T(8,128)(2,1)S(1)}, bf16[4,72,128]{2,1,0:T(8,128)(2,1)S(1)}, u32[]{:S(2)}, u32[]{:S(2)}) collective-permute-start(bf16[4,72,128]{2,1,0:T(8,128)(2,1)S(1)} %pad_maximum_fusion.3), channel_id=1, source_target_pairs={{8,0},{16,8},{24,16},{0,24},{9,1},{17,9},{25,17},{1,25},{10,2},{18... | collective-permute-start | bytes 221192 | tf_op jit(solution)/shard_map/ppermute | solution.py:602
  48.6 7.2 %inner.1 = (f32[64,64,128]{2,1,0:T(8,128)}, f32[16,72,128]{2,1,0:T(8,128)S(1)}, f32[16,72,128]{2,1,0:T(8,128)S(1)}, f32[2,4,64,128]{3,2,1,0:T(8,128)S(1)}) custom-call(f32[64,64,128]{2,1,0:T(8,128)} %get-tuple-element.39.adj_hbm, f32[64,64,128]{2,1,0:T(8,128)} %control_hbm.7, bf16[64,4,128]{2,1,0:T(4,128)(2,1)S(1)} %collective-permute-done.4.east_ref, ...), custom_call_target="tpu_custom_call" | custom-call | flops 4000000000 | bytes 16000000 | tf_op jit(solution)/shard_map/inner/pallas_call | solution.py:783
  55.8 0.0 collective-permute-done.6.north_ref
  55.8 0.0 collective-permute-done.7.south_ref
  55.8 2.2 %rims.1 = f32[64,64,128]{2,1,0:T(8,128)} custom-call(f32[16,72,128]{2,1,0:T(8,128)S(1)} %get-tuple-element.42.rim_ref, f32[16,72,128]{2,1,0:T(8,128)S(1)} %get-tuple-element.43.rim_kap_ref, f32[2,4,64,128]{3,2,1,0:T(8,128)S(1)} %get-tuple-element.44.control_ref, ...), custom_call_target="tpu_custom_call", output_to_operand_aliasing={{}: (8, {})} | custom-call | flops 1000000000 | bytes 2000000 | tf_op jit(solution)/shard_map/rims/pallas_call | solution.py:801
  58.0 0.0 all-to-all-done.1
  58.0 2.3 %give_back.1 = f32[64,1024]{1,0:T(8,128)} custom-call(s32[1]{0:T(128)S(6)} %copy.19.count_ref, s32[512,128]{1,0:T(8,128)S(1)} %bitcast.11, s32[1,1024]{1,0:T(1,128)S(1)} %get-tuple-element.49.key_ref, f32[64,1024]{1,0:T(8,128)S(1)} %bitcast.13, f32[1,1024]{1,0:T(1,128)S(1)} %bitcast.17, f32[64,64]{1,0:T(8,128)S(1)} %copy-done.4), custom_call_target="tpu_custom_call" | custom-call | flops 500000000 | bytes 2000000 | tf_op jit(solution)/shard_map/give_back/pallas_call | solution.py:819
  (23 shorter events, 0.1 us)
Async XLA Ops:
  0.6 7.9 %copy-start.1 = (f32[64,64]{1,0:T(8,128)S(1)}, f32[64,64]{1,0:T(8,128)}, u32[]{:S(2)}) copy-start(f32[64,64]{1,0:T(8,128)} %kappa_ref.5) | copy-start | bytes 49156
  0.6 7.9 %copy-start.6 = (s32[1024]{0:T(1024)S(1)}, s32[1024]{0:T(1024)}, u32[]{:S(2)}) copy-start(s32[1024]{0:T(1024)} %param.22) | copy-start | bytes 12292
  0.7 7.9 %copy-start.5 = (s32[1024,1]{0,1:T(1,128)S(1)}, s32[1024,1]{0,1:T(1,128)}, u32[]{:S(2)}) copy-start(s32[1024,1]{0,1:T(1,128)} %param.21) | copy-start | bytes 12292
  0.7 7.9 %copy-start.7 = (f32[1024]{0:T(1024)S(1)}, f32[1024]{0:T(1024)}, u32[]{:S(2)}) copy-start(f32[1024]{0:T(1024)} %param.20) | copy-start | bytes 12292
  0.7 7.9 %copy-start.2 = (f32[1024,64]{0,1:T(8,128)S(1)}, f32[1024,64]{0,1:T(8,128)}, u32[]{:S(2)}) copy-start(f32[1024,64]{0,1:T(8,128)} %param.19) | copy-start | bytes 786436
  1.9 15.3 %collective-permute-start = (bf16[2,64,4,128]{3,2,1,0:T(4,128)(2,1)S(1)}, bf16[2,64,4,128]{3,2,1,0:T(4,128)(2,1)S(1)}, u32[]{:S(2)}, u32[]{:S(2)}) collective-permute-start(bf16[2,64,4,128]{3,2,1,0:T(4,128)(2,1)S(1)} %get-tuple-element.30), channel_id=1, source_target_pairs={{1,0},{2,1},{3,2},{4,3},{5,4},{6,5},{7,6},{0,7},{9,8},{10,9},{11,1... | collective-permute-start | bytes 393224 | tf_op jit(solution)/shard_map/ppermute | solution.py:597
  7.9 9.3 %collective-permute-start.1 = (bf16[2,64,4,128]{3,2,1,0:T(4,128)(2,1)S(1)}, bf16[2,64,4,128]{3,2,1,0:T(4,128)(2,1)S(1)}, u32[]{:S(2)}, u32[]{:S(2)}) collective-permute-start(bf16[2,64,4,128]{3,2,1,0:T(4,128)(2,1)S(1)} %get-tuple-element.31), channel_id=1, source_target_pairs={{0,1},{1,2},{2,3},{3,4},{4,5},{5,6},{6,7},{7,0},{8,9},{9,10},{10,1... | collective-permute-start | bytes 393224 | tf_op jit(solution)/shard_map/ppermute | solution.py:597
  8.6 10.3 %copy-start = (f32[128,128]{1,0:T(8,128)S(1)}, f32[128,128]{1,0:T(8,128)}, u32[]{:S(2)}) copy-start(f32[128,128]{1,0:T(8,128)} %vertical_ref.7) | copy-start | bytes 196612
  8.6 10.3 %copy-start.3 = (bf16[616,128]{1,0:T(8,128)(2,1)S(1)}, bf16[616,128]{1,0:T(8,128)(2,1)}, u32[]{:S(2)}) copy-start(bf16[616,128]{1,0:T(8,128)(2,1)} %table_ref.1) | copy-start | bytes 473092
  8.6 10.3 %copy-start.8 = (s32[64]{0:T(128)S(1)}, s32[64]{0:T(128)}, u32[]{:S(2)}) copy-start(s32[64]{0:T(128)} %param.17) | copy-start | bytes 772
  11.1 17.1 %all-to-all-start = ((s32[32,1,2176]{2,1,0:T(1,128)}), s32[32,1,2176]{2,1,0:T(1,128)S(1)}, u32[]{:S(2)}, u32[]{:S(2)}) async-start(s32[32,1,2176]{2,1,0:T(1,128)} %bitcast.4), calls=%async_computation | async-start | bytes 557056 | tf_op jit(solution)/shard_map/all_to_all | solution.py:682
  17.2 8.1 %collective-permute-start.3 = (bf16[2,4,72,128]{3,2,1,0:T(8,128)(2,1)S(1)}, bf16[2,4,72,128]{3,2,1,0:T(8,128)(2,1)S(1)}, u32[]{:S(2)}, u32[]{:S(2)}) collective-permute-start(bf16[2,4,72,128]{3,2,1,0:T(8,128)(2,1)S(1)} %pad_maximum_fusion.1), channel_id=1, source_target_pairs={{8,0},{16,8},{24,16},{0,24},{9,1},{17,9},{25,17},{1,25},{10,2},{18... | collective-permute-start | bytes 442376 | tf_op jit(solution)/shard_map/ppermute | solution.py:602
  18.8 6.9 %collective-permute-start.2 = (bf16[2,4,72,128]{3,2,1,0:T(8,128)(2,1)S(1)}, bf16[2,4,72,128]{3,2,1,0:T(8,128)(2,1)S(1)}, u32[]{:S(2)}, u32[]{:S(2)}) collective-permute-start(bf16[2,4,72,128]{3,2,1,0:T(8,128)(2,1)S(1)} %pad_maximum_fusion), channel_id=1, source_target_pairs={{0,8},{8,16},{16,24},{24,0},{1,9},{9,17},{17,25},{25,1},{2,10},{10... | collective-permute-start | bytes 442376 | tf_op jit(solution)/shard_map/ppermute | solution.py:602
  25.3 3.0 %copy-start.4 = (f32[64,64]{1,0:T(8,128)S(1)}, f32[64,64]{1,0:T(8,128)}, u32[]{:S(2)}) copy-start(f32[64,64]{1,0:T(8,128)} %rinv_ref.3) | copy-start | bytes 49156
  35.8 8.9 %collective-permute-start.4 = (bf16[64,4,128]{2,1,0:T(4,128)(2,1)}, bf16[64,4,128]{2,1,0:T(4,128)(2,1)S(1)}, u32[]{:S(2)}, u32[]{:S(2)}) collective-permute-start(bf16[64,4,128]{2,1,0:T(4,128)(2,1)} %get-tuple-element.40.first_hbm), channel_id=1, source_target_pairs={{1,0},{2,1},{3,2},{4,3},{5,4},{6,5},{7,6},{0,7},{9,8},{10,9},{11,1... | collective-permute-start | bytes 196616 | tf_op jit(solution)/shard_map/ppermute | solution.py:597
  39.5 7.2 %collective-permute-start.5 = (bf16[64,4,128]{2,1,0:T(4,128)(2,1)}, bf16[64,4,128]{2,1,0:T(4,128)(2,1)S(1)}, u32[]{:S(2)}, u32[]{:S(2)}) collective-permute-start(bf16[64,4,128]{2,1,0:T(4,128)(2,1)} %get-tuple-element.41.second_hbm), channel_id=1, source_target_pairs={{0,1},{1,2},{2,3},{3,4},{4,5},{5,6},{6,7},{7,0},{8,9},{9,10},{10,1... | collective-permute-start | bytes 196616 | tf_op jit(solution)/shard_map/ppermute | solution.py:597
  39.5 18.5 %all-to-all-start.1 = ((s32[32,16,128]{2,1,0:T(8,128)}), s32[32,16,128]{2,1,0:T(8,128)S(1)}, u32[]{:S(2)}, u32[]{:S(2)}) async-start(s32[32,16,128]{2,1,0:T(8,128)} %bitcast.19), calls=%async_computation.1 | async-start | bytes 524288 | tf_op jit(solution)/shard_map/all_to_all | solution.py:770
  46.7 9.1 %collective-permute-start.6 = (bf16[4,72,128]{2,1,0:T(8,128)(2,1)S(1)}, bf16[4,72,128]{2,1,0:T(8,128)(2,1)S(1)}, u32[]{:S(2)}, u32[]{:S(2)}) collective-permute-start(bf16[4,72,128]{2,1,0:T(8,128)(2,1)S(1)} %pad_maximum_fusion.2), channel_id=1, source_target_pairs={{0,8},{8,16},{16,24},{24,0},{1,9},{9,17},{17,25},{25,1},{2,10},{10... | collective-permute-start | bytes 221192 | tf_op jit(solution)/shard_map/ppermute | solution.py:602
  46.8 9.0 %collective-permute-start.7 = (bf16[4,72,128]{2,1,0:T(8,128)(2,1)S(1)}, bf16[4,72,128]{2,1,0:T(8,128)(2,1)S(1)}, u32[]{:S(2)}, u32[]{:S(2)}) collective-permute-start(bf16[4,72,128]{2,1,0:T(8,128)(2,1)S(1)} %pad_maximum_fusion.3), channel_id=1, source_target_pairs={{8,0},{16,8},{24,16},{0,24},{9,1},{17,9},{25,17},{1,25},{10,2},{18... | collective-permute-start | bytes 221192 | tf_op jit(solution)/shard_map/ppermute | solution.py:602

commit v7 on v6

--- a/solution.py
+++ b/solution.py
@@ -168,9 +168,16 @@
     bottom_ref[0] = ends_ref[1].astype(BF16)
 
 
+LEAD = 16
+
+
+def tile_of(cols):
+    return slice(LEAD, LEAD + cols)
+
+
 def put_sides(wide_ref, at, count, cols, east, west):
-    wide_ref[at : at + count, cols : cols + NSTEP, :] = east.astype(F32)
-    wide_ref[at : at + count, cols + NSTEP :, :] = west.astype(F32)
+    wide_ref[at : at + count, LEAD + cols : LEAD + cols + NSTEP, :] = east.astype(F32)
+    wide_ref[at : at + count, LEAD - NSTEP : LEAD, :] = west.astype(F32)
 
 
 def spread_kappa(kappa, low=0, high=None):
@@ -207,18 +214,19 @@
 
 
 def sweep_rows(source, target, kap_ref, low, high, block=8):
-    cols = source.shape[1]
+    width = source.shape[1]
+    here_at = slice(8, width - 8)
 
     def update(first, count):
-        rows = [source[first + i] for i in range(-1, count + 1)]
+        rows = [source[first + i, here_at, :] for i in range(-1, count + 1)]
         for i in range(count):
             here = rows[i + 1]
             change = (
                 (rows[i] + rows[i + 2])
-                + (pltpu.roll(here, 1, 0) + pltpu.roll(here, cols - 1, 0))
+                + (source[first + i, 7 : width - 9, :] + source[first + i, 9 : width - 7, :])
                 - 4.0 * here
             )
-            target[first + i] = here + kap_ref[first + i] * change
+            target[first + i, here_at, :] = here + kap_ref[first + i, here_at, :] * change
 
     whole = (high - low) // block
 
@@ -273,10 +281,10 @@
 ):
     rows, cols, levels = control_hbm.shape
     tile_in = start_copies(
-        [(control_hbm, first_ref.at[pl.ds(0, rows), pl.ds(0, cols)])], sem_ref
+        [(control_hbm, first_ref.at[pl.ds(0, rows), pl.ds(LEAD, cols)])], sem_ref
     )
     put_sides(first_ref, 0, rows, cols, east_ref[0], west_ref[0])
-    kap_ref[:rows, :cols, :] = spread_kappa(kappa_ref[...])
+    kap_ref[:rows, tile_of(cols), :] = spread_kappa(kappa_ref[...])
     put_sides(kap_ref, 0, rows, cols, east_ref[1], west_ref[1])
     wait_copies(tile_in)
     sigma_in = start_copies([(sigma_hbm, sigma_ref)], sem_ref, 1)
@@ -296,7 +304,7 @@
         row = NSTEP + index * count
         where = pl.ds(row // 4 * cols, count // 4 * cols)
         out_ref[where, :] = project_rows(
-            done[row : row + count, :cols, :], sigma_ref[row : row + count], mixing
+            done[row : row + count, tile_of(cols), :], sigma_ref[row : row + count], mixing
         )
 
 
@@ -312,10 +320,13 @@
     return jnp.where(at > 0, 1.0, 0.0), jnp.where(at < last, 1.0, 0.0)
 
 
-def put_rims(wide_ref, rim_ref, north, south):
-    wide_ref[:NSTEP] = north
+def put_rims(wide_ref, rim_ref, north, south, cols):
     wide_ref[NSTEP : 5 * NSTEP] = rim_ref[...]
-    wide_ref[5 * NSTEP :] = south
+    for at, rim in ((0, north), (5 * NSTEP, south)):
+        wide_ref[at : at + NSTEP, tile_of(cols), :] = rim[:, :cols]
+        put_sides(
+            wide_ref, at, NSTEP, cols, rim[:, cols : cols + NSTEP], rim[:, cols + NSTEP :]
+        )
 
 
 def ends_kernel(
@@ -326,17 +337,17 @@
     north_on, south_on = pole_flags()
     put_rims(
         kap_ref, rim_kap_ref, north_ref[1].astype(F32) * north_on,
-        south_ref[1].astype(F32) * south_on,
+        south_ref[1].astype(F32) * south_on, cols,
     )
     put_rims(
         first_ref, rim_ref, north_ref[0].astype(F32) * north_on,
-        south_ref[0].astype(F32) * south_on,
+        south_ref[0].astype(F32) * south_on, cols,
     )
     done = sweeps(first_ref, second_ref, kap_ref, 6 * NSTEP)
     mixing = forward_mixing(vertical_ref[...])
     for end in range(2):
         at = slice((1 + 3 * end) * NSTEP, (2 + 3 * end) * NSTEP)
-        out_ref[end] = project_rows(done[at, :cols, :], sigma_ref[end], mixing)
+        out_ref[end] = project_rows(done[at, tile_of(cols), :], sigma_ref[end], mixing)
 
 
 def owner_kernel(
@@ -494,8 +505,8 @@
     control_ref, sem_ref,
 ):
     rows, cols, levels = control_hbm.shape
-    tile_in = start_copies([(adj_hbm, first_ref.at[pl.ds(0, rows), pl.ds(0, cols)])], sem_ref)
-    kap_ref[:rows, :cols, :] = spread_kappa(kappa_ref[...])
+    tile_in = start_copies([(adj_hbm, first_ref.at[pl.ds(0, rows), pl.ds(LEAD, cols)])], sem_ref)
+    kap_ref[:rows, tile_of(cols), :] = spread_kappa(kappa_ref[...])
     put_sides(kap_ref, 0, rows, cols, keast_ref[1], kwest_ref[1])
     put_sides(first_ref, 0, rows, cols, east_ref[...], west_ref[...])
     wait_copies(tile_in)
@@ -514,7 +525,7 @@
         row = NSTEP + index * count
         at = pl.ds(row, count)
         out_ref[at] = control_ref[at] + finish_rows(
-            done[row : row + count, :cols, :], kap_ref[row : row + count, :cols, :], mixing
+            done[row : row + count, tile_of(cols), :], kap_ref[row : row + count, tile_of(cols), :], mixing
         )
         copies += start_copies([(out_ref.at[at], out_hbm.at[at])], sem_ref, index)
     wait_copies(copies)
@@ -530,18 +541,19 @@
     north_on, south_on = pole_flags()
     put_rims(
         kap_ref, rim_kap_ref, knorth_ref[1].astype(F32) * north_on,
-        ksouth_ref[1].astype(F32) * south_on,
+        ksouth_ref[1].astype(F32) * south_on, cols,
     )
     put_rims(
-        first_ref, rim_ref, north_ref[...].astype(F32) * kap_ref[:NSTEP],
-        south_ref[...].astype(F32) * kap_ref[5 * NSTEP :],
-    )
+        first_ref, rim_ref, north_ref[...].astype(F32), south_ref[...].astype(F32), cols
+    )
+    for at in (0, 5 * NSTEP):
+        first_ref[at : at + NSTEP] = first_ref[at : at + NSTEP] * kap_ref[at : at + NSTEP]
     done = sweeps(first_ref, second_ref, kap_ref, 6 * NSTEP)
     mixing = backward_mixing(vertical_ref[...])
     copies = []
     for end in range(2):
         at = pl.ds((1 + 3 * end) * NSTEP, NSTEP)
-        back = finish_rows(done[at, :cols, :], kap_ref[at, :cols, :], mixing)
+        back = finish_rows(done[at, tile_of(cols), :], kap_ref[at, tile_of(cols), :], mixing)
         edge_ref[end] = control_ref[end] + back
         copies += start_copies(
             [(edge_ref.at[end], out_ref.at[pl.ds(end * (lat_rows - NSTEP), NSTEP)])], sem_ref, end
@@ -628,9 +640,9 @@
     quarter = capacity // 4
     rows_half = devices_all * quarter
     columns = lat_rows * lon_cols
-    wide = (lat_rows + 1, lon_cols + 2 * NSTEP, levels)
-    rim_tile = (4 * NSTEP, lon_cols + 2 * NSTEP, levels)
-    rim = (6 * NSTEP, lon_cols + 2 * NSTEP, levels)
+    wide = (lat_rows + 1, lon_cols + 2 * LEAD, levels)
+    rim_tile = (4 * NSTEP, lon_cols + 2 * LEAD, levels)
+    rim = (6 * NSTEP, lon_cols + 2 * LEAD, levels)
     smem = pl.BlockSpec(memory_space=pltpu.SMEM)
     anywhere = pl.BlockSpec(memory_space=pl.ANY)
 

time: 60.6 us -> 59.4 us (0.980)
  Pallas kernels: 30.6 us -> 28.6 us
  waiting for transfers between devices: 3.44 us -> 4.49 us
    ppermute x2, waiting for transfers between devices: 0.45 us -> 1.27 us  [exchange_rims(): lax.ppermute(bottom, 'lat', forward)]
    pallas_call x1, Pallas kernels: 6.35 us -> 5.53 us  [body(): pl.pallas_call(forward_kernel, out_shape=(pltpu.VMEM((columns // 4, 8 * c...]
    pallas_call x1, Pallas kernels: 7.22 us -> 6.45 us  [body(): pl.pallas_call(inner_kernel, out_shape=(pltpu.HBM(control.shape, F32), pl...]
  transfers between devices with their start and end apart: 10 -> 10, of which waited for: 3 -> 3; matrix products, arithmetic and copies ran while one was open for 0% -> 0% of each run, Pallas kernels for 32% -> 30%
where the time goes in v7:
time: 59.4 us; the launch traced here: 59.1 us
  Pallas kernels  28.6 us (48%)
  starting transfers between devices  24.2 us (41%)
  waiting for transfers between devices  4.49 us (8%)
  between operations  1.61 us (3%)
    ppermute x2, starting transfers between devices, exchange_sides(): lax.ppermute(left, 'lon', backward)  9.47 us
    pallas_call x1, Pallas kernels, body(): pl.pallas_call(functools.partial(owner_kernel, devices_all, quarter), out...  7.61 us
    pallas_call x1, Pallas kernels, body(): pl.pallas_call(inner_kernel, out_shape=(pltpu.HBM(control.shape, F32), pl...  6.45 us
    all_to_all x1, starting transfers between devices, body(): lax.all_to_all(payload.reshape(devices_all, 1, (quarter + 1) * 128), ('la...  6.02 us
    pallas_call x1, Pallas kernels, body(): pl.pallas_call(forward_kernel, out_shape=(pltpu.VMEM((columns // 4, 8 * c...  5.53 us
    all_to_all x1, starting transfers between devices, body(): lax.all_to_all(returned.reshape(devices_all, quarter, 128), ('lat', 'lon'...  5.26 us
    ppermute x2, starting transfers between devices, exchange_rims(): lax.ppermute(top, 'lat', backward)  3.35 us
    pallas_call x1, Pallas kernels, body(): pl.pallas_call(functools.partial(address_kernel, devices_all, quarter), o...  2.45 us
  transfers between devices with their start and end apart: 10, of which 3 were waited for; matrix products, arithmetic and copies ran while one was open for 0% of the time, Pallas kernels for 30%

profile of v7, /device:TPU:0, one launch (start us, length us, event | category | flops | bytes accessed | tf_op | source)
XLA Modules:
  0.0 59.1 jit_solution(6626482145581506075)
XLA Ops:
  0.7 1.2 %pack.1 = (bf16[2,64,4,128]{3,2,1,0:T(4,128)(2,1)S(1)}, bf16[2,64,4,128]{3,2,1,0:T(4,128)(2,1)S(1)}) custom-call(f32[64,64,128]{2,1,0:T(8,128)} %control_hbm.7, f32[64,64]{1,0:T(8,128)} %kappa_ref.5), custom_call_target="tpu_custom_call" | custom-call | tf_op jit(solution)/shard_map/pack/pallas_call | solution.py:650
  1.9 6.1 %collective-permute-start = (bf16[2,64,4,128]{3,2,1,0:T(4,128)(2,1)S(1)}, bf16[2,64,4,128]{3,2,1,0:T(4,128)(2,1)S(1)}, u32[]{:S(2)}, u32[]{:S(2)}) collective-permute-start(bf16[2,64,4,128]{3,2,1,0:T(4,128)(2,1)S(1)} %get-tuple-element.30), channel_id=1, source_target_pairs={{1,0},{2,1},{3,2},{4,3},{5,4},{6,5},{7,6},{0,7},{9,8},{10,9},{11,1... | collective-permute-start | bytes 393224 | tf_op jit(solution)/shard_map/ppermute | solution.py:609
  7.9 0.0 collective-permute-start.1
  8.6 0.0 copy-start
  8.6 0.0 copy-start.3
  8.6 0.0 copy-start.8
  8.7 2.4 %address.1 = (s32[544,128]{1,0:T(8,128)}, s32[1,1024]{1,0:T(1,128)S(1)}, bf16[2,4,64,128]{3,2,1,0:T(8,128)(2,1)S(1)}, bf16[2,4,64,128]{3,2,1,0:T(8,128)(2,1)S(1)}) custom-call(s32[1]{0:T(128)S(6)} %copy.19.count_ref, s32[1,1024]{1,0:T(1,128)S(1)} %bitcast.14, s32[1,1024]{1,0:T(1,128)S(1)} %bitcast.15, f32[1,1024]{1,0:T(1,128)S(1)} %bitcast.16, ...), custom_call_target="tpu_custom_call" | custom-call | flops 2000000000 | bytes 8000000 | tf_op jit(solution)/shard_map/address/pallas_call | solution.py:667
  11.1 6.0 %all-to-all-start = ((s32[32,1,2176]{2,1,0:T(1,128)}), s32[32,1,2176]{2,1,0:T(1,128)S(1)}, u32[]{:S(2)}, u32[]{:S(2)}) async-start(s32[32,1,2176]{2,1,0:T(1,128)} %bitcast.4), calls=%async_computation | async-start | bytes 557056 | tf_op jit(solution)/shard_map/all_to_all | solution.py:694
  17.1 0.0 collective-permute-done.east_ref.keast_ref
  17.2 0.0 collective-permute-done.1.west_ref.kwest_ref
  17.2 1.6 %collective-permute-start.3 = (bf16[2,4,72,128]{3,2,1,0:T(8,128)(2,1)S(1)}, bf16[2,4,72,128]{3,2,1,0:T(8,128)(2,1)S(1)}, u32[]{:S(2)}, u32[]{:S(2)}) collective-permute-start(bf16[2,4,72,128]{3,2,1,0:T(8,128)(2,1)S(1)} %pad_maximum_fusion.1), channel_id=1, source_target_pairs={{8,0},{16,8},{24,16},{0,24},{9,1},{17,9},{25,17},{1,25},{10,2},{18... | collective-permute-start | bytes 442376 | tf_op jit(solution)/shard_map/ppermute | solution.py:614
  18.8 0.1 collective-permute-start.2
  18.9 5.5 %forward.1 = (bf16[1024,512]{1,0:T(8,128)(2,1)S(1)}, bf16[256,512]{1,0:T(8,128)(2,1)S(1)}, f32[16,96,128]{2,1,0:T(8,128)S(1)}, f32[16,96,128]{2,1,0:T(8,128)S(1)}, f32[2,4,64,128]{3,2,1,0:T(8,128)S(1)}) custom-call(f32[64,64,128]{2,1,0:T(8,128)} %control_hbm.7, f32[64,64,128]{2,1,0:T(8,128)} %sigma_hbm.3, ...), custom_call_target="tpu_custom_call" | custom-call | flops 4000000000 | bytes 16000000 | tf_op jit(solution)/shard_map/forward/pallas_call | solution.py:709
  24.4 0.0 copy-start.4
  24.5 0.0 collective-permute-done.3.south_ref.ksouth_ref
  24.5 1.3 %collective-permute-done.2.north_ref.knorth_ref = bf16[2,4,72,128]{3,2,1,0:T(8,128)(2,1)S(1)} collective-permute-done((bf16[2,4,72,128]{3,2,1,0:T(8,128)(2,1)S(1)}, bf16[2,4,72,128]{3,2,1,0:T(8,128)(2,1)S(1)}, u32[]{:S(2)}, u32[]{:S(2)}) %collective-permute-start.2) | collective-permute-done | bytes 147488 | tf_op jit(solution)/shard_map/ppermute | solution.py:614
  25.7 1.2 %ends.1.ends_ref = bf16[2,64,512]{2,1,0:T(8,128)(2,1)S(1)} custom-call(f32[16,96,128]{2,1,0:T(8,128)S(1)} %get-tuple-element.33.rim_ref, f32[16,96,128]{2,1,0:T(8,128)S(1)} %get-tuple-element.34.rim_kap_ref, f32[2,4,64,128]{3,2,1,0:T(8,128)S(1)} %get-tuple-element.35.sigma_ref, bf16[2,4,72,128]{3,2,1,0:T(8,128)(2,1)S(1)} %collective-permute-done.2.north_ref.knorth_ref, ...), custom_call_target="tpu_custom_call" | custom-call | flops 1000000000 | bytes 2000000 | tf_op jit(solution)/shard_map/ends/pallas_call | solution.py:730
  26.9 1.3 %all-to-all-done = s32[32,1,2176]{2,1,0:T(1,128)S(1)} async-done(((s32[32,1,2176]{2,1,0:T(1,128)}), s32[32,1,2176]{2,1,0:T(1,128)S(1)}, u32[]{:S(2)}, u32[]{:S(2)}) %all-to-all-start) | async-done | bytes 278560 | tf_op jit(solution)/shard_map/all_to_all | solution.py:694
  28.2 7.6 %owner.1 = (s32[512,128]{1,0:T(8,128)}, f32[64,64,128]{2,1,0:T(8,128)}, bf16[64,4,128]{2,1,0:T(4,128)(2,1)}, bf16[64,4,128]{2,1,0:T(4,128)(2,1)}, bf16[4,64,128]...) custom-call(s32[544,128]{1,0:T(8,128)S(1)} %bitcast.10, f32[64,64,128]{2,1,0:T(8,128)} %sigma_hbm.3, ...), custom_call_target="tpu_custom_call" | custom-call | flops 4000000000 | bytes 16000000 | tf_op jit(solution)/shard_map/owner/pallas_call | solution.py:741
  35.8 3.4 %collective-permute-start.4 = (bf16[64,4,128]{2,1,0:T(4,128)(2,1)}, bf16[64,4,128]{2,1,0:T(4,128)(2,1)S(1)}, u32[]{:S(2)}, u32[]{:S(2)}) collective-permute-start(bf16[64,4,128]{2,1,0:T(4,128)(2,1)} %get-tuple-element.40.first_hbm), channel_id=1, source_target_pairs={{1,0},{2,1},{3,2},{4,3},{5,4},{6,5},{7,6},{0,7},{9,8},{10,9},{11,1... | collective-permute-start | bytes 196616 | tf_op jit(solution)/shard_map/ppermute | solution.py:609
  39.3 0.0 collective-permute-start.5
  39.3 5.3 %all-to-all-start.1 = ((s32[32,16,128]{2,1,0:T(8,128)}), s32[32,16,128]{2,1,0:T(8,128)S(1)}, u32[]{:S(2)}, u32[]{:S(2)}) async-start(s32[32,16,128]{2,1,0:T(8,128)} %bitcast.19), calls=%async_computation.1 | async-start | bytes 524288 | tf_op jit(solution)/shard_map/all_to_all | solution.py:782
  44.5 0.0 collective-permute-done.4.east_ref
  44.6 1.9 %collective-permute-done.5.west_ref = bf16[64,4,128]{2,1,0:T(4,128)(2,1)S(1)} collective-permute-done((bf16[64,4,128]{2,1,0:T(4,128)(2,1)}, bf16[64,4,128]{2,1,0:T(4,128)(2,1)S(1)}, u32[]{:S(2)}, u32[]{:S(2)}) %collective-permute-start.5) | collective-permute-done | bytes 65568 | tf_op jit(solution)/shard_map/ppermute | solution.py:609
  46.5 0.1 collective-permute-start.6
  46.5 1.8 %collective-permute-start.7 = (bf16[4,72,128]{2,1,0:T(8,128)(2,1)S(1)}, bf16[4,72,128]{2,1,0:T(8,128)(2,1)S(1)}, u32[]{:S(2)}, u32[]{:S(2)}) collective-permute-start(bf16[4,72,128]{2,1,0:T(8,128)(2,1)S(1)} %pad_maximum_fusion.3), channel_id=1, source_target_pairs={{8,0},{16,8},{24,16},{0,24},{9,1},{17,9},{25,17},{1,25},{10,2},{18... | collective-permute-start | bytes 221192 | tf_op jit(solution)/shard_map/ppermute | solution.py:614
  48.3 6.5 %inner.1 = (f32[64,64,128]{2,1,0:T(8,128)}, f32[16,96,128]{2,1,0:T(8,128)S(1)}, f32[16,96,128]{2,1,0:T(8,128)S(1)}, f32[2,4,64,128]{3,2,1,0:T(8,128)S(1)}) custom-call(f32[64,64,128]{2,1,0:T(8,128)} %get-tuple-element.39.adj_hbm, f32[64,64,128]{2,1,0:T(8,128)} %control_hbm.7, bf16[64,4,128]{2,1,0:T(4,128)(2,1)S(1)} %collective-permute-done.4.east_ref, ...), custom_call_target="tpu_custom_call" | custom-call | flops 4000000000 | bytes 16000000 | tf_op jit(solution)/shard_map/inner/pallas_call | solution.py:795
  54.8 0.0 collective-permute-done.6.north_ref
  54.8 0.0 collective-permute-done.7.south_ref
  54.8 1.9 %rims.1 = f32[64,64,128]{2,1,0:T(8,128)} custom-call(f32[16,96,128]{2,1,0:T(8,128)S(1)} %get-tuple-element.42.rim_ref, f32[16,96,128]{2,1,0:T(8,128)S(1)} %get-tuple-element.43.rim_kap_ref, f32[2,4,64,128]{3,2,1,0:T(8,128)S(1)} %get-tuple-element.44.control_ref, ...), custom_call_target="tpu_custom_call", output_to_operand_aliasing={{}: (8, {})} | custom-call | flops 1000000000 | bytes 2000000 | tf_op jit(solution)/shard_map/rims/pallas_call | solution.py:813
  56.7 0.0 all-to-all-done.1
  56.8 2.3 %give_back.1 = f32[64,1024]{1,0:T(8,128)} custom-call(s32[1]{0:T(128)S(6)} %copy.19.count_ref, s32[512,128]{1,0:T(8,128)S(1)} %bitcast.11, s32[1,1024]{1,0:T(1,128)S(1)} %get-tuple-element.49.key_ref, f32[64,1024]{1,0:T(8,128)S(1)} %bitcast.13, f32[1,1024]{1,0:T(1,128)S(1)} %bitcast.17, f32[64,64]{1,0:T(8,128)S(1)} %copy-done.4), custom_call_target="tpu_custom_call" | custom-call | flops 500000000 | bytes 2000000 | tf_op jit(solution)/shard_map/give_back/pallas_call | solution.py:831
  (23 shorter events, 0.1 us)
Async XLA Ops:
  0.6 7.9 %copy-start.1 = (f32[64,64]{1,0:T(8,128)S(1)}, f32[64,64]{1,0:T(8,128)}, u32[]{:S(2)}) copy-start(f32[64,64]{1,0:T(8,128)} %kappa_ref.5) | copy-start | bytes 49156
  0.6 7.9 %copy-start.6 = (s32[1024]{0:T(1024)S(1)}, s32[1024]{0:T(1024)}, u32[]{:S(2)}) copy-start(s32[1024]{0:T(1024)} %param.22) | copy-start | bytes 12292
  0.7 7.9 %copy-start.5 = (s32[1024,1]{0,1:T(1,128)S(1)}, s32[1024,1]{0,1:T(1,128)}, u32[]{:S(2)}) copy-start(s32[1024,1]{0,1:T(1,128)} %param.21) | copy-start | bytes 12292
  0.7 7.9 %copy-start.7 = (f32[1024]{0:T(1024)S(1)}, f32[1024]{0:T(1024)}, u32[]{:S(2)}) copy-start(f32[1024]{0:T(1024)} %param.20) | copy-start | bytes 12292
  0.7 7.9 %copy-start.2 = (f32[1024,64]{0,1:T(8,128)S(1)}, f32[1024,64]{0,1:T(8,128)}, u32[]{:S(2)}) copy-start(f32[1024,64]{0,1:T(8,128)} %param.19) | copy-start | bytes 786436
  1.9 15.3 %collective-permute-start = (bf16[2,64,4,128]{3,2,1,0:T(4,128)(2,1)S(1)}, bf16[2,64,4,128]{3,2,1,0:T(4,128)(2,1)S(1)}, u32[]{:S(2)}, u32[]{:S(2)}) collective-permute-start(bf16[2,64,4,128]{3,2,1,0:T(4,128)(2,1)S(1)} %get-tuple-element.30), channel_id=1, source_target_pairs={{1,0},{2,1},{3,2},{4,3},{5,4},{6,5},{7,6},{0,7},{9,8},{10,9},{11,1... | collective-permute-start | bytes 393224 | tf_op jit(solution)/shard_map/ppermute | solution.py:609
  7.9 9.3 %collective-permute-start.1 = (bf16[2,64,4,128]{3,2,1,0:T(4,128)(2,1)S(1)}, bf16[2,64,4,128]{3,2,1,0:T(4,128)(2,1)S(1)}, u32[]{:S(2)}, u32[]{:S(2)}) collective-permute-start(bf16[2,64,4,128]{3,2,1,0:T(4,128)(2,1)S(1)} %get-tuple-element.31), channel_id=1, source_target_pairs={{0,1},{1,2},{2,3},{3,4},{4,5},{5,6},{6,7},{7,0},{8,9},{9,10},{10,1... | collective-permute-start | bytes 393224 | tf_op jit(solution)/shard_map/ppermute | solution.py:609
  8.6 10.3 %copy-start = (f32[128,128]{1,0:T(8,128)S(1)}, f32[128,128]{1,0:T(8,128)}, u32[]{:S(2)}) copy-start(f32[128,128]{1,0:T(8,128)} %vertical_ref.7) | copy-start | bytes 196612
  8.6 10.3 %copy-start.3 = (bf16[616,128]{1,0:T(8,128)(2,1)S(1)}, bf16[616,128]{1,0:T(8,128)(2,1)}, u32[]{:S(2)}) copy-start(bf16[616,128]{1,0:T(8,128)(2,1)} %table_ref.1) | copy-start | bytes 473092
  8.6 10.3 %copy-start.8 = (s32[64]{0:T(128)S(1)}, s32[64]{0:T(128)}, u32[]{:S(2)}) copy-start(s32[64]{0:T(128)} %param.17) | copy-start | bytes 772
  11.1 17.1 %all-to-all-start = ((s32[32,1,2176]{2,1,0:T(1,128)}), s32[32,1,2176]{2,1,0:T(1,128)S(1)}, u32[]{:S(2)}, u32[]{:S(2)}) async-start(s32[32,1,2176]{2,1,0:T(1,128)} %bitcast.4), calls=%async_computation | async-start | bytes 557056 | tf_op jit(solution)/shard_map/all_to_all | solution.py:694
  17.2 7.2 %collective-permute-start.3 = (bf16[2,4,72,128]{3,2,1,0:T(8,128)(2,1)S(1)}, bf16[2,4,72,128]{3,2,1,0:T(8,128)(2,1)S(1)}, u32[]{:S(2)}, u32[]{:S(2)}) collective-permute-start(bf16[2,4,72,128]{3,2,1,0:T(8,128)(2,1)S(1)} %pad_maximum_fusion.1), channel_id=1, source_target_pairs={{8,0},{16,8},{24,16},{0,24},{9,1},{17,9},{25,17},{1,25},{10,2},{18... | collective-permute-start | bytes 442376 | tf_op jit(solution)/shard_map/ppermute | solution.py:614
  18.8 6.9 %collective-permute-start.2 = (bf16[2,4,72,128]{3,2,1,0:T(8,128)(2,1)S(1)}, bf16[2,4,72,128]{3,2,1,0:T(8,128)(2,1)S(1)}, u32[]{:S(2)}, u32[]{:S(2)}) collective-permute-start(bf16[2,4,72,128]{3,2,1,0:T(8,128)(2,1)S(1)} %pad_maximum_fusion), channel_id=1, source_target_pairs={{0,8},{8,16},{16,24},{24,0},{1,9},{9,17},{17,25},{25,1},{2,10},{10... | collective-permute-start | bytes 442376 | tf_op jit(solution)/shard_map/ppermute | solution.py:614
  24.4 3.8 %copy-start.4 = (f32[64,64]{1,0:T(8,128)S(1)}, f32[64,64]{1,0:T(8,128)}, u32[]{:S(2)}) copy-start(f32[64,64]{1,0:T(8,128)} %rinv_ref.3) | copy-start | bytes 49156
  35.8 8.7 %collective-permute-start.4 = (bf16[64,4,128]{2,1,0:T(4,128)(2,1)}, bf16[64,4,128]{2,1,0:T(4,128)(2,1)S(1)}, u32[]{:S(2)}, u32[]{:S(2)}) collective-permute-start(bf16[64,4,128]{2,1,0:T(4,128)(2,1)} %get-tuple-element.40.first_hbm), channel_id=1, source_target_pairs={{1,0},{2,1},{3,2},{4,3},{5,4},{6,5},{7,6},{0,7},{9,8},{10,9},{11,1... | collective-permute-start | bytes 196616 | tf_op jit(solution)/shard_map/ppermute | solution.py:609
  39.3 7.2 %collective-permute-start.5 = (bf16[64,4,128]{2,1,0:T(4,128)(2,1)}, bf16[64,4,128]{2,1,0:T(4,128)(2,1)S(1)}, u32[]{:S(2)}, u32[]{:S(2)}) collective-permute-start(bf16[64,4,128]{2,1,0:T(4,128)(2,1)} %get-tuple-element.41.second_hbm), channel_id=1, source_target_pairs={{0,1},{1,2},{2,3},{3,4},{4,5},{5,6},{6,7},{7,0},{8,9},{9,10},{10,1... | collective-permute-start | bytes 196616 | tf_op jit(solution)/shard_map/ppermute | solution.py:609
  39.3 17.5 %all-to-all-start.1 = ((s32[32,16,128]{2,1,0:T(8,128)}), s32[32,16,128]{2,1,0:T(8,128)S(1)}, u32[]{:S(2)}, u32[]{:S(2)}) async-start(s32[32,16,128]{2,1,0:T(8,128)} %bitcast.19), calls=%async_computation.1 | async-start | bytes 524288 | tf_op jit(solution)/shard_map/all_to_all | solution.py:782
  46.5 8.3 %collective-permute-start.6 = (bf16[4,72,128]{2,1,0:T(8,128)(2,1)S(1)}, bf16[4,72,128]{2,1,0:T(8,128)(2,1)S(1)}, u32[]{:S(2)}, u32[]{:S(2)}) collective-permute-start(bf16[4,72,128]{2,1,0:T(8,128)(2,1)S(1)} %pad_maximum_fusion.2), channel_id=1, source_target_pairs={{0,8},{8,16},{16,24},{24,0},{1,9},{9,17},{17,25},{25,1},{2,10},{10... | collective-permute-start | bytes 221192 | tf_op jit(solution)/shard_map/ppermute | solution.py:614
  46.5 8.3 %collective-permute-start.7 = (bf16[4,72,128]{2,1,0:T(8,128)(2,1)S(1)}, bf16[4,72,128]{2,1,0:T(8,128)(2,1)S(1)}, u32[]{:S(2)}, u32[]{:S(2)}) collective-permute-start(bf16[4,72,128]{2,1,0:T(8,128)(2,1)S(1)} %pad_maximum_fusion.3), channel_id=1, source_target_pairs={{8,0},{16,8},{24,16},{0,24},{9,1},{17,9},{25,17},{1,25},{10,2},{18... | collective-permute-start | bytes 221192 | tf_op jit(solution)/shard_map/ppermute | solution.py:614

commit v8 on v7

--- a/solution.py
+++ b/solution.py
@@ -85,7 +85,7 @@
 
 
 def address_kernel(
-    devices_all, quarter, count_ref, owner_ref, cell_ref, scale_ref, innov_ref, kappa_ref,
+    devices_all, quarter, owner_ref, cell_ref, weight_ref, innov_ref, kappa_ref,
     control_hbm, out_ref, key_ref, top_ref, bottom_ref, word_ref, ends_ref, sem_ref,
 ):
     grid_rows = control_hbm.shape[0]
@@ -119,10 +119,7 @@
         (group // 2) * rows + (group % 2) * rows_half + owner * quarter + position % quarter
     )
     key_ref[...] = key
-    scale = scale_ref[...]
-    valid = iota((1, obs), 1) < count_ref[0]
-    weight = jnp.where(valid, 1.0 / (scale * scale), 0.0)
-    weight = jnp.minimum(jnp.floor(weight * (1.0 / WEIGHT_STEP) + 0.5), 65535.0)
+    weight = jnp.minimum(jnp.floor(weight_ref[...] * (1.0 / WEIGHT_STEP) + 0.5), 65535.0)
     weight_high = jnp.floor(weight * (1.0 / 256.0))
     weight_low = weight - 256.0 * weight_high
     cell_high = (cell // 64).astype(F32)
@@ -393,10 +390,11 @@
     pick_pair = jnp.transpose(
         pick_ref[: 2 * channels, : 2 * levels].astype(F32)
     ).astype(BF16)
-    acc_ref[...] = jnp.zeros_like(acc_ref)
+    all_hots, all_wides = [], []
     chunk = min(512, rows_half)
     left_lane = iota((chunk, 128), 1) < 64
     lane_half = iota((chunk, 128), 1) // 64
+    zero_hot = jnp.zeros((chunk, 128), BF16)
     per_half = rows_half // chunk
     for step in range(rows // chunk):
         half = step // per_half
@@ -416,8 +414,17 @@
             lon = jnp.sum(jnp.where(take, lon_lane, 0.0), axis=1, keepdims=True).astype(I32)
             weight.append(jnp.sum(jnp.where(take, weight_lane, 0.0), axis=1, keepdims=True))
             part = lat & 3
-            inside = (lat >> 2) * cols + lon
-            hot = (iota((chunk, cells_part), 1) == inside).astype(F32).astype(BF16)
+            lon_hot = (lane % cols == lon).astype(F32).astype(BF16)
+            band = jnp.broadcast_to((lat >> 2).astype(F32), (chunk, 128)).astype(BF16)
+            hot = jnp.concatenate(
+                [
+                    jnp.where(
+                        band == (lane // cols + first).astype(F32).astype(BF16), lon_hot, zero_hot
+                    )
+                    for first in range(0, lat_rows // 4, 128 // cols)
+                ],
+                axis=1,
+            )
             got = dot_f32(hot, table_ref[...])
             low_parts = jnp.where(part == 0, got[:, :levels], got[:, levels : 2 * levels])
             high_parts = jnp.where(
@@ -448,7 +455,11 @@
                 ],
                 axis=1,
             )
-            acc_ref[...] += dot_tn(hots[side], wide)
+            all_hots.append(hots[side])
+            all_wides.append(wide)
+    acc_ref[...] = dot_tn(
+        jnp.concatenate(all_hots, axis=0), jnp.concatenate(all_wides, axis=0)
+    )
     ret_ref[...] = (dep_ref[:rows_half, :] << 16) | dep_ref[rows_half:, :]
     copies = start_copies([(ret_ref, ret_hbm)], sem_ref)
     wait_copies(sigma_in)
@@ -566,7 +577,7 @@
 
 
 def return_kernel(
-    devices_all, quarter, count_ref, recv_ref, key_ref, innov_ref, scale_ref, rinv_ref, out_ref,
+    devices_all, quarter, recv_ref, key_ref, innov_ref, weight_ref, rinv_ref, out_ref,
     pair_ref,
 ):
     rows_half = devices_all * quarter
@@ -578,9 +589,7 @@
         high, low = split_hi_lo(decode(code))
         pair_ref[half * rows_half : (half + 1) * rows_half, :128] = high
         pair_ref[half * rows_half : (half + 1) * rows_half, 128:] = low
-    scale = scale_ref[...]
-    valid = iota((1, obs), 1) < count_ref[0]
-    weight = jnp.where(valid, 1.0 / (scale * scale), 0.0)
+    weight = weight_ref[...]
     chunk = min(512, obs)
     for start in range(0, obs, chunk):
         key = key_ref[:, start : start + chunk]
@@ -643,7 +652,6 @@
     wide = (lat_rows + 1, lon_cols + 2 * LEAD, levels)
     rim_tile = (4 * NSTEP, lon_cols + 2 * LEAD, levels)
     rim = (6 * NSTEP, lon_cols + 2 * LEAD, levels)
-    smem = pl.BlockSpec(memory_space=pltpu.SMEM)
     anywhere = pl.BlockSpec(memory_space=pl.ANY)
 
     control, sigma = in_hbm(control), in_hbm(sigma)
@@ -661,6 +669,9 @@
         compiler_params=params(6),
         name="pack",
     )(control, in_hbm(kappa))
+    valid = jnp.arange(obs_slots, dtype=I32) < obs_count[0]
+    weight = jnp.where(valid, 1.0 / (error_scale * error_scale), F32(0.0))
+    weight = weight.reshape(1, obs_slots)
     near, far, obs_cell = lax.optimization_barrier((near, far, obs_cell))
     east, west = exchange_sides(near, far)
 
@@ -672,7 +683,7 @@
             jax.ShapeDtypeStruct((2, NSTEP, lon_cols, levels), BF16),
             jax.ShapeDtypeStruct((2, NSTEP, lon_cols, levels), BF16),
         ),
-        in_specs=[smem] + vmem_specs(5) + [HBM_SPEC],
+        in_specs=vmem_specs(5) + [HBM_SPEC],
         out_specs=tuple(vmem_specs(4)),
         scratch_shapes=[
             pltpu.VMEM((rows_half, 128), I32),
@@ -683,10 +694,9 @@
         cost_estimate=estimate(2_000_000_000, 8_000_000),
         name="address",
     )(
-        obs_count,
         obs_owner.reshape(1, obs_slots),
         obs_cell.reshape(1, obs_slots),
-        error_scale.reshape(1, obs_slots),
+        weight,
         innovations.T,
         kappa,
         control,
@@ -831,14 +841,14 @@
     departures = pl.pallas_call(
         functools.partial(return_kernel, devices_all, quarter),
         out_shape=jax.ShapeDtypeStruct((channels, obs_slots), F32),
-        in_specs=[smem] + vmem_specs(5),
+        in_specs=vmem_specs(5),
         out_specs=vmem_specs(1)[0],
         scratch_shapes=[pltpu.VMEM((2 * rows_half, 256), BF16)],
         compiler_params=params(10),
         cost_estimate=estimate(500_000_000, 2_000_000),
         name="give_back",
     )(
-        obs_count, home, key, innovations.T, error_scale.reshape(1, obs_slots),
+        home, key, innovations.T, weight,
         r_inverse,
     )
     return (gradient, departures.T)

time: 59.4 us -> 59 us (level)
  Pallas kernels: 28.6 us -> 28 us
where the time goes in v8:
time: 59 us; the launch traced here: 58.7 us
  Pallas kernels  28 us (47%)
  starting transfers between devices  24.4 us (41%)
  waiting for transfers between devices  4.5 us (8%)
  between operations  1.62 us (3%)
    ppermute x2, starting transfers between devices, exchange_sides(): lax.ppermute(left, 'lon', backward)  9.48 us
    pallas_call x1, Pallas kernels, body(): pl.pallas_call(functools.partial(owner_kernel, devices_all, quarter), out...  7.04 us
    pallas_call x1, Pallas kernels, body(): pl.pallas_call(inner_kernel, out_shape=(pltpu.HBM(control.shape, F32), pl...  6.45 us
    all_to_all x1, starting transfers between devices, body(): lax.all_to_all(payload.reshape(devices_all, 1, (quarter + 1) * 128), ('la...  6.02 us
    pallas_call x1, Pallas kernels, body(): pl.pallas_call(forward_kernel, out_shape=(pltpu.VMEM((columns // 4, 8 * c...  5.53 us
    all_to_all x1, starting transfers between devices, body(): lax.all_to_all(returned.reshape(devices_all, quarter, 128), ('lat', 'lon'...  5.25 us
    ppermute x2, starting transfers between devices, exchange_rims(): lax.ppermute(top, 'lat', backward)  3.53 us
    pallas_call x1, Pallas kernels, body(): pl.pallas_call(functools.partial(address_kernel, devices_all, quarter), o...  2.44 us
  transfers between devices with their start and end apart: 10, of which 3 were waited for; matrix products, arithmetic and copies ran while one was open for 0% of the time, Pallas kernels for 30%

profile of v8, /device:TPU:0, one launch (start us, length us, event | category | flops | bytes accessed | tf_op | source)
XLA Modules:
  0.0 58.7 jit_solution(4187020041369504423)
XLA Ops:
  0.7 1.2 %pack.1 = (bf16[2,64,4,128]{3,2,1,0:T(4,128)(2,1)S(1)}, bf16[2,64,4,128]{3,2,1,0:T(4,128)(2,1)S(1)}) custom-call(f32[64,64,128]{2,1,0:T(8,128)} %control_hbm.7, f32[64,64]{1,0:T(8,128)} %kappa_ref.5), custom_call_target="tpu_custom_call" | custom-call | tf_op jit(solution)/shard_map/pack/pallas_call | solution.py:658
  1.9 6.1 %collective-permute-start = (bf16[2,64,4,128]{3,2,1,0:T(4,128)(2,1)S(1)}, bf16[2,64,4,128]{3,2,1,0:T(4,128)(2,1)S(1)}, u32[]{:S(2)}, u32[]{:S(2)}) collective-permute-start(bf16[2,64,4,128]{3,2,1,0:T(4,128)(2,1)S(1)} %get-tuple-element.30), channel_id=1, source_target_pairs={{1,0},{2,1},{3,2},{4,3},{5,4},{6,5},{7,6},{0,7},{9,8},{10,9},{11,1... | collective-permute-start | bytes 393224 | tf_op jit(solution)/shard_map/ppermute | solution.py:618
  7.9 0.0 collective-permute-start.1
  8.6 0.0 copy-start
  8.6 0.0 copy-start.3
  8.7 0.0 copy-start.7
  8.7 2.4 %address.1 = (s32[544,128]{1,0:T(8,128)}, s32[1,1024]{1,0:T(1,128)S(1)}, bf16[2,4,64,128]{3,2,1,0:T(8,128)(2,1)S(1)}, bf16[2,4,64,128]{3,2,1,0:T(8,128)(2,1)S(1)}) custom-call(s32[1,1024]{1,0:T(1,128)S(1)} %bitcast.18, s32[1,1024]{1,0:T(1,128)S(1)} %bitcast.19, f32[1,1024]{1,0:T(1,128)S(1)} %bitcast.14, f32[64,1024]{1,0:T(8,128)S(1)} %bitcast.16, ...), custom_call_target="tpu_custom_call" | custom-call | flops 2000000000 | bytes 8000000 | tf_op jit(solution)/shard_map/address/pallas_call | solution.py:678
  11.1 6.0 %all-to-all-start = ((s32[32,1,2176]{2,1,0:T(1,128)}), s32[32,1,2176]{2,1,0:T(1,128)S(1)}, u32[]{:S(2)}, u32[]{:S(2)}) async-start(s32[32,1,2176]{2,1,0:T(1,128)} %bitcast.5), calls=%async_computation | async-start | bytes 557056 | tf_op jit(solution)/shard_map/all_to_all | solution.py:704
  17.1 0.0 collective-permute-done.east_ref.keast_ref
  17.2 0.0 collective-permute-done.1.west_ref.kwest_ref
  17.2 1.6 %collective-permute-start.3 = (bf16[2,4,72,128]{3,2,1,0:T(8,128)(2,1)S(1)}, bf16[2,4,72,128]{3,2,1,0:T(8,128)(2,1)S(1)}, u32[]{:S(2)}, u32[]{:S(2)}) collective-permute-start(bf16[2,4,72,128]{3,2,1,0:T(8,128)(2,1)S(1)} %pad_maximum_fusion.1), channel_id=1, source_target_pairs={{8,0},{16,8},{24,16},{0,24},{9,1},{17,9},{25,17},{1,25},{10,2},{18... | collective-permute-start | bytes 442376 | tf_op jit(solution)/shard_map/ppermute | solution.py:623
  18.8 0.1 collective-permute-start.2
  18.9 5.5 %forward.1 = (bf16[1024,512]{1,0:T(8,128)(2,1)S(1)}, bf16[256,512]{1,0:T(8,128)(2,1)S(1)}, f32[16,96,128]{2,1,0:T(8,128)S(1)}, f32[16,96,128]{2,1,0:T(8,128)S(1)}, f32[2,4,64,128]{3,2,1,0:T(8,128)S(1)}) custom-call(f32[64,64,128]{2,1,0:T(8,128)} %control_hbm.7, f32[64,64,128]{2,1,0:T(8,128)} %sigma_hbm.3, ...), custom_call_target="tpu_custom_call" | custom-call | flops 4000000000 | bytes 16000000 | tf_op jit(solution)/shard_map/forward/pallas_call | solution.py:719
  24.4 0.0 copy-start.4
  24.5 0.0 collective-permute-done.3.south_ref.ksouth_ref
  24.5 1.3 %collective-permute-done.2.north_ref.knorth_ref = bf16[2,4,72,128]{3,2,1,0:T(8,128)(2,1)S(1)} collective-permute-done((bf16[2,4,72,128]{3,2,1,0:T(8,128)(2,1)S(1)}, bf16[2,4,72,128]{3,2,1,0:T(8,128)(2,1)S(1)}, u32[]{:S(2)}, u32[]{:S(2)}) %collective-permute-start.2) | collective-permute-done | bytes 147488 | tf_op jit(solution)/shard_map/ppermute | solution.py:623
  25.7 1.2 %ends.1.ends_ref = bf16[2,64,512]{2,1,0:T(8,128)(2,1)S(1)} custom-call(f32[16,96,128]{2,1,0:T(8,128)S(1)} %get-tuple-element.33.rim_ref, f32[16,96,128]{2,1,0:T(8,128)S(1)} %get-tuple-element.34.rim_kap_ref, f32[2,4,64,128]{3,2,1,0:T(8,128)S(1)} %get-tuple-element.35.sigma_ref, bf16[2,4,72,128]{3,2,1,0:T(8,128)(2,1)S(1)} %collective-permute-done.2.north_ref.knorth_ref, ...), custom_call_target="tpu_custom_call" | custom-call | flops 1000000000 | bytes 2000000 | tf_op jit(solution)/shard_map/ends/pallas_call | solution.py:740
  26.9 1.3 %all-to-all-done = s32[32,1,2176]{2,1,0:T(1,128)S(1)} async-done(((s32[32,1,2176]{2,1,0:T(1,128)}), s32[32,1,2176]{2,1,0:T(1,128)S(1)}, u32[]{:S(2)}, u32[]{:S(2)}) %all-to-all-start) | async-done | bytes 278560 | tf_op jit(solution)/shard_map/all_to_all | solution.py:704
  28.2 7.0 %owner.1 = (s32[512,128]{1,0:T(8,128)}, f32[64,64,128]{2,1,0:T(8,128)}, bf16[64,4,128]{2,1,0:T(4,128)(2,1)}, bf16[64,4,128]{2,1,0:T(4,128)(2,1)}, bf16[4,64,128]...) custom-call(s32[544,128]{1,0:T(8,128)S(1)} %bitcast.12, f32[64,64,128]{2,1,0:T(8,128)} %sigma_hbm.3, ...), custom_call_target="tpu_custom_call" | custom-call | flops 4000000000 | bytes 16000000 | tf_op jit(solution)/shard_map/owner/pallas_call | solution.py:751
  35.3 3.4 %collective-permute-start.4 = (bf16[64,4,128]{2,1,0:T(4,128)(2,1)}, bf16[64,4,128]{2,1,0:T(4,128)(2,1)S(1)}, u32[]{:S(2)}, u32[]{:S(2)}) collective-permute-start(bf16[64,4,128]{2,1,0:T(4,128)(2,1)} %get-tuple-element.40.first_hbm), channel_id=1, source_target_pairs={{1,0},{2,1},{3,2},{4,3},{5,4},{6,5},{7,6},{0,7},{9,8},{10,9},{11,1... | collective-permute-start | bytes 196616 | tf_op jit(solution)/shard_map/ppermute | solution.py:618
  38.7 0.0 collective-permute-start.5
  38.7 5.3 %all-to-all-start.1 = ((s32[32,16,128]{2,1,0:T(8,128)}), s32[32,16,128]{2,1,0:T(8,128)S(1)}, u32[]{:S(2)}, u32[]{:S(2)}) async-start(s32[32,16,128]{2,1,0:T(8,128)} %bitcast.21), calls=%async_computation.1 | async-start | bytes 524288 | tf_op jit(solution)/shard_map/all_to_all | solution.py:792
  44.0 0.0 collective-permute-done.4.east_ref
  44.0 1.9 %collective-permute-done.5.west_ref = bf16[64,4,128]{2,1,0:T(4,128)(2,1)S(1)} collective-permute-done((bf16[64,4,128]{2,1,0:T(4,128)(2,1)}, bf16[64,4,128]{2,1,0:T(4,128)(2,1)S(1)}, u32[]{:S(2)}, u32[]{:S(2)}) %collective-permute-start.5) | collective-permute-done | bytes 65568 | tf_op jit(solution)/shard_map/ppermute | solution.py:618
  45.9 0.1 collective-permute-start.6
  46.0 2.0 %collective-permute-start.7 = (bf16[4,72,128]{2,1,0:T(8,128)(2,1)S(1)}, bf16[4,72,128]{2,1,0:T(8,128)(2,1)S(1)}, u32[]{:S(2)}, u32[]{:S(2)}) collective-permute-start(bf16[4,72,128]{2,1,0:T(8,128)(2,1)S(1)} %pad_maximum_fusion.3), channel_id=1, source_target_pairs={{8,0},{16,8},{24,16},{0,24},{9,1},{17,9},{25,17},{1,25},{10,2},{18... | collective-permute-start | bytes 221192 | tf_op jit(solution)/shard_map/ppermute | solution.py:623
  47.9 6.5 %inner.1 = (f32[64,64,128]{2,1,0:T(8,128)}, f32[16,96,128]{2,1,0:T(8,128)S(1)}, f32[16,96,128]{2,1,0:T(8,128)S(1)}, f32[2,4,64,128]{3,2,1,0:T(8,128)S(1)}) custom-call(f32[64,64,128]{2,1,0:T(8,128)} %get-tuple-element.39.adj_hbm, f32[64,64,128]{2,1,0:T(8,128)} %control_hbm.7, bf16[64,4,128]{2,1,0:T(4,128)(2,1)S(1)} %collective-permute-done.4.east_ref, ...), custom_call_target="tpu_custom_call" | custom-call | flops 4000000000 | bytes 16000000 | tf_op jit(solution)/shard_map/inner/pallas_call | solution.py:805
  54.4 0.0 collective-permute-done.6.north_ref
  54.4 0.0 collective-permute-done.7.south_ref
  54.4 1.9 %rims.1 = f32[64,64,128]{2,1,0:T(8,128)} custom-call(f32[16,96,128]{2,1,0:T(8,128)S(1)} %get-tuple-element.42.rim_ref, f32[16,96,128]{2,1,0:T(8,128)S(1)} %get-tuple-element.43.rim_kap_ref, f32[2,4,64,128]{3,2,1,0:T(8,128)S(1)} %get-tuple-element.44.control_ref, ...), custom_call_target="tpu_custom_call", output_to_operand_aliasing={{}: (8, {})} | custom-call | flops 1000000000 | bytes 2000000 | tf_op jit(solution)/shard_map/rims/pallas_call | solution.py:823
  56.4 0.0 all-to-all-done.1
  56.4 2.3 %give_back.1 = f32[64,1024]{1,0:T(8,128)} custom-call(s32[512,128]{1,0:T(8,128)S(1)} %bitcast.13, s32[1,1024]{1,0:T(1,128)S(1)} %get-tuple-element.49.key_ref, f32[64,1024]{1,0:T(8,128)S(1)} %bitcast.17, f32[1,1024]{1,0:T(1,128)S(1)} %bitcast.15, f32[64,64]{1,0:T(8,128)S(1)} %copy-done.4), custom_call_target="tpu_custom_call" | custom-call | flops 500000000 | bytes 2000000 | tf_op jit(solution)/shard_map/give_back/pallas_call | solution.py:841
  (24 shorter events, 0.1 us)
Async XLA Ops:
  0.6 8.0 %copy-start.1 = (f32[64,64]{1,0:T(8,128)S(1)}, f32[64,64]{1,0:T(8,128)}, u32[]{:S(2)}) copy-start(f32[64,64]{1,0:T(8,128)} %kappa_ref.5) | copy-start | bytes 49156
  0.6 8.0 %copy-start.6 = (s32[1024]{0:T(1024)S(1)}, s32[1024]{0:T(1024)}, u32[]{:S(2)}) copy-start(s32[1024]{0:T(1024)} %param.22) | copy-start | bytes 12292
  0.7 7.9 %copy-start.8 = (f32[1024]{0:T(1024)S(1)}, f32[1024]{0:T(1024)}, u32[]{:S(2)}) copy-start(f32[1024]{0:T(1024)} %param.20) | copy-start | bytes 12292
  0.7 8.0 %copy-start.5 = (s32[1024,1]{0,1:T(1,128)S(1)}, s32[1024,1]{0,1:T(1,128)}, u32[]{:S(2)}) copy-start(s32[1024,1]{0,1:T(1,128)} %param.21) | copy-start | bytes 12292
  0.7 8.0 %copy-start.2 = (f32[1024,64]{0,1:T(8,128)S(1)}, f32[1024,64]{0,1:T(8,128)}, u32[]{:S(2)}) copy-start(f32[1024,64]{0,1:T(8,128)} %param.19) | copy-start | bytes 786436
  1.9 15.3 %collective-permute-start = (bf16[2,64,4,128]{3,2,1,0:T(4,128)(2,1)S(1)}, bf16[2,64,4,128]{3,2,1,0:T(4,128)(2,1)S(1)}, u32[]{:S(2)}, u32[]{:S(2)}) collective-permute-start(bf16[2,64,4,128]{3,2,1,0:T(4,128)(2,1)S(1)} %get-tuple-element.30), channel_id=1, source_target_pairs={{1,0},{2,1},{3,2},{4,3},{5,4},{6,5},{7,6},{0,7},{9,8},{10,9},{11,1... | collective-permute-start | bytes 393224 | tf_op jit(solution)/shard_map/ppermute | solution.py:618
  7.9 9.3 %collective-permute-start.1 = (bf16[2,64,4,128]{3,2,1,0:T(4,128)(2,1)S(1)}, bf16[2,64,4,128]{3,2,1,0:T(4,128)(2,1)S(1)}, u32[]{:S(2)}, u32[]{:S(2)}) collective-permute-start(bf16[2,64,4,128]{3,2,1,0:T(4,128)(2,1)S(1)} %get-tuple-element.31), channel_id=1, source_target_pairs={{0,1},{1,2},{2,3},{3,4},{4,5},{5,6},{6,7},{7,0},{8,9},{9,10},{10,1... | collective-permute-start | bytes 393224 | tf_op jit(solution)/shard_map/ppermute | solution.py:618
  8.6 10.3 %copy-start = (f32[128,128]{1,0:T(8,128)S(1)}, f32[128,128]{1,0:T(8,128)}, u32[]{:S(2)}) copy-start(f32[128,128]{1,0:T(8,128)} %vertical_ref.7) | copy-start | bytes 196612
  8.6 10.2 %copy-start.3 = (bf16[616,128]{1,0:T(8,128)(2,1)S(1)}, bf16[616,128]{1,0:T(8,128)(2,1)}, u32[]{:S(2)}) copy-start(bf16[616,128]{1,0:T(8,128)(2,1)} %table_ref.1) | copy-start | bytes 473092
  8.7 10.2 %copy-start.7 = (s32[64]{0:T(128)S(1)}, s32[64]{0:T(128)}, u32[]{:S(2)}) copy-start(s32[64]{0:T(128)} %param.17) | copy-start | bytes 772
  11.1 17.1 %all-to-all-start = ((s32[32,1,2176]{2,1,0:T(1,128)}), s32[32,1,2176]{2,1,0:T(1,128)S(1)}, u32[]{:S(2)}, u32[]{:S(2)}) async-start(s32[32,1,2176]{2,1,0:T(1,128)} %bitcast.5), calls=%async_computation | async-start | bytes 557056 | tf_op jit(solution)/shard_map/all_to_all | solution.py:704
  17.2 7.2 %collective-permute-start.3 = (bf16[2,4,72,128]{3,2,1,0:T(8,128)(2,1)S(1)}, bf16[2,4,72,128]{3,2,1,0:T(8,128)(2,1)S(1)}, u32[]{:S(2)}, u32[]{:S(2)}) collective-permute-start(bf16[2,4,72,128]{3,2,1,0:T(8,128)(2,1)S(1)} %pad_maximum_fusion.1), channel_id=1, source_target_pairs={{8,0},{16,8},{24,16},{0,24},{9,1},{17,9},{25,17},{1,25},{10,2},{18... | collective-permute-start | bytes 442376 | tf_op jit(solution)/shard_map/ppermute | solution.py:623
  18.8 6.9 %collective-permute-start.2 = (bf16[2,4,72,128]{3,2,1,0:T(8,128)(2,1)S(1)}, bf16[2,4,72,128]{3,2,1,0:T(8,128)(2,1)S(1)}, u32[]{:S(2)}, u32[]{:S(2)}) collective-permute-start(bf16[2,4,72,128]{3,2,1,0:T(8,128)(2,1)S(1)} %pad_maximum_fusion), channel_id=1, source_target_pairs={{0,8},{8,16},{16,24},{24,0},{1,9},{9,17},{17,25},{25,1},{2,10},{10... | collective-permute-start | bytes 442376 | tf_op jit(solution)/shard_map/ppermute | solution.py:623
  24.4 3.8 %copy-start.4 = (f32[64,64]{1,0:T(8,128)S(1)}, f32[64,64]{1,0:T(8,128)}, u32[]{:S(2)}) copy-start(f32[64,64]{1,0:T(8,128)} %rinv_ref.3) | copy-start | bytes 49156
  35.3 8.7 %collective-permute-start.4 = (bf16[64,4,128]{2,1,0:T(4,128)(2,1)}, bf16[64,4,128]{2,1,0:T(4,128)(2,1)S(1)}, u32[]{:S(2)}, u32[]{:S(2)}) collective-permute-start(bf16[64,4,128]{2,1,0:T(4,128)(2,1)} %get-tuple-element.40.first_hbm), channel_id=1, source_target_pairs={{1,0},{2,1},{3,2},{4,3},{5,4},{6,5},{7,6},{0,7},{9,8},{10,9},{11,1... | collective-permute-start | bytes 196616 | tf_op jit(solution)/shard_map/ppermute | solution.py:618
  38.7 7.2 %collective-permute-start.5 = (bf16[64,4,128]{2,1,0:T(4,128)(2,1)}, bf16[64,4,128]{2,1,0:T(4,128)(2,1)S(1)}, u32[]{:S(2)}, u32[]{:S(2)}) collective-permute-start(bf16[64,4,128]{2,1,0:T(4,128)(2,1)} %get-tuple-element.41.second_hbm), channel_id=1, source_target_pairs={{0,1},{1,2},{2,3},{3,4},{4,5},{5,6},{6,7},{7,0},{8,9},{9,10},{10,1... | collective-permute-start | bytes 196616 | tf_op jit(solution)/shard_map/ppermute | solution.py:618
  38.7 17.7 %all-to-all-start.1 = ((s32[32,16,128]{2,1,0:T(8,128)}), s32[32,16,128]{2,1,0:T(8,128)S(1)}, u32[]{:S(2)}, u32[]{:S(2)}) async-start(s32[32,16,128]{2,1,0:T(8,128)} %bitcast.21), calls=%async_computation.1 | async-start | bytes 524288 | tf_op jit(solution)/shard_map/all_to_all | solution.py:792
  45.9 8.5 %collective-permute-start.6 = (bf16[4,72,128]{2,1,0:T(8,128)(2,1)S(1)}, bf16[4,72,128]{2,1,0:T(8,128)(2,1)S(1)}, u32[]{:S(2)}, u32[]{:S(2)}) collective-permute-start(bf16[4,72,128]{2,1,0:T(8,128)(2,1)S(1)} %pad_maximum_fusion.2), channel_id=1, source_target_pairs={{0,8},{8,16},{16,24},{24,0},{1,9},{9,17},{17,25},{25,1},{2,10},{10... | collective-permute-start | bytes 221192 | tf_op jit(solution)/shard_map/ppermute | solution.py:623
  46.0 8.4 %collective-permute-start.7 = (bf16[4,72,128]{2,1,0:T(8,128)(2,1)S(1)}, bf16[4,72,128]{2,1,0:T(8,128)(2,1)S(1)}, u32[]{:S(2)}, u32[]{:S(2)}) collective-permute-start(bf16[4,72,128]{2,1,0:T(8,128)(2,1)S(1)} %pad_maximum_fusion.3), channel_id=1, source_target_pairs={{8,0},{16,8},{24,16},{0,24},{9,1},{17,9},{25,17},{1,25},{10,2},{18... | collective-permute-start | bytes 221192 | tf_op jit(solution)/shard_map/ppermute | solution.py:623

commit v9 on v8

--- a/solution.py
+++ b/solution.py
@@ -141,7 +141,7 @@
     low = (level - 256.0 * high).astype(BF16)
     high = high.astype(BF16)
     bytes_of = [jnp.concatenate([high, low], axis=0), jnp.concatenate([low, high], axis=0)]
-    chunk = min(256, rows_half)
+    chunk = rows_half
     left_lane = iota((chunk, 128), 1) < 64
     for base in range(0, rows_half, chunk):
         total = []
@@ -210,7 +210,7 @@
     far_ref[0] = right_ref[:, 8 - NSTEP :].astype(BF16)
 
 
-def sweep_rows(source, target, kap_ref, low, high, block=8):
+def sweep_rows(source, target, kap_ref, low, high, block=16):
     width = source.shape[1]
     here_at = slice(8, width - 8)
 
@@ -236,7 +236,7 @@
         update(low + whole * block, high - low - whole * block)
 
 
-def sweeps(first_ref, second_ref, kap_ref, rows, block=8):
+def sweeps(first_ref, second_ref, kap_ref, rows, block=16):
     source, target = first_ref, second_ref
     for sweep in range(1, NSTEP + 1):
         sweep_rows(source, target, kap_ref, sweep, rows - sweep, block)
@@ -590,7 +590,7 @@
         pair_ref[half * rows_half : (half + 1) * rows_half, :128] = high
         pair_ref[half * rows_half : (half + 1) * rows_half, 128:] = low
     weight = weight_ref[...]
-    chunk = min(512, obs)
+    chunk = obs
     for start in range(0, obs, chunk):
         key = key_ref[:, start : start + chunk]
         side = key >= rows
@@ -690,7 +690,7 @@
             pltpu.VMEM((2, NSTEP, lon_cols, levels), F32),
             pltpu.SemaphoreType.DMA((2,)),
         ],
-        compiler_params=params(10),
+        compiler_params=params(16),
         cost_estimate=estimate(2_000_000_000, 8_000_000),
         name="address",
     )(
@@ -844,7 +844,7 @@
         in_specs=vmem_specs(5),
         out_specs=vmem_specs(1)[0],
         scratch_shapes=[pltpu.VMEM((2 * rows_half, 256), BF16)],
-        compiler_params=params(10),
+        compiler_params=params(16),
         cost_estimate=estimate(500_000_000, 2_000_000),
         name="give_back",
     )(

time: 59 us -> 58.3 us (0.988)
  Pallas kernels: 28 us -> 27.3 us
where the time goes in v9:
time: 58.3 us; the launch traced here: 58 us
  Pallas kernels  27.3 us (47%)
  starting transfers between devices  24.2 us (42%)
  waiting for transfers between devices  4.68 us (8%)
  between operations  1.61 us (3%)
    ppermute x2, starting transfers between devices, exchange_sides(): lax.ppermute(left, 'lon', backward)  9.48 us
    pallas_call x1, Pallas kernels, body(): pl.pallas_call(functools.partial(owner_kernel, devices_all, quarter), out...  7.03 us
    pallas_call x1, Pallas kernels, body(): pl.pallas_call(inner_kernel, out_shape=(pltpu.HBM(control.shape, F32), pl...  6.3 us
    all_to_all x1, starting transfers between devices, body(): lax.all_to_all(payload.reshape(devices_all, 1, (quarter + 1) * 128), ('la...  6.02 us
    pallas_call x1, Pallas kernels, body(): pl.pallas_call(forward_kernel, out_shape=(pltpu.VMEM((columns // 4, 8 * c...  5.38 us
    all_to_all x1, starting transfers between devices, body(): lax.all_to_all(returned.reshape(devices_all, quarter, 128), ('lat', 'lon'...  5.24 us
    ppermute x2, starting transfers between devices, exchange_rims(): lax.ppermute(top, 'lat', backward)  3.35 us
    pallas_call x1, Pallas kernels, body(): pl.pallas_call(functools.partial(address_kernel, devices_all, quarter), o...  2.39 us
  transfers between devices with their start and end apart: 10, of which 3 were waited for; matrix products, arithmetic and copies ran while one was open for 0% of the time, Pallas kernels for 30%

profile of v9, /device:TPU:0, one launch (start us, length us, event | category | flops | bytes accessed | tf_op | source)
XLA Modules:
  0.0 58.0 jit_solution(16671341185910187221)
XLA Ops:
  0.7 1.2 %pack.1 = (bf16[2,64,4,128]{3,2,1,0:T(4,128)(2,1)S(1)}, bf16[2,64,4,128]{3,2,1,0:T(4,128)(2,1)S(1)}) custom-call(f32[64,64,128]{2,1,0:T(8,128)} %control_hbm.7, f32[64,64]{1,0:T(8,128)} %kappa_ref.5), custom_call_target="tpu_custom_call" | custom-call | tf_op jit(solution)/shard_map/pack/pallas_call | solution.py:658
  1.9 6.1 %collective-permute-start = (bf16[2,64,4,128]{3,2,1,0:T(4,128)(2,1)S(1)}, bf16[2,64,4,128]{3,2,1,0:T(4,128)(2,1)S(1)}, u32[]{:S(2)}, u32[]{:S(2)}) collective-permute-start(bf16[2,64,4,128]{3,2,1,0:T(4,128)(2,1)S(1)} %get-tuple-element.30), channel_id=1, source_target_pairs={{1,0},{2,1},{3,2},{4,3},{5,4},{6,5},{7,6},{0,7},{9,8},{10,9},{11,1... | collective-permute-start | bytes 393224 | tf_op jit(solution)/shard_map/ppermute | solution.py:618
  7.9 0.0 collective-permute-start.1
  8.6 0.0 copy-start
  8.6 0.0 copy-start.3
  8.7 0.0 copy-start.7
  8.7 2.4 %address.1 = (s32[544,128]{1,0:T(8,128)}, s32[1,1024]{1,0:T(1,128)S(1)}, bf16[2,4,64,128]{3,2,1,0:T(8,128)(2,1)S(1)}, bf16[2,4,64,128]{3,2,1,0:T(8,128)(2,1)S(1)}) custom-call(s32[1,1024]{1,0:T(1,128)S(1)} %bitcast.18, s32[1,1024]{1,0:T(1,128)S(1)} %bitcast.19, f32[1,1024]{1,0:T(1,128)S(1)} %bitcast.14, f32[64,1024]{1,0:T(8,128)S(1)} %bitcast.16, ...), custom_call_target="tpu_custom_call" | custom-call | flops 2000000000 | bytes 8000000 | tf_op jit(solution)/shard_map/address/pallas_call | solution.py:678
  11.1 6.0 %all-to-all-start = ((s32[32,1,2176]{2,1,0:T(1,128)}), s32[32,1,2176]{2,1,0:T(1,128)S(1)}, u32[]{:S(2)}, u32[]{:S(2)}) async-start(s32[32,1,2176]{2,1,0:T(1,128)} %bitcast.5), calls=%async_computation | async-start | bytes 557056 | tf_op jit(solution)/shard_map/all_to_all | solution.py:704
  17.1 0.0 collective-permute-done.east_ref.keast_ref
  17.1 0.0 collective-permute-done.1.west_ref.kwest_ref
  17.2 1.6 %collective-permute-start.3 = (bf16[2,4,72,128]{3,2,1,0:T(8,128)(2,1)S(1)}, bf16[2,4,72,128]{3,2,1,0:T(8,128)(2,1)S(1)}, u32[]{:S(2)}, u32[]{:S(2)}) collective-permute-start(bf16[2,4,72,128]{3,2,1,0:T(8,128)(2,1)S(1)} %pad_maximum_fusion.1), channel_id=1, source_target_pairs={{8,0},{16,8},{24,16},{0,24},{9,1},{17,9},{25,17},{1,25},{10,2},{18... | collective-permute-start | bytes 442376 | tf_op jit(solution)/shard_map/ppermute | solution.py:623
  18.8 0.1 collective-permute-start.2
  18.9 5.4 %forward.1 = (bf16[1024,512]{1,0:T(8,128)(2,1)S(1)}, bf16[256,512]{1,0:T(8,128)(2,1)S(1)}, f32[16,96,128]{2,1,0:T(8,128)S(1)}, f32[16,96,128]{2,1,0:T(8,128)S(1)}, f32[2,4,64,128]{3,2,1,0:T(8,128)S(1)}) custom-call(f32[64,64,128]{2,1,0:T(8,128)} %control_hbm.7, f32[64,64,128]{2,1,0:T(8,128)} %sigma_hbm.3, ...), custom_call_target="tpu_custom_call" | custom-call | flops 4000000000 | bytes 16000000 | tf_op jit(solution)/shard_map/forward/pallas_call | solution.py:719
  24.3 0.0 copy-start.4
  24.3 0.0 collective-permute-done.3.south_ref.ksouth_ref
  24.3 1.4 %collective-permute-done.2.north_ref.knorth_ref = bf16[2,4,72,128]{3,2,1,0:T(8,128)(2,1)S(1)} collective-permute-done((bf16[2,4,72,128]{3,2,1,0:T(8,128)(2,1)S(1)}, bf16[2,4,72,128]{3,2,1,0:T(8,128)(2,1)S(1)}, u32[]{:S(2)}, u32[]{:S(2)}) %collective-permute-start.2) | collective-permute-done | bytes 147488 | tf_op jit(solution)/shard_map/ppermute | solution.py:623
  25.7 1.1 %ends.1.ends_ref = bf16[2,64,512]{2,1,0:T(8,128)(2,1)S(1)} custom-call(f32[16,96,128]{2,1,0:T(8,128)S(1)} %get-tuple-element.33.rim_ref, f32[16,96,128]{2,1,0:T(8,128)S(1)} %get-tuple-element.34.rim_kap_ref, f32[2,4,64,128]{3,2,1,0:T(8,128)S(1)} %get-tuple-element.35.sigma_ref, bf16[2,4,72,128]{3,2,1,0:T(8,128)(2,1)S(1)} %collective-permute-done.2.north_ref.knorth_ref, ...), custom_call_target="tpu_custom_call" | custom-call | flops 1000000000 | bytes 2000000 | tf_op jit(solution)/shard_map/ends/pallas_call | solution.py:740
  26.8 1.3 %all-to-all-done = s32[32,1,2176]{2,1,0:T(1,128)S(1)} async-done(((s32[32,1,2176]{2,1,0:T(1,128)}), s32[32,1,2176]{2,1,0:T(1,128)S(1)}, u32[]{:S(2)}, u32[]{:S(2)}) %all-to-all-start) | async-done | bytes 278560 | tf_op jit(solution)/shard_map/all_to_all | solution.py:704
  28.2 7.0 %owner.1 = (s32[512,128]{1,0:T(8,128)}, f32[64,64,128]{2,1,0:T(8,128)}, bf16[64,4,128]{2,1,0:T(4,128)(2,1)}, bf16[64,4,128]{2,1,0:T(4,128)(2,1)}, bf16[4,64,128]...) custom-call(s32[544,128]{1,0:T(8,128)S(1)} %bitcast.12, f32[64,64,128]{2,1,0:T(8,128)} %sigma_hbm.3, ...), custom_call_target="tpu_custom_call" | custom-call | flops 4000000000 | bytes 16000000 | tf_op jit(solution)/shard_map/owner/pallas_call | solution.py:751
  35.2 3.4 %collective-permute-start.4 = (bf16[64,4,128]{2,1,0:T(4,128)(2,1)}, bf16[64,4,128]{2,1,0:T(4,128)(2,1)S(1)}, u32[]{:S(2)}, u32[]{:S(2)}) collective-permute-start(bf16[64,4,128]{2,1,0:T(4,128)(2,1)} %get-tuple-element.40.first_hbm), channel_id=1, source_target_pairs={{1,0},{2,1},{3,2},{4,3},{5,4},{6,5},{7,6},{0,7},{9,8},{10,9},{11,1... | collective-permute-start | bytes 196616 | tf_op jit(solution)/shard_map/ppermute | solution.py:618
  38.7 0.0 collective-permute-start.5
  38.7 5.2 %all-to-all-start.1 = ((s32[32,16,128]{2,1,0:T(8,128)}), s32[32,16,128]{2,1,0:T(8,128)S(1)}, u32[]{:S(2)}, u32[]{:S(2)}) async-start(s32[32,16,128]{2,1,0:T(8,128)} %bitcast.21), calls=%async_computation.1 | async-start | bytes 524288 | tf_op jit(solution)/shard_map/all_to_all | solution.py:792
  43.9 0.0 collective-permute-done.4.east_ref
  43.9 1.9 %collective-permute-done.5.west_ref = bf16[64,4,128]{2,1,0:T(4,128)(2,1)S(1)} collective-permute-done((bf16[64,4,128]{2,1,0:T(4,128)(2,1)}, bf16[64,4,128]{2,1,0:T(4,128)(2,1)S(1)}, u32[]{:S(2)}, u32[]{:S(2)}) %collective-permute-start.5) | collective-permute-done | bytes 65568 | tf_op jit(solution)/shard_map/ppermute | solution.py:618
  45.8 0.1 collective-permute-start.6
  45.9 1.8 %collective-permute-start.7 = (bf16[4,72,128]{2,1,0:T(8,128)(2,1)S(1)}, bf16[4,72,128]{2,1,0:T(8,128)(2,1)S(1)}, u32[]{:S(2)}, u32[]{:S(2)}) collective-permute-start(bf16[4,72,128]{2,1,0:T(8,128)(2,1)S(1)} %pad_maximum_fusion.3), channel_id=1, source_target_pairs={{8,0},{16,8},{24,16},{0,24},{9,1},{17,9},{25,17},{1,25},{10,2},{18... | collective-permute-start | bytes 221192 | tf_op jit(solution)/shard_map/ppermute | solution.py:623
  47.7 6.3 %inner.1 = (f32[64,64,128]{2,1,0:T(8,128)}, f32[16,96,128]{2,1,0:T(8,128)S(1)}, f32[16,96,128]{2,1,0:T(8,128)S(1)}, f32[2,4,64,128]{3,2,1,0:T(8,128)S(1)}) custom-call(f32[64,64,128]{2,1,0:T(8,128)} %get-tuple-element.39.adj_hbm, f32[64,64,128]{2,1,0:T(8,128)} %control_hbm.7, bf16[64,4,128]{2,1,0:T(4,128)(2,1)S(1)} %collective-permute-done.4.east_ref, ...), custom_call_target="tpu_custom_call" | custom-call | flops 4000000000 | bytes 16000000 | tf_op jit(solution)/shard_map/inner/pallas_call | solution.py:805
  54.0 0.0 collective-permute-done.6.north_ref
  54.0 0.0 collective-permute-done.7.south_ref
  54.0 1.9 %rims.1 = f32[64,64,128]{2,1,0:T(8,128)} custom-call(f32[16,96,128]{2,1,0:T(8,128)S(1)} %get-tuple-element.42.rim_ref, f32[16,96,128]{2,1,0:T(8,128)S(1)} %get-tuple-element.43.rim_kap_ref, f32[2,4,64,128]{3,2,1,0:T(8,128)S(1)} %get-tuple-element.44.control_ref, ...), custom_call_target="tpu_custom_call", output_to_operand_aliasing={{}: (8, {})} | custom-call | flops 1000000000 | bytes 2000000 | tf_op jit(solution)/shard_map/rims/pallas_call | solution.py:823
  55.9 0.0 all-to-all-done.1
  56.0 2.0 %give_back.1 = f32[64,1024]{1,0:T(8,128)} custom-call(s32[512,128]{1,0:T(8,128)S(1)} %bitcast.13, s32[1,1024]{1,0:T(1,128)S(1)} %get-tuple-element.49.key_ref, f32[64,1024]{1,0:T(8,128)S(1)} %bitcast.17, f32[1,1024]{1,0:T(1,128)S(1)} %bitcast.15, f32[64,64]{1,0:T(8,128)S(1)} %copy-done.4), custom_call_target="tpu_custom_call" | custom-call | flops 500000000 | bytes 2000000 | tf_op jit(solution)/shard_map/give_back/pallas_call | solution.py:841
  (24 shorter events, 0.1 us)
Async XLA Ops:
  0.6 8.0 %copy-start.1 = (f32[64,64]{1,0:T(8,128)S(1)}, f32[64,64]{1,0:T(8,128)}, u32[]{:S(2)}) copy-start(f32[64,64]{1,0:T(8,128)} %kappa_ref.5) | copy-start | bytes 49156
  0.6 8.0 %copy-start.6 = (s32[1024]{0:T(1024)S(1)}, s32[1024]{0:T(1024)}, u32[]{:S(2)}) copy-start(s32[1024]{0:T(1024)} %param.22) | copy-start | bytes 12292
  0.7 7.9 %copy-start.8 = (f32[1024]{0:T(1024)S(1)}, f32[1024]{0:T(1024)}, u32[]{:S(2)}) copy-start(f32[1024]{0:T(1024)} %param.20) | copy-start | bytes 12292
  0.7 8.0 %copy-start.5 = (s32[1024,1]{0,1:T(1,128)S(1)}, s32[1024,1]{0,1:T(1,128)}, u32[]{:S(2)}) copy-start(s32[1024,1]{0,1:T(1,128)} %param.21) | copy-start | bytes 12292
  0.7 8.0 %copy-start.2 = (f32[1024,64]{0,1:T(8,128)S(1)}, f32[1024,64]{0,1:T(8,128)}, u32[]{:S(2)}) copy-start(f32[1024,64]{0,1:T(8,128)} %param.19) | copy-start | bytes 786436
  1.9 15.2 %collective-permute-start = (bf16[2,64,4,128]{3,2,1,0:T(4,128)(2,1)S(1)}, bf16[2,64,4,128]{3,2,1,0:T(4,128)(2,1)S(1)}, u32[]{:S(2)}, u32[]{:S(2)}) collective-permute-start(bf16[2,64,4,128]{3,2,1,0:T(4,128)(2,1)S(1)} %get-tuple-element.30), channel_id=1, source_target_pairs={{1,0},{2,1},{3,2},{4,3},{5,4},{6,5},{7,6},{0,7},{9,8},{10,9},{11,1... | collective-permute-start | bytes 393224 | tf_op jit(solution)/shard_map/ppermute | solution.py:618
  7.9 9.2 %collective-permute-start.1 = (bf16[2,64,4,128]{3,2,1,0:T(4,128)(2,1)S(1)}, bf16[2,64,4,128]{3,2,1,0:T(4,128)(2,1)S(1)}, u32[]{:S(2)}, u32[]{:S(2)}) collective-permute-start(bf16[2,64,4,128]{3,2,1,0:T(4,128)(2,1)S(1)} %get-tuple-element.31), channel_id=1, source_target_pairs={{0,1},{1,2},{2,3},{3,4},{4,5},{5,6},{6,7},{7,0},{8,9},{9,10},{10,1... | collective-permute-start | bytes 393224 | tf_op jit(solution)/shard_map/ppermute | solution.py:618
  8.6 10.2 %copy-start = (f32[128,128]{1,0:T(8,128)S(1)}, f32[128,128]{1,0:T(8,128)}, u32[]{:S(2)}) copy-start(f32[128,128]{1,0:T(8,128)} %vertical_ref.7) | copy-start | bytes 196612
  8.6 10.2 %copy-start.3 = (bf16[616,128]{1,0:T(8,128)(2,1)S(1)}, bf16[616,128]{1,0:T(8,128)(2,1)}, u32[]{:S(2)}) copy-start(bf16[616,128]{1,0:T(8,128)(2,1)} %table_ref.1) | copy-start | bytes 473092
  8.7 10.2 %copy-start.7 = (s32[64]{0:T(128)S(1)}, s32[64]{0:T(128)}, u32[]{:S(2)}) copy-start(s32[64]{0:T(128)} %param.17) | copy-start | bytes 772
  11.1 17.1 %all-to-all-start = ((s32[32,1,2176]{2,1,0:T(1,128)}), s32[32,1,2176]{2,1,0:T(1,128)S(1)}, u32[]{:S(2)}, u32[]{:S(2)}) async-start(s32[32,1,2176]{2,1,0:T(1,128)} %bitcast.5), calls=%async_computation | async-start | bytes 557056 | tf_op jit(solution)/shard_map/all_to_all | solution.py:704
  17.2 7.1 %collective-permute-start.3 = (bf16[2,4,72,128]{3,2,1,0:T(8,128)(2,1)S(1)}, bf16[2,4,72,128]{3,2,1,0:T(8,128)(2,1)S(1)}, u32[]{:S(2)}, u32[]{:S(2)}) collective-permute-start(bf16[2,4,72,128]{3,2,1,0:T(8,128)(2,1)S(1)} %pad_maximum_fusion.1), channel_id=1, source_target_pairs={{8,0},{16,8},{24,16},{0,24},{9,1},{17,9},{25,17},{1,25},{10,2},{18... | collective-permute-start | bytes 442376 | tf_op jit(solution)/shard_map/ppermute | solution.py:623
  18.8 6.9 %collective-permute-start.2 = (bf16[2,4,72,128]{3,2,1,0:T(8,128)(2,1)S(1)}, bf16[2,4,72,128]{3,2,1,0:T(8,128)(2,1)S(1)}, u32[]{:S(2)}, u32[]{:S(2)}) collective-permute-start(bf16[2,4,72,128]{3,2,1,0:T(8,128)(2,1)S(1)} %pad_maximum_fusion), channel_id=1, source_target_pairs={{0,8},{8,16},{16,24},{24,0},{1,9},{9,17},{17,25},{25,1},{2,10},{10... | collective-permute-start | bytes 442376 | tf_op jit(solution)/shard_map/ppermute | solution.py:623
  24.3 3.9 %copy-start.4 = (f32[64,64]{1,0:T(8,128)S(1)}, f32[64,64]{1,0:T(8,128)}, u32[]{:S(2)}) copy-start(f32[64,64]{1,0:T(8,128)} %rinv_ref.3) | copy-start | bytes 49156
  35.2 8.7 %collective-permute-start.4 = (bf16[64,4,128]{2,1,0:T(4,128)(2,1)}, bf16[64,4,128]{2,1,0:T(4,128)(2,1)S(1)}, u32[]{:S(2)}, u32[]{:S(2)}) collective-permute-start(bf16[64,4,128]{2,1,0:T(4,128)(2,1)} %get-tuple-element.40.first_hbm), channel_id=1, source_target_pairs={{1,0},{2,1},{3,2},{4,3},{5,4},{6,5},{7,6},{0,7},{9,8},{10,9},{11,1... | collective-permute-start | bytes 196616 | tf_op jit(solution)/shard_map/ppermute | solution.py:618
  38.7 7.2 %collective-permute-start.5 = (bf16[64,4,128]{2,1,0:T(4,128)(2,1)}, bf16[64,4,128]{2,1,0:T(4,128)(2,1)S(1)}, u32[]{:S(2)}, u32[]{:S(2)}) collective-permute-start(bf16[64,4,128]{2,1,0:T(4,128)(2,1)} %get-tuple-element.41.second_hbm), channel_id=1, source_target_pairs={{0,1},{1,2},{2,3},{3,4},{4,5},{5,6},{6,7},{7,0},{8,9},{9,10},{10,1... | collective-permute-start | bytes 196616 | tf_op jit(solution)/shard_map/ppermute | solution.py:618
  38.7 17.3 %all-to-all-start.1 = ((s32[32,16,128]{2,1,0:T(8,128)}), s32[32,16,128]{2,1,0:T(8,128)S(1)}, u32[]{:S(2)}, u32[]{:S(2)}) async-start(s32[32,16,128]{2,1,0:T(8,128)} %bitcast.21), calls=%async_computation.1 | async-start | bytes 524288 | tf_op jit(solution)/shard_map/all_to_all | solution.py:792
  45.8 8.2 %collective-permute-start.6 = (bf16[4,72,128]{2,1,0:T(8,128)(2,1)S(1)}, bf16[4,72,128]{2,1,0:T(8,128)(2,1)S(1)}, u32[]{:S(2)}, u32[]{:S(2)}) collective-permute-start(bf16[4,72,128]{2,1,0:T(8,128)(2,1)S(1)} %pad_maximum_fusion.2), channel_id=1, source_target_pairs={{0,8},{8,16},{16,24},{24,0},{1,9},{9,17},{17,25},{25,1},{2,10},{10... | collective-permute-start | bytes 221192 | tf_op jit(solution)/shard_map/ppermute | solution.py:623
  45.9 8.1 %collective-permute-start.7 = (bf16[4,72,128]{2,1,0:T(8,128)(2,1)S(1)}, bf16[4,72,128]{2,1,0:T(8,128)(2,1)S(1)}, u32[]{:S(2)}, u32[]{:S(2)}) collective-permute-start(bf16[4,72,128]{2,1,0:T(8,128)(2,1)S(1)} %pad_maximum_fusion.3), channel_id=1, source_target_pairs={{8,0},{16,8},{24,16},{0,24},{9,1},{17,9},{25,17},{1,25},{10,2},{18... | collective-permute-start | bytes 221192 | tf_op jit(solution)/shard_map/ppermute | solution.py:623

commit v10 on v9

--- a/solution.py
+++ b/solution.py
@@ -210,7 +210,7 @@
     far_ref[0] = right_ref[:, 8 - NSTEP :].astype(BF16)
 
 
-def sweep_rows(source, target, kap_ref, low, high, block=16):
+def sweep_rows(source, target, kap_ref, low, high, block=32):
     width = source.shape[1]
     here_at = slice(8, width - 8)
 
@@ -236,7 +236,7 @@
         update(low + whole * block, high - low - whole * block)
 
 
-def sweeps(first_ref, second_ref, kap_ref, rows, block=16):
+def sweeps(first_ref, second_ref, kap_ref, rows, block=32):
     source, target = first_ref, second_ref
     for sweep in range(1, NSTEP + 1):
         sweep_rows(source, target, kap_ref, sweep, rows - sweep, block)

time: 58.3 us -> 58.6 us (level)
  no operation moved by 1% of the time
where the time goes in v10:
time: 58.6 us; the launch traced here: 58.2 us
  Pallas kernels  27.4 us (47%)
  starting transfers between devices  24.6 us (42%)
  waiting for transfers between devices  4.47 us (8%)
  between operations  1.61 us (3%)
    ppermute x2, starting transfers between devices, exchange_sides(): lax.ppermute(left, 'lon', backward)  9.46 us
    pallas_call x1, Pallas kernels, body(): pl.pallas_call(functools.partial(owner_kernel, devices_all, quarter), out...  7.03 us
    pallas_call x1, Pallas kernels, body(): pl.pallas_call(inner_kernel, out_shape=(pltpu.HBM(control.shape, F32), pl...  6.38 us
    all_to_all x1, starting transfers between devices, body(): lax.all_to_all(payload.reshape(devices_all, 1, (quarter + 1) * 128), ('la...  6.02 us
    pallas_call x1, Pallas kernels, body(): pl.pallas_call(forward_kernel, out_shape=(pltpu.VMEM((columns // 4, 8 * c...  5.44 us
    all_to_all x1, starting transfers between devices, body(): lax.all_to_all(returned.reshape(devices_all, quarter, 128), ('lat', 'lon'...  5.24 us
    ppermute x2, starting transfers between devices, exchange_rims(): lax.ppermute(top, 'lat', backward)  3.57 us
    pallas_call x1, Pallas kernels, body(): pl.pallas_call(functools.partial(address_kernel, devices_all, quarter), o...  2.39 us
  transfers between devices with their start and end apart: 10, of which 3 were waited for; matrix products, arithmetic and copies ran while one was open for 0% of the time, Pallas kernels for 30%

profile of v10, /device:TPU:0, one launch (start us, length us, event | category | flops | bytes accessed | tf_op | source)
XLA Modules:
  0.0 58.2 jit_solution(17476623271553037383)
XLA Ops:
  0.7 1.2 %pack.1 = (bf16[2,64,4,128]{3,2,1,0:T(4,128)(2,1)S(1)}, bf16[2,64,4,128]{3,2,1,0:T(4,128)(2,1)S(1)}) custom-call(f32[64,64,128]{2,1,0:T(8,128)} %control_hbm.7, f32[64,64]{1,0:T(8,128)} %kappa_ref.5), custom_call_target="tpu_custom_call" | custom-call | tf_op jit(solution)/shard_map/pack/pallas_call | solution.py:658
  1.9 6.1 %collective-permute-start = (bf16[2,64,4,128]{3,2,1,0:T(4,128)(2,1)S(1)}, bf16[2,64,4,128]{3,2,1,0:T(4,128)(2,1)S(1)}, u32[]{:S(2)}, u32[]{:S(2)}) collective-permute-start(bf16[2,64,4,128]{3,2,1,0:T(4,128)(2,1)S(1)} %get-tuple-element.30), channel_id=1, source_target_pairs={{1,0},{2,1},{3,2},{4,3},{5,4},{6,5},{7,6},{0,7},{9,8},{10,9},{11,1... | collective-permute-start | bytes 393224 | tf_op jit(solution)/shard_map/ppermute | solution.py:618
  7.9 0.0 collective-permute-start.1
  8.6 0.0 copy-start
  8.6 0.0 copy-start.3
  8.7 0.0 copy-start.7
  8.7 2.4 %address.1 = (s32[544,128]{1,0:T(8,128)}, s32[1,1024]{1,0:T(1,128)S(1)}, bf16[2,4,64,128]{3,2,1,0:T(8,128)(2,1)S(1)}, bf16[2,4,64,128]{3,2,1,0:T(8,128)(2,1)S(1)}) custom-call(s32[1,1024]{1,0:T(1,128)S(1)} %bitcast.18, s32[1,1024]{1,0:T(1,128)S(1)} %bitcast.19, f32[1,1024]{1,0:T(1,128)S(1)} %bitcast.14, f32[64,1024]{1,0:T(8,128)S(1)} %bitcast.16, ...), custom_call_target="tpu_custom_call" | custom-call | flops 2000000000 | bytes 8000000 | tf_op jit(solution)/shard_map/address/pallas_call | solution.py:678
  11.1 6.0 %all-to-all-start = ((s32[32,1,2176]{2,1,0:T(1,128)}), s32[32,1,2176]{2,1,0:T(1,128)S(1)}, u32[]{:S(2)}, u32[]{:S(2)}) async-start(s32[32,1,2176]{2,1,0:T(1,128)} %bitcast.5), calls=%async_computation | async-start | bytes 557056 | tf_op jit(solution)/shard_map/all_to_all | solution.py:704
  17.1 0.0 collective-permute-done.east_ref.keast_ref
  17.1 0.0 collective-permute-done.1.west_ref.kwest_ref
  17.2 1.6 %collective-permute-start.3 = (bf16[2,4,72,128]{3,2,1,0:T(8,128)(2,1)S(1)}, bf16[2,4,72,128]{3,2,1,0:T(8,128)(2,1)S(1)}, u32[]{:S(2)}, u32[]{:S(2)}) collective-permute-start(bf16[2,4,72,128]{3,2,1,0:T(8,128)(2,1)S(1)} %pad_maximum_fusion.1), channel_id=1, source_target_pairs={{8,0},{16,8},{24,16},{0,24},{9,1},{17,9},{25,17},{1,25},{10,2},{18... | collective-permute-start | bytes 442376 | tf_op jit(solution)/shard_map/ppermute | solution.py:623
  18.8 0.2 collective-permute-start.2
  19.0 5.4 %forward.1 = (bf16[1024,512]{1,0:T(8,128)(2,1)S(1)}, bf16[256,512]{1,0:T(8,128)(2,1)S(1)}, f32[16,96,128]{2,1,0:T(8,128)S(1)}, f32[16,96,128]{2,1,0:T(8,128)S(1)}, f32[2,4,64,128]{3,2,1,0:T(8,128)S(1)}) custom-call(f32[64,64,128]{2,1,0:T(8,128)} %control_hbm.7, f32[64,64,128]{2,1,0:T(8,128)} %sigma_hbm.3, ...), custom_call_target="tpu_custom_call" | custom-call | flops 4000000000 | bytes 16000000 | tf_op jit(solution)/shard_map/forward/pallas_call | solution.py:719
  24.5 0.0 copy-start.4
  24.5 0.0 collective-permute-done.3.south_ref.ksouth_ref
  24.5 1.2 %collective-permute-done.2.north_ref.knorth_ref = bf16[2,4,72,128]{3,2,1,0:T(8,128)(2,1)S(1)} collective-permute-done((bf16[2,4,72,128]{3,2,1,0:T(8,128)(2,1)S(1)}, bf16[2,4,72,128]{3,2,1,0:T(8,128)(2,1)S(1)}, u32[]{:S(2)}, u32[]{:S(2)}) %collective-permute-start.2) | collective-permute-done | bytes 147488 | tf_op jit(solution)/shard_map/ppermute | solution.py:623
  25.7 1.1 %ends.1.ends_ref = bf16[2,64,512]{2,1,0:T(8,128)(2,1)S(1)} custom-call(f32[16,96,128]{2,1,0:T(8,128)S(1)} %get-tuple-element.33.rim_ref, f32[16,96,128]{2,1,0:T(8,128)S(1)} %get-tuple-element.34.rim_kap_ref, f32[2,4,64,128]{3,2,1,0:T(8,128)S(1)} %get-tuple-element.35.sigma_ref, bf16[2,4,72,128]{3,2,1,0:T(8,128)(2,1)S(1)} %collective-permute-done.2.north_ref.knorth_ref, ...), custom_call_target="tpu_custom_call" | custom-call | flops 1000000000 | bytes 2000000 | tf_op jit(solution)/shard_map/ends/pallas_call | solution.py:740
  26.8 1.4 %all-to-all-done = s32[32,1,2176]{2,1,0:T(1,128)S(1)} async-done(((s32[32,1,2176]{2,1,0:T(1,128)}), s32[32,1,2176]{2,1,0:T(1,128)S(1)}, u32[]{:S(2)}, u32[]{:S(2)}) %all-to-all-start) | async-done | bytes 278560 | tf_op jit(solution)/shard_map/all_to_all | solution.py:704
  28.2 7.0 %owner.1 = (s32[512,128]{1,0:T(8,128)}, f32[64,64,128]{2,1,0:T(8,128)}, bf16[64,4,128]{2,1,0:T(4,128)(2,1)}, bf16[64,4,128]{2,1,0:T(4,128)(2,1)}, bf16[4,64,128]...) custom-call(s32[544,128]{1,0:T(8,128)S(1)} %bitcast.12, f32[64,64,128]{2,1,0:T(8,128)} %sigma_hbm.3, ...), custom_call_target="tpu_custom_call" | custom-call | flops 4000000000 | bytes 16000000 | tf_op jit(solution)/shard_map/owner/pallas_call | solution.py:751
  35.2 3.4 %collective-permute-start.4 = (bf16[64,4,128]{2,1,0:T(4,128)(2,1)}, bf16[64,4,128]{2,1,0:T(4,128)(2,1)S(1)}, u32[]{:S(2)}, u32[]{:S(2)}) collective-permute-start(bf16[64,4,128]{2,1,0:T(4,128)(2,1)} %get-tuple-element.40.first_hbm), channel_id=1, source_target_pairs={{1,0},{2,1},{3,2},{4,3},{5,4},{6,5},{7,6},{0,7},{9,8},{10,9},{11,1... | collective-permute-start | bytes 196616 | tf_op jit(solution)/shard_map/ppermute | solution.py:618
  38.6 0.0 collective-permute-start.5
  38.6 5.2 %all-to-all-start.1 = ((s32[32,16,128]{2,1,0:T(8,128)}), s32[32,16,128]{2,1,0:T(8,128)S(1)}, u32[]{:S(2)}, u32[]{:S(2)}) async-start(s32[32,16,128]{2,1,0:T(8,128)} %bitcast.21), calls=%async_computation.1 | async-start | bytes 524288 | tf_op jit(solution)/shard_map/all_to_all | solution.py:792
  43.9 0.0 collective-permute-done.4.east_ref
  43.9 1.9 %collective-permute-done.5.west_ref = bf16[64,4,128]{2,1,0:T(4,128)(2,1)S(1)} collective-permute-done((bf16[64,4,128]{2,1,0:T(4,128)(2,1)}, bf16[64,4,128]{2,1,0:T(4,128)(2,1)S(1)}, u32[]{:S(2)}, u32[]{:S(2)}) %collective-permute-start.5) | collective-permute-done | bytes 65568 | tf_op jit(solution)/shard_map/ppermute | solution.py:618
  45.8 0.1 collective-permute-start.6
  45.9 2.0 %collective-permute-start.7 = (bf16[4,72,128]{2,1,0:T(8,128)(2,1)S(1)}, bf16[4,72,128]{2,1,0:T(8,128)(2,1)S(1)}, u32[]{:S(2)}, u32[]{:S(2)}) collective-permute-start(bf16[4,72,128]{2,1,0:T(8,128)(2,1)S(1)} %pad_maximum_fusion.3), channel_id=1, source_target_pairs={{8,0},{16,8},{24,16},{0,24},{9,1},{17,9},{25,17},{1,25},{10,2},{18... | collective-permute-start | bytes 221192 | tf_op jit(solution)/shard_map/ppermute | solution.py:623
  47.9 6.4 %inner.1 = (f32[64,64,128]{2,1,0:T(8,128)}, f32[16,96,128]{2,1,0:T(8,128)S(1)}, f32[16,96,128]{2,1,0:T(8,128)S(1)}, f32[2,4,64,128]{3,2,1,0:T(8,128)S(1)}) custom-call(f32[64,64,128]{2,1,0:T(8,128)} %get-tuple-element.39.adj_hbm, f32[64,64,128]{2,1,0:T(8,128)} %control_hbm.7, bf16[64,4,128]{2,1,0:T(4,128)(2,1)S(1)} %collective-permute-done.4.east_ref, ...), custom_call_target="tpu_custom_call" | custom-call | flops 4000000000 | bytes 16000000 | tf_op jit(solution)/shard_map/inner/pallas_call | solution.py:805
  54.3 0.0 collective-permute-done.6.north_ref
  54.3 0.0 collective-permute-done.7.south_ref
  54.3 1.9 %rims.1 = f32[64,64,128]{2,1,0:T(8,128)} custom-call(f32[16,96,128]{2,1,0:T(8,128)S(1)} %get-tuple-element.42.rim_ref, f32[16,96,128]{2,1,0:T(8,128)S(1)} %get-tuple-element.43.rim_kap_ref, f32[2,4,64,128]{3,2,1,0:T(8,128)S(1)} %get-tuple-element.44.control_ref, ...), custom_call_target="tpu_custom_call", output_to_operand_aliasing={{}: (8, {})} | custom-call | flops 1000000000 | bytes 2000000 | tf_op jit(solution)/shard_map/rims/pallas_call | solution.py:823
  56.2 0.0 all-to-all-done.1
  56.2 2.0 %give_back.1 = f32[64,1024]{1,0:T(8,128)} custom-call(s32[512,128]{1,0:T(8,128)S(1)} %bitcast.13, s32[1,1024]{1,0:T(1,128)S(1)} %get-tuple-element.49.key_ref, f32[64,1024]{1,0:T(8,128)S(1)} %bitcast.17, f32[1,1024]{1,0:T(1,128)S(1)} %bitcast.15, f32[64,64]{1,0:T(8,128)S(1)} %copy-done.4), custom_call_target="tpu_custom_call" | custom-call | flops 500000000 | bytes 2000000 | tf_op jit(solution)/shard_map/give_back/pallas_call | solution.py:841
  (24 shorter events, 0.1 us)
Async XLA Ops:
  0.6 8.0 %copy-start.1 = (f32[64,64]{1,0:T(8,128)S(1)}, f32[64,64]{1,0:T(8,128)}, u32[]{:S(2)}) copy-start(f32[64,64]{1,0:T(8,128)} %kappa_ref.5) | copy-start | bytes 49156
  0.6 8.0 %copy-start.6 = (s32[1024]{0:T(1024)S(1)}, s32[1024]{0:T(1024)}, u32[]{:S(2)}) copy-start(s32[1024]{0:T(1024)} %param.22) | copy-start | bytes 12292
  0.7 7.9 %copy-start.8 = (f32[1024]{0:T(1024)S(1)}, f32[1024]{0:T(1024)}, u32[]{:S(2)}) copy-start(f32[1024]{0:T(1024)} %param.20) | copy-start | bytes 12292
  0.7 8.0 %copy-start.5 = (s32[1024,1]{0,1:T(1,128)S(1)}, s32[1024,1]{0,1:T(1,128)}, u32[]{:S(2)}) copy-start(s32[1024,1]{0,1:T(1,128)} %param.21) | copy-start | bytes 12292
  0.7 8.0 %copy-start.2 = (f32[1024,64]{0,1:T(8,128)S(1)}, f32[1024,64]{0,1:T(8,128)}, u32[]{:S(2)}) copy-start(f32[1024,64]{0,1:T(8,128)} %param.19) | copy-start | bytes 786436
  1.9 15.2 %collective-permute-start = (bf16[2,64,4,128]{3,2,1,0:T(4,128)(2,1)S(1)}, bf16[2,64,4,128]{3,2,1,0:T(4,128)(2,1)S(1)}, u32[]{:S(2)}, u32[]{:S(2)}) collective-permute-start(bf16[2,64,4,128]{3,2,1,0:T(4,128)(2,1)S(1)} %get-tuple-element.30), channel_id=1, source_target_pairs={{1,0},{2,1},{3,2},{4,3},{5,4},{6,5},{7,6},{0,7},{9,8},{10,9},{11,1... | collective-permute-start | bytes 393224 | tf_op jit(solution)/shard_map/ppermute | solution.py:618
  7.9 9.2 %collective-permute-start.1 = (bf16[2,64,4,128]{3,2,1,0:T(4,128)(2,1)S(1)}, bf16[2,64,4,128]{3,2,1,0:T(4,128)(2,1)S(1)}, u32[]{:S(2)}, u32[]{:S(2)}) collective-permute-start(bf16[2,64,4,128]{3,2,1,0:T(4,128)(2,1)S(1)} %get-tuple-element.31), channel_id=1, source_target_pairs={{0,1},{1,2},{2,3},{3,4},{4,5},{5,6},{6,7},{7,0},{8,9},{9,10},{10,1... | collective-permute-start | bytes 393224 | tf_op jit(solution)/shard_map/ppermute | solution.py:618
  8.6 10.4 %copy-start = (f32[128,128]{1,0:T(8,128)S(1)}, f32[128,128]{1,0:T(8,128)}, u32[]{:S(2)}) copy-start(f32[128,128]{1,0:T(8,128)} %vertical_ref.7) | copy-start | bytes 196612
  8.6 10.4 %copy-start.3 = (bf16[616,128]{1,0:T(8,128)(2,1)S(1)}, bf16[616,128]{1,0:T(8,128)(2,1)}, u32[]{:S(2)}) copy-start(bf16[616,128]{1,0:T(8,128)(2,1)} %table_ref.1) | copy-start | bytes 473092
  8.7 10.4 %copy-start.7 = (s32[64]{0:T(128)S(1)}, s32[64]{0:T(128)}, u32[]{:S(2)}) copy-start(s32[64]{0:T(128)} %param.17) | copy-start | bytes 772
  11.1 17.1 %all-to-all-start = ((s32[32,1,2176]{2,1,0:T(1,128)}), s32[32,1,2176]{2,1,0:T(1,128)S(1)}, u32[]{:S(2)}, u32[]{:S(2)}) async-start(s32[32,1,2176]{2,1,0:T(1,128)} %bitcast.5), calls=%async_computation | async-start | bytes 557056 | tf_op jit(solution)/shard_map/all_to_all | solution.py:704
  17.2 7.3 %collective-permute-start.3 = (bf16[2,4,72,128]{3,2,1,0:T(8,128)(2,1)S(1)}, bf16[2,4,72,128]{3,2,1,0:T(8,128)(2,1)S(1)}, u32[]{:S(2)}, u32[]{:S(2)}) collective-permute-start(bf16[2,4,72,128]{3,2,1,0:T(8,128)(2,1)S(1)} %pad_maximum_fusion.1), channel_id=1, source_target_pairs={{8,0},{16,8},{24,16},{0,24},{9,1},{17,9},{25,17},{1,25},{10,2},{18... | collective-permute-start | bytes 442376 | tf_op jit(solution)/shard_map/ppermute | solution.py:623
  18.8 6.9 %collective-permute-start.2 = (bf16[2,4,72,128]{3,2,1,0:T(8,128)(2,1)S(1)}, bf16[2,4,72,128]{3,2,1,0:T(8,128)(2,1)S(1)}, u32[]{:S(2)}, u32[]{:S(2)}) collective-permute-start(bf16[2,4,72,128]{3,2,1,0:T(8,128)(2,1)S(1)} %pad_maximum_fusion), channel_id=1, source_target_pairs={{0,8},{8,16},{16,24},{24,0},{1,9},{9,17},{17,25},{25,1},{2,10},{10... | collective-permute-start | bytes 442376 | tf_op jit(solution)/shard_map/ppermute | solution.py:623
  24.5 3.7 %copy-start.4 = (f32[64,64]{1,0:T(8,128)S(1)}, f32[64,64]{1,0:T(8,128)}, u32[]{:S(2)}) copy-start(f32[64,64]{1,0:T(8,128)} %rinv_ref.3) | copy-start | bytes 49156
  35.2 8.7 %collective-permute-start.4 = (bf16[64,4,128]{2,1,0:T(4,128)(2,1)}, bf16[64,4,128]{2,1,0:T(4,128)(2,1)S(1)}, u32[]{:S(2)}, u32[]{:S(2)}) collective-permute-start(bf16[64,4,128]{2,1,0:T(4,128)(2,1)} %get-tuple-element.40.first_hbm), channel_id=1, source_target_pairs={{1,0},{2,1},{3,2},{4,3},{5,4},{6,5},{7,6},{0,7},{9,8},{10,9},{11,1... | collective-permute-start | bytes 196616 | tf_op jit(solution)/shard_map/ppermute | solution.py:618
  38.6 7.2 %collective-permute-start.5 = (bf16[64,4,128]{2,1,0:T(4,128)(2,1)}, bf16[64,4,128]{2,1,0:T(4,128)(2,1)S(1)}, u32[]{:S(2)}, u32[]{:S(2)}) collective-permute-start(bf16[64,4,128]{2,1,0:T(4,128)(2,1)} %get-tuple-element.41.second_hbm), channel_id=1, source_target_pairs={{0,1},{1,2},{2,3},{3,4},{4,5},{5,6},{6,7},{7,0},{8,9},{9,10},{10,1... | collective-permute-start | bytes 196616 | tf_op jit(solution)/shard_map/ppermute | solution.py:618
  38.6 17.6 %all-to-all-start.1 = ((s32[32,16,128]{2,1,0:T(8,128)}), s32[32,16,128]{2,1,0:T(8,128)S(1)}, u32[]{:S(2)}, u32[]{:S(2)}) async-start(s32[32,16,128]{2,1,0:T(8,128)} %bitcast.21), calls=%async_computation.1 | async-start | bytes 524288 | tf_op jit(solution)/shard_map/all_to_all | solution.py:792
  45.8 8.5 %collective-permute-start.6 = (bf16[4,72,128]{2,1,0:T(8,128)(2,1)S(1)}, bf16[4,72,128]{2,1,0:T(8,128)(2,1)S(1)}, u32[]{:S(2)}, u32[]{:S(2)}) collective-permute-start(bf16[4,72,128]{2,1,0:T(8,128)(2,1)S(1)} %pad_maximum_fusion.2), channel_id=1, source_target_pairs={{0,8},{8,16},{16,24},{24,0},{1,9},{9,17},{17,25},{25,1},{2,10},{10... | collective-permute-start | bytes 221192 | tf_op jit(solution)/shard_map/ppermute | solution.py:623
  45.9 8.4 %collective-permute-start.7 = (bf16[4,72,128]{2,1,0:T(8,128)(2,1)S(1)}, bf16[4,72,128]{2,1,0:T(8,128)(2,1)S(1)}, u32[]{:S(2)}, u32[]{:S(2)}) collective-permute-start(bf16[4,72,128]{2,1,0:T(8,128)(2,1)S(1)} %pad_maximum_fusion.3), channel_id=1, source_target_pairs={{8,0},{16,8},{24,16},{0,24},{9,1},{17,9},{25,17},{1,25},{10,2},{18... | collective-permute-start | bytes 221192 | tf_op jit(solution)/shard_map/ppermute | solution.py:623
